TPU v7x, 512 devices: a whole 4x8x8 slice. The times are simulated.
512 devices in a mesh: seq: 64 (over y, z_lo, core), tensor: 8 (over z_hi, x).
Axes of the slice: x: 4, y: 8, z: 8 (z_hi: 2, z_lo: 4; z = z_hi * 4 + z_lo), core: 2. Of those that a mesh axis runs over, the one named last changes fastest.
Arguments:
- queries: bfloat16 [16384, 3072], P('seq', 'tensor'), may hold values from -100 to 100
- key_tiles: bfloat16 [16384, 3072], P('seq', 'tensor'), may hold values from -6 to 6
- value_tiles: bfloat16 [16384, 3072], P('seq', 'tensor'), may hold values from -6 to 6
- cache_keys: bfloat16 [128, 128, 3072], P('seq', None, 'tensor'), may hold values from -6 to 6
- cache_values: bfloat16 [128, 128, 3072], P('seq', None, 'tensor'), may hold values from -6 to 6
- hidden: bfloat16 [16384, 5120], P('seq', 'tensor'), may hold values from -6 to 6
- out_weight: bfloat16 [3072, 5120], P('seq', 'tensor'), may hold values from -0.21875 to 0.21875
- gate_table: float32 [1000, 5120], P(None, 'tensor'), may hold values from 0.3 to 2.5
- lengths: int32 [16], replicated, may hold values from 512 to 1536, as said below
- page_table: int32 [16, 4], replicated, may hold values from 0 to 127, as said below
- page_count: int32 [16], replicated, may hold values from 0 to 4
- timestep: int32 [16], replicated, may hold values from 0 to 999
Outputs:
- layer_out: bfloat16 [16384, 5120], P('seq', 'tensor')
Inputs may be any that keep to these rules, and one draw needn't show every extreme that they name: The lengths sum to 16384. `page_table`: a page named by clip c lies on a seq index that holds some token of clip c (page p lies on seq index p // 2); a page may be named by several clips or twice.
All inputs are finite; a program needn't handle non-finite values.
Results may differ from a plain program's by a relative error of at most 0.018.
Values may be sent and summed in bfloat16 or wider, within the bound.
No kernel may reach another device: no remote copies, remote signals or barrier semaphores. Data moves between devices by JAX's collectives and lax.ppermute only.
A program may use at most 64 MiB of HBM per device.

v0:
```python
import math

import jax
import jax.numpy as jnp
from jax import lax
from jax.sharding import PartitionSpec as P

HD = 128
PAGE = 128
POOL = 2
REACH = 6


low_score = -1e30


def shifted(block, axis, distance):
    devices = range(lax.axis_size(axis))
    route = [(i - distance, i) for i in devices if i - distance in devices]
    return lax.ppermute(block, axis, route)


def clip_index(positions, clip_ends):
    return jnp.sum((positions[:, None] >= clip_ends[None, :]).astype(jnp.int32), axis=1)


def allowed_keys(query_clip, source, clip_ends, page_table, page_count, block_total, row_count):
    key_pos = source * row_count + jnp.arange(row_count, dtype=jnp.int32)
    in_range = (source >= 0) & (source < block_total)
    same_clip = (query_clip[:, None] == clip_index(key_pos, clip_ends)[None, :]) & in_range
    clip_total = clip_ends.shape[0]
    page_ids = source * POOL + jnp.arange(POOL, dtype=jnp.int32)
    live_slots = jnp.arange(page_table.shape[1], dtype=jnp.int32)[None, :] < page_count[:, None]
    named_pages = jnp.any(
        live_slots[:, :, None] & (page_table[:, :, None] == page_ids[None, None, :]), axis=1
    )
    member = query_clip[:, None] == jnp.arange(clip_total, dtype=jnp.int32)[None, :]
    page_ok = jnp.any(member[:, :, None] & named_pages[None], axis=1) & in_range
    page_ok = jnp.repeat(page_ok, PAGE, axis=1)
    return jnp.concatenate([same_clip, page_ok], axis=1)


def attend(carry_state, query_heads, key_heads, value_heads, allowed):
    running_max, totals, accumulated = carry_state
    scores = jnp.einsum(
        "qhd,khd->hqk", query_heads, key_heads, preferred_element_type=jnp.float32
    ) * (1.0 / math.sqrt(HD))
    scores = jnp.where(allowed[None], scores, low_score)
    new_max = jnp.maximum(running_max, jnp.max(scores, axis=2))
    factor = jnp.exp(running_max - new_max)
    weights = jnp.where(allowed[None], jnp.exp(scores - new_max[:, :, None]), 0.0)
    totals = totals * factor + jnp.sum(weights, axis=2)
    accumulated = accumulated * factor[:, :, None] + jnp.einsum(
        "hqk,khd->hqd",
        weights.astype(jnp.bfloat16),
        value_heads,
        preferred_element_type=jnp.float32,
    )
    return (new_max, totals, accumulated)


def empty_state(head_count, row_count):
    return (
        jnp.full((head_count, row_count), low_score, jnp.float32),
        jnp.zeros((head_count, row_count), jnp.float32),
        jnp.zeros((head_count, row_count, HD), jnp.float32),
    )


def visit_block(carry_state, packed, source, query_heads, query_clip, context):
    clip_ends, page_table, page_count, block_total = context
    row_count = query_heads.shape[0]
    head_count = query_heads.shape[1]
    allowed = allowed_keys(
        query_clip, source, clip_ends, page_table, page_count, block_total, row_count
    )
    key_heads = packed[0].reshape(-1, head_count, HD)
    value_heads = packed[1].reshape(-1, head_count, HD)
    return attend(carry_state, query_heads, key_heads, value_heads, allowed)


def fetch_direct(packed, offset):
    return shifted(packed, "seq", offset)


def local(
    queries,
    key_tiles,
    value_tiles,
    cache_keys,
    cache_values,
    hidden,
    out_weight,
    gate_table,
    lengths,
    page_table,
    page_count,
    timestep,
):
    row_count = queries.shape[0]
    tile_width = queries.shape[1]
    head_count = tile_width // HD
    block_total = lax.axis_size("seq")
    seq_index = lax.axis_index("seq")
    clip_ends = jnp.cumsum(lengths, dtype=jnp.int32)
    row_ids = jnp.arange(row_count, dtype=jnp.int32)
    positions = seq_index * row_count + row_ids
    query_clip = clip_index(positions, clip_ends)
    query_heads = queries.reshape(row_count, head_count, HD)
    context = (clip_ends, page_table, page_count, block_total)
    packed = jnp.stack(
        [
            jnp.concatenate([key_tiles, cache_keys.reshape(-1, tile_width)], axis=0),
            jnp.concatenate([value_tiles, cache_values.reshape(-1, tile_width)], axis=0),
        ]
    )
    carry_state = visit_block(
        empty_state(head_count, row_count), packed, seq_index, query_heads, query_clip, context
    )
    for offset in range(1, REACH + 1):
        from_below = fetch_direct(packed, offset)
        carry_state = visit_block(
            carry_state, from_below, seq_index - offset, query_heads, query_clip, context
        )
        from_above = fetch_direct(packed, -offset)
        carry_state = visit_block(
            carry_state, from_above, seq_index + offset, query_heads, query_clip, context
        )
    running_max, totals, accumulated = carry_state
    result = accumulated / totals[:, :, None]
    attention_local = (
        jnp.transpose(result, (1, 0, 2)).reshape(row_count, tile_width).astype(jnp.bfloat16)
    )
    attention = lax.all_gather(attention_local, "tensor", axis=1, tiled=True)
    projected = jnp.dot(
        attention,
        lax.all_gather(out_weight, "seq", axis=0, tiled=True),
        preferred_element_type=jnp.float32,
    )
    clip_total = lengths.shape[0]
    step_onehot = (
        timestep[:, None] == jnp.arange(gate_table.shape[0], dtype=jnp.int32)[None, :]
    ).astype(jnp.float32)
    clip_gate = jnp.dot(
        step_onehot, gate_table, precision=lax.Precision.HIGHEST, preferred_element_type=jnp.float32
    )
    clip_onehot = (query_clip[:, None] == jnp.arange(clip_total, dtype=jnp.int32)[None, :]).astype(
        jnp.float32
    )
    token_gate = jnp.dot(
        clip_onehot, clip_gate, precision=lax.Precision.HIGHEST, preferred_element_type=jnp.float32
    )
    return (hidden.astype(jnp.float32) + token_gate * projected).astype(jnp.bfloat16)


def solution(mesh):
    return jax.shard_map(
        local,
        mesh=mesh,
        in_specs=(
            P("seq", "tensor"),
            P("seq", "tensor"),
            P("seq", "tensor"),
            P("seq", None, "tensor"),
            P("seq", None, "tensor"),
            P("seq", "tensor"),
            P("seq", "tensor"),
            P(None, "tensor"),
            P(),
            P(),
            P(),
            P(),
        ),
        out_specs=P("seq", "tensor"),
        check_vma=False,
    )
```

profile of v0, /device:TPU:1, one launch (start us, length us, event | category | flops | bytes accessed | tf_op | source)
XLA Modules:
  0.0 506.3 jit_solution(10120251715169249315)
XLA Ops:
  6.5 1.2 copy.107
  12.1 1.3 collective-permute-start.9
  13.4 10.5 %collective-permute-start.8 = (bf16[2,512,384]{1,2,0:T(8,128)(2,1)}, bf16[2,512,384]{1,2,0:T(8,128)(2,1)}, u32[]{:S(2)}, u32[]{:S(2)}) collective-permute-start(bf16[2,512,384]{1,2,0:T(8,128)(2,1)} %pad_maximum_fusion), channel_id=1, source_target_pairs={{0,40},{8,48},{16,56},{24,64},{32,72},{40,80},{48,88},{56,96},{64,... | collective-permute-start | bytes 2359304 | tf_op jit(solution)/shard_map/ppermute | solution.py:20
  23.9 1.3 collective-permute-start.7
  25.2 5.8 %collective-permute-start.6 = (bf16[2,512,384]{1,2,0:T(8,128)(2,1)}, bf16[2,512,384]{1,2,0:T(8,128)(2,1)}, u32[]{:S(2)}, u32[]{:S(2)}) collective-permute-start(bf16[2,512,384]{1,2,0:T(8,128)(2,1)} %pad_maximum_fusion), channel_id=1, source_target_pairs={{0,32},{8,40},{16,48},{24,56},{32,64},{40,72},{48,80},{56,88},{64,... | collective-permute-start | bytes 2359304 | tf_op jit(solution)/shard_map/ppermute | solution.py:20
  31.0 1.3 collective-permute-start.5
  41.8 2.6 fusion.175
  46.5 1.8 copy.114
  48.3 1.7 concatenate.64
  50.0 5.2 %collective-permute-start.4 = (bf16[2,512,384]{1,2,0:T(8,128)(2,1)}, bf16[2,512,384]{1,2,0:T(8,128)(2,1)S(1)}, u32[]{:S(2)}, u32[]{:S(2)}) collective-permute-start(bf16[2,512,384]{1,2,0:T(8,128)(2,1)} %pad_maximum_fusion), channel_id=1, source_target_pairs={{0,24},{8,32},{16,40},{24,48},{32,56},{40,64},{48,72},{56,80},{64,... | collective-permute-start | bytes 2359304 | tf_op jit(solution)/shard_map/ppermute | solution.py:20
  56.4 64.8 %collective-permute-done.8 = bf16[2,512,384]{1,2,0:T(8,128)(2,1)} collective-permute-done((bf16[2,512,384]{1,2,0:T(8,128)(2,1)}, bf16[2,512,384]{1,2,0:T(8,128)(2,1)}, u32[]{:S(2)}, u32[]{:S(2)}) %collective-permute-start.8) | collective-permute-done | bytes 786464 | tf_op jit(solution)/shard_map/ppermute | solution.py:20
  121.2 1.3 collective-permute-start.3
  122.5 1.2 fusion.154
  123.7 4.0 collective-permute-start.2
  127.7 1.2 fusion.155
  128.9 9.2 %collective-permute-done.6 = bf16[2,512,384]{1,2,0:T(8,128)(2,1)} collective-permute-done((bf16[2,512,384]{1,2,0:T(8,128)(2,1)}, bf16[2,512,384]{1,2,0:T(8,128)(2,1)}, u32[]{:S(2)}, u32[]{:S(2)}) %collective-permute-start.6) | collective-permute-done | bytes 786464 | tf_op jit(solution)/shard_map/ppermute | solution.py:20
  138.0 43.7 %collective-permute-start.1 = (bf16[2,512,384]{1,2,0:T(8,128)(2,1)}, bf16[2,512,384]{1,2,0:T(8,128)(2,1)S(1)}, u32[]{:S(2)}, u32[]{:S(2)}) collective-permute-start(bf16[2,512,384]{1,2,0:T(8,128)(2,1)} %pad_maximum_fusion), channel_id=1, source_target_pairs={{8,0},{16,8},{24,16},{32,24},{40,32},{48,40},{56,48},{64,56},{72,6... | collective-permute-start | bytes 2359304 | tf_op jit(solution)/shard_map/ppermute | solution.py:20
  182.9 23.6 %collective-permute-start.10 = (bf16[2,512,384]{1,2,0:T(8,128)(2,1)}, bf16[2,512,384]{1,2,0:T(8,128)(2,1)S(1)}, u32[]{:S(2)}, u32[]{:S(2)}) collective-permute-start(bf16[2,512,384]{1,2,0:T(8,128)(2,1)} %pad_maximum_fusion), channel_id=1, source_target_pairs={{0,48},{8,56},{16,64},{24,72},{32,80},{40,88},{48,96},{56,104},{64... | collective-permute-start | bytes 2359304 | tf_op jit(solution)/shard_map/ppermute | solution.py:20
  207.7 34.8 %collective-permute-start = (bf16[2,512,384]{1,2,0:T(8,128)(2,1)}, bf16[2,512,384]{1,2,0:T(8,128)(2,1)S(1)}, u32[]{:S(2)}, u32[]{:S(2)}) collective-permute-start(bf16[2,512,384]{1,2,0:T(8,128)(2,1)} %pad_maximum_fusion), channel_id=1, source_target_pairs={{0,8},{8,16},{16,24},{24,32},{32,40},{40,48},{48,56},{56,64},{64,7... | collective-permute-start | bytes 2359304 | tf_op jit(solution)/shard_map/ppermute | solution.py:20
  243.1 1.5 collective-permute-start.11
  249.5 19.1 %collective-permute-done = bf16[2,512,384]{1,2,0:T(8,128)(2,1)S(1)} collective-permute-done((bf16[2,512,384]{1,2,0:T(8,128)(2,1)}, bf16[2,512,384]{1,2,0:T(8,128)(2,1)S(1)}, u32[]{:S(2)}, u32[]{:S(2)}) %collective-permute-start) | collective-permute-done | bytes 786464 | tf_op jit(solution)/shard_map/ppermute | solution.py:20
  284.8 89.4 %all-gather.3.cloned.1.call-done = bf16[256,3072]{0,1:T(8,128)(2,1)} async-done(((bf16[256,384]{0,1:T(8,128)(2,1)}), bf16[256,3072]{0,1:T(8,128)(2,1)}) %all-gather.3.cloned.1.call-update) | async-done | bytes 1572880 | tf_op jit(solution)/shard_map/all_gather | solution.py:134
  374.2 120.5 %all-gather.5.cloned.1.call-done = bf16[3072,640]{1,0:T(8,128)(2,1)} async-done(((bf16[48,640]{1,0:T(8,128)(2,1)}), bf16[3072,640]{1,0:T(8,128)(2,1)}) %all-gather.5.cloned.1.call-update) | async-done | bytes 3932176 | tf_op jit(solution)/shard_map/all_gather | solution.py:137
  494.7 4.7 fusion.27
  (180 shorter events, 40.2 us)
Async XLA Ops:
  6.5 276.8 %copy-start = (f32[1000,640]{1,0:T(8,128)S(1)}, f32[1000,640]{1,0:T(8,128)}, u32[]{:S(2)}) copy-start(f32[1000,640]{1,0:T(8,128)} %param.19) | copy-start | bytes 7680004
  6.5 367.7 %all-gather.3.cloned.1.call-start = ((), (), s32[]{:S(2)}) async-start(), calls=%async_computation | async-start | bytes 1769472 | tf_op jit(solution)/shard_map/all_gather | solution.py:134
  11.0 21.4 %copy-start.8 = (bf16[2,128,384]{2,1,0:T(8,128)(2,1)S(1)}, bf16[2,128,384]{2,1,0:T(8,128)(2,1)}, u32[]{:S(2)}) copy-start(bf16[2,128,384]{2,1,0:T(8,128)(2,1)} %param.15) | copy-start | bytes 589828
  11.0 21.4 %copy-start.17 = (s32[16]{0:T(128)S(1)}, s32[16]{0:T(128)}, u32[]{:S(2)}) copy-start(s32[16]{0:T(128)} %param.20) | copy-start | bytes 196
  11.1 22.5 %copy-start.20 = (s32[16]{0:T(128)S(1)}, s32[16]{0:T(128)}, u32[]{:S(2)}) copy-start(s32[16]{0:T(128)} %param.22) | copy-start | bytes 196
  11.1 25.1 %copy-start.16 = (s32[16,4]{0,1:T(4,128)S(1)}, s32[16,4]{0,1:T(4,128)}, u32[]{:S(2)}) copy-start(s32[16,4]{0,1:T(4,128)} %param.21) | copy-start | bytes 772
  12.1 37.9 %collective-permute-start.9 = (bf16[2,512,384]{1,2,0:T(8,128)(2,1)}, bf16[2,512,384]{1,2,0:T(8,128)(2,1)}, u32[]{:S(2)}, u32[]{:S(2)}) collective-permute-start(bf16[2,512,384]{1,2,0:T(8,128)(2,1)} %pad_maximum_fusion), channel_id=1, source_target_pairs={{40,0},{48,8},{56,16},{64,24},{72,32},{80,40},{88,48},{96,56},{104... | collective-permute-start | bytes 2359304 | tf_op jit(solution)/shard_map/ppermute | solution.py:20
  13.4 107.8 %collective-permute-start.8 = (bf16[2,512,384]{1,2,0:T(8,128)(2,1)}, bf16[2,512,384]{1,2,0:T(8,128)(2,1)}, u32[]{:S(2)}, u32[]{:S(2)}) collective-permute-start(bf16[2,512,384]{1,2,0:T(8,128)(2,1)} %pad_maximum_fusion), channel_id=1, source_target_pairs={{0,40},{8,48},{16,56},{24,64},{32,72},{40,80},{48,88},{56,96},{64,... | collective-permute-start | bytes 2359304 | tf_op jit(solution)/shard_map/ppermute | solution.py:20
  23.9 99.7 %collective-permute-start.7 = (bf16[2,512,384]{1,2,0:T(8,128)(2,1)}, bf16[2,512,384]{1,2,0:T(8,128)(2,1)}, u32[]{:S(2)}, u32[]{:S(2)}) collective-permute-start(bf16[2,512,384]{1,2,0:T(8,128)(2,1)} %pad_maximum_fusion), channel_id=1, source_target_pairs={{32,0},{40,8},{48,16},{56,24},{64,32},{72,40},{80,48},{88,56},{96,... | collective-permute-start | bytes 2359304 | tf_op jit(solution)/shard_map/ppermute | solution.py:20
  25.2 112.8 %collective-permute-start.6 = (bf16[2,512,384]{1,2,0:T(8,128)(2,1)}, bf16[2,512,384]{1,2,0:T(8,128)(2,1)}, u32[]{:S(2)}, u32[]{:S(2)}) collective-permute-start(bf16[2,512,384]{1,2,0:T(8,128)(2,1)} %pad_maximum_fusion), channel_id=1, source_target_pairs={{0,32},{8,40},{16,48},{24,56},{32,64},{40,72},{48,80},{56,88},{64,... | collective-permute-start | bytes 2359304 | tf_op jit(solution)/shard_map/ppermute | solution.py:20
  31.0 151.9 %collective-permute-start.5 = (bf16[2,512,384]{1,2,0:T(8,128)(2,1)}, bf16[2,512,384]{1,2,0:T(8,128)(2,1)}, u32[]{:S(2)}, u32[]{:S(2)}) collective-permute-start(bf16[2,512,384]{1,2,0:T(8,128)(2,1)} %pad_maximum_fusion), channel_id=1, source_target_pairs={{24,0},{32,8},{40,16},{48,24},{56,32},{64,40},{72,48},{80,56},{88,... | collective-permute-start | bytes 2359304 | tf_op jit(solution)/shard_map/ppermute | solution.py:20
  40.8 3.6 copy-start.14
  41.8 4.0 copy-start.11
  50.0 157.7 %collective-permute-start.4 = (bf16[2,512,384]{1,2,0:T(8,128)(2,1)}, bf16[2,512,384]{1,2,0:T(8,128)(2,1)S(1)}, u32[]{:S(2)}, u32[]{:S(2)}) collective-permute-start(bf16[2,512,384]{1,2,0:T(8,128)(2,1)} %pad_maximum_fusion), channel_id=1, source_target_pairs={{0,24},{8,32},{16,40},{24,48},{32,56},{40,64},{48,72},{56,80},{64,... | collective-permute-start | bytes 2359304 | tf_op jit(solution)/shard_map/ppermute | solution.py:20
  121.2 121.9 %collective-permute-start.3 = (bf16[2,512,384]{1,2,0:T(8,128)(2,1)}, bf16[2,512,384]{1,2,0:T(8,128)(2,1)S(1)}, u32[]{:S(2)}, u32[]{:S(2)}) collective-permute-start(bf16[2,512,384]{1,2,0:T(8,128)(2,1)} %pad_maximum_fusion), channel_id=1, source_target_pairs={{16,0},{24,8},{32,16},{40,24},{48,32},{56,40},{64,48},{72,56},{80,... | collective-permute-start | bytes 2359304 | tf_op jit(solution)/shard_map/ppermute | solution.py:20
  123.7 121.9 %collective-permute-start.2 = (bf16[2,512,384]{1,2,0:T(8,128)(2,1)}, bf16[2,512,384]{1,2,0:T(8,128)(2,1)S(1)}, u32[]{:S(2)}, u32[]{:S(2)}) collective-permute-start(bf16[2,512,384]{1,2,0:T(8,128)(2,1)} %pad_maximum_fusion), channel_id=1, source_target_pairs={{0,16},{8,24},{16,32},{24,40},{32,48},{40,56},{48,64},{56,72},{64,... | collective-permute-start | bytes 2359304 | tf_op jit(solution)/shard_map/ppermute | solution.py:20
  138.0 108.6 %collective-permute-start.1 = (bf16[2,512,384]{1,2,0:T(8,128)(2,1)}, bf16[2,512,384]{1,2,0:T(8,128)(2,1)S(1)}, u32[]{:S(2)}, u32[]{:S(2)}) collective-permute-start(bf16[2,512,384]{1,2,0:T(8,128)(2,1)} %pad_maximum_fusion), channel_id=1, source_target_pairs={{8,0},{16,8},{24,16},{32,24},{40,32},{48,40},{56,48},{64,56},{72,6... | collective-permute-start | bytes 2359304 | tf_op jit(solution)/shard_map/ppermute | solution.py:20
  182.9 65.2 %collective-permute-start.10 = (bf16[2,512,384]{1,2,0:T(8,128)(2,1)}, bf16[2,512,384]{1,2,0:T(8,128)(2,1)S(1)}, u32[]{:S(2)}, u32[]{:S(2)}) collective-permute-start(bf16[2,512,384]{1,2,0:T(8,128)(2,1)} %pad_maximum_fusion), channel_id=1, source_target_pairs={{0,48},{8,56},{16,64},{24,72},{32,80},{40,88},{48,96},{56,104},{64... | collective-permute-start | bytes 2359304 | tf_op jit(solution)/shard_map/ppermute | solution.py:20
  207.7 60.9 %collective-permute-start = (bf16[2,512,384]{1,2,0:T(8,128)(2,1)}, bf16[2,512,384]{1,2,0:T(8,128)(2,1)S(1)}, u32[]{:S(2)}, u32[]{:S(2)}) collective-permute-start(bf16[2,512,384]{1,2,0:T(8,128)(2,1)} %pad_maximum_fusion), channel_id=1, source_target_pairs={{0,8},{8,16},{16,24},{24,32},{32,40},{40,48},{48,56},{56,64},{64,7... | collective-permute-start | bytes 2359304 | tf_op jit(solution)/shard_map/ppermute | solution.py:20
  243.1 26.6 %collective-permute-start.11 = (bf16[2,512,384]{1,2,0:T(8,128)(2,1)}, bf16[2,512,384]{1,2,0:T(8,128)(2,1)S(1)}, u32[]{:S(2)}, u32[]{:S(2)}) collective-permute-start(bf16[2,512,384]{1,2,0:T(8,128)(2,1)} %pad_maximum_fusion), channel_id=1, source_target_pairs={{48,0},{56,8},{64,16},{72,24},{80,32},{88,40},{96,48},{104,56},{11... | collective-permute-start | bytes 2359304 | tf_op jit(solution)/shard_map/ppermute | solution.py:20
  249.0 19.7 %copy-start.2 = (pred[256,512]{0,1:T(8,128)(4,1)S(1)}, pred[256,512]{0,1:T(8,128)(4,1)}, u32[]{:S(2)}) copy-start(pred[256,512]{0,1:T(8,128)(4,1)} %pad_add_fusion.11) | copy-start | bytes 393220
  249.5 19.7 %copy-start.5 = (pred[256,512]{0,1:T(8,128)(4,1)S(1)}, pred[256,512]{0,1:T(8,128)(4,1)}, u32[]{:S(2)}) copy-start(pred[256,512]{0,1:T(8,128)(4,1)} %pad_add_fusion.1) | copy-start | bytes 393220
  282.6 212.2 %all-gather.5.cloned.1.call-start = ((), (), s32[]{:S(2)}) async-start(), calls=%async_computation.1 | async-start | bytes 3993600 | tf_op jit(solution)/shard_map/all_gather | solution.py:137
  283.3 211.4 %copy-start.19 = (bf16[256,640]{1,0:T(8,128)(2,1)S(1)}, bf16[256,640]{1,0:T(8,128)(2,1)}, u32[]{:S(2)}) copy-start(bf16[256,640]{1,0:T(8,128)(2,1)} %param.17) | copy-start | bytes 983044
  (11 other events, 17.3 us)
Sparse Core Ops, SparseCore 0:
  282.7 91.4 all-gather.2
  376.3 118.3 all-gather.4
where the time goes:
time: 507 us; the launch traced here: 506 us
  waiting for transfers between devices  304 us (60%)
  starting transfers between devices  134 us (26%)
  matrix products  21.3 us (4%)
  local copies, waits for them, and re-layouts  19.2 us (4%)
  between operations  14.4 us (3%)
  other arithmetic  13.3 us (3%)
    ppermute x12, starting transfers between devices, shifted(): return lax.ppermute(block, axis, route)  134 us
    all_gather x1, waiting for transfers between devices, local(): lax.all_gather(out_weight, 'seq', axis=0, tiled=True)  121 us
    ppermute x12, waiting for transfers between devices, shifted(): return lax.ppermute(block, axis, route)  93.1 us
    all_gather x1, waiting for transfers between devices, local(): attention = lax.all_gather(attention_local, 'tensor', axis=1, tiled=True)  89.4 us
  transfers between devices with their start and end apart: 14, of which 5 were waited for; matrix products, arithmetic and copies ran while one was open for 6% of the time, Pallas kernels for 0%

commit v1 on v0

v1 whole, which is shorter than its diff:
```python
import math

import numpy as np
import jax
import jax.numpy as jnp
from jax import lax
from jax.sharding import Mesh, PartitionSpec as P

HD = 128
PAGE = 128
POOL = 2
REACH = 6

AXES = ("y", "zl", "c", "zh", "x")
SEQ = ("y", "zl", "c")
TENSOR = ("zh", "x")
CHIP = ("y", "zl")

low_score = -1e30


def shifted(block, axes, size, distance, wrap=False):
    if wrap:
        route = [(i, (i + distance) % size) for i in range(size)]
    else:
        route = [(i, i + distance) for i in range(size) if 0 <= i + distance < size]
    return lax.ppermute(block, axes, route)


def swap_cores(block):
    return lax.ppermute(block, "c", [(0, 1), (1, 0)])


def clip_index(positions, clip_ends):
    return jnp.sum((positions[:, None] >= clip_ends[None, :]).astype(jnp.int32), axis=1)


def allowed_keys(query_clip, source, clip_ends, page_table, page_count, block_total, row_count):
    key_pos = source * row_count + jnp.arange(row_count, dtype=jnp.int32)
    in_range = (source >= 0) & (source < block_total)
    same_clip = (query_clip[:, None] == clip_index(key_pos, clip_ends)[None, :]) & in_range
    clip_total = clip_ends.shape[0]
    page_ids = source * POOL + jnp.arange(POOL, dtype=jnp.int32)
    live_slots = jnp.arange(page_table.shape[1], dtype=jnp.int32)[None, :] < page_count[:, None]
    named_pages = jnp.any(
        live_slots[:, :, None] & (page_table[:, :, None] == page_ids[None, None, :]), axis=1
    )
    member = query_clip[:, None] == jnp.arange(clip_total, dtype=jnp.int32)[None, :]
    page_ok = jnp.any(member[:, :, None] & named_pages[None], axis=1) & in_range
    page_ok = jnp.repeat(page_ok, PAGE, axis=1)
    return jnp.concatenate([same_clip, page_ok], axis=1)


def attend(carry_state, query_heads, key_heads, value_heads, allowed):
    running_max, totals, accumulated = carry_state
    scores = jnp.einsum(
        "qhd,khd->hqk", query_heads, key_heads, preferred_element_type=jnp.float32
    ) * (1.0 / math.sqrt(HD))
    scores = jnp.where(allowed[None], scores, low_score)
    new_max = jnp.maximum(running_max, jnp.max(scores, axis=2))
    factor = jnp.exp(running_max - new_max)
    weights = jnp.where(allowed[None], jnp.exp(scores - new_max[:, :, None]), 0.0)
    totals = totals * factor + jnp.sum(weights, axis=2)
    accumulated = accumulated * factor[:, :, None] + jnp.einsum(
        "hqk,khd->hqd",
        weights.astype(jnp.bfloat16),
        value_heads,
        preferred_element_type=jnp.float32,
    )
    return (new_max, totals, accumulated)


def empty_state(head_count, row_count):
    return (
        jnp.full((head_count, row_count), low_score, jnp.float32),
        jnp.zeros((head_count, row_count), jnp.float32),
        jnp.zeros((head_count, row_count, HD), jnp.float32),
    )


def visit_block(carry_state, packed, source, query_heads, query_clip, context):
    clip_ends, page_table, page_count, block_total = context
    row_count = query_heads.shape[0]
    head_count = query_heads.shape[1]
    allowed = allowed_keys(
        query_clip, source, clip_ends, page_table, page_count, block_total, row_count
    )
    key_heads = packed[0].reshape(-1, head_count, HD)
    value_heads = packed[1].reshape(-1, head_count, HD)
    return attend(carry_state, query_heads, key_heads, value_heads, allowed)


def gather_weight(out_weight, sizes, is_first):
    n_y, n_zl = sizes["y"], sizes["zl"]
    rows, cols = out_weight.shape
    other = swap_cores(out_weight)
    pair = jnp.where(
        is_first,
        jnp.concatenate([out_weight, other], axis=0),
        jnp.concatenate([other, out_weight], axis=0),
    )
    zl = lax.axis_index("zl")
    row_block = jnp.zeros((n_zl, 2 * rows, cols), out_weight.dtype)
    row_block = lax.dynamic_update_index_in_dim(row_block, pair, zl, 0)
    for d in range(1, n_zl):
        got = shifted(pair, "zl", n_zl, d, wrap=True)
        row_block = lax.dynamic_update_index_in_dim(row_block, got, (zl - d) % n_zl, 0)
    row_block = row_block.reshape(n_zl * 2 * rows, cols)

    y = lax.axis_index("y")
    full = jnp.zeros((n_y, n_zl * 2 * rows, cols), out_weight.dtype)
    full = lax.dynamic_update_index_in_dim(full, row_block, y, 0)
    below_count = n_y // 2
    above_count = (n_y - 1) // 2
    for j in range(1, below_count + 1):
        route = [(yy * 2, ((yy + j) % n_y) * 2) for yy in range(n_y)]
        if j <= above_count:
            route += [(yy * 2 + 1, ((yy - j) % n_y) * 2 + 1) for yy in range(n_y)]
        got = lax.ppermute(row_block, ("y", "c"), route)
        if j <= above_count:
            traded = swap_cores(got)
            here = jnp.where(is_first, (y - j) % n_y, (y + j) % n_y)
            there = jnp.where(is_first, (y + j) % n_y, (y - j) % n_y)
            full = lax.dynamic_update_index_in_dim(full, got, here, 0)
            full = lax.dynamic_update_index_in_dim(full, traded, there, 0)
        else:
            traded = lax.ppermute(got, "c", [(0, 1)])
            value = jnp.where(is_first, got, traded)
            full = lax.dynamic_update_index_in_dim(full, value, (y - j) % n_y, 0)
    return full.reshape(n_y * n_zl * 2 * rows, cols)


def gather_attention(attention_local, sizes):
    n_x = sizes["x"]
    n_tensor = sizes["zh"] * n_x
    row_count, width = attention_local.shape
    zh = lax.axis_index("zh")
    x = lax.axis_index("x")
    partner = lax.ppermute(attention_local, "zh", [(0, 1), (1, 0)])
    pieces = [(attention_local, zh, x), (partner, 1 - zh, x)]
    for d in range(1, n_x):
        pieces.append((shifted(attention_local, "x", n_x, d, wrap=True), zh, (x - d) % n_x))
        pieces.append((shifted(partner, "x", n_x, d, wrap=True), 1 - zh, (x - d) % n_x))
    full = jnp.zeros((row_count, n_tensor * width), attention_local.dtype)
    for piece, piece_zh, piece_x in pieces:
        start = pl_multiple((piece_zh * n_x + piece_x) * width)
        full = lax.dynamic_update_slice(full, piece, (jnp.int32(0), start))
    return full


def pl_multiple(value):
    return value.astype(jnp.int32)


def make_local(sizes):
    n_chip = sizes["y"] * sizes["zl"]

    def local(
        queries,
        key_tiles,
        value_tiles,
        cache_keys,
        cache_values,
        hidden,
        out_weight,
        gate_table,
        lengths,
        page_table,
        page_count,
        timestep,
    ):
        row_count = queries.shape[0]
        tile_width = queries.shape[1]
        head_count = tile_width // HD
        block_total = n_chip * 2
        chip = lax.axis_index("y") * sizes["zl"] + lax.axis_index("zl")
        core = lax.axis_index("c")
        is_first = core == 0
        seq_index = chip * 2 + core
        clip_ends = jnp.cumsum(lengths, dtype=jnp.int32)
        row_ids = jnp.arange(row_count, dtype=jnp.int32)
        positions = seq_index * row_count + row_ids
        query_clip = clip_index(positions, clip_ends)
        query_heads = queries.reshape(row_count, head_count, HD)
        context = (clip_ends, page_table, page_count, block_total)
        packed = jnp.stack(
            [
                jnp.concatenate([key_tiles, cache_keys.reshape(-1, tile_width)], axis=0),
                jnp.concatenate([value_tiles, cache_values.reshape(-1, tile_width)], axis=0),
            ]
        )
        weight_full = gather_weight(out_weight, sizes, is_first)

        carry_state = visit_block(
            empty_state(head_count, row_count), packed, seq_index, query_heads, query_clip, context
        )
        above = {}
        below = {}
        for d in range(1, 4):
            above[d] = shifted(packed, CHIP, n_chip, -d)
            carry_state = visit_block(
                carry_state, above[d], seq_index + 2 * d, query_heads, query_clip, context
            )
            below[d] = shifted(packed, CHIP, n_chip, d)
            carry_state = visit_block(
                carry_state, below[d], seq_index - 2 * d, query_heads, query_clip, context
            )
        sign = 1 - 2 * core
        outgoing = [
            (packed, 1),
            (jnp.where(is_first, above[1], below[1]), -1),
            (jnp.where(is_first, above[2], below[2]), -3),
            (jnp.where(is_first, above[3], below[3]), -5),
            (jnp.where(is_first, below[1], above[1]), 3),
            (jnp.where(is_first, below[2], above[2]), 5),
        ]
        for block, offset in outgoing:
            got = swap_cores(block)
            carry_state = visit_block(
                carry_state, got, seq_index + sign * offset, query_heads, query_clip, context
            )
        running_max, totals, accumulated = carry_state
        result = accumulated / totals[:, :, None]
        attention_local = (
            jnp.transpose(result, (1, 0, 2)).reshape(row_count, tile_width).astype(jnp.bfloat16)
        )
        attention = gather_attention(attention_local, sizes)
        projected = jnp.dot(attention, weight_full, preferred_element_type=jnp.float32)
        clip_total = lengths.shape[0]
        step_onehot = (
            timestep[:, None] == jnp.arange(gate_table.shape[0], dtype=jnp.int32)[None, :]
        ).astype(jnp.float32)
        clip_gate = jnp.dot(
            step_onehot, gate_table, precision=lax.Precision.HIGHEST, preferred_element_type=jnp.float32
        )
        clip_onehot = (
            query_clip[:, None] == jnp.arange(clip_total, dtype=jnp.int32)[None, :]
        ).astype(jnp.float32)
        token_gate = jnp.dot(
            clip_onehot, clip_gate, precision=lax.Precision.HIGHEST, preferred_element_type=jnp.float32
        )
        return (hidden.astype(jnp.float32) + token_gate * projected).astype(jnp.bfloat16)

    return local


def solution(mesh):
    n_seq = mesh.shape["seq"]
    n_tensor = mesh.shape["tensor"]
    sizes = {"y": n_seq // 8, "zl": 4, "c": 2, "zh": 2, "x": n_tensor // 2}
    devices = np.asarray(mesh.devices).reshape(tuple(sizes[a] for a in AXES))
    fine = Mesh(devices, AXES)
    return jax.shard_map(
        make_local(sizes),
        mesh=fine,
        in_specs=(
            P(SEQ, TENSOR),
            P(SEQ, TENSOR),
            P(SEQ, TENSOR),
            P(SEQ, None, TENSOR),
            P(SEQ, None, TENSOR),
            P(SEQ, TENSOR),
            P(SEQ, TENSOR),
            P(None, TENSOR),
            P(),
            P(),
            P(),
            P(),
        ),
        out_specs=P(SEQ, TENSOR),
        check_vma=False,
    )
```

time: 507 us -> 279 us (0.55)
  the two profiles are of different devices: /device:TPU:1 before, /device:TPU:240 now
where the time goes in v1:
time: 279 us; the launch traced here: 277 us
  starting transfers between devices  119 us (43%)
  waiting for transfers between devices  97.7 us (35%)
  other arithmetic  20.7 us (7%)
  local copies, waits for them, and re-layouts  19.7 us (7%)
  matrix products  18.3 us (7%)
    ppermute x15, starting transfers between devices, shifted(): return lax.ppermute(block, axes, route)  71.1 us
    ppermute x15, waiting for transfers between devices, shifted(): return lax.ppermute(block, axes, route)  70.1 us
    ppermute x4, waiting for transfers between devices, gather_weight(): got = lax.ppermute(row_block, ('y', 'c'), route)  27.5 us
    ppermute x10, starting transfers between devices, swap_cores(): return lax.ppermute(block, 'c', [(0, 1), (1, 0)])  21.3 us
    ppermute x4, starting transfers between devices, gather_weight(): got = lax.ppermute(row_block, ('y', 'c'), route)  14.8 us
    ppermute x1, starting transfers between devices, gather_attention(): partner = lax.ppermute(attention_local, 'zh', [(0, 1), (1, 0)])  9.04 us
    dot_general x13, matrix products, attend(): jnp.einsum('qhd,khd->hqk', query_heads, key_heads, preferred_element_type...  7.35 us
    concatenate x13, other arithmetic, allowed_keys(): return jnp.concatenate([same_clip, page_ok], axis=1)  6.61 us
  transfers between devices with their start and end apart: 31, of which 9 were waited for; matrix products, arithmetic and copies ran while one was open for 16% of the time, Pallas kernels for 0%

profile of v1, /device:TPU:240, one launch (start us, length us, event | category | flops | bytes accessed | tf_op | source)
XLA Modules:
  0.0 277.1 jit_solution(17338208167872854309)
XLA Ops:
  10.5 4.7 %collective-permute-start.4 = (bf16[2,512,384]{1,2,0:T(8,128)(2,1)}, bf16[2,512,384]{1,2,0:T(8,128)(2,1)S(1)}, u32[]{:S(2)}, u32[]{:S(2)}) collective-permute-start(bf16[2,512,384]{1,2,0:T(8,128)(2,1)} %pad_maximum_fusion), channel_id=1, source_target_pairs={{48,0},{64,16},{80,32},{96,48},{112,64},{128,80},{144,96},{160,112... | collective-permute-start | bytes 2359304 | tf_op jit(solution)/shard_map/ppermute | solution.py:27
  40.5 5.6 %collective-permute-start.20 = (bf16[96,640]{1,0:T(8,128)(2,1)S(1)}, bf16[96,640]{1,0:T(8,128)(2,1)S(1)}, u32[]{:S(2)}, u32[]{:S(2)}) collective-permute-start(bf16[96,640]{1,0:T(8,128)(2,1)S(1)} %maximum_select_fusion.1), channel_id=1, source_target_pairs={{0,16},{16,32},{32,48},{48,0},{1,17},{17,33},{33,49},{49,1},{2,18}... | collective-permute-start | bytes 368648 | tf_op jit(solution)/shard_map/ppermute | solution.py:27
  47.8 16.4 %collective-permute-done.20 = bf16[96,640]{1,0:T(8,128)(2,1)S(1)} collective-permute-done((bf16[96,640]{1,0:T(8,128)(2,1)S(1)}, bf16[96,640]{1,0:T(8,128)(2,1)S(1)}, u32[]{:S(2)}, u32[]{:S(2)}) %collective-permute-start.20) | collective-permute-done | bytes 122912 | tf_op jit(solution)/shard_map/ppermute | solution.py:27
  64.2 23.8 %collective-permute-start.21 = (bf16[96,640]{1,0:T(8,128)(2,1)S(1)}, bf16[96,640]{1,0:T(8,128)(2,1)S(1)}, u32[]{:S(2)}, u32[]{:S(2)}) collective-permute-start(bf16[96,640]{1,0:T(8,128)(2,1)S(1)} %maximum_select_fusion.1), channel_id=1, source_target_pairs={{0,32},{16,48},{32,0},{48,16},{1,33},{17,49},{33,1},{49,17},{2,34}... | collective-permute-start | bytes 368648 | tf_op jit(solution)/shard_map/ppermute | solution.py:27
  88.0 6.1 %collective-permute-done.21 = bf16[96,640]{1,0:T(8,128)(2,1)S(1)} collective-permute-done((bf16[96,640]{1,0:T(8,128)(2,1)S(1)}, bf16[96,640]{1,0:T(8,128)(2,1)S(1)}, u32[]{:S(2)}, u32[]{:S(2)}) %collective-permute-start.21) | collective-permute-done | bytes 122912 | tf_op jit(solution)/shard_map/ppermute | solution.py:27
  96.0 6.6 %collective-permute-done.22 = bf16[96,640]{1,0:T(8,128)(2,1)S(1)} collective-permute-done((bf16[96,640]{1,0:T(8,128)(2,1)S(1)}, bf16[96,640]{1,0:T(8,128)(2,1)S(1)}, u32[]{:S(2)}, u32[]{:S(2)}) %collective-permute-start.22) | collective-permute-done | bytes 122912 | tf_op jit(solution)/shard_map/ppermute | solution.py:27
  108.3 5.1 %collective-permute-done.23 = bf16[384,640]{1,0:T(8,128)(2,1)S(1)} collective-permute-done((bf16[384,640]{1,0:T(8,128)(2,1)S(1)}, bf16[384,640]{1,0:T(8,128)(2,1)S(1)}, u32[]{:S(2)}, u32[]{:S(2)}) %collective-permute-start.23) | collective-permute-done | bytes 491552 | tf_op jit(solution)/shard_map/ppermute | solution.py:119
  118.7 6.8 %collective-permute-start.1 = (bf16[2,512,384]{1,2,0:T(8,128)(2,1)}, bf16[2,512,384]{1,2,0:T(8,128)(2,1)S(1)}, u32[]{:S(2)}, u32[]{:S(2)}) collective-permute-start(bf16[2,512,384]{1,2,0:T(8,128)(2,1)} %pad_maximum_fusion), channel_id=1, source_target_pairs={{0,16},{16,32},{32,48},{48,64},{64,80},{80,96},{96,112},{112,128},... | collective-permute-start | bytes 2359304 | tf_op jit(solution)/shard_map/ppermute | solution.py:27
  126.6 3.1 %collective-permute-start.25 = (bf16[384,640]{1,0:T(8,128)(2,1)S(1)}, bf16[384,640]{1,0:T(8,128)(2,1)S(1)}, u32[]{:S(2)}, u32[]{:S(2)}) collective-permute-start(bf16[384,640]{1,0:T(8,128)(2,1)S(1)} %bitcast.431), channel_id=1, source_target_pairs={{0,128},{64,192},{128,256},{192,320},{256,384},{320,448},{384,0},{... | collective-permute-start | bytes 1474568 | tf_op jit(solution)/shard_map/ppermute | solution.py:119
  130.8 34.7 %collective-permute-done.3 = bf16[2,512,384]{1,2,0:T(8,128)(2,1)S(1)} collective-permute-done((bf16[2,512,384]{1,2,0:T(8,128)(2,1)}, bf16[2,512,384]{1,2,0:T(8,128)(2,1)S(1)}, u32[]{:S(2)}, u32[]{:S(2)}) %collective-permute-start.3) | collective-permute-done | bytes 786464 | tf_op jit(solution)/shard_map/ppermute | solution.py:27
  165.5 2.8 %collective-permute-start.27 = (bf16[384,640]{1,0:T(8,128)(2,1)S(1)}, bf16[384,640]{1,0:T(8,128)(2,1)S(1)}, u32[]{:S(2)}, u32[]{:S(2)}) collective-permute-start(bf16[384,640]{1,0:T(8,128)(2,1)S(1)} %bitcast.432), channel_id=1, source_target_pairs={{0,192},{64,256},{128,320},{192,384},{256,448},{320,0},{384,64},{4... | collective-permute-start | bytes 1474568 | tf_op jit(solution)/shard_map/ppermute | solution.py:119
  169.4 7.0 %collective-permute-start.29 = (bf16[384,640]{1,0:T(8,128)(2,1)S(1)}, bf16[384,640]{1,0:T(8,128)(2,1)S(1)}, u32[]{:S(2)}, u32[]{:S(2)}) collective-permute-start(bf16[384,640]{1,0:T(8,128)(2,1)S(1)} %bitcast.433), channel_id=1, source_target_pairs={{0,256},{64,320},{128,384},{192,448},{256,0},{320,64},{384,128},{4... | collective-permute-start | bytes 1474568 | tf_op jit(solution)/shard_map/ppermute | solution.py:119
  180.0 9.9 %collective-permute-done.27 = bf16[384,640]{1,0:T(8,128)(2,1)S(1)} collective-permute-done((bf16[384,640]{1,0:T(8,128)(2,1)S(1)}, bf16[384,640]{1,0:T(8,128)(2,1)S(1)}, u32[]{:S(2)}, u32[]{:S(2)}) %collective-permute-start.27) | collective-permute-done | bytes 491552 | tf_op jit(solution)/shard_map/ppermute | solution.py:119
  191.8 12.5 %collective-permute-done.29 = bf16[384,640]{1,0:T(8,128)(2,1)S(1)} collective-permute-done((bf16[384,640]{1,0:T(8,128)(2,1)S(1)}, bf16[384,640]{1,0:T(8,128)(2,1)S(1)}, u32[]{:S(2)}, u32[]{:S(2)}) %collective-permute-start.29) | collective-permute-done | bytes 491552 | tf_op jit(solution)/shard_map/ppermute | solution.py:119
  206.3 2.4 collective-permute-start.30
  220.5 2.6 collective-permute-start.7
  238.4 9.0 %collective-permute-start.12 = (bf16[256,384]{0,1:T(8,128)(2,1)S(1)}, bf16[256,384]{0,1:T(8,128)(2,1)S(1)}, u32[]{:S(2)}, u32[]{:S(2)}) collective-permute-start(bf16[256,384]{0,1:T(8,128)(2,1)S(1)} %bitcast.475), channel_id=1, source_target_pairs={{0,4},{4,0},{1,5},{5,1},{2,6},{6,2},{3,7},{7,3},{8,12},{12,8},{9,1... | collective-permute-start | bytes 589832 | tf_op jit(solution)/shard_map/ppermute | solution.py:139
  247.6 3.4 %collective-permute-start.13 = (bf16[256,384]{0,1:T(8,128)(2,1)S(1)}, bf16[256,384]{0,1:T(8,128)(2,1)S(1)}, u32[]{:S(2)}, u32[]{:S(2)}) collective-permute-start(bf16[256,384]{0,1:T(8,128)(2,1)S(1)} %bitcast.476), channel_id=1, source_target_pairs={{0,1},{1,2},{2,3},{3,0},{4,5},{5,6},{6,7},{7,4},{8,9},{9,10},{10,1... | collective-permute-start | bytes 589832 | tf_op jit(solution)/shard_map/ppermute | solution.py:27
  251.0 4.6 %collective-permute-start.15 = (bf16[256,384]{0,1:T(8,128)(2,1)S(1)}, bf16[256,384]{0,1:T(8,128)(2,1)S(1)}, u32[]{:S(2)}, u32[]{:S(2)}) collective-permute-start(bf16[256,384]{0,1:T(8,128)(2,1)S(1)} %bitcast.477), channel_id=1, source_target_pairs={{0,2},{1,3},{2,0},{3,1},{4,6},{5,7},{6,4},{7,5},{8,10},{9,11},{10,... | collective-permute-start | bytes 589832 | tf_op jit(solution)/shard_map/ppermute | solution.py:27
  255.7 3.4 %collective-permute-start.17 = (bf16[256,384]{0,1:T(8,128)(2,1)S(1)}, bf16[256,384]{0,1:T(8,128)(2,1)S(1)}, u32[]{:S(2)}, u32[]{:S(2)}) collective-permute-start(bf16[256,384]{0,1:T(8,128)(2,1)S(1)} %bitcast.478), channel_id=1, source_target_pairs={{0,3},{1,0},{2,1},{3,2},{4,7},{5,4},{6,5},{7,6},{8,11},{9,8},{10,9... | collective-permute-start | bytes 589832 | tf_op jit(solution)/shard_map/ppermute | solution.py:27
  259.2 2.6 collective-permute-start.14
  261.8 2.8 %collective-permute-start.16 = (bf16[256,384]{0,1:T(8,128)(2,1)S(1)}, bf16[256,384]{0,1:T(8,128)(2,1)S(1)}, u32[]{:S(2)}, u32[]{:S(2)}) collective-permute-start(bf16[256,384]{0,1:T(8,128)(2,1)S(1)} %collective-permute-done.12), channel_id=1, source_target_pairs={{0,2},{1,3},{2,0},{3,1},{4,6},{5,7},{6,4},{7,5},{8,10},{9,11},{10,... | collective-permute-start | bytes 589832 | tf_op jit(solution)/shard_map/ppermute | solution.py:27
  264.7 3.7 %collective-permute-start.18 = (bf16[256,384]{0,1:T(8,128)(2,1)S(1)}, bf16[256,384]{0,1:T(8,128)(2,1)S(1)}, u32[]{:S(2)}, u32[]{:S(2)}) collective-permute-start(bf16[256,384]{0,1:T(8,128)(2,1)S(1)} %collective-permute-done.12), channel_id=1, source_target_pairs={{0,3},{1,0},{2,1},{3,2},{4,7},{5,4},{6,5},{7,6},{8,11},{9,8},{10,9... | collective-permute-start | bytes 589832 | tf_op jit(solution)/shard_map/ppermute | solution.py:27
  268.4 3.9 %collective-permute-done.14 = bf16[256,384]{0,1:T(8,128)(2,1)S(1)} collective-permute-done((bf16[256,384]{0,1:T(8,128)(2,1)S(1)}, bf16[256,384]{0,1:T(8,128)(2,1)S(1)}, u32[]{:S(2)}, u32[]{:S(2)}) %collective-permute-start.14) | collective-permute-done | bytes 196640 | tf_op jit(solution)/shard_map/ppermute | solution.py:27
  (269 shorter events, 91.7 us)
Async XLA Ops:
  8.6 160.8 %collective-permute-start.2 = (bf16[2,512,384]{1,2,0:T(8,128)(2,1)}, bf16[2,512,384]{1,2,0:T(8,128)(2,1)}, u32[]{:S(2)}, u32[]{:S(2)}) collective-permute-start(bf16[2,512,384]{1,2,0:T(8,128)(2,1)} %pad_maximum_fusion), channel_id=1, source_target_pairs={{32,0},{48,16},{64,32},{80,48},{96,64},{112,80},{128,96},{144,112}... | collective-permute-start | bytes 2359304 | tf_op jit(solution)/shard_map/ppermute | solution.py:27
  10.5 116.1 %collective-permute-start.4 = (bf16[2,512,384]{1,2,0:T(8,128)(2,1)}, bf16[2,512,384]{1,2,0:T(8,128)(2,1)S(1)}, u32[]{:S(2)}, u32[]{:S(2)}) collective-permute-start(bf16[2,512,384]{1,2,0:T(8,128)(2,1)} %pad_maximum_fusion), channel_id=1, source_target_pairs={{48,0},{64,16},{80,32},{96,48},{112,64},{128,80},{144,96},{160,112... | collective-permute-start | bytes 2359304 | tf_op jit(solution)/shard_map/ppermute | solution.py:27
  15.2 103.4 %collective-permute-start.5 = (bf16[2,512,384]{1,2,0:T(8,128)(2,1)}, bf16[2,512,384]{1,2,0:T(8,128)(2,1)}, u32[]{:S(2)}, u32[]{:S(2)}) collective-permute-start(bf16[2,512,384]{1,2,0:T(8,128)(2,1)} %pad_maximum_fusion), channel_id=1, source_target_pairs={{0,48},{16,64},{32,80},{48,96},{64,112},{80,128},{96,144},{112,160... | collective-permute-start | bytes 2359304 | tf_op jit(solution)/shard_map/ppermute | solution.py:27
  17.3 98.1 %collective-permute-start.6 = (bf16[2,512,384]{1,2,0:T(8,128)(2,1)}, bf16[2,512,384]{1,2,0:T(8,128)(2,1)}, u32[]{:S(2)}, u32[]{:S(2)}) collective-permute-start(bf16[2,512,384]{1,2,0:T(8,128)(2,1)} %pad_maximum_fusion), channel_id=1, source_target_pairs={{0,8},{8,0},{1,9},{9,1},{2,10},{10,2},{3,11},{11,3},{4,12},{12,4},... | collective-permute-start | bytes 2359304 | tf_op jit(solution)/shard_map/ppermute | solution.py:31
  19.3 20.3 %collective-permute-start.19 = (bf16[48,640]{1,0:T(8,128)(2,1)}, bf16[48,640]{1,0:T(8,128)(2,1)}, u32[]{:S(2)}, u32[]{:S(2)}) collective-permute-start(bf16[48,640]{1,0:T(8,128)(2,1)} %param.18), channel_id=1, source_target_pairs={{0,8},{8,0},{1,9},{9,1},{2,10},{10,2},{3,11},{11,3},{4,12},{12,4},... | collective-permute-start | bytes 184328 | tf_op jit(solution)/shard_map/ppermute | solution.py:31
  40.5 23.7 %collective-permute-start.20 = (bf16[96,640]{1,0:T(8,128)(2,1)S(1)}, bf16[96,640]{1,0:T(8,128)(2,1)S(1)}, u32[]{:S(2)}, u32[]{:S(2)}) collective-permute-start(bf16[96,640]{1,0:T(8,128)(2,1)S(1)} %maximum_select_fusion.1), channel_id=1, source_target_pairs={{0,16},{16,32},{32,48},{48,0},{1,17},{17,33},{33,49},{49,1},{2,18}... | collective-permute-start | bytes 368648 | tf_op jit(solution)/shard_map/ppermute | solution.py:27
  64.2 29.9 %collective-permute-start.21 = (bf16[96,640]{1,0:T(8,128)(2,1)S(1)}, bf16[96,640]{1,0:T(8,128)(2,1)S(1)}, u32[]{:S(2)}, u32[]{:S(2)}) collective-permute-start(bf16[96,640]{1,0:T(8,128)(2,1)S(1)} %maximum_select_fusion.1), channel_id=1, source_target_pairs={{0,32},{16,48},{32,0},{48,16},{1,33},{17,49},{33,1},{49,17},{2,34}... | collective-permute-start | bytes 368648 | tf_op jit(solution)/shard_map/ppermute | solution.py:27
  102.7 10.7 %collective-permute-start.23 = (bf16[384,640]{1,0:T(8,128)(2,1)S(1)}, bf16[384,640]{1,0:T(8,128)(2,1)S(1)}, u32[]{:S(2)}, u32[]{:S(2)}) collective-permute-start(bf16[384,640]{1,0:T(8,128)(2,1)S(1)} %bitcast.429), channel_id=1, source_target_pairs={{0,64},{64,128},{128,192},{192,256},{256,320},{320,384},{384,448},... | collective-permute-start | bytes 1474568 | tf_op jit(solution)/shard_map/ppermute | solution.py:119
  113.4 52.1 %collective-permute-start.3 = (bf16[2,512,384]{1,2,0:T(8,128)(2,1)}, bf16[2,512,384]{1,2,0:T(8,128)(2,1)S(1)}, u32[]{:S(2)}, u32[]{:S(2)}) collective-permute-start(bf16[2,512,384]{1,2,0:T(8,128)(2,1)} %pad_maximum_fusion), channel_id=1, source_target_pairs={{0,32},{16,48},{32,64},{48,80},{64,96},{80,112},{96,128},{112,144}... | collective-permute-start | bytes 2359304 | tf_op jit(solution)/shard_map/ppermute | solution.py:27
  115.4 95.3 %collective-permute-start = (bf16[2,512,384]{1,2,0:T(8,128)(2,1)}, bf16[2,512,384]{1,2,0:T(8,128)(2,1)S(1)}, u32[]{:S(2)}, u32[]{:S(2)}) collective-permute-start(bf16[2,512,384]{1,2,0:T(8,128)(2,1)} %pad_maximum_fusion), channel_id=1, source_target_pairs={{16,0},{32,16},{48,32},{64,48},{80,64},{96,80},{112,96},{128,112},... | collective-permute-start | bytes 2359304 | tf_op jit(solution)/shard_map/ppermute | solution.py:27
  118.7 87.6 %collective-permute-start.1 = (bf16[2,512,384]{1,2,0:T(8,128)(2,1)}, bf16[2,512,384]{1,2,0:T(8,128)(2,1)S(1)}, u32[]{:S(2)}, u32[]{:S(2)}) collective-permute-start(bf16[2,512,384]{1,2,0:T(8,128)(2,1)} %pad_maximum_fusion), channel_id=1, source_target_pairs={{0,16},{16,32},{32,48},{48,64},{64,80},{80,96},{96,112},{112,128},... | collective-permute-start | bytes 2359304 | tf_op jit(solution)/shard_map/ppermute | solution.py:27
  126.6 51.4 %collective-permute-start.25 = (bf16[384,640]{1,0:T(8,128)(2,1)S(1)}, bf16[384,640]{1,0:T(8,128)(2,1)S(1)}, u32[]{:S(2)}, u32[]{:S(2)}) collective-permute-start(bf16[384,640]{1,0:T(8,128)(2,1)S(1)} %bitcast.431), channel_id=1, source_target_pairs={{0,128},{64,192},{128,256},{192,320},{256,384},{320,448},{384,0},{... | collective-permute-start | bytes 1474568 | tf_op jit(solution)/shard_map/ppermute | solution.py:119
  165.5 24.4 %collective-permute-start.27 = (bf16[384,640]{1,0:T(8,128)(2,1)S(1)}, bf16[384,640]{1,0:T(8,128)(2,1)S(1)}, u32[]{:S(2)}, u32[]{:S(2)}) collective-permute-start(bf16[384,640]{1,0:T(8,128)(2,1)S(1)} %bitcast.432), channel_id=1, source_target_pairs={{0,192},{64,256},{128,320},{192,384},{256,448},{320,0},{384,64},{4... | collective-permute-start | bytes 1474568 | tf_op jit(solution)/shard_map/ppermute | solution.py:119
  169.4 35.0 %collective-permute-start.29 = (bf16[384,640]{1,0:T(8,128)(2,1)S(1)}, bf16[384,640]{1,0:T(8,128)(2,1)S(1)}, u32[]{:S(2)}, u32[]{:S(2)}) collective-permute-start(bf16[384,640]{1,0:T(8,128)(2,1)S(1)} %bitcast.433), channel_id=1, source_target_pairs={{0,256},{64,320},{128,384},{192,448},{256,0},{320,64},{384,128},{4... | collective-permute-start | bytes 1474568 | tf_op jit(solution)/shard_map/ppermute | solution.py:119
  178.1 35.7 %collective-permute-start.24 = (bf16[384,640]{1,0:T(8,128)(2,1)S(1)}, bf16[384,640]{1,0:T(8,128)(2,1)S(1)}, u32[]{:S(2)}, u32[]{:S(2)}) collective-permute-start(bf16[384,640]{1,0:T(8,128)(2,1)S(1)} %copy-done.19), channel_id=1, source_target_pairs={{0,8},{8,0},{1,9},{9,1},{2,10},{10,2},{3,11},{11,3},{4,12},{12,4},... | collective-permute-start | bytes 1474568 | tf_op jit(solution)/shard_map/ppermute | solution.py:31
  189.9 26.0 %collective-permute-start.26 = (bf16[384,640]{1,0:T(8,128)(2,1)S(1)}, bf16[384,640]{1,0:T(8,128)(2,1)S(1)}, u32[]{:S(2)}, u32[]{:S(2)}) collective-permute-start(bf16[384,640]{1,0:T(8,128)(2,1)S(1)} %collective-permute-done.25), channel_id=1, source_target_pairs={{0,8},{8,0},{1,9},{9,1},{2,10},{10,2},{3,11},{11,3},{4,12},{12,4},... | collective-permute-start | bytes 1474568 | tf_op jit(solution)/shard_map/ppermute | solution.py:31
  204.4 14.1 %collective-permute-start.28 = (bf16[384,640]{1,0:T(8,128)(2,1)S(1)}, bf16[384,640]{1,0:T(8,128)(2,1)S(1)}, u32[]{:S(2)}, u32[]{:S(2)}) collective-permute-start(bf16[384,640]{1,0:T(8,128)(2,1)S(1)} %collective-permute-done.27), channel_id=1, source_target_pairs={{0,8},{8,0},{1,9},{9,1},{2,10},{10,2},{3,11},{11,3},{4,12},{12,4},... | collective-permute-start | bytes 1474568 | tf_op jit(solution)/shard_map/ppermute | solution.py:31
  206.3 41.1 %collective-permute-start.30 = (bf16[384,640]{1,0:T(8,128)(2,1)S(1)}, bf16[384,640]{1,0:T(8,128)(2,1)S(1)}, u32[]{:S(2)}, u32[]{:S(2)}) collective-permute-start(bf16[384,640]{1,0:T(8,128)(2,1)S(1)} %collective-permute-done.29), channel_id=1, source_target_pairs={{0,8},{1,9},{2,10},{3,11},{4,12},{5,13},{6,14},{7,15},{16,24},{17,... | collective-permute-start | bytes 1474568 | tf_op jit(solution)/shard_map/ppermute | solution.py:127
  238.4 20.8 %collective-permute-start.12 = (bf16[256,384]{0,1:T(8,128)(2,1)S(1)}, bf16[256,384]{0,1:T(8,128)(2,1)S(1)}, u32[]{:S(2)}, u32[]{:S(2)}) collective-permute-start(bf16[256,384]{0,1:T(8,128)(2,1)S(1)} %bitcast.475), channel_id=1, source_target_pairs={{0,4},{4,0},{1,5},{5,1},{2,6},{6,2},{3,7},{7,3},{8,12},{12,8},{9,1... | collective-permute-start | bytes 589832 | tf_op jit(solution)/shard_map/ppermute | solution.py:139
  247.6 17.1 %collective-permute-start.13 = (bf16[256,384]{0,1:T(8,128)(2,1)S(1)}, bf16[256,384]{0,1:T(8,128)(2,1)S(1)}, u32[]{:S(2)}, u32[]{:S(2)}) collective-permute-start(bf16[256,384]{0,1:T(8,128)(2,1)S(1)} %bitcast.476), channel_id=1, source_target_pairs={{0,1},{1,2},{2,3},{3,0},{4,5},{5,6},{6,7},{7,4},{8,9},{9,10},{10,1... | collective-permute-start | bytes 589832 | tf_op jit(solution)/shard_map/ppermute | solution.py:27
  251.0 21.3 %collective-permute-start.15 = (bf16[256,384]{0,1:T(8,128)(2,1)S(1)}, bf16[256,384]{0,1:T(8,128)(2,1)S(1)}, u32[]{:S(2)}, u32[]{:S(2)}) collective-permute-start(bf16[256,384]{0,1:T(8,128)(2,1)S(1)} %bitcast.477), channel_id=1, source_target_pairs={{0,2},{1,3},{2,0},{3,1},{4,6},{5,7},{6,4},{7,5},{8,10},{9,11},{10,... | collective-permute-start | bytes 589832 | tf_op jit(solution)/shard_map/ppermute | solution.py:27
  255.7 16.8 %collective-permute-start.17 = (bf16[256,384]{0,1:T(8,128)(2,1)S(1)}, bf16[256,384]{0,1:T(8,128)(2,1)S(1)}, u32[]{:S(2)}, u32[]{:S(2)}) collective-permute-start(bf16[256,384]{0,1:T(8,128)(2,1)S(1)} %bitcast.478), channel_id=1, source_target_pairs={{0,3},{1,0},{2,1},{3,2},{4,7},{5,4},{6,5},{7,6},{8,11},{9,8},{10,9... | collective-permute-start | bytes 589832 | tf_op jit(solution)/shard_map/ppermute | solution.py:27
  259.2 13.2 %collective-permute-start.14 = (bf16[256,384]{0,1:T(8,128)(2,1)S(1)}, bf16[256,384]{0,1:T(8,128)(2,1)S(1)}, u32[]{:S(2)}, u32[]{:S(2)}) collective-permute-start(bf16[256,384]{0,1:T(8,128)(2,1)S(1)} %collective-permute-done.12), channel_id=1, source_target_pairs={{0,1},{1,2},{2,3},{3,0},{4,5},{5,6},{6,7},{7,4},{8,9},{9,10},{10,1... | collective-permute-start | bytes 589832 | tf_op jit(solution)/shard_map/ppermute | solution.py:27
  261.8 10.6 %collective-permute-start.16 = (bf16[256,384]{0,1:T(8,128)(2,1)S(1)}, bf16[256,384]{0,1:T(8,128)(2,1)S(1)}, u32[]{:S(2)}, u32[]{:S(2)}) collective-permute-start(bf16[256,384]{0,1:T(8,128)(2,1)S(1)} %collective-permute-done.12), channel_id=1, source_target_pairs={{0,2},{1,3},{2,0},{3,1},{4,6},{5,7},{6,4},{7,5},{8,10},{9,11},{10,... | collective-permute-start | bytes 589832 | tf_op jit(solution)/shard_map/ppermute | solution.py:27
  (43 other events, 434.9 us)

commit v2 on v1

--- a/solution.py
+++ b/solution.py
@@ -88,6 +88,33 @@
     key_heads = packed[0].reshape(-1, head_count, HD)
     value_heads = packed[1].reshape(-1, head_count, HD)
     return attend(carry_state, query_heads, key_heads, value_heads, allowed)
+
+
+def split_exact(value):
+    high = value.astype(jnp.bfloat16)
+    rest = value - high.astype(jnp.float32)
+    middle = rest.astype(jnp.bfloat16)
+    low = (rest - middle.astype(jnp.float32)).astype(jnp.bfloat16)
+    return [high, middle, low]
+
+
+def pack_partial(state):
+    running_max, totals, accumulated = state
+    head_count, row_count = totals.shape
+    safe = jnp.where(totals > 0, totals, 1.0)
+    mean = (accumulated / safe[:, :, None]).astype(jnp.bfloat16)
+    stats = jnp.stack(split_exact(running_max) + split_exact(totals), axis=1)
+    stats = stats.reshape(head_count, 6 * row_count // HD, HD)
+    return jnp.concatenate([mean, stats], axis=1)
+
+
+def unpack_partial(packet, row_count):
+    head_count = packet.shape[0]
+    mean = packet[:, :row_count].astype(jnp.float32)
+    stats = packet[:, row_count:].reshape(head_count, 6, row_count).astype(jnp.float32)
+    part_max = (stats[:, 0] + stats[:, 1]) + stats[:, 2]
+    part_total = (stats[:, 3] + stats[:, 4]) + stats[:, 5]
+    return part_max, part_total, mean
 
 
 def gather_weight(out_weight, sizes, is_first):
@@ -191,35 +218,36 @@
         )
         weight_full = gather_weight(out_weight, sizes, is_first)
 
-        carry_state = visit_block(
-            empty_state(head_count, row_count), packed, seq_index, query_heads, query_clip, context
-        )
-        above = {}
-        below = {}
+        partner_kv = swap_cores(packed)
+        sign = 1 - 2 * core
+
+        def partial_for(q_heads, q_seq):
+            q_clip = clip_index(q_seq * row_count + row_ids, clip_ends)
+            state = visit_block(
+                empty_state(head_count, row_count), packed, seq_index, q_heads, q_clip, context
+            )
+            return visit_block(state, partner_kv, seq_index + sign, q_heads, q_clip, context)
+
+        own_max, own_total, own_acc = partial_for(query_heads, seq_index)
+        returned = []
         for d in range(1, 4):
-            above[d] = shifted(packed, CHIP, n_chip, -d)
-            carry_state = visit_block(
-                carry_state, above[d], seq_index + 2 * d, query_heads, query_clip, context
-            )
-            below[d] = shifted(packed, CHIP, n_chip, d)
-            carry_state = visit_block(
-                carry_state, below[d], seq_index - 2 * d, query_heads, query_clip, context
-            )
-        sign = 1 - 2 * core
-        outgoing = [
-            (packed, 1),
-            (jnp.where(is_first, above[1], below[1]), -1),
-            (jnp.where(is_first, above[2], below[2]), -3),
-            (jnp.where(is_first, above[3], below[3]), -5),
-            (jnp.where(is_first, below[1], above[1]), 3),
-            (jnp.where(is_first, below[2], above[2]), 5),
-        ]
-        for block, offset in outgoing:
-            got = swap_cores(block)
-            carry_state = visit_block(
-                carry_state, got, seq_index + sign * offset, query_heads, query_clip, context
-            )
-        running_max, totals, accumulated = carry_state
+            for direction in (1, -1):
+                visitor = shifted(queries, CHIP, n_chip, -direction * d)
+                state = partial_for(
+                    visitor.reshape(row_count, head_count, HD), seq_index + 2 * direction * d
+                )
+                back = shifted(pack_partial(state), CHIP, n_chip, direction * d)
+                returned.append(unpack_partial(back, row_count))
+        top = own_max
+        for part_max, part_total, _ in returned:
+            top = jnp.maximum(top, jnp.where(part_total > 0, part_max, low_score))
+        own_scale = jnp.exp(own_max - top)
+        totals = own_total * own_scale
+        accumulated = own_acc * own_scale[:, :, None]
+        for part_max, part_total, part_mean in returned:
+            scale = jnp.where(part_total > 0, part_total * jnp.exp(part_max - top), 0.0)
+            totals = totals + scale
+            accumulated = accumulated + part_mean * scale[:, :, None]
         result = accumulated / totals[:, :, None]
         attention_local = (
             jnp.transpose(result, (1, 0, 2)).reshape(row_count, tile_width).astype(jnp.bfloat16)

time: 279 us -> 350 us (1.25)
  the two profiles are of different devices: /device:TPU:240 before, /device:TPU:34 now
where the time goes in v2:
time: 350 us; the launch traced here: 347 us
  starting transfers between devices  122 us (35%)
  other arithmetic  72.6 us (21%)
  waiting for transfers between devices  66.1 us (19%)
  matrix products  52.8 us (15%)
  local copies, waits for them, and re-layouts  30.3 us (9%)
    ppermute x21, starting transfers between devices, shifted(): return lax.ppermute(block, axes, route)  82.8 us
    ppermute x21, waiting for transfers between devices, shifted(): return lax.ppermute(block, axes, route)  47.1 us
    dot_general x14, matrix products, attend(): jnp.einsum('qhd,khd->hqk', query_heads, key_heads, preferred_element_type...  30.7 us
    ppermute x4, waiting for transfers between devices, gather_weight(): got = lax.ppermute(row_block, ('y', 'c'), route)  18.9 us
    dot_general x14, matrix products, attend(): jnp.einsum('hqk,khd->hqd', weights.astype(jnp.bfloat16), value_heads, pre...  15.5 us
    and x14, other arithmetic, allowed_keys(): page_ok = jnp.any(member[:, :, None] & named_pages[None], axis=1) & in_range  15.3 us
    reduce_sum x14, other arithmetic, attend(): totals = totals * factor + jnp.sum(weights, axis=2)  14.7 us
    ppermute x4, starting transfers between devices, gather_weight(): got = lax.ppermute(row_block, ('y', 'c'), route)  14.5 us
  transfers between devices with their start and end apart: 32, of which 11 were waited for; matrix products, arithmetic and copies ran while one was open for 42% of the time, Pallas kernels for 0%

profile of v2, /device:TPU:34, one launch (start us, length us, event | category | flops | bytes accessed | tf_op | source)
XLA Modules:
  0.0 346.9 jit_solution(7083588989524016266)
XLA Ops:
  1.9 7.9 %collective-permute-start.11 = (bf16[256,384]{0,1:T(8,128)(2,1)}, bf16[256,384]{0,1:T(8,128)(2,1)}, u32[]{:S(2)}, u32[]{:S(2)}) collective-permute-start(bf16[256,384]{0,1:T(8,128)(2,1)} %copy.426), channel_id=1, source_target_pairs={{0,48},{16,64},{32,80},{48,96},{64,112},{80,128},{96,144},{112,160... | collective-permute-start | bytes 589832 | tf_op jit(solution)/shard_map/ppermute | solution.py:27
  11.7 4.2 %collective-permute-start.7 = (bf16[256,384]{0,1:T(8,128)(2,1)}, bf16[256,384]{0,1:T(8,128)(2,1)}, u32[]{:S(2)}, u32[]{:S(2)}) collective-permute-start(bf16[256,384]{0,1:T(8,128)(2,1)} %copy.426), channel_id=1, source_target_pairs={{0,32},{16,48},{32,64},{48,80},{64,96},{80,112},{96,128},{112,144}... | collective-permute-start | bytes 589832 | tf_op jit(solution)/shard_map/ppermute | solution.py:27
  16.0 4.6 %collective-permute-start.5 = (bf16[256,384]{0,1:T(8,128)(2,1)}, bf16[256,384]{0,1:T(8,128)(2,1)}, u32[]{:S(2)}, u32[]{:S(2)}) collective-permute-start(bf16[256,384]{0,1:T(8,128)(2,1)} %copy.426), channel_id=1, source_target_pairs={{32,0},{48,16},{64,32},{80,48},{96,64},{112,80},{128,96},{144,112}... | collective-permute-start | bytes 589832 | tf_op jit(solution)/shard_map/ppermute | solution.py:27
  70.5 5.1 %collective-permute-done.21 = bf16[96,640]{1,0:T(8,128)(2,1)} collective-permute-done((bf16[96,640]{1,0:T(8,128)(2,1)}, bf16[96,640]{1,0:T(8,128)(2,1)}, u32[]{:S(2)}, u32[]{:S(2)}) %collective-permute-start.21) | collective-permute-done | bytes 122912 | tf_op jit(solution)/shard_map/ppermute | solution.py:27
  78.5 5.9 %collective-permute-done.22 = bf16[96,640]{1,0:T(8,128)(2,1)S(1)} collective-permute-done((bf16[96,640]{1,0:T(8,128)(2,1)}, bf16[96,640]{1,0:T(8,128)(2,1)S(1)}, u32[]{:S(2)}, u32[]{:S(2)}) %collective-permute-start.22) | collective-permute-done | bytes 122912 | tf_op jit(solution)/shard_map/ppermute | solution.py:27
  84.3 3.7 %collective-permute-start.23 = (bf16[96,640]{1,0:T(8,128)(2,1)}, bf16[96,640]{1,0:T(8,128)(2,1)S(1)}, u32[]{:S(2)}, u32[]{:S(2)}) collective-permute-start(bf16[96,640]{1,0:T(8,128)(2,1)} %maximum_select_fusion.1), channel_id=1, source_target_pairs={{0,48},{16,0},{32,16},{48,32},{1,49},{17,1},{33,17},{49,33},{2,50}... | collective-permute-start | bytes 368648 | tf_op jit(solution)/shard_map/ppermute | solution.py:27
  88.0 3.3 collective-permute-done.23
  93.7 8.0 %collective-permute-start.1 = (bf16[256,384]{0,1:T(8,128)(2,1)}, bf16[256,384]{0,1:T(8,128)(2,1)S(1)}, u32[]{:S(2)}, u32[]{:S(2)}) collective-permute-start(bf16[256,384]{0,1:T(8,128)(2,1)} %copy.426), channel_id=1, source_target_pairs={{16,0},{32,16},{48,32},{64,48},{80,64},{96,80},{112,96},{128,112},... | collective-permute-start | bytes 589832 | tf_op jit(solution)/shard_map/ppermute | solution.py:27
  120.5 6.7 %collective-permute-start.30 = (bf16[384,640]{1,0:T(8,128)(2,1)S(1)}, bf16[384,640]{1,0:T(8,128)(2,1)}, u32[]{:S(2)}, u32[]{:S(2)}) collective-permute-start(bf16[384,640]{1,0:T(8,128)(2,1)S(1)} %bitcast.499), channel_id=1, source_target_pairs={{0,256},{64,320},{128,384},{192,448},{256,0},{320,64},{384,128},{4... | collective-permute-start | bytes 1474568 | tf_op jit(solution)/shard_map/ppermute | solution.py:146
  134.9 18.9 %collective-permute-done.28 = bf16[384,640]{1,0:T(8,128)(2,1)} collective-permute-done((bf16[384,640]{1,0:T(8,128)(2,1)S(1)}, bf16[384,640]{1,0:T(8,128)(2,1)}, u32[]{:S(2)}, u32[]{:S(2)}) %collective-permute-start.28) | collective-permute-done | bytes 491552 | tf_op jit(solution)/shard_map/ppermute | solution.py:146
  227.7 5.8 %collective-permute-start.10 = (bf16[3,268,128]{2,1,0:T(8,128)(2,1)}, bf16[3,268,128]{2,1,0:T(8,128)(2,1)}, u32[]{:S(2)}, u32[]{:S(2)}) collective-permute-start(bf16[3,268,128]{2,1,0:T(8,128)(2,1)} %pad_maximum_fusion.7), channel_id=1, source_target_pairs={{0,48},{16,64},{32,80},{48,96},{64,112},{80,128},{96,144},{112,160... | collective-permute-start | bytes 617480 | tf_op jit(solution)/shard_map/ppermute | solution.py:27
  234.3 3.7 %collective-permute-done.10 = bf16[3,268,128]{2,1,0:T(8,128)(2,1)} collective-permute-done((bf16[3,268,128]{2,1,0:T(8,128)(2,1)}, bf16[3,268,128]{2,1,0:T(8,128)(2,1)}, u32[]{:S(2)}, u32[]{:S(2)}) %collective-permute-start.10) | collective-permute-done | bytes 205856 | tf_op jit(solution)/shard_map/ppermute | solution.py:27
  238.0 5.8 %collective-permute-start.8 = (bf16[3,268,128]{2,1,0:T(8,128)(2,1)}, bf16[3,268,128]{2,1,0:T(8,128)(2,1)}, u32[]{:S(2)}, u32[]{:S(2)}) collective-permute-start(bf16[3,268,128]{2,1,0:T(8,128)(2,1)} %pad_maximum_fusion.6), channel_id=1, source_target_pairs={{32,0},{48,16},{64,32},{80,48},{96,64},{112,80},{128,96},{144,112}... | collective-permute-start | bytes 617480 | tf_op jit(solution)/shard_map/ppermute | solution.py:27
  244.5 6.2 %collective-permute-done.8 = bf16[3,268,128]{2,1,0:T(8,128)(2,1)} collective-permute-done((bf16[3,268,128]{2,1,0:T(8,128)(2,1)}, bf16[3,268,128]{2,1,0:T(8,128)(2,1)}, u32[]{:S(2)}, u32[]{:S(2)}) %collective-permute-start.8) | collective-permute-done | bytes 205856 | tf_op jit(solution)/shard_map/ppermute | solution.py:27
  250.7 4.6 %collective-permute-start.6 = (bf16[3,268,128]{2,1,0:T(8,128)(2,1)}, bf16[3,268,128]{2,1,0:T(8,128)(2,1)}, u32[]{:S(2)}, u32[]{:S(2)}) collective-permute-start(bf16[3,268,128]{2,1,0:T(8,128)(2,1)} %pad_maximum_fusion.5), channel_id=1, source_target_pairs={{0,32},{16,48},{32,64},{48,80},{64,96},{80,112},{96,128},{112,144}... | collective-permute-start | bytes 617480 | tf_op jit(solution)/shard_map/ppermute | solution.py:27
  256.7 7.1 %collective-permute-done.6 = bf16[3,268,128]{2,1,0:T(8,128)(2,1)} collective-permute-done((bf16[3,268,128]{2,1,0:T(8,128)(2,1)}, bf16[3,268,128]{2,1,0:T(8,128)(2,1)}, u32[]{:S(2)}, u32[]{:S(2)}) %collective-permute-start.6) | collective-permute-done | bytes 205856 | tf_op jit(solution)/shard_map/ppermute | solution.py:27
  263.7 5.5 %collective-permute-start.4 = (bf16[3,268,128]{2,1,0:T(8,128)(2,1)S(1)}, bf16[3,268,128]{2,1,0:T(8,128)(2,1)}, u32[]{:S(2)}, u32[]{:S(2)}) collective-permute-start(bf16[3,268,128]{2,1,0:T(8,128)(2,1)S(1)} %pad_maximum_fusion.4), channel_id=1, source_target_pairs={{16,0},{32,16},{48,32},{64,48},{80,64},{96,80},{112,96},{128,112},... | collective-permute-start | bytes 617480 | tf_op jit(solution)/shard_map/ppermute | solution.py:27
  276.7 8.4 %collective-permute-done.2 = bf16[3,268,128]{2,1,0:T(8,128)(2,1)} collective-permute-done((bf16[3,268,128]{2,1,0:T(8,128)(2,1)S(1)}, bf16[3,268,128]{2,1,0:T(8,128)(2,1)}, u32[]{:S(2)}, u32[]{:S(2)}) %collective-permute-start.2) | collective-permute-done | bytes 205856 | tf_op jit(solution)/shard_map/ppermute | solution.py:27
  293.9 11.6 %collective-permute-start.13 = (bf16[256,384]{0,1:T(8,128)(2,1)S(1)}, bf16[256,384]{0,1:T(8,128)(2,1)S(1)}, u32[]{:S(2)}, u32[]{:S(2)}) collective-permute-start(bf16[256,384]{0,1:T(8,128)(2,1)S(1)} %bitcast.510), channel_id=1, source_target_pairs={{0,4},{4,0},{1,5},{5,1},{2,6},{6,2},{3,7},{7,3},{8,12},{12,8},{9,1... | collective-permute-start | bytes 589832 | tf_op jit(solution)/shard_map/ppermute | solution.py:166
  305.7 3.4 collective-permute-start.14
  319.6 4.1 %collective-permute-start.18 = (bf16[256,384]{0,1:T(8,128)(2,1)S(1)}, bf16[256,384]{0,1:T(8,128)(2,1)S(1)}, u32[]{:S(2)}, u32[]{:S(2)}) collective-permute-start(bf16[256,384]{0,1:T(8,128)(2,1)S(1)} %bitcast.514), channel_id=1, source_target_pairs={{0,3},{1,0},{2,1},{3,2},{4,7},{5,4},{6,5},{7,6},{8,11},{9,8},{10,9... | collective-permute-start | bytes 589832 | tf_op jit(solution)/shard_map/ppermute | solution.py:27
  329.6 5.4 %collective-permute-start.17 = (bf16[256,384]{0,1:T(8,128)(2,1)S(1)}, bf16[256,384]{0,1:T(8,128)(2,1)S(1)}, u32[]{:S(2)}, u32[]{:S(2)}) collective-permute-start(bf16[256,384]{0,1:T(8,128)(2,1)S(1)} %collective-permute-done.13), channel_id=1, source_target_pairs={{0,2},{1,3},{2,0},{3,1},{4,6},{5,7},{6,4},{7,5},{8,10},{9,11},{10,... | collective-permute-start | bytes 589832 | tf_op jit(solution)/shard_map/ppermute | solution.py:27
  338.7 3.9 %collective-permute-done.19 = bf16[256,384]{0,1:T(8,128)(2,1)S(1)} collective-permute-done((bf16[256,384]{0,1:T(8,128)(2,1)S(1)}, bf16[256,384]{0,1:T(8,128)(2,1)S(1)}, u32[]{:S(2)}, u32[]{:S(2)}) %collective-permute-start.19) | collective-permute-done | bytes 196640 | tf_op jit(solution)/shard_map/ppermute | solution.py:27
  342.6 4.3 %fusion.29 = bf16[256,640]{1,0:T(8,128)(2,1)} fusion(f32[256,640]{1,0:T(8,128)S(1)} %copy-done.37, bf16[256,3072]{0,1:T(8,128)(2,1)S(1)} %constant_dynamic-update-slice_fusion.36, bf16[3072,640]{1,0:T(8,128)(2,1)} %bitcast.494, bf16[256,640]{1,0:T(8,128)(2,1)S(1)} %copy-done.135), kind=kOutput, calls=%fused_computation.58 | convolution fusion | flops 1007288320 | bytes 6815744 | tf_op jit(solution)/shard_map/dot_general | solution.py:256
  (545 shorter events, 196.2 us)
Async XLA Ops:
  1.9 91.8 %collective-permute-start.11 = (bf16[256,384]{0,1:T(8,128)(2,1)}, bf16[256,384]{0,1:T(8,128)(2,1)}, u32[]{:S(2)}, u32[]{:S(2)}) collective-permute-start(bf16[256,384]{0,1:T(8,128)(2,1)} %copy.426), channel_id=1, source_target_pairs={{0,48},{16,64},{32,80},{48,96},{64,112},{80,128},{96,144},{112,160... | collective-permute-start | bytes 589832 | tf_op jit(solution)/shard_map/ppermute | solution.py:27
  9.8 93.3 %collective-permute-start.9 = (bf16[256,384]{0,1:T(8,128)(2,1)}, bf16[256,384]{0,1:T(8,128)(2,1)}, u32[]{:S(2)}, u32[]{:S(2)}) collective-permute-start(bf16[256,384]{0,1:T(8,128)(2,1)} %copy.426), channel_id=1, source_target_pairs={{48,0},{64,16},{80,32},{96,48},{112,64},{128,80},{144,96},{160,112... | collective-permute-start | bytes 589832 | tf_op jit(solution)/shard_map/ppermute | solution.py:27
  11.7 95.9 %collective-permute-start.7 = (bf16[256,384]{0,1:T(8,128)(2,1)}, bf16[256,384]{0,1:T(8,128)(2,1)}, u32[]{:S(2)}, u32[]{:S(2)}) collective-permute-start(bf16[256,384]{0,1:T(8,128)(2,1)} %copy.426), channel_id=1, source_target_pairs={{0,32},{16,48},{32,64},{48,80},{64,96},{80,112},{96,128},{112,144}... | collective-permute-start | bytes 589832 | tf_op jit(solution)/shard_map/ppermute | solution.py:27
  16.0 96.2 %collective-permute-start.5 = (bf16[256,384]{0,1:T(8,128)(2,1)}, bf16[256,384]{0,1:T(8,128)(2,1)}, u32[]{:S(2)}, u32[]{:S(2)}) collective-permute-start(bf16[256,384]{0,1:T(8,128)(2,1)} %copy.426), channel_id=1, source_target_pairs={{32,0},{48,16},{64,32},{80,48},{96,64},{112,80},{128,96},{144,112}... | collective-permute-start | bytes 589832 | tf_op jit(solution)/shard_map/ppermute | solution.py:27
  20.6 43.7 %collective-permute-start.20 = (bf16[48,640]{1,0:T(8,128)(2,1)}, bf16[48,640]{1,0:T(8,128)(2,1)}, u32[]{:S(2)}, u32[]{:S(2)}) collective-permute-start(bf16[48,640]{1,0:T(8,128)(2,1)} %param.18), channel_id=1, source_target_pairs={{0,8},{8,0},{1,9},{9,1},{2,10},{10,2},{3,11},{11,3},{4,12},{12,4},... | collective-permute-start | bytes 184328 | tf_op jit(solution)/shard_map/ppermute | solution.py:31
  91.3 26.5 %collective-permute-start.3 = (bf16[256,384]{0,1:T(8,128)(2,1)}, bf16[256,384]{0,1:T(8,128)(2,1)S(1)}, u32[]{:S(2)}, u32[]{:S(2)}) collective-permute-start(bf16[256,384]{0,1:T(8,128)(2,1)} %copy.426), channel_id=1, source_target_pairs={{0,16},{16,32},{32,48},{48,64},{64,80},{80,96},{96,112},{112,128},... | collective-permute-start | bytes 589832 | tf_op jit(solution)/shard_map/ppermute | solution.py:27
  93.7 26.8 %collective-permute-start.1 = (bf16[256,384]{0,1:T(8,128)(2,1)}, bf16[256,384]{0,1:T(8,128)(2,1)S(1)}, u32[]{:S(2)}, u32[]{:S(2)}) collective-permute-start(bf16[256,384]{0,1:T(8,128)(2,1)} %copy.426), channel_id=1, source_target_pairs={{16,0},{32,16},{48,32},{64,48},{80,64},{96,80},{112,96},{128,112},... | collective-permute-start | bytes 589832 | tf_op jit(solution)/shard_map/ppermute | solution.py:27
  103.1 56.9 %collective-permute-start = (bf16[2,512,384]{1,2,0:T(8,128)(2,1)S(1)}, bf16[2,512,384]{1,2,0:T(8,128)(2,1)S(1)}, u32[]{:S(2)}, u32[]{:S(2)}) collective-permute-start(bf16[2,512,384]{1,2,0:T(8,128)(2,1)S(1)} %copy-done.35), channel_id=1, source_target_pairs={{0,8},{8,0},{1,9},{9,1},{2,10},{10,2},{3,11},{11,3},{4,12},{12,4},... | collective-permute-start | bytes 2359304 | tf_op jit(solution)/shard_map/ppermute | solution.py:31
  107.6 22.8 %collective-permute-start.24 = (bf16[384,640]{1,0:T(8,128)(2,1)S(1)}, bf16[384,640]{1,0:T(8,128)(2,1)}, u32[]{:S(2)}, u32[]{:S(2)}) collective-permute-start(bf16[384,640]{1,0:T(8,128)(2,1)S(1)} %bitcast.496), channel_id=1, source_target_pairs={{0,64},{64,128},{128,192},{192,256},{256,320},{320,384},{384,448},... | collective-permute-start | bytes 1474568 | tf_op jit(solution)/shard_map/ppermute | solution.py:146
  112.2 20.2 %collective-permute-start.26 = (bf16[384,640]{1,0:T(8,128)(2,1)S(1)}, bf16[384,640]{1,0:T(8,128)(2,1)}, u32[]{:S(2)}, u32[]{:S(2)}) collective-permute-start(bf16[384,640]{1,0:T(8,128)(2,1)S(1)} %bitcast.497), channel_id=1, source_target_pairs={{0,128},{64,192},{128,256},{192,320},{256,384},{320,448},{384,0},{... | collective-permute-start | bytes 1474568 | tf_op jit(solution)/shard_map/ppermute | solution.py:146
  117.8 36.0 %collective-permute-start.28 = (bf16[384,640]{1,0:T(8,128)(2,1)S(1)}, bf16[384,640]{1,0:T(8,128)(2,1)}, u32[]{:S(2)}, u32[]{:S(2)}) collective-permute-start(bf16[384,640]{1,0:T(8,128)(2,1)S(1)} %bitcast.498), channel_id=1, source_target_pairs={{0,192},{64,256},{128,320},{192,384},{256,448},{320,0},{384,64},{4... | collective-permute-start | bytes 1474568 | tf_op jit(solution)/shard_map/ppermute | solution.py:146
  120.5 35.2 %collective-permute-start.30 = (bf16[384,640]{1,0:T(8,128)(2,1)S(1)}, bf16[384,640]{1,0:T(8,128)(2,1)}, u32[]{:S(2)}, u32[]{:S(2)}) collective-permute-start(bf16[384,640]{1,0:T(8,128)(2,1)S(1)} %bitcast.499), channel_id=1, source_target_pairs={{0,256},{64,320},{128,384},{192,448},{256,0},{320,64},{384,128},{4... | collective-permute-start | bytes 1474568 | tf_op jit(solution)/shard_map/ppermute | solution.py:146
  130.4 175.3 %collective-permute-start.25 = (bf16[384,640]{1,0:T(8,128)(2,1)}, bf16[384,640]{1,0:T(8,128)(2,1)}, u32[]{:S(2)}, u32[]{:S(2)}) collective-permute-start(bf16[384,640]{1,0:T(8,128)(2,1)} %collective-permute-done.24), channel_id=1, source_target_pairs={{0,8},{8,0},{1,9},{9,1},{2,10},{10,2},{3,11},{11,3},{4,12},{12,4},... | collective-permute-start | bytes 1474568 | tf_op jit(solution)/shard_map/ppermute | solution.py:31
  132.4 180.4 %collective-permute-start.27 = (bf16[384,640]{1,0:T(8,128)(2,1)}, bf16[384,640]{1,0:T(8,128)(2,1)}, u32[]{:S(2)}, u32[]{:S(2)}) collective-permute-start(bf16[384,640]{1,0:T(8,128)(2,1)} %collective-permute-done.26), channel_id=1, source_target_pairs={{0,8},{8,0},{1,9},{9,1},{2,10},{10,2},{3,11},{11,3},{4,12},{12,4},... | collective-permute-start | bytes 1474568 | tf_op jit(solution)/shard_map/ppermute | solution.py:31
  153.8 165.8 %collective-permute-start.29 = (bf16[384,640]{1,0:T(8,128)(2,1)}, bf16[384,640]{1,0:T(8,128)(2,1)}, u32[]{:S(2)}, u32[]{:S(2)}) collective-permute-start(bf16[384,640]{1,0:T(8,128)(2,1)} %collective-permute-done.28), channel_id=1, source_target_pairs={{0,8},{8,0},{1,9},{9,1},{2,10},{10,2},{3,11},{11,3},{4,12},{12,4},... | collective-permute-start | bytes 1474568 | tf_op jit(solution)/shard_map/ppermute | solution.py:31
  155.7 169.8 %collective-permute-start.31 = (bf16[384,640]{1,0:T(8,128)(2,1)}, bf16[384,640]{1,0:T(8,128)(2,1)}, u32[]{:S(2)}, u32[]{:S(2)}) collective-permute-start(bf16[384,640]{1,0:T(8,128)(2,1)} %collective-permute-done.30), channel_id=1, source_target_pairs={{0,8},{1,9},{2,10},{3,11},{4,12},{5,13},{6,14},{7,15},{16,24},{17,... | collective-permute-start | bytes 1474568 | tf_op jit(solution)/shard_map/ppermute | solution.py:154
  185.6 42.0 %collective-permute-start.12 = (bf16[3,268,128]{2,1,0:T(8,128)(2,1)}, bf16[3,268,128]{2,1,0:T(8,128)(2,1)}, u32[]{:S(2)}, u32[]{:S(2)}) collective-permute-start(bf16[3,268,128]{2,1,0:T(8,128)(2,1)} %pad_maximum_fusion.8), channel_id=1, source_target_pairs={{48,0},{64,16},{80,32},{96,48},{112,64},{128,80},{144,96},{160,112... | collective-permute-start | bytes 617480 | tf_op jit(solution)/shard_map/ppermute | solution.py:27
  238.0 12.7 %collective-permute-start.8 = (bf16[3,268,128]{2,1,0:T(8,128)(2,1)}, bf16[3,268,128]{2,1,0:T(8,128)(2,1)}, u32[]{:S(2)}, u32[]{:S(2)}) collective-permute-start(bf16[3,268,128]{2,1,0:T(8,128)(2,1)} %pad_maximum_fusion.6), channel_id=1, source_target_pairs={{32,0},{48,16},{64,32},{80,48},{96,64},{112,80},{128,96},{144,112}... | collective-permute-start | bytes 617480 | tf_op jit(solution)/shard_map/ppermute | solution.py:27
  250.7 13.1 %collective-permute-start.6 = (bf16[3,268,128]{2,1,0:T(8,128)(2,1)}, bf16[3,268,128]{2,1,0:T(8,128)(2,1)}, u32[]{:S(2)}, u32[]{:S(2)}) collective-permute-start(bf16[3,268,128]{2,1,0:T(8,128)(2,1)} %pad_maximum_fusion.5), channel_id=1, source_target_pairs={{0,32},{16,48},{32,64},{48,80},{64,96},{80,112},{96,128},{112,144}... | collective-permute-start | bytes 617480 | tf_op jit(solution)/shard_map/ppermute | solution.py:27
  272.6 12.5 %collective-permute-start.2 = (bf16[3,268,128]{2,1,0:T(8,128)(2,1)S(1)}, bf16[3,268,128]{2,1,0:T(8,128)(2,1)}, u32[]{:S(2)}, u32[]{:S(2)}) collective-permute-start(bf16[3,268,128]{2,1,0:T(8,128)(2,1)S(1)} %pad_maximum_fusion.3), channel_id=1, source_target_pairs={{0,16},{16,32},{32,48},{48,64},{64,80},{80,96},{96,112},{112,128},... | collective-permute-start | bytes 617480 | tf_op jit(solution)/shard_map/ppermute | solution.py:27
  293.9 33.6 %collective-permute-start.13 = (bf16[256,384]{0,1:T(8,128)(2,1)S(1)}, bf16[256,384]{0,1:T(8,128)(2,1)S(1)}, u32[]{:S(2)}, u32[]{:S(2)}) collective-permute-start(bf16[256,384]{0,1:T(8,128)(2,1)S(1)} %bitcast.510), channel_id=1, source_target_pairs={{0,4},{4,0},{1,5},{5,1},{2,6},{6,2},{3,7},{7,3},{8,12},{12,8},{9,1... | collective-permute-start | bytes 589832 | tf_op jit(solution)/shard_map/ppermute | solution.py:166
  305.7 29.3 %collective-permute-start.14 = (bf16[256,384]{0,1:T(8,128)(2,1)S(1)}, bf16[256,384]{0,1:T(8,128)(2,1)S(1)}, u32[]{:S(2)}, u32[]{:S(2)}) collective-permute-start(bf16[256,384]{0,1:T(8,128)(2,1)S(1)} %bitcast.512), channel_id=1, source_target_pairs={{0,1},{1,2},{2,3},{3,0},{4,5},{5,6},{6,7},{7,4},{8,9},{9,10},{10,1... | collective-permute-start | bytes 589832 | tf_op jit(solution)/shard_map/ppermute | solution.py:27
  312.9 24.1 %collective-permute-start.16 = (bf16[256,384]{0,1:T(8,128)(2,1)S(1)}, bf16[256,384]{0,1:T(8,128)(2,1)S(1)}, u32[]{:S(2)}, u32[]{:S(2)}) collective-permute-start(bf16[256,384]{0,1:T(8,128)(2,1)S(1)} %bitcast.513), channel_id=1, source_target_pairs={{0,2},{1,3},{2,0},{3,1},{4,6},{5,7},{6,4},{7,5},{8,10},{9,11},{10,... | collective-permute-start | bytes 589832 | tf_op jit(solution)/shard_map/ppermute | solution.py:27
  319.6 19.0 %collective-permute-start.18 = (bf16[256,384]{0,1:T(8,128)(2,1)S(1)}, bf16[256,384]{0,1:T(8,128)(2,1)S(1)}, u32[]{:S(2)}, u32[]{:S(2)}) collective-permute-start(bf16[256,384]{0,1:T(8,128)(2,1)S(1)} %bitcast.514), channel_id=1, source_target_pairs={{0,3},{1,0},{2,1},{3,2},{4,7},{5,4},{6,5},{7,6},{8,11},{9,8},{10,9... | collective-permute-start | bytes 589832 | tf_op jit(solution)/shard_map/ppermute | solution.py:27
  (144 other events, 1018.9 us)

commit v3 on v1

--- a/solution.py
+++ b/solution.py
@@ -105,29 +105,35 @@
     for d in range(1, n_zl):
         got = shifted(pair, "zl", n_zl, d, wrap=True)
         row_block = lax.dynamic_update_index_in_dim(row_block, got, (zl - d) % n_zl, 0)
-    row_block = row_block.reshape(n_zl * 2 * rows, cols)
-
+    return row_block.reshape(n_zl * 2 * rows, cols)
+
+
+def spread_weight(row_block, sizes, is_first):
+    n_y = sizes["y"]
     y = lax.axis_index("y")
-    full = jnp.zeros((n_y, n_zl * 2 * rows, cols), out_weight.dtype)
+    cols = row_block.shape[1]
+    full = jnp.zeros((n_y,) + row_block.shape, row_block.dtype)
     full = lax.dynamic_update_index_in_dim(full, row_block, y, 0)
     below_count = n_y // 2
     above_count = (n_y - 1) // 2
+    received = []
     for j in range(1, below_count + 1):
         route = [(yy * 2, ((yy + j) % n_y) * 2) for yy in range(n_y)]
         if j <= above_count:
             route += [(yy * 2 + 1, ((yy - j) % n_y) * 2 + 1) for yy in range(n_y)]
-        got = lax.ppermute(row_block, ("y", "c"), route)
+        received.append(lax.ppermute(row_block, ("y", "c"), route))
+    traded = swap_cores(jnp.stack(received))
+    for j in range(1, below_count + 1):
+        got = received[j - 1]
         if j <= above_count:
-            traded = swap_cores(got)
             here = jnp.where(is_first, (y - j) % n_y, (y + j) % n_y)
             there = jnp.where(is_first, (y + j) % n_y, (y - j) % n_y)
             full = lax.dynamic_update_index_in_dim(full, got, here, 0)
-            full = lax.dynamic_update_index_in_dim(full, traded, there, 0)
+            full = lax.dynamic_update_index_in_dim(full, traded[j - 1], there, 0)
         else:
-            traded = lax.ppermute(got, "c", [(0, 1)])
-            value = jnp.where(is_first, got, traded)
+            value = jnp.where(is_first, got, traded[j - 1])
             full = lax.dynamic_update_index_in_dim(full, value, (y - j) % n_y, 0)
-    return full.reshape(n_y * n_zl * 2 * rows, cols)
+    return full.reshape(n_y * row_block.shape[0], cols)
 
 
 def gather_attention(attention_local, sizes):
@@ -137,14 +143,21 @@
     zh = lax.axis_index("zh")
     x = lax.axis_index("x")
     partner = lax.ppermute(attention_local, "zh", [(0, 1), (1, 0)])
-    pieces = [(attention_local, zh, x), (partner, 1 - zh, x)]
+    both = jnp.where(
+        zh == 0,
+        jnp.concatenate([attention_local, partner], axis=1),
+        jnp.concatenate([partner, attention_local], axis=1),
+    )
+    pieces = [(both, x)]
     for d in range(1, n_x):
-        pieces.append((shifted(attention_local, "x", n_x, d, wrap=True), zh, (x - d) % n_x))
-        pieces.append((shifted(partner, "x", n_x, d, wrap=True), 1 - zh, (x - d) % n_x))
+        pieces.append((shifted(both, "x", n_x, d, wrap=True), (x - d) % n_x))
     full = jnp.zeros((row_count, n_tensor * width), attention_local.dtype)
-    for piece, piece_zh, piece_x in pieces:
-        start = pl_multiple((piece_zh * n_x + piece_x) * width)
-        full = lax.dynamic_update_slice(full, piece, (jnp.int32(0), start))
+    for piece, piece_x in pieces:
+        for half in range(2):
+            start = pl_multiple((half * n_x + piece_x) * width)
+            full = lax.dynamic_update_slice(
+                full, piece[:, half * width:(half + 1) * width], (jnp.int32(0), start)
+            )
     return full
 
 
@@ -189,7 +202,9 @@
                 jnp.concatenate([value_tiles, cache_values.reshape(-1, tile_width)], axis=0),
             ]
         )
-        weight_full = gather_weight(out_weight, sizes, is_first)
+        row_block = gather_weight(out_weight, sizes, is_first)
+        packed, row_block = lax.optimization_barrier((packed, row_block))
+        weight_full = spread_weight(row_block, sizes, is_first)
 
         carry_state = visit_block(
             empty_state(head_count, row_count), packed, seq_index, query_heads, query_clip, context

time: 279 us -> 275 us (0.986)
  the two profiles are of different devices: /device:TPU:240 before, /device:TPU:147 now
where the time goes in v3:
time: 275 us; the launch traced here: 273 us
  starting transfers between devices  106 us (39%)
  waiting for transfers between devices  103 us (37%)
  other arithmetic  27.4 us (10%)
  local copies, waits for them, and re-layouts  18.8 us (7%)
  matrix products  16.6 us (6%)
    ppermute x12, waiting for transfers between devices, shifted(): return lax.ppermute(block, axes, route)  74.7 us
    ppermute x12, starting transfers between devices, shifted(): return lax.ppermute(block, axes, route)  64.7 us
    ppermute x4, waiting for transfers between devices, spread_weight(): received.append(lax.ppermute(row_block, ('y', 'c'), route))  23.8 us
    ppermute x8, starting transfers between devices, swap_cores(): return lax.ppermute(block, 'c', [(0, 1), (1, 0)])  21.8 us
    ppermute x4, starting transfers between devices, spread_weight(): received.append(lax.ppermute(row_block, ('y', 'c'), route))  12.4 us
    unnamed x41, local copies, waits for them, and re-layouts  8.21 us
    concatenate x13, other arithmetic, allowed_keys(): return jnp.concatenate([same_clip, page_ok], axis=1)  7.93 us
    ppermute x1, starting transfers between devices, gather_attention(): partner = lax.ppermute(attention_local, 'zh', [(0, 1), (1, 0)])  7.36 us
  transfers between devices with their start and end apart: 25, of which 9 were waited for; matrix products, arithmetic and copies ran while one was open for 19% of the time, Pallas kernels for 0%

profile of v3, /device:TPU:147, one launch (start us, length us, event | category | flops | bytes accessed | tf_op | source)
XLA Modules:
  0.0 273.1 jit_solution(14358851977311453314)
XLA Ops:
  0.0 2.8 %collective-permute-start = (bf16[48,640]{1,0:T(8,128)(2,1)}, bf16[48,640]{1,0:T(8,128)(2,1)}, u32[]{:S(2)}, u32[]{:S(2)}) collective-permute-start(bf16[48,640]{1,0:T(8,128)(2,1)} %param.18), channel_id=1, source_target_pairs={{0,8},{8,0},{1,9},{9,1},{2,10},{10,2},{3,11},{11,3},{4,12},{12,4},... | collective-permute-start | bytes 184328 | tf_op jit(solution)/shard_map/ppermute | solution.py:31
  28.0 4.0 %collective-permute-start.1 = (bf16[96,640]{1,0:T(8,128)(2,1)}, bf16[96,640]{1,0:T(8,128)(2,1)}, u32[]{:S(2)}, u32[]{:S(2)}) collective-permute-start(bf16[96,640]{1,0:T(8,128)(2,1)} %maximum_select_fusion.2), channel_id=1, source_target_pairs={{0,16},{16,32},{32,48},{48,0},{1,17},{17,33},{33,49},{49,1},{2,18}... | collective-permute-start | bytes 368648 | tf_op jit(solution)/shard_map/ppermute | solution.py:27
  34.6 3.1 %collective-permute-start.3 = (bf16[96,640]{1,0:T(8,128)(2,1)}, bf16[96,640]{1,0:T(8,128)(2,1)S(1)}, u32[]{:S(2)}, u32[]{:S(2)}) collective-permute-start(bf16[96,640]{1,0:T(8,128)(2,1)} %maximum_select_fusion.2), channel_id=1, source_target_pairs={{0,48},{16,0},{32,16},{48,32},{1,49},{17,1},{33,17},{49,33},{2,50}... | collective-permute-start | bytes 368648 | tf_op jit(solution)/shard_map/ppermute | solution.py:27
  46.7 5.1 %collective-permute-start.6 = (bf16[2,512,384]{1,2,0:T(8,128)(2,1)S(1)}, bf16[2,512,384]{1,2,0:T(8,128)(2,1)S(1)}, u32[]{:S(2)}, u32[]{:S(2)}) collective-permute-start(bf16[2,512,384]{1,2,0:T(8,128)(2,1)S(1)} %pad_maximum_fusion.1), channel_id=1, source_target_pairs={{32,0},{48,16},{64,32},{80,48},{96,64},{112,80},{128,96},{144,112}... | collective-permute-start | bytes 2359304 | tf_op jit(solution)/shard_map/ppermute | solution.py:27
  53.8 5.8 %collective-permute-start.22 = (bf16[384,640]{1,0:T(8,128)(2,1)}, bf16[384,640]{1,0:T(8,128)(2,1)S(1)}, u32[]{:S(2)}, u32[]{:S(2)}) collective-permute-start(bf16[384,640]{1,0:T(8,128)(2,1)} %bitcast.11), channel_id=1, source_target_pairs={{0,192},{64,256},{128,320},{192,384},{256,448},{320,0},{384,64},{4... | collective-permute-start | bytes 1474568 | tf_op jit(solution)/shard_map/ppermute | solution.py:124
  62.0 3.8 %collective-permute-start.21 = (bf16[384,640]{1,0:T(8,128)(2,1)}, bf16[384,640]{1,0:T(8,128)(2,1)S(1)}, u32[]{:S(2)}, u32[]{:S(2)}) collective-permute-start(bf16[384,640]{1,0:T(8,128)(2,1)} %bitcast.11), channel_id=1, source_target_pairs={{0,128},{64,192},{128,256},{192,320},{256,384},{320,448},{384,0},{... | collective-permute-start | bytes 1474568 | tf_op jit(solution)/shard_map/ppermute | solution.py:124
  66.0 3.4 %collective-permute-start.4 = (bf16[2,512,384]{1,2,0:T(8,128)(2,1)S(1)}, bf16[2,512,384]{1,2,0:T(8,128)(2,1)S(1)}, u32[]{:S(2)}, u32[]{:S(2)}) collective-permute-start(bf16[2,512,384]{1,2,0:T(8,128)(2,1)S(1)} %pad_maximum_fusion.1), channel_id=1, source_target_pairs={{16,0},{32,16},{48,32},{64,48},{80,64},{96,80},{112,96},{128,112},... | collective-permute-start | bytes 2359304 | tf_op jit(solution)/shard_map/ppermute | solution.py:27
  69.3 16.1 %collective-permute-done.22 = bf16[384,640]{1,0:T(8,128)(2,1)S(1)} collective-permute-done((bf16[384,640]{1,0:T(8,128)(2,1)}, bf16[384,640]{1,0:T(8,128)(2,1)S(1)}, u32[]{:S(2)}, u32[]{:S(2)}) %collective-permute-start.22) | collective-permute-done | bytes 491552 | tf_op jit(solution)/shard_map/ppermute | solution.py:124
  89.1 7.7 %collective-permute-done.21 = bf16[384,640]{1,0:T(8,128)(2,1)S(1)} collective-permute-done((bf16[384,640]{1,0:T(8,128)(2,1)}, bf16[384,640]{1,0:T(8,128)(2,1)S(1)}, u32[]{:S(2)}, u32[]{:S(2)}) %collective-permute-start.21) | collective-permute-done | bytes 491552 | tf_op jit(solution)/shard_map/ppermute | solution.py:124
  96.8 28.4 %collective-permute-start.8 = (bf16[2,512,384]{1,2,0:T(8,128)(2,1)S(1)}, bf16[2,512,384]{1,2,0:T(8,128)(2,1)S(1)}, u32[]{:S(2)}, u32[]{:S(2)}) collective-permute-start(bf16[2,512,384]{1,2,0:T(8,128)(2,1)S(1)} %pad_maximum_fusion.1), channel_id=1, source_target_pairs={{48,0},{64,16},{80,32},{96,48},{112,64},{128,80},{144,96},{160,112... | collective-permute-start | bytes 2359304 | tf_op jit(solution)/shard_map/ppermute | solution.py:27
  125.2 5.0 %collective-permute-start.9 = (bf16[2,512,384]{1,2,0:T(8,128)(2,1)S(1)}, bf16[2,512,384]{1,2,0:T(8,128)(2,1)S(1)}, u32[]{:S(2)}, u32[]{:S(2)}) collective-permute-start(bf16[2,512,384]{1,2,0:T(8,128)(2,1)S(1)} %pad_maximum_fusion.1), channel_id=1, source_target_pairs={{0,48},{16,64},{32,80},{48,96},{64,112},{80,128},{96,144},{112,160... | collective-permute-start | bytes 2359304 | tf_op jit(solution)/shard_map/ppermute | solution.py:27
  133.0 5.2 %collective-permute-start.10 = (bf16[2,512,384]{1,2,0:T(8,128)(2,1)S(1)}, bf16[2,512,384]{1,2,0:T(8,128)(2,1)S(1)}, u32[]{:S(2)}, u32[]{:S(2)}) collective-permute-start(bf16[2,512,384]{1,2,0:T(8,128)(2,1)S(1)} %pad_maximum_fusion.1), channel_id=1, source_target_pairs={{0,8},{8,0},{1,9},{9,1},{2,10},{10,2},{3,11},{11,3},{4,12},{12,4},... | collective-permute-start | bytes 2359304 | tf_op jit(solution)/shard_map/ppermute | solution.py:31
  138.3 48.6 %collective-permute-done.4 = bf16[2,512,384]{1,2,0:T(8,128)(2,1)S(1)} collective-permute-done((bf16[2,512,384]{1,2,0:T(8,128)(2,1)S(1)}, bf16[2,512,384]{1,2,0:T(8,128)(2,1)S(1)}, u32[]{:S(2)}, u32[]{:S(2)}) %collective-permute-start.4) | collective-permute-done | bytes 786464 | tf_op jit(solution)/shard_map/ppermute | solution.py:27
  186.9 2.5 collective-permute-start.24
  189.4 9.4 %collective-permute-done.5 = bf16[2,512,384]{1,2,0:T(8,128)(2,1)S(1)} collective-permute-done((bf16[2,512,384]{1,2,0:T(8,128)(2,1)S(1)}, bf16[2,512,384]{1,2,0:T(8,128)(2,1)S(1)}, u32[]{:S(2)}, u32[]{:S(2)}) %collective-permute-start.5) | collective-permute-done | bytes 786464 | tf_op jit(solution)/shard_map/ppermute | solution.py:27
  203.5 2.4 collective-permute-start.13
  214.0 2.4 collective-permute-start.11
  231.1 7.4 %collective-permute-start.16 = (bf16[256,384]{0,1:T(8,128)(2,1)S(1)}, bf16[256,384]{0,1:T(8,128)(2,1)S(1)}, u32[]{:S(2)}, u32[]{:S(2)}) collective-permute-start(bf16[256,384]{0,1:T(8,128)(2,1)S(1)} %bitcast.478), channel_id=1, source_target_pairs={{0,4},{4,0},{1,5},{5,1},{2,6},{6,2},{3,7},{7,3},{8,12},{12,8},{9,1... | collective-permute-start | bytes 589832 | tf_op jit(solution)/shard_map/ppermute | solution.py:145
  239.5 4.0 %collective-permute-done.16 = bf16[256,384]{0,1:T(8,128)(2,1)S(1)} collective-permute-done((bf16[256,384]{0,1:T(8,128)(2,1)S(1)}, bf16[256,384]{0,1:T(8,128)(2,1)S(1)}, u32[]{:S(2)}, u32[]{:S(2)}) %collective-permute-start.16) | collective-permute-done | bytes 196640 | tf_op jit(solution)/shard_map/ppermute | solution.py:145
  243.7 3.1 %collective-permute-start.17 = (bf16[256,768]{0,1:T(8,128)(2,1)S(1)}, bf16[256,768]{0,1:T(8,128)(2,1)S(1)}, u32[]{:S(2)}, u32[]{:S(2)}) collective-permute-start(bf16[256,768]{0,1:T(8,128)(2,1)S(1)} %maximum_select_fusion), channel_id=1, source_target_pairs={{0,1},{1,2},{2,3},{3,0},{4,5},{5,6},{6,7},{7,4},{8,9},{9,10},{10,1... | collective-permute-start | bytes 1179656 | tf_op jit(solution)/shard_map/ppermute | solution.py:27
  246.9 2.8 %collective-permute-start.18 = (bf16[256,768]{0,1:T(8,128)(2,1)S(1)}, bf16[256,768]{0,1:T(8,128)(2,1)S(1)}, u32[]{:S(2)}, u32[]{:S(2)}) collective-permute-start(bf16[256,768]{0,1:T(8,128)(2,1)S(1)} %maximum_select_fusion), channel_id=1, source_target_pairs={{0,2},{1,3},{2,0},{3,1},{4,6},{5,7},{6,4},{7,5},{8,10},{9,11},{10,... | collective-permute-start | bytes 1179656 | tf_op jit(solution)/shard_map/ppermute | solution.py:27
  249.7 3.7 %collective-permute-start.19 = (bf16[256,768]{0,1:T(8,128)(2,1)S(1)}, bf16[256,768]{0,1:T(8,128)(2,1)S(1)}, u32[]{:S(2)}, u32[]{:S(2)}) collective-permute-start(bf16[256,768]{0,1:T(8,128)(2,1)S(1)} %maximum_select_fusion), channel_id=1, source_target_pairs={{0,3},{1,0},{2,1},{3,2},{4,7},{5,4},{6,5},{7,6},{8,11},{9,8},{10,9... | collective-permute-start | bytes 1179656 | tf_op jit(solution)/shard_map/ppermute | solution.py:27
  255.6 4.3 %collective-permute-done.18 = bf16[256,768]{0,1:T(8,128)(2,1)S(1)} collective-permute-done((bf16[256,768]{0,1:T(8,128)(2,1)S(1)}, bf16[256,768]{0,1:T(8,128)(2,1)S(1)}, u32[]{:S(2)}, u32[]{:S(2)}) %collective-permute-start.18) | collective-permute-done | bytes 393248 | tf_op jit(solution)/shard_map/ppermute | solution.py:27
  260.0 9.7 %collective-permute-done.19 = bf16[256,768]{0,1:T(8,128)(2,1)S(1)} collective-permute-done((bf16[256,768]{0,1:T(8,128)(2,1)S(1)}, bf16[256,768]{0,1:T(8,128)(2,1)S(1)}, u32[]{:S(2)}, u32[]{:S(2)}) %collective-permute-start.19) | collective-permute-done | bytes 393248 | tf_op jit(solution)/shard_map/ppermute | solution.py:27
  (221 shorter events, 80.9 us)
Async XLA Ops:
  0.0 26.4 %collective-permute-start = (bf16[48,640]{1,0:T(8,128)(2,1)}, bf16[48,640]{1,0:T(8,128)(2,1)}, u32[]{:S(2)}, u32[]{:S(2)}) collective-permute-start(bf16[48,640]{1,0:T(8,128)(2,1)} %param.18), channel_id=1, source_target_pairs={{0,8},{8,0},{1,9},{9,1},{2,10},{10,2},{3,11},{11,3},{4,12},{12,4},... | collective-permute-start | bytes 184328 | tf_op jit(solution)/shard_map/ppermute | solution.py:31
  28.0 12.1 %collective-permute-start.1 = (bf16[96,640]{1,0:T(8,128)(2,1)}, bf16[96,640]{1,0:T(8,128)(2,1)}, u32[]{:S(2)}, u32[]{:S(2)}) collective-permute-start(bf16[96,640]{1,0:T(8,128)(2,1)} %maximum_select_fusion.2), channel_id=1, source_target_pairs={{0,16},{16,32},{32,48},{48,0},{1,17},{17,33},{33,49},{49,1},{2,18}... | collective-permute-start | bytes 368648 | tf_op jit(solution)/shard_map/ppermute | solution.py:27
  32.7 9.0 %collective-permute-start.2 = (bf16[96,640]{1,0:T(8,128)(2,1)}, bf16[96,640]{1,0:T(8,128)(2,1)S(1)}, u32[]{:S(2)}, u32[]{:S(2)}) collective-permute-start(bf16[96,640]{1,0:T(8,128)(2,1)} %maximum_select_fusion.2), channel_id=1, source_target_pairs={{0,32},{16,48},{32,0},{48,16},{1,33},{17,49},{33,1},{49,17},{2,34}... | collective-permute-start | bytes 368648 | tf_op jit(solution)/shard_map/ppermute | solution.py:27
  34.6 8.4 %collective-permute-start.3 = (bf16[96,640]{1,0:T(8,128)(2,1)}, bf16[96,640]{1,0:T(8,128)(2,1)S(1)}, u32[]{:S(2)}, u32[]{:S(2)}) collective-permute-start(bf16[96,640]{1,0:T(8,128)(2,1)} %maximum_select_fusion.2), channel_id=1, source_target_pairs={{0,48},{16,0},{32,16},{48,32},{1,49},{17,1},{33,17},{49,33},{2,50}... | collective-permute-start | bytes 368648 | tf_op jit(solution)/shard_map/ppermute | solution.py:27
  43.7 18.4 %collective-permute-start.20 = (bf16[384,640]{1,0:T(8,128)(2,1)}, bf16[384,640]{1,0:T(8,128)(2,1)}, u32[]{:S(2)}, u32[]{:S(2)}) collective-permute-start(bf16[384,640]{1,0:T(8,128)(2,1)} %bitcast.11), channel_id=1, source_target_pairs={{0,64},{64,128},{128,192},{192,256},{256,320},{320,384},{384,448},... | collective-permute-start | bytes 1474568 | tf_op jit(solution)/shard_map/ppermute | solution.py:124
  46.7 78.5 %collective-permute-start.6 = (bf16[2,512,384]{1,2,0:T(8,128)(2,1)S(1)}, bf16[2,512,384]{1,2,0:T(8,128)(2,1)S(1)}, u32[]{:S(2)}, u32[]{:S(2)}) collective-permute-start(bf16[2,512,384]{1,2,0:T(8,128)(2,1)S(1)} %pad_maximum_fusion.1), channel_id=1, source_target_pairs={{32,0},{48,16},{64,32},{80,48},{96,64},{112,80},{128,96},{144,112}... | collective-permute-start | bytes 2359304 | tf_op jit(solution)/shard_map/ppermute | solution.py:27
  53.1 12.8 %collective-permute-start.23 = (bf16[384,640]{1,0:T(8,128)(2,1)}, bf16[384,640]{1,0:T(8,128)(2,1)S(1)}, u32[]{:S(2)}, u32[]{:S(2)}) collective-permute-start(bf16[384,640]{1,0:T(8,128)(2,1)} %bitcast.11), channel_id=1, source_target_pairs={{0,256},{64,320},{128,384},{192,448},{256,0},{320,64},{384,128},{4... | collective-permute-start | bytes 1474568 | tf_op jit(solution)/shard_map/ppermute | solution.py:124
  53.8 31.7 %collective-permute-start.22 = (bf16[384,640]{1,0:T(8,128)(2,1)}, bf16[384,640]{1,0:T(8,128)(2,1)S(1)}, u32[]{:S(2)}, u32[]{:S(2)}) collective-permute-start(bf16[384,640]{1,0:T(8,128)(2,1)} %bitcast.11), channel_id=1, source_target_pairs={{0,192},{64,256},{128,320},{192,384},{256,448},{320,0},{384,64},{4... | collective-permute-start | bytes 1474568 | tf_op jit(solution)/shard_map/ppermute | solution.py:124
  60.1 72.9 %collective-permute-start.7 = (bf16[2,512,384]{1,2,0:T(8,128)(2,1)S(1)}, bf16[2,512,384]{1,2,0:T(8,128)(2,1)S(1)}, u32[]{:S(2)}, u32[]{:S(2)}) collective-permute-start(bf16[2,512,384]{1,2,0:T(8,128)(2,1)S(1)} %pad_maximum_fusion.1), channel_id=1, source_target_pairs={{0,32},{16,48},{32,64},{48,80},{64,96},{80,112},{96,128},{112,144}... | collective-permute-start | bytes 2359304 | tf_op jit(solution)/shard_map/ppermute | solution.py:27
  62.0 34.8 %collective-permute-start.21 = (bf16[384,640]{1,0:T(8,128)(2,1)}, bf16[384,640]{1,0:T(8,128)(2,1)S(1)}, u32[]{:S(2)}, u32[]{:S(2)}) collective-permute-start(bf16[384,640]{1,0:T(8,128)(2,1)} %bitcast.11), channel_id=1, source_target_pairs={{0,128},{64,192},{128,256},{192,320},{256,384},{320,448},{384,0},{... | collective-permute-start | bytes 1474568 | tf_op jit(solution)/shard_map/ppermute | solution.py:124
  66.0 121.0 %collective-permute-start.4 = (bf16[2,512,384]{1,2,0:T(8,128)(2,1)S(1)}, bf16[2,512,384]{1,2,0:T(8,128)(2,1)S(1)}, u32[]{:S(2)}, u32[]{:S(2)}) collective-permute-start(bf16[2,512,384]{1,2,0:T(8,128)(2,1)S(1)} %pad_maximum_fusion.1), channel_id=1, source_target_pairs={{16,0},{32,16},{48,32},{64,48},{80,64},{96,80},{112,96},{128,112},... | collective-permute-start | bytes 2359304 | tf_op jit(solution)/shard_map/ppermute | solution.py:27
  85.5 113.3 %collective-permute-start.5 = (bf16[2,512,384]{1,2,0:T(8,128)(2,1)S(1)}, bf16[2,512,384]{1,2,0:T(8,128)(2,1)S(1)}, u32[]{:S(2)}, u32[]{:S(2)}) collective-permute-start(bf16[2,512,384]{1,2,0:T(8,128)(2,1)S(1)} %pad_maximum_fusion.1), channel_id=1, source_target_pairs={{0,16},{16,32},{32,48},{48,64},{64,80},{80,96},{96,112},{112,128},... | collective-permute-start | bytes 2359304 | tf_op jit(solution)/shard_map/ppermute | solution.py:27
  96.8 104.5 %collective-permute-start.8 = (bf16[2,512,384]{1,2,0:T(8,128)(2,1)S(1)}, bf16[2,512,384]{1,2,0:T(8,128)(2,1)S(1)}, u32[]{:S(2)}, u32[]{:S(2)}) collective-permute-start(bf16[2,512,384]{1,2,0:T(8,128)(2,1)S(1)} %pad_maximum_fusion.1), channel_id=1, source_target_pairs={{48,0},{64,16},{80,32},{96,48},{112,64},{128,80},{144,96},{160,112... | collective-permute-start | bytes 2359304 | tf_op jit(solution)/shard_map/ppermute | solution.py:27
  125.2 78.2 %collective-permute-start.9 = (bf16[2,512,384]{1,2,0:T(8,128)(2,1)S(1)}, bf16[2,512,384]{1,2,0:T(8,128)(2,1)S(1)}, u32[]{:S(2)}, u32[]{:S(2)}) collective-permute-start(bf16[2,512,384]{1,2,0:T(8,128)(2,1)S(1)} %pad_maximum_fusion.1), channel_id=1, source_target_pairs={{0,48},{16,64},{32,80},{48,96},{64,112},{80,128},{96,144},{112,160... | collective-permute-start | bytes 2359304 | tf_op jit(solution)/shard_map/ppermute | solution.py:27
  133.0 72.9 %collective-permute-start.10 = (bf16[2,512,384]{1,2,0:T(8,128)(2,1)S(1)}, bf16[2,512,384]{1,2,0:T(8,128)(2,1)S(1)}, u32[]{:S(2)}, u32[]{:S(2)}) collective-permute-start(bf16[2,512,384]{1,2,0:T(8,128)(2,1)S(1)} %pad_maximum_fusion.1), channel_id=1, source_target_pairs={{0,8},{8,0},{1,9},{9,1},{2,10},{10,2},{3,11},{11,3},{4,12},{12,4},... | collective-permute-start | bytes 2359304 | tf_op jit(solution)/shard_map/ppermute | solution.py:31
  186.9 82.8 %collective-permute-start.24 = (bf16[4,384,640]{2,1,0:T(8,128)(2,1)S(1)}, bf16[4,384,640]{2,1,0:T(8,128)(2,1)S(1)}, u32[]{:S(2)}, u32[]{:S(2)}) collective-permute-start(bf16[4,384,640]{2,1,0:T(8,128)(2,1)S(1)} %pad_maximum_fusion), channel_id=1, source_target_pairs={{0,8},{8,0},{1,9},{9,1},{2,10},{10,2},{3,11},{11,3},{4,12},{12,4},... | collective-permute-start | bytes 5898248 | tf_op jit(solution)/shard_map/ppermute | solution.py:31
  198.8 15.2 %collective-permute-start.15 = (bf16[2,512,384]{1,2,0:T(8,128)(2,1)S(1)}, bf16[2,512,384]{1,2,0:T(8,128)(2,1)S(1)}, u32[]{:S(2)}, u32[]{:S(2)}) collective-permute-start(bf16[2,512,384]{1,2,0:T(8,128)(2,1)S(1)} %get-tuple-element.79), channel_id=1, source_target_pairs={{0,8},{8,0},{1,9},{9,1},{2,10},{10,2},{3,11},{11,3},{4,12},{12,4},... | collective-permute-start | bytes 2359304 | tf_op jit(solution)/shard_map/ppermute | solution.py:31
  201.3 15.2 %collective-permute-start.14 = (bf16[2,512,384]{1,2,0:T(8,128)(2,1)S(1)}, bf16[2,512,384]{1,2,0:T(8,128)(2,1)S(1)}, u32[]{:S(2)}, u32[]{:S(2)}) collective-permute-start(bf16[2,512,384]{1,2,0:T(8,128)(2,1)S(1)} %get-tuple-element.77), channel_id=1, source_target_pairs={{0,8},{8,0},{1,9},{9,1},{2,10},{10,2},{3,11},{11,3},{4,12},{12,4},... | collective-permute-start | bytes 2359304 | tf_op jit(solution)/shard_map/ppermute | solution.py:31
  203.5 13.1 %collective-permute-start.13 = (bf16[2,512,384]{1,2,0:T(8,128)(2,1)S(1)}, bf16[2,512,384]{1,2,0:T(8,128)(2,1)S(1)}, u32[]{:S(2)}, u32[]{:S(2)}) collective-permute-start(bf16[2,512,384]{1,2,0:T(8,128)(2,1)S(1)} %broadcast_select_fusion.2), channel_id=1, source_target_pairs={{0,8},{8,0},{1,9},{9,1},{2,10},{10,2},{3,11},{11,3},{4,12},{12,4},... | collective-permute-start | bytes 2359304 | tf_op jit(solution)/shard_map/ppermute | solution.py:31
  205.9 12.5 %collective-permute-start.12 = (bf16[2,512,384]{1,2,0:T(8,128)(2,1)S(1)}, bf16[2,512,384]{1,2,0:T(8,128)(2,1)S(1)}, u32[]{:S(2)}, u32[]{:S(2)}) collective-permute-start(bf16[2,512,384]{1,2,0:T(8,128)(2,1)S(1)} %get-tuple-element.78), channel_id=1, source_target_pairs={{0,8},{8,0},{1,9},{9,1},{2,10},{10,2},{3,11},{11,3},{4,12},{12,4},... | collective-permute-start | bytes 2359304 | tf_op jit(solution)/shard_map/ppermute | solution.py:31
  231.1 12.5 %collective-permute-start.16 = (bf16[256,384]{0,1:T(8,128)(2,1)S(1)}, bf16[256,384]{0,1:T(8,128)(2,1)S(1)}, u32[]{:S(2)}, u32[]{:S(2)}) collective-permute-start(bf16[256,384]{0,1:T(8,128)(2,1)S(1)} %bitcast.478), channel_id=1, source_target_pairs={{0,4},{4,0},{1,5},{5,1},{2,6},{6,2},{3,7},{7,3},{8,12},{12,8},{9,1... | collective-permute-start | bytes 589832 | tf_op jit(solution)/shard_map/ppermute | solution.py:145
  243.7 11.8 %collective-permute-start.17 = (bf16[256,768]{0,1:T(8,128)(2,1)S(1)}, bf16[256,768]{0,1:T(8,128)(2,1)S(1)}, u32[]{:S(2)}, u32[]{:S(2)}) collective-permute-start(bf16[256,768]{0,1:T(8,128)(2,1)S(1)} %maximum_select_fusion), channel_id=1, source_target_pairs={{0,1},{1,2},{2,3},{3,0},{4,5},{5,6},{6,7},{7,4},{8,9},{9,10},{10,1... | collective-permute-start | bytes 1179656 | tf_op jit(solution)/shard_map/ppermute | solution.py:27
  246.9 13.1 %collective-permute-start.18 = (bf16[256,768]{0,1:T(8,128)(2,1)S(1)}, bf16[256,768]{0,1:T(8,128)(2,1)S(1)}, u32[]{:S(2)}, u32[]{:S(2)}) collective-permute-start(bf16[256,768]{0,1:T(8,128)(2,1)S(1)} %maximum_select_fusion), channel_id=1, source_target_pairs={{0,2},{1,3},{2,0},{3,1},{4,6},{5,7},{6,4},{7,5},{8,10},{9,11},{10,... | collective-permute-start | bytes 1179656 | tf_op jit(solution)/shard_map/ppermute | solution.py:27
  249.7 20.0 %collective-permute-start.19 = (bf16[256,768]{0,1:T(8,128)(2,1)S(1)}, bf16[256,768]{0,1:T(8,128)(2,1)S(1)}, u32[]{:S(2)}, u32[]{:S(2)}) collective-permute-start(bf16[256,768]{0,1:T(8,128)(2,1)S(1)} %maximum_select_fusion), channel_id=1, source_target_pairs={{0,3},{1,0},{2,1},{3,2},{4,7},{5,4},{6,5},{7,6},{8,11},{9,8},{10,9... | collective-permute-start | bytes 1179656 | tf_op jit(solution)/shard_map/ppermute | solution.py:27
  (20 other events, 107.8 us)

commit v4 on v3

--- a/solution.py
+++ b/solution.py
@@ -202,9 +202,6 @@
                 jnp.concatenate([value_tiles, cache_values.reshape(-1, tile_width)], axis=0),
             ]
         )
-        row_block = gather_weight(out_weight, sizes, is_first)
-        packed, row_block = lax.optimization_barrier((packed, row_block))
-        weight_full = spread_weight(row_block, sizes, is_first)
 
         carry_state = visit_block(
             empty_state(head_count, row_count), packed, seq_index, query_heads, query_clip, context
@@ -221,6 +218,13 @@
                 carry_state, below[d], seq_index - 2 * d, query_heads, query_clip, context
             )
         sign = 1 - 2 * core
+        gated = lax.optimization_barrier(
+            (out_weight, above[1], above[2], above[3], below[1], below[2], below[3])
+        )
+        out_weight = gated[0]
+        above = dict(zip((1, 2, 3), gated[1:4]))
+        below = dict(zip((1, 2, 3), gated[4:7]))
+        weight_full = spread_weight(gather_weight(out_weight, sizes, is_first), sizes, is_first)
         outgoing = [
             (packed, 1),
             (jnp.where(is_first, above[1], below[1]), -1),

time: 275 us -> 300 us (1.091)
  the two profiles are of different devices: /device:TPU:147 before, /device:TPU:11 now
where the time goes in v4:
time: 300 us; the launch traced here: 299 us
  starting transfers between devices  110 us (37%)
  waiting for transfers between devices  109 us (36%)
  other arithmetic  37.6 us (13%)
  local copies, waits for them, and re-layouts  23.9 us (8%)
  matrix products  16.4 us (5%)
    ppermute x12, waiting for transfers between devices, shifted(): return lax.ppermute(block, axes, route)  101 us
    ppermute x8, starting transfers between devices, swap_cores(): return lax.ppermute(block, 'c', [(0, 1), (1, 0)])  46.3 us
    ppermute x12, starting transfers between devices, shifted(): return lax.ppermute(block, axes, route)  42.4 us
    ppermute x4, starting transfers between devices, spread_weight(): received.append(lax.ppermute(row_block, ('y', 'c'), route))  13.8 us
    unnamed x52, local copies, waits for them, and re-layouts  9.2 us
    concatenate x13, other arithmetic, allowed_keys(): return jnp.concatenate([same_clip, page_ok], axis=1)  9.15 us
    ppermute x1, starting transfers between devices, gather_attention(): partner = lax.ppermute(attention_local, 'zh', [(0, 1), (1, 0)])  8 us
    ppermute x1, waiting for transfers between devices, gather_attention(): partner = lax.ppermute(attention_local, 'zh', [(0, 1), (1, 0)])  7.66 us
  transfers between devices with their start and end apart: 25, of which 8 were waited for; matrix products, arithmetic and copies ran while one was open for 22% of the time, Pallas kernels for 0%

profile of v4, /device:TPU:11, one launch (start us, length us, event | category | flops | bytes accessed | tf_op | source)
XLA Modules:
  0.0 298.7 jit_solution(6579258051702857186)
XLA Ops:
  5.6 7.6 %collective-permute-start = (bf16[2,512,384]{1,2,0:T(8,128)(2,1)}, bf16[2,512,384]{1,2,0:T(8,128)(2,1)}, u32[]{:S(2)}, u32[]{:S(2)}) collective-permute-start(bf16[2,512,384]{1,2,0:T(8,128)(2,1)} %pad_maximum_fusion.1), channel_id=1, source_target_pairs={{16,0},{32,16},{48,32},{64,48},{80,64},{96,80},{112,96},{128,112},... | collective-permute-start | bytes 2359304 | tf_op jit(solution)/shard_map/ppermute | solution.py:27
  17.1 2.2 collective-permute-start.1
  19.3 5.2 %collective-permute-start.3 = (bf16[2,512,384]{1,2,0:T(8,128)(2,1)}, bf16[2,512,384]{1,2,0:T(8,128)(2,1)}, u32[]{:S(2)}, u32[]{:S(2)}) collective-permute-start(bf16[2,512,384]{1,2,0:T(8,128)(2,1)} %pad_maximum_fusion.1), channel_id=1, source_target_pairs={{0,32},{16,48},{32,64},{48,80},{64,96},{80,112},{96,128},{112,144}... | collective-permute-start | bytes 2359304 | tf_op jit(solution)/shard_map/ppermute | solution.py:27
  62.4 4.2 %collective-permute-start.5 = (bf16[2,512,384]{1,2,0:T(8,128)(2,1)}, bf16[2,512,384]{1,2,0:T(8,128)(2,1)S(1)}, u32[]{:S(2)}, u32[]{:S(2)}) collective-permute-start(bf16[2,512,384]{1,2,0:T(8,128)(2,1)} %pad_maximum_fusion.1), channel_id=1, source_target_pairs={{0,48},{16,64},{32,80},{48,96},{64,112},{80,128},{96,144},{112,160... | collective-permute-start | bytes 2359304 | tf_op jit(solution)/shard_map/ppermute | solution.py:27
  69.2 77.8 %collective-permute-done.2 = bf16[2,512,384]{1,2,0:T(8,128)(2,1)} collective-permute-done((bf16[2,512,384]{1,2,0:T(8,128)(2,1)}, bf16[2,512,384]{1,2,0:T(8,128)(2,1)}, u32[]{:S(2)}, u32[]{:S(2)}) %collective-permute-start.2) | collective-permute-done | bytes 786464 | tf_op jit(solution)/shard_map/ppermute | solution.py:27
  147.1 3.1 %collective-permute-start.6 = (bf16[2,512,384]{1,2,0:T(8,128)(2,1)}, bf16[2,512,384]{1,2,0:T(8,128)(2,1)S(1)}, u32[]{:S(2)}, u32[]{:S(2)}) collective-permute-start(bf16[2,512,384]{1,2,0:T(8,128)(2,1)} %pad_maximum_fusion.1), channel_id=1, source_target_pairs={{0,8},{8,0},{1,9},{9,1},{2,10},{10,2},{3,11},{11,3},{4,12},{12,4},... | collective-permute-start | bytes 2359304 | tf_op jit(solution)/shard_map/ppermute | solution.py:31
  153.6 2.4 collective-permute-start.16
  164.2 2.8 collective-permute-start.17
  168.2 5.0 %collective-permute-start.18 = (bf16[96,640]{1,0:T(8,128)(2,1)S(1)}, bf16[96,640]{1,0:T(8,128)(2,1)S(1)}, u32[]{:S(2)}, u32[]{:S(2)}) collective-permute-start(bf16[96,640]{1,0:T(8,128)(2,1)S(1)} %maximum_select_fusion.2), channel_id=1, source_target_pairs={{0,32},{16,48},{32,0},{48,16},{1,33},{17,49},{33,1},{49,17},{2,34}... | collective-permute-start | bytes 368648 | tf_op jit(solution)/shard_map/ppermute | solution.py:27
  175.3 4.1 %collective-permute-done.18 = bf16[96,640]{1,0:T(8,128)(2,1)S(1)} collective-permute-done((bf16[96,640]{1,0:T(8,128)(2,1)S(1)}, bf16[96,640]{1,0:T(8,128)(2,1)S(1)}, u32[]{:S(2)}, u32[]{:S(2)}) %collective-permute-start.18) | collective-permute-done | bytes 122912 | tf_op jit(solution)/shard_map/ppermute | solution.py:27
  179.4 2.6 collective-permute-done.19
  185.2 7.2 %collective-permute-start.22 = (bf16[384,640]{1,0:T(8,128)(2,1)S(1)}, bf16[384,640]{1,0:T(8,128)(2,1)S(1)}, u32[]{:S(2)}, u32[]{:S(2)}) collective-permute-start(bf16[384,640]{1,0:T(8,128)(2,1)S(1)} %bitcast.439), channel_id=1, source_target_pairs={{0,192},{64,256},{128,320},{192,384},{256,448},{320,0},{384,64},{4... | collective-permute-start | bytes 1474568 | tf_op jit(solution)/shard_map/ppermute | solution.py:124
  192.4 3.9 %collective-permute-start.21 = (bf16[384,640]{1,0:T(8,128)(2,1)S(1)}, bf16[384,640]{1,0:T(8,128)(2,1)S(1)}, u32[]{:S(2)}, u32[]{:S(2)}) collective-permute-start(bf16[384,640]{1,0:T(8,128)(2,1)S(1)} %bitcast.440), channel_id=1, source_target_pairs={{0,128},{64,192},{128,256},{192,320},{256,384},{320,448},{384,0},{... | collective-permute-start | bytes 1474568 | tf_op jit(solution)/shard_map/ppermute | solution.py:124
  197.5 6.8 %collective-permute-start.10 = (bf16[2,512,384]{1,2,0:T(8,128)(2,1)S(1)}, bf16[2,512,384]{1,2,0:T(8,128)(2,1)S(1)}, u32[]{:S(2)}, u32[]{:S(2)}) collective-permute-start(bf16[2,512,384]{1,2,0:T(8,128)(2,1)S(1)} %get-tuple-element.87), channel_id=1, source_target_pairs={{0,8},{8,0},{1,9},{9,1},{2,10},{10,2},{3,11},{11,3},{4,12},{12,4},... | collective-permute-start | bytes 2359304 | tf_op jit(solution)/shard_map/ppermute | solution.py:31
  204.8 18.5 %collective-permute-start.9 = (bf16[2,512,384]{1,2,0:T(8,128)(2,1)S(1)}, bf16[2,512,384]{1,2,0:T(8,128)(2,1)S(1)}, u32[]{:S(2)}, u32[]{:S(2)}) collective-permute-start(bf16[2,512,384]{1,2,0:T(8,128)(2,1)S(1)} %broadcast_select_fusion.2), channel_id=1, source_target_pairs={{0,8},{8,0},{1,9},{9,1},{2,10},{10,2},{3,11},{11,3},{4,12},{12,4},... | collective-permute-start | bytes 2359304 | tf_op jit(solution)/shard_map/ppermute | solution.py:31
  226.7 9.5 %collective-permute-start.7 = (bf16[2,512,384]{1,2,0:T(8,128)(2,1)S(1)}, bf16[2,512,384]{1,2,0:T(8,128)(2,1)S(1)}, u32[]{:S(2)}, u32[]{:S(2)}) collective-permute-start(bf16[2,512,384]{1,2,0:T(8,128)(2,1)S(1)} %get-tuple-element.86), channel_id=1, source_target_pairs={{0,8},{8,0},{1,9},{9,1},{2,10},{10,2},{3,11},{11,3},{4,12},{12,4},... | collective-permute-start | bytes 2359304 | tf_op jit(solution)/shard_map/ppermute | solution.py:31
  253.4 8.0 %collective-permute-start.12 = (bf16[256,384]{0,1:T(8,128)(2,1)S(1)}, bf16[256,384]{0,1:T(8,128)(2,1)S(1)}, u32[]{:S(2)}, u32[]{:S(2)}) collective-permute-start(bf16[256,384]{0,1:T(8,128)(2,1)S(1)} %bitcast.486), channel_id=1, source_target_pairs={{0,4},{4,0},{1,5},{5,1},{2,6},{6,2},{3,7},{7,3},{8,12},{12,8},{9,1... | collective-permute-start | bytes 589832 | tf_op jit(solution)/shard_map/ppermute | solution.py:145
  261.5 7.7 %collective-permute-done.12 = bf16[256,384]{0,1:T(8,128)(2,1)S(1)} collective-permute-done((bf16[256,384]{0,1:T(8,128)(2,1)S(1)}, bf16[256,384]{0,1:T(8,128)(2,1)S(1)}, u32[]{:S(2)}, u32[]{:S(2)}) %collective-permute-start.12) | collective-permute-done | bytes 196640 | tf_op jit(solution)/shard_map/ppermute | solution.py:145
  269.3 3.1 %collective-permute-start.13 = (bf16[256,768]{0,1:T(8,128)(2,1)S(1)}, bf16[256,768]{0,1:T(8,128)(2,1)S(1)}, u32[]{:S(2)}, u32[]{:S(2)}) collective-permute-start(bf16[256,768]{0,1:T(8,128)(2,1)S(1)} %maximum_select_fusion), channel_id=1, source_target_pairs={{0,1},{1,2},{2,3},{3,0},{4,5},{5,6},{6,7},{7,4},{8,9},{9,10},{10,1... | collective-permute-start | bytes 1179656 | tf_op jit(solution)/shard_map/ppermute | solution.py:27
  272.4 2.7 collective-permute-start.14
  275.1 3.8 %collective-permute-start.15 = (bf16[256,768]{0,1:T(8,128)(2,1)S(1)}, bf16[256,768]{0,1:T(8,128)(2,1)S(1)}, u32[]{:S(2)}, u32[]{:S(2)}) collective-permute-start(bf16[256,768]{0,1:T(8,128)(2,1)S(1)} %maximum_select_fusion), channel_id=1, source_target_pairs={{0,3},{1,0},{2,1},{3,2},{4,7},{5,4},{6,5},{7,6},{8,11},{9,8},{10,9... | collective-permute-start | bytes 1179656 | tf_op jit(solution)/shard_map/ppermute | solution.py:27
  280.8 4.3 %collective-permute-done.14 = bf16[256,768]{0,1:T(8,128)(2,1)S(1)} collective-permute-done((bf16[256,768]{0,1:T(8,128)(2,1)S(1)}, bf16[256,768]{0,1:T(8,128)(2,1)S(1)}, u32[]{:S(2)}, u32[]{:S(2)}) %collective-permute-start.14) | collective-permute-done | bytes 393248 | tf_op jit(solution)/shard_map/ppermute | solution.py:27
  285.1 10.1 %collective-permute-done.15 = bf16[256,768]{0,1:T(8,128)(2,1)S(1)} collective-permute-done((bf16[256,768]{0,1:T(8,128)(2,1)S(1)}, bf16[256,768]{0,1:T(8,128)(2,1)S(1)}, u32[]{:S(2)}, u32[]{:S(2)}) %collective-permute-start.15) | collective-permute-done | bytes 393248 | tf_op jit(solution)/shard_map/ppermute | solution.py:27
  296.5 2.2 fusion.27
  (235 shorter events, 92.7 us)
Async XLA Ops:
  5.6 56.8 %collective-permute-start = (bf16[2,512,384]{1,2,0:T(8,128)(2,1)}, bf16[2,512,384]{1,2,0:T(8,128)(2,1)}, u32[]{:S(2)}, u32[]{:S(2)}) collective-permute-start(bf16[2,512,384]{1,2,0:T(8,128)(2,1)} %pad_maximum_fusion.1), channel_id=1, source_target_pairs={{16,0},{32,16},{48,32},{64,48},{80,64},{96,80},{112,96},{128,112},... | collective-permute-start | bytes 2359304 | tf_op jit(solution)/shard_map/ppermute | solution.py:27
  13.2 133.8 %collective-permute-start.2 = (bf16[2,512,384]{1,2,0:T(8,128)(2,1)}, bf16[2,512,384]{1,2,0:T(8,128)(2,1)}, u32[]{:S(2)}, u32[]{:S(2)}) collective-permute-start(bf16[2,512,384]{1,2,0:T(8,128)(2,1)} %pad_maximum_fusion.1), channel_id=1, source_target_pairs={{32,0},{48,16},{64,32},{80,48},{96,64},{112,80},{128,96},{144,112}... | collective-permute-start | bytes 2359304 | tf_op jit(solution)/shard_map/ppermute | solution.py:27
  15.1 135.1 %collective-permute-start.4 = (bf16[2,512,384]{1,2,0:T(8,128)(2,1)}, bf16[2,512,384]{1,2,0:T(8,128)(2,1)S(1)}, u32[]{:S(2)}, u32[]{:S(2)}) collective-permute-start(bf16[2,512,384]{1,2,0:T(8,128)(2,1)} %pad_maximum_fusion.1), channel_id=1, source_target_pairs={{48,0},{64,16},{80,32},{96,48},{112,64},{128,80},{144,96},{160,112... | collective-permute-start | bytes 2359304 | tf_op jit(solution)/shard_map/ppermute | solution.py:27
  17.1 133.1 %collective-permute-start.1 = (bf16[2,512,384]{1,2,0:T(8,128)(2,1)}, bf16[2,512,384]{1,2,0:T(8,128)(2,1)}, u32[]{:S(2)}, u32[]{:S(2)}) collective-permute-start(bf16[2,512,384]{1,2,0:T(8,128)(2,1)} %pad_maximum_fusion.1), channel_id=1, source_target_pairs={{0,16},{16,32},{32,48},{48,64},{64,80},{80,96},{96,112},{112,128},... | collective-permute-start | bytes 2359304 | tf_op jit(solution)/shard_map/ppermute | solution.py:27
  19.3 130.9 %collective-permute-start.3 = (bf16[2,512,384]{1,2,0:T(8,128)(2,1)}, bf16[2,512,384]{1,2,0:T(8,128)(2,1)}, u32[]{:S(2)}, u32[]{:S(2)}) collective-permute-start(bf16[2,512,384]{1,2,0:T(8,128)(2,1)} %pad_maximum_fusion.1), channel_id=1, source_target_pairs={{0,32},{16,48},{32,64},{48,80},{64,96},{80,112},{96,128},{112,144}... | collective-permute-start | bytes 2359304 | tf_op jit(solution)/shard_map/ppermute | solution.py:27
  62.4 87.8 %collective-permute-start.5 = (bf16[2,512,384]{1,2,0:T(8,128)(2,1)}, bf16[2,512,384]{1,2,0:T(8,128)(2,1)S(1)}, u32[]{:S(2)}, u32[]{:S(2)}) collective-permute-start(bf16[2,512,384]{1,2,0:T(8,128)(2,1)} %pad_maximum_fusion.1), channel_id=1, source_target_pairs={{0,48},{16,64},{32,80},{48,96},{64,112},{80,128},{96,144},{112,160... | collective-permute-start | bytes 2359304 | tf_op jit(solution)/shard_map/ppermute | solution.py:27
  147.1 10.6 %collective-permute-start.6 = (bf16[2,512,384]{1,2,0:T(8,128)(2,1)}, bf16[2,512,384]{1,2,0:T(8,128)(2,1)S(1)}, u32[]{:S(2)}, u32[]{:S(2)}) collective-permute-start(bf16[2,512,384]{1,2,0:T(8,128)(2,1)} %pad_maximum_fusion.1), channel_id=1, source_target_pairs={{0,8},{8,0},{1,9},{9,1},{2,10},{10,2},{3,11},{11,3},{4,12},{12,4},... | collective-permute-start | bytes 2359304 | tf_op jit(solution)/shard_map/ppermute | solution.py:31
  151.7 84.8 %collective-permute-start.11 = (bf16[2,512,384]{1,2,0:T(8,128)(2,1)S(1)}, bf16[2,512,384]{1,2,0:T(8,128)(2,1)S(1)}, u32[]{:S(2)}, u32[]{:S(2)}) collective-permute-start(bf16[2,512,384]{1,2,0:T(8,128)(2,1)S(1)} %get-tuple-element.89), channel_id=1, source_target_pairs={{0,8},{8,0},{1,9},{9,1},{2,10},{10,2},{3,11},{11,3},{4,12},{12,4},... | collective-permute-start | bytes 2359304 | tf_op jit(solution)/shard_map/ppermute | solution.py:31
  153.6 10.5 %collective-permute-start.16 = (bf16[48,640]{1,0:T(8,128)(2,1)S(1)}, bf16[48,640]{1,0:T(8,128)(2,1)S(1)}, u32[]{:S(2)}, u32[]{:S(2)}) collective-permute-start(bf16[48,640]{1,0:T(8,128)(2,1)S(1)} %copy-done.16), channel_id=1, source_target_pairs={{0,8},{8,0},{1,9},{9,1},{2,10},{10,2},{3,11},{11,3},{4,12},{12,4},... | collective-permute-start | bytes 184328 | tf_op jit(solution)/shard_map/ppermute | solution.py:31
  164.2 11.0 %collective-permute-start.17 = (bf16[96,640]{1,0:T(8,128)(2,1)S(1)}, bf16[96,640]{1,0:T(8,128)(2,1)S(1)}, u32[]{:S(2)}, u32[]{:S(2)}) collective-permute-start(bf16[96,640]{1,0:T(8,128)(2,1)S(1)} %maximum_select_fusion.2), channel_id=1, source_target_pairs={{0,16},{16,32},{32,48},{48,0},{1,17},{17,33},{33,49},{49,1},{2,18}... | collective-permute-start | bytes 368648 | tf_op jit(solution)/shard_map/ppermute | solution.py:27
  168.2 11.2 %collective-permute-start.18 = (bf16[96,640]{1,0:T(8,128)(2,1)S(1)}, bf16[96,640]{1,0:T(8,128)(2,1)S(1)}, u32[]{:S(2)}, u32[]{:S(2)}) collective-permute-start(bf16[96,640]{1,0:T(8,128)(2,1)S(1)} %maximum_select_fusion.2), channel_id=1, source_target_pairs={{0,32},{16,48},{32,0},{48,16},{1,33},{17,49},{33,1},{49,17},{2,34}... | collective-permute-start | bytes 368648 | tf_op jit(solution)/shard_map/ppermute | solution.py:27
  182.0 15.5 %collective-permute-start.20 = (bf16[384,640]{1,0:T(8,128)(2,1)S(1)}, bf16[384,640]{1,0:T(8,128)(2,1)S(1)}, u32[]{:S(2)}, u32[]{:S(2)}) collective-permute-start(bf16[384,640]{1,0:T(8,128)(2,1)S(1)} %bitcast.437), channel_id=1, source_target_pairs={{0,64},{64,128},{128,192},{192,256},{256,320},{320,384},{384,448},... | collective-permute-start | bytes 1474568 | tf_op jit(solution)/shard_map/ppermute | solution.py:124
  184.5 20.3 %collective-permute-start.23 = (bf16[384,640]{1,0:T(8,128)(2,1)S(1)}, bf16[384,640]{1,0:T(8,128)(2,1)S(1)}, u32[]{:S(2)}, u32[]{:S(2)}) collective-permute-start(bf16[384,640]{1,0:T(8,128)(2,1)S(1)} %bitcast.438), channel_id=1, source_target_pairs={{0,256},{64,320},{128,384},{192,448},{256,0},{320,64},{384,128},{4... | collective-permute-start | bytes 1474568 | tf_op jit(solution)/shard_map/ppermute | solution.py:124
  185.2 38.5 %collective-permute-start.22 = (bf16[384,640]{1,0:T(8,128)(2,1)S(1)}, bf16[384,640]{1,0:T(8,128)(2,1)S(1)}, u32[]{:S(2)}, u32[]{:S(2)}) collective-permute-start(bf16[384,640]{1,0:T(8,128)(2,1)S(1)} %bitcast.439), channel_id=1, source_target_pairs={{0,192},{64,256},{128,320},{192,384},{256,448},{320,0},{384,64},{4... | collective-permute-start | bytes 1474568 | tf_op jit(solution)/shard_map/ppermute | solution.py:124
  192.4 34.3 %collective-permute-start.21 = (bf16[384,640]{1,0:T(8,128)(2,1)S(1)}, bf16[384,640]{1,0:T(8,128)(2,1)S(1)}, u32[]{:S(2)}, u32[]{:S(2)}) collective-permute-start(bf16[384,640]{1,0:T(8,128)(2,1)S(1)} %bitcast.440), channel_id=1, source_target_pairs={{0,128},{64,192},{128,256},{192,320},{256,384},{320,448},{384,0},{... | collective-permute-start | bytes 1474568 | tf_op jit(solution)/shard_map/ppermute | solution.py:124
  197.5 41.0 %collective-permute-start.10 = (bf16[2,512,384]{1,2,0:T(8,128)(2,1)S(1)}, bf16[2,512,384]{1,2,0:T(8,128)(2,1)S(1)}, u32[]{:S(2)}, u32[]{:S(2)}) collective-permute-start(bf16[2,512,384]{1,2,0:T(8,128)(2,1)S(1)} %get-tuple-element.87), channel_id=1, source_target_pairs={{0,8},{8,0},{1,9},{9,1},{2,10},{10,2},{3,11},{11,3},{4,12},{12,4},... | collective-permute-start | bytes 2359304 | tf_op jit(solution)/shard_map/ppermute | solution.py:31
  204.8 33.8 %collective-permute-start.9 = (bf16[2,512,384]{1,2,0:T(8,128)(2,1)S(1)}, bf16[2,512,384]{1,2,0:T(8,128)(2,1)S(1)}, u32[]{:S(2)}, u32[]{:S(2)}) collective-permute-start(bf16[2,512,384]{1,2,0:T(8,128)(2,1)S(1)} %broadcast_select_fusion.2), channel_id=1, source_target_pairs={{0,8},{8,0},{1,9},{9,1},{2,10},{10,2},{3,11},{11,3},{4,12},{12,4},... | collective-permute-start | bytes 2359304 | tf_op jit(solution)/shard_map/ppermute | solution.py:31
  223.7 16.7 %collective-permute-start.8 = (bf16[2,512,384]{1,2,0:T(8,128)(2,1)S(1)}, bf16[2,512,384]{1,2,0:T(8,128)(2,1)S(1)}, u32[]{:S(2)}, u32[]{:S(2)}) collective-permute-start(bf16[2,512,384]{1,2,0:T(8,128)(2,1)S(1)} %get-tuple-element.88), channel_id=1, source_target_pairs={{0,8},{8,0},{1,9},{9,1},{2,10},{10,2},{3,11},{11,3},{4,12},{12,4},... | collective-permute-start | bytes 2359304 | tf_op jit(solution)/shard_map/ppermute | solution.py:31
  226.7 15.1 %collective-permute-start.7 = (bf16[2,512,384]{1,2,0:T(8,128)(2,1)S(1)}, bf16[2,512,384]{1,2,0:T(8,128)(2,1)S(1)}, u32[]{:S(2)}, u32[]{:S(2)}) collective-permute-start(bf16[2,512,384]{1,2,0:T(8,128)(2,1)S(1)} %get-tuple-element.86), channel_id=1, source_target_pairs={{0,8},{8,0},{1,9},{9,1},{2,10},{10,2},{3,11},{11,3},{4,12},{12,4},... | collective-permute-start | bytes 2359304 | tf_op jit(solution)/shard_map/ppermute | solution.py:31
  236.5 58.8 %collective-permute-start.24 = (bf16[4,384,640]{2,1,0:T(8,128)(2,1)S(1)}, bf16[4,384,640]{2,1,0:T(8,128)(2,1)S(1)}, u32[]{:S(2)}, u32[]{:S(2)}) collective-permute-start(bf16[4,384,640]{2,1,0:T(8,128)(2,1)S(1)} %pad_maximum_fusion), channel_id=1, source_target_pairs={{0,8},{8,0},{1,9},{9,1},{2,10},{10,2},{3,11},{11,3},{4,12},{12,4},... | collective-permute-start | bytes 5898248 | tf_op jit(solution)/shard_map/ppermute | solution.py:31
  253.4 15.7 %collective-permute-start.12 = (bf16[256,384]{0,1:T(8,128)(2,1)S(1)}, bf16[256,384]{0,1:T(8,128)(2,1)S(1)}, u32[]{:S(2)}, u32[]{:S(2)}) collective-permute-start(bf16[256,384]{0,1:T(8,128)(2,1)S(1)} %bitcast.486), channel_id=1, source_target_pairs={{0,4},{4,0},{1,5},{5,1},{2,6},{6,2},{3,7},{7,3},{8,12},{12,8},{9,1... | collective-permute-start | bytes 589832 | tf_op jit(solution)/shard_map/ppermute | solution.py:145
  269.3 11.4 %collective-permute-start.13 = (bf16[256,768]{0,1:T(8,128)(2,1)S(1)}, bf16[256,768]{0,1:T(8,128)(2,1)S(1)}, u32[]{:S(2)}, u32[]{:S(2)}) collective-permute-start(bf16[256,768]{0,1:T(8,128)(2,1)S(1)} %maximum_select_fusion), channel_id=1, source_target_pairs={{0,1},{1,2},{2,3},{3,0},{4,5},{5,6},{6,7},{7,4},{8,9},{9,10},{10,1... | collective-permute-start | bytes 1179656 | tf_op jit(solution)/shard_map/ppermute | solution.py:27
  272.4 12.7 %collective-permute-start.14 = (bf16[256,768]{0,1:T(8,128)(2,1)S(1)}, bf16[256,768]{0,1:T(8,128)(2,1)S(1)}, u32[]{:S(2)}, u32[]{:S(2)}) collective-permute-start(bf16[256,768]{0,1:T(8,128)(2,1)S(1)} %maximum_select_fusion), channel_id=1, source_target_pairs={{0,2},{1,3},{2,0},{3,1},{4,6},{5,7},{6,4},{7,5},{8,10},{9,11},{10,... | collective-permute-start | bytes 1179656 | tf_op jit(solution)/shard_map/ppermute | solution.py:27
  275.1 20.1 %collective-permute-start.15 = (bf16[256,768]{0,1:T(8,128)(2,1)S(1)}, bf16[256,768]{0,1:T(8,128)(2,1)S(1)}, u32[]{:S(2)}, u32[]{:S(2)}) collective-permute-start(bf16[256,768]{0,1:T(8,128)(2,1)S(1)} %maximum_select_fusion), channel_id=1, source_target_pairs={{0,3},{1,0},{2,1},{3,2},{4,7},{5,4},{6,5},{7,6},{8,11},{9,8},{10,9... | collective-permute-start | bytes 1179656 | tf_op jit(solution)/shard_map/ppermute | solution.py:27
  (25 other events, 275.7 us)

commit v5 on v3

--- a/solution.py
+++ b/solution.py
@@ -202,9 +202,9 @@
                 jnp.concatenate([value_tiles, cache_values.reshape(-1, tile_width)], axis=0),
             ]
         )
-        row_block = gather_weight(out_weight, sizes, is_first)
-        packed, row_block = lax.optimization_barrier((packed, row_block))
-        weight_full = spread_weight(row_block, sizes, is_first)
+        weight_full = out_weight
+        for axis in ("c", "zl", "y"):
+            weight_full = lax.all_gather(weight_full, axis, axis=0, tiled=True)
 
         carry_state = visit_block(
             empty_state(head_count, row_count), packed, seq_index, query_heads, query_clip, context

time: 275 us -> 315 us (1.15)
  the two profiles are of different devices: /device:TPU:147 before, /device:TPU:75 now
where the time goes in v5:
time: 315 us; the launch traced here: 313 us
  blocking collectives  115 us (37%)
  starting transfers between devices  58.3 us (19%)
  other arithmetic  39.2 us (12%)
  waiting for transfers between devices  34.7 us (11%)
  local copies, waits for them, and re-layouts  32.5 us (10%)
  matrix products  19.3 us (6%)
  between operations  14.4 us (5%)
    all_gather x2, blocking collectives, local(): weight_full = lax.all_gather(weight_full, axis, axis=0, tiled=True)  115 us
    ppermute x9, starting transfers between devices, shifted(): return lax.ppermute(block, axes, route)  32.9 us
    ppermute x9, waiting for transfers between devices, shifted(): return lax.ppermute(block, axes, route)  24.4 us
    ppermute x6, starting transfers between devices, swap_cores(): return lax.ppermute(block, 'c', [(0, 1), (1, 0)])  19.5 us
    and x13, other arithmetic, allowed_keys(): page_ok = jnp.any(member[:, :, None] & named_pages[None], axis=1) & in_range  10.5 us
    ppermute x1, waiting for transfers between devices, gather_attention(): partner = lax.ppermute(attention_local, 'zh', [(0, 1), (1, 0)])  10.3 us
    concatenate x13, other arithmetic, allowed_keys(): return jnp.concatenate([same_clip, page_ok], axis=1)  8.98 us
    unnamed x60, local copies, waits for them, and re-layouts  7.71 us
  transfers between devices with their start and end apart: 17, of which 4 were waited for; matrix products, arithmetic and copies ran while one was open for 24% of the time, Pallas kernels for 0%

profile of v5, /device:TPU:75, one launch (start us, length us, event | category | flops | bytes accessed | tf_op | source)
XLA Modules:
  0.0 313.3 jit_solution(12555999028312856234)
XLA Ops:
  13.8 2.1 collective-permute-start
  15.8 4.0 %collective-permute-start.1 = (bf16[2,512,384]{1,2,0:T(8,128)(2,1)}, bf16[2,512,384]{1,2,0:T(8,128)(2,1)}, u32[]{:S(2)}, u32[]{:S(2)}) collective-permute-start(bf16[2,512,384]{1,2,0:T(8,128)(2,1)} %pad_maximum_fusion), channel_id=1, source_target_pairs={{0,16},{16,32},{32,48},{48,64},{64,80},{80,96},{96,112},{112,128},... | collective-permute-start | bytes 2359304 | tf_op jit(solution)/shard_map/ppermute | solution.py:27
  19.9 7.8 %collective-permute-start.2 = (bf16[2,512,384]{1,2,0:T(8,128)(2,1)}, bf16[2,512,384]{1,2,0:T(8,128)(2,1)}, u32[]{:S(2)}, u32[]{:S(2)}) collective-permute-start(bf16[2,512,384]{1,2,0:T(8,128)(2,1)} %pad_maximum_fusion), channel_id=1, source_target_pairs={{32,0},{48,16},{64,32},{80,48},{96,64},{112,80},{128,96},{144,112}... | collective-permute-start | bytes 2359304 | tf_op jit(solution)/shard_map/ppermute | solution.py:27
  27.6 2.0 collective-permute-start.3
  29.7 1.9 collective-permute-start.4
  31.6 3.1 all_gather.9
  34.7 111.7 %all_gather.10 = bf16[384,640]{1,0:T(8,128)(2,1)} all-gather(bf16[96,640]{1,0:T(8,128)(2,1)S(1)} %all_gather.9), channel_id=1, replica_groups=mesh['y'=8,'zl'=4,'c'=2,'zh'=2,'x'=4] {'zl'}, dimensions={0}, use_global_device_ids=true | all-gather | bytes 614400 | tf_op jit(solution)/shard_map/all_gather | solution.py:207
  169.4 2.0 compare_and_fusion.10
  191.5 5.6 %collective-permute-start.5 = (bf16[2,512,384]{1,2,0:T(8,128)(2,1)}, bf16[2,512,384]{1,2,0:T(8,128)(2,1)S(1)}, u32[]{:S(2)}, u32[]{:S(2)}) collective-permute-start(bf16[2,512,384]{1,2,0:T(8,128)(2,1)} %pad_maximum_fusion), channel_id=1, source_target_pairs={{0,48},{16,64},{32,80},{48,96},{64,112},{80,128},{96,144},{112,160... | collective-permute-start | bytes 2359304 | tf_op jit(solution)/shard_map/ppermute | solution.py:27
  197.2 6.6 %collective-permute-start.6 = (bf16[2,512,384]{1,2,0:T(8,128)(2,1)}, bf16[2,512,384]{1,2,0:T(8,128)(2,1)S(1)}, u32[]{:S(2)}, u32[]{:S(2)}) collective-permute-start(bf16[2,512,384]{1,2,0:T(8,128)(2,1)} %pad_maximum_fusion), channel_id=1, source_target_pairs={{0,8},{8,0},{1,9},{9,1},{2,10},{10,2},{3,11},{11,3},{4,12},{12,4},... | collective-permute-start | bytes 2359304 | tf_op jit(solution)/shard_map/ppermute | solution.py:31
  205.3 1.9 collective-permute-start.7
  208.7 2.5 collective-permute-start.8
  211.3 13.4 %collective-permute-done.5 = bf16[2,512,384]{1,2,0:T(8,128)(2,1)S(1)} collective-permute-done((bf16[2,512,384]{1,2,0:T(8,128)(2,1)}, bf16[2,512,384]{1,2,0:T(8,128)(2,1)S(1)}, u32[]{:S(2)}, u32[]{:S(2)}) %collective-permute-start.5) | collective-permute-done | bytes 786464 | tf_op jit(solution)/shard_map/ppermute | solution.py:27
  224.8 3.9 %collective-permute-start.9 = (bf16[2,512,384]{1,2,0:T(8,128)(2,1)S(1)}, bf16[2,512,384]{1,2,0:T(8,128)(2,1)S(1)}, u32[]{:S(2)}, u32[]{:S(2)}) collective-permute-start(bf16[2,512,384]{1,2,0:T(8,128)(2,1)S(1)} %broadcast_select_fusion.2), channel_id=1, source_target_pairs={{0,8},{8,0},{1,9},{9,1},{2,10},{10,2},{3,11},{11,3},{4,12},{12,4},... | collective-permute-start | bytes 2359304 | tf_op jit(solution)/shard_map/ppermute | solution.py:31
  228.6 1.9 collective-permute-start.10
  230.6 2.6 collective-permute-start.11
  257.2 5.9 %collective-permute-start.12 = (bf16[256,384]{0,1:T(8,128)(2,1)S(1)}, bf16[256,384]{0,1:T(8,128)(2,1)S(1)}, u32[]{:S(2)}, u32[]{:S(2)}) collective-permute-start(bf16[256,384]{0,1:T(8,128)(2,1)S(1)} %bitcast.442), channel_id=1, source_target_pairs={{0,4},{4,0},{1,5},{5,1},{2,6},{6,2},{3,7},{7,3},{8,12},{12,8},{9,1... | collective-permute-start | bytes 589832 | tf_op jit(solution)/shard_map/ppermute | solution.py:145
  263.7 10.3 %collective-permute-done.12 = bf16[256,384]{0,1:T(8,128)(2,1)S(1)} collective-permute-done((bf16[256,384]{0,1:T(8,128)(2,1)S(1)}, bf16[256,384]{0,1:T(8,128)(2,1)S(1)}, u32[]{:S(2)}, u32[]{:S(2)}) %collective-permute-start.12) | collective-permute-done | bytes 196640 | tf_op jit(solution)/shard_map/ppermute | solution.py:145
  274.2 3.1 collective-permute-start.13
  277.3 2.8 collective-permute-start.14
  280.0 3.7 %collective-permute-start.15 = (bf16[256,768]{0,1:T(8,128)(2,1)S(1)}, bf16[256,768]{0,1:T(8,128)(2,1)S(1)}, u32[]{:S(2)}, u32[]{:S(2)}) collective-permute-start(bf16[256,768]{0,1:T(8,128)(2,1)S(1)} %maximum_select_fusion), channel_id=1, source_target_pairs={{0,3},{1,0},{2,1},{3,2},{4,7},{5,4},{6,5},{7,6},{8,11},{9,8},{10,9... | collective-permute-start | bytes 1179656 | tf_op jit(solution)/shard_map/ppermute | solution.py:27
  287.8 2.8 collective-permute-done.14
  292.0 8.1 %collective-permute-done.15 = bf16[256,768]{0,1:T(8,128)(2,1)S(1)} collective-permute-done((bf16[256,768]{0,1:T(8,128)(2,1)S(1)}, bf16[256,768]{0,1:T(8,128)(2,1)S(1)}, u32[]{:S(2)}, u32[]{:S(2)}) %collective-permute-start.15) | collective-permute-done | bytes 393248 | tf_op jit(solution)/shard_map/ppermute | solution.py:27
  301.5 4.9 %fusion.27 = bf16[256,640]{1,0:T(8,128)(2,1)} fusion(f32[256,640]{1,0:T(8,128)S(1)} %fusion.146, bf16[256,3072]{0,1:T(8,128)(2,1)} %slice_dynamic-update-slice_fusion, bf16[3072,640]{1,0:T(8,128)(2,1)} %all-gather.2.cloned.1.call-done, bf16[256,640]{1,0:T(8,128)(2,1)} %param.17), kind=kOutput, calls=%fused_computation.54 | convolution fusion | flops 1007288320 | bytes 6815744 | tf_op jit(solution)/shard_map/dot_general | solution.py:243
  (214 shorter events, 84.2 us)
Async XLA Ops:
  6.5 182.8 %copy-start = (f32[1000,640]{1,0:T(8,128)S(1)}, f32[1000,640]{1,0:T(8,128)}, u32[]{:S(2)}) copy-start(f32[1000,640]{1,0:T(8,128)} %param.19) | copy-start | bytes 7680004
  6.5 295.0 %all-gather.2.cloned.1.call-start = ((), (), s32[]{:S(2)}) async-start(), calls=%async_computation | async-start | bytes 4423680 | tf_op jit(solution)/shard_map/all_gather | solution.py:207
  11.8 19.8 %copy-start.25 = (bf16[48,640]{1,0:T(8,128)(2,1)S(1)}, bf16[48,640]{1,0:T(8,128)(2,1)}, u32[]{:S(2)}) copy-start(bf16[48,640]{1,0:T(8,128)(2,1)} %param.18) | copy-start | bytes 184324
  12.8 133.7 %copy-start.13 = (bf16[2,128,384]{2,1,0:T(8,128)(2,1)S(1)}, bf16[2,128,384]{2,1,0:T(8,128)(2,1)}, u32[]{:S(2)}) copy-start(bf16[2,128,384]{2,1,0:T(8,128)(2,1)} %param.15) | copy-start | bytes 589828
  13.8 135.8 %copy-start.27 = (s32[16]{0:T(128)S(1)}, s32[16]{0:T(128)}, u32[]{:S(2)}) copy-start(s32[16]{0:T(128)} %param.22) | copy-start | bytes 196
  13.8 136.3 %copy-start.26 = (s32[16]{0:T(128)S(1)}, s32[16]{0:T(128)}, u32[]{:S(2)}) copy-start(s32[16]{0:T(128)} %param.20) | copy-start | bytes 196
  13.8 177.7 %collective-permute-start = (bf16[2,512,384]{1,2,0:T(8,128)(2,1)}, bf16[2,512,384]{1,2,0:T(8,128)(2,1)}, u32[]{:S(2)}, u32[]{:S(2)}) collective-permute-start(bf16[2,512,384]{1,2,0:T(8,128)(2,1)} %pad_maximum_fusion), channel_id=1, source_target_pairs={{16,0},{32,16},{48,32},{64,48},{80,64},{96,80},{112,96},{128,112},... | collective-permute-start | bytes 2359304 | tf_op jit(solution)/shard_map/ppermute | solution.py:27
  15.8 181.3 %collective-permute-start.1 = (bf16[2,512,384]{1,2,0:T(8,128)(2,1)}, bf16[2,512,384]{1,2,0:T(8,128)(2,1)}, u32[]{:S(2)}, u32[]{:S(2)}) collective-permute-start(bf16[2,512,384]{1,2,0:T(8,128)(2,1)} %pad_maximum_fusion), channel_id=1, source_target_pairs={{0,16},{16,32},{32,48},{48,64},{64,80},{80,96},{96,112},{112,128},... | collective-permute-start | bytes 2359304 | tf_op jit(solution)/shard_map/ppermute | solution.py:27
  19.9 185.4 %collective-permute-start.2 = (bf16[2,512,384]{1,2,0:T(8,128)(2,1)}, bf16[2,512,384]{1,2,0:T(8,128)(2,1)}, u32[]{:S(2)}, u32[]{:S(2)}) collective-permute-start(bf16[2,512,384]{1,2,0:T(8,128)(2,1)} %pad_maximum_fusion), channel_id=1, source_target_pairs={{32,0},{48,16},{64,32},{80,48},{96,64},{112,80},{128,96},{144,112}... | collective-permute-start | bytes 2359304 | tf_op jit(solution)/shard_map/ppermute | solution.py:27
  27.6 179.6 %collective-permute-start.3 = (bf16[2,512,384]{1,2,0:T(8,128)(2,1)}, bf16[2,512,384]{1,2,0:T(8,128)(2,1)}, u32[]{:S(2)}, u32[]{:S(2)}) collective-permute-start(bf16[2,512,384]{1,2,0:T(8,128)(2,1)} %pad_maximum_fusion), channel_id=1, source_target_pairs={{0,32},{16,48},{32,64},{48,80},{64,96},{80,112},{96,128},{112,144}... | collective-permute-start | bytes 2359304 | tf_op jit(solution)/shard_map/ppermute | solution.py:27
  29.7 181.6 %collective-permute-start.4 = (bf16[2,512,384]{1,2,0:T(8,128)(2,1)}, bf16[2,512,384]{1,2,0:T(8,128)(2,1)S(1)}, u32[]{:S(2)}, u32[]{:S(2)}) collective-permute-start(bf16[2,512,384]{1,2,0:T(8,128)(2,1)} %pad_maximum_fusion), channel_id=1, source_target_pairs={{48,0},{64,16},{80,32},{96,48},{112,64},{128,80},{144,96},{160,112... | collective-permute-start | bytes 2359304 | tf_op jit(solution)/shard_map/ppermute | solution.py:27
  175.3 11.9 %copy-start.19 = (pred[256,256]{0,1:T(8,128)(4,1)S(1)}, pred[256,256]{0,1:T(8,128)(4,1)}, u32[]{:S(2)}) copy-start(pred[256,256]{0,1:T(8,128)(4,1)} %get-tuple-element.104) | copy-start | bytes 196612
  191.5 33.2 %collective-permute-start.5 = (bf16[2,512,384]{1,2,0:T(8,128)(2,1)}, bf16[2,512,384]{1,2,0:T(8,128)(2,1)S(1)}, u32[]{:S(2)}, u32[]{:S(2)}) collective-permute-start(bf16[2,512,384]{1,2,0:T(8,128)(2,1)} %pad_maximum_fusion), channel_id=1, source_target_pairs={{0,48},{16,64},{32,80},{48,96},{64,112},{80,128},{96,144},{112,160... | collective-permute-start | bytes 2359304 | tf_op jit(solution)/shard_map/ppermute | solution.py:27
  197.2 33.4 %collective-permute-start.6 = (bf16[2,512,384]{1,2,0:T(8,128)(2,1)}, bf16[2,512,384]{1,2,0:T(8,128)(2,1)S(1)}, u32[]{:S(2)}, u32[]{:S(2)}) collective-permute-start(bf16[2,512,384]{1,2,0:T(8,128)(2,1)} %pad_maximum_fusion), channel_id=1, source_target_pairs={{0,8},{8,0},{1,9},{9,1},{2,10},{10,2},{3,11},{11,3},{4,12},{12,4},... | collective-permute-start | bytes 2359304 | tf_op jit(solution)/shard_map/ppermute | solution.py:31
  205.3 36.9 %collective-permute-start.7 = (bf16[2,512,384]{1,2,0:T(8,128)(2,1)S(1)}, bf16[2,512,384]{1,2,0:T(8,128)(2,1)S(1)}, u32[]{:S(2)}, u32[]{:S(2)}) collective-permute-start(bf16[2,512,384]{1,2,0:T(8,128)(2,1)S(1)} %get-tuple-element.72), channel_id=1, source_target_pairs={{0,8},{8,0},{1,9},{9,1},{2,10},{10,2},{3,11},{11,3},{4,12},{12,4},... | collective-permute-start | bytes 2359304 | tf_op jit(solution)/shard_map/ppermute | solution.py:31
  208.7 24.5 %copy-start.6 = (pred[256,512]{0,1:T(8,128)(4,1)S(1)}, pred[256,512]{0,1:T(8,128)(4,1)}, u32[]{:S(2)}) copy-start(pred[256,512]{0,1:T(8,128)(4,1)} %pad_add_fusion.7) | copy-start | bytes 393220
  208.7 33.6 %collective-permute-start.8 = (bf16[2,512,384]{1,2,0:T(8,128)(2,1)S(1)}, bf16[2,512,384]{1,2,0:T(8,128)(2,1)S(1)}, u32[]{:S(2)}, u32[]{:S(2)}) collective-permute-start(bf16[2,512,384]{1,2,0:T(8,128)(2,1)S(1)} %get-tuple-element.74), channel_id=1, source_target_pairs={{0,8},{8,0},{1,9},{9,1},{2,10},{10,2},{3,11},{11,3},{4,12},{12,4},... | collective-permute-start | bytes 2359304 | tf_op jit(solution)/shard_map/ppermute | solution.py:31
  224.8 17.6 %collective-permute-start.9 = (bf16[2,512,384]{1,2,0:T(8,128)(2,1)S(1)}, bf16[2,512,384]{1,2,0:T(8,128)(2,1)S(1)}, u32[]{:S(2)}, u32[]{:S(2)}) collective-permute-start(bf16[2,512,384]{1,2,0:T(8,128)(2,1)S(1)} %broadcast_select_fusion.2), channel_id=1, source_target_pairs={{0,8},{8,0},{1,9},{9,1},{2,10},{10,2},{3,11},{11,3},{4,12},{12,4},... | collective-permute-start | bytes 2359304 | tf_op jit(solution)/shard_map/ppermute | solution.py:31
  228.6 15.6 %collective-permute-start.10 = (bf16[2,512,384]{1,2,0:T(8,128)(2,1)S(1)}, bf16[2,512,384]{1,2,0:T(8,128)(2,1)S(1)}, u32[]{:S(2)}, u32[]{:S(2)}) collective-permute-start(bf16[2,512,384]{1,2,0:T(8,128)(2,1)S(1)} %get-tuple-element.73), channel_id=1, source_target_pairs={{0,8},{8,0},{1,9},{9,1},{2,10},{10,2},{3,11},{11,3},{4,12},{12,4},... | collective-permute-start | bytes 2359304 | tf_op jit(solution)/shard_map/ppermute | solution.py:31
  230.6 15.0 %collective-permute-start.11 = (bf16[2,512,384]{1,2,0:T(8,128)(2,1)S(1)}, bf16[2,512,384]{1,2,0:T(8,128)(2,1)S(1)}, u32[]{:S(2)}, u32[]{:S(2)}) collective-permute-start(bf16[2,512,384]{1,2,0:T(8,128)(2,1)S(1)} %get-tuple-element.75), channel_id=1, source_target_pairs={{0,8},{8,0},{1,9},{9,1},{2,10},{10,2},{3,11},{11,3},{4,12},{12,4},... | collective-permute-start | bytes 2359304 | tf_op jit(solution)/shard_map/ppermute | solution.py:31
  257.2 16.8 %collective-permute-start.12 = (bf16[256,384]{0,1:T(8,128)(2,1)S(1)}, bf16[256,384]{0,1:T(8,128)(2,1)S(1)}, u32[]{:S(2)}, u32[]{:S(2)}) collective-permute-start(bf16[256,384]{0,1:T(8,128)(2,1)S(1)} %bitcast.442), channel_id=1, source_target_pairs={{0,4},{4,0},{1,5},{5,1},{2,6},{6,2},{3,7},{7,3},{8,12},{12,8},{9,1... | collective-permute-start | bytes 589832 | tf_op jit(solution)/shard_map/ppermute | solution.py:145
  274.2 12.3 %collective-permute-start.13 = (bf16[256,768]{0,1:T(8,128)(2,1)S(1)}, bf16[256,768]{0,1:T(8,128)(2,1)S(1)}, u32[]{:S(2)}, u32[]{:S(2)}) collective-permute-start(bf16[256,768]{0,1:T(8,128)(2,1)S(1)} %maximum_select_fusion), channel_id=1, source_target_pairs={{0,1},{1,2},{2,3},{3,0},{4,5},{5,6},{6,7},{7,4},{8,9},{9,10},{10,1... | collective-permute-start | bytes 1179656 | tf_op jit(solution)/shard_map/ppermute | solution.py:27
  277.3 13.4 %collective-permute-start.14 = (bf16[256,768]{0,1:T(8,128)(2,1)S(1)}, bf16[256,768]{0,1:T(8,128)(2,1)S(1)}, u32[]{:S(2)}, u32[]{:S(2)}) collective-permute-start(bf16[256,768]{0,1:T(8,128)(2,1)S(1)} %maximum_select_fusion), channel_id=1, source_target_pairs={{0,2},{1,3},{2,0},{3,1},{4,6},{5,7},{6,4},{7,5},{8,10},{9,11},{10,... | collective-permute-start | bytes 1179656 | tf_op jit(solution)/shard_map/ppermute | solution.py:27
  280.0 20.1 %collective-permute-start.15 = (bf16[256,768]{0,1:T(8,128)(2,1)S(1)}, bf16[256,768]{0,1:T(8,128)(2,1)S(1)}, u32[]{:S(2)}, u32[]{:S(2)}) collective-permute-start(bf16[256,768]{0,1:T(8,128)(2,1)S(1)} %maximum_select_fusion), channel_id=1, source_target_pairs={{0,3},{1,0},{2,1},{3,2},{4,7},{5,4},{6,5},{7,6},{8,11},{9,8},{10,9... | collective-permute-start | bytes 1179656 | tf_op jit(solution)/shard_map/ppermute | solution.py:27
  (21 other events, 68.3 us)
Sparse Core Ops, SparseCore 0:
  146.5 69.2 all-gather.1

commit v6 on v5

--- a/solution.py
+++ b/solution.py
@@ -88,6 +88,17 @@
     key_heads = packed[0].reshape(-1, head_count, HD)
     value_heads = packed[1].reshape(-1, head_count, HD)
     return attend(carry_state, query_heads, key_heads, value_heads, allowed)
+
+
+def gather_row_weight(out_weight, sizes):
+    n_zl = sizes["zl"]
+    zl = lax.axis_index("zl")
+    row_part = jnp.zeros((n_zl,) + out_weight.shape, out_weight.dtype)
+    row_part = lax.dynamic_update_index_in_dim(row_part, out_weight, zl, 0)
+    for d in range(1, n_zl):
+        got = shifted(out_weight, "zl", n_zl, d, wrap=True)
+        row_part = lax.dynamic_update_index_in_dim(row_part, got, (zl - d) % n_zl, 0)
+    return row_part
 
 
 def gather_weight(out_weight, sizes, is_first):
@@ -202,9 +213,13 @@
                 jnp.concatenate([value_tiles, cache_values.reshape(-1, tile_width)], axis=0),
             ]
         )
-        weight_full = out_weight
-        for axis in ("c", "zl", "y"):
-            weight_full = lax.all_gather(weight_full, axis, axis=0, tiled=True)
+        row_part = gather_row_weight(out_weight, sizes)
+        packed, row_part = lax.optimization_barrier((packed, row_part))
+        column = lax.all_gather(row_part, "y", axis=0)
+        other = swap_cores(column)
+        weight_full = jnp.where(
+            is_first, jnp.stack([column, other], axis=2), jnp.stack([other, column], axis=2)
+        ).reshape(-1, out_weight.shape[1])
 
         carry_state = visit_block(
             empty_state(head_count, row_count), packed, seq_index, query_heads, query_clip, context

time: 315 us -> 280 us (0.89)
  the two profiles are of different devices: /device:TPU:75 before, /device:TPU:11 now
where the time goes in v6:
time: 280 us; the launch traced here: 278 us
  starting transfers between devices  112 us (40%)
  waiting for transfers between devices  78.1 us (28%)
  other arithmetic  33.1 us (12%)
  local copies, waits for them, and re-layouts  22.9 us (8%)
  matrix products  17.2 us (6%)
  between operations  14.7 us (5%)
    ppermute x12, waiting for transfers between devices, shifted(): return lax.ppermute(block, axes, route)  72.6 us
    ppermute x7, starting transfers between devices, swap_cores(): return lax.ppermute(block, 'c', [(0, 1), (1, 0)])  65.3 us
    ppermute x12, starting transfers between devices, shifted(): return lax.ppermute(block, axes, route)  38.6 us
    concatenate x13, other arithmetic, allowed_keys(): return jnp.concatenate([same_clip, page_ok], axis=1)  13.6 us
    ppermute x1, starting transfers between devices, gather_attention(): partner = lax.ppermute(attention_local, 'zh', [(0, 1), (1, 0)])  7.95 us
    and x13, other arithmetic, allowed_keys(): page_ok = jnp.any(member[:, :, None] & named_pages[None], axis=1) & in_range  7.26 us
    unnamed x77, local copies, waits for them, and re-layouts  6.97 us
    dot_general x13, matrix products, attend(): jnp.einsum('qhd,khd->hqk', query_heads, key_heads, preferred_element_type...  6.29 us
  transfers between devices with their start and end apart: 21, of which 7 were waited for; matrix products, arithmetic and copies ran while one was open for 23% of the time, Pallas kernels for 0%

profile of v6, /device:TPU:11, one launch (start us, length us, event | category | flops | bytes accessed | tf_op | source)
XLA Modules:
  0.0 278.0 jit_solution(10539888236293923096)
XLA Ops:
  6.6 4.3 %collective-permute-start = (bf16[48,640]{1,0:T(8,128)(2,1)}, bf16[48,640]{1,0:T(8,128)(2,1)}, u32[]{:S(2)}, u32[]{:S(2)}) collective-permute-start(bf16[48,640]{1,0:T(8,128)(2,1)} %param.18), channel_id=1, source_target_pairs={{0,16},{16,32},{32,48},{48,0},{1,17},{17,33},{33,49},{49,1},{2,18}... | collective-permute-start | bytes 184328 | tf_op jit(solution)/shard_map/ppermute | solution.py:27
  10.9 5.8 %collective-permute-start.1 = (bf16[48,640]{1,0:T(8,128)(2,1)}, bf16[48,640]{1,0:T(8,128)(2,1)}, u32[]{:S(2)}, u32[]{:S(2)}) collective-permute-start(bf16[48,640]{1,0:T(8,128)(2,1)} %param.18), channel_id=1, source_target_pairs={{0,32},{16,48},{32,0},{48,16},{1,33},{17,49},{33,1},{49,17},{2,34}... | collective-permute-start | bytes 184328 | tf_op jit(solution)/shard_map/ppermute | solution.py:27
  16.7 2.2 collective-permute-start.2
  56.1 2.7 collective-permute-start.3
  65.1 2.6 collective-permute-start.4
  67.7 2.2 fusion.107
  69.9 3.1 %collective-permute-start.7 = (bf16[2,512,384]{1,2,0:T(8,128)(2,1)S(1)}, bf16[2,512,384]{1,2,0:T(8,128)(2,1)S(1)}, u32[]{:S(2)}, u32[]{:S(2)}) collective-permute-start(bf16[2,512,384]{1,2,0:T(8,128)(2,1)S(1)} %pad_maximum_fusion), channel_id=1, source_target_pairs={{48,0},{64,16},{80,32},{96,48},{112,64},{128,80},{144,96},{160,112... | collective-permute-start | bytes 2359304 | tf_op jit(solution)/shard_map/ppermute | solution.py:27
  73.1 4.5 %collective-permute-start.8 = (bf16[2,512,384]{1,2,0:T(8,128)(2,1)S(1)}, bf16[2,512,384]{1,2,0:T(8,128)(2,1)S(1)}, u32[]{:S(2)}, u32[]{:S(2)}) collective-permute-start(bf16[2,512,384]{1,2,0:T(8,128)(2,1)S(1)} %pad_maximum_fusion), channel_id=1, source_target_pairs={{0,48},{16,64},{32,80},{48,96},{64,112},{80,128},{96,144},{112,160... | collective-permute-start | bytes 2359304 | tf_op jit(solution)/shard_map/ppermute | solution.py:27
  79.5 30.7 %collective-permute-done.3 = bf16[2,512,384]{1,2,0:T(8,128)(2,1)} collective-permute-done((bf16[2,512,384]{1,2,0:T(8,128)(2,1)S(1)}, bf16[2,512,384]{1,2,0:T(8,128)(2,1)}, u32[]{:S(2)}, u32[]{:S(2)}) %collective-permute-start.3) | collective-permute-done | bytes 786464 | tf_op jit(solution)/shard_map/ppermute | solution.py:27
  112.8 14.8 %collective-permute-done.4 = bf16[2,512,384]{1,2,0:T(8,128)(2,1)} collective-permute-done((bf16[2,512,384]{1,2,0:T(8,128)(2,1)S(1)}, bf16[2,512,384]{1,2,0:T(8,128)(2,1)}, u32[]{:S(2)}, u32[]{:S(2)}) %collective-permute-start.4) | collective-permute-done | bytes 786464 | tf_op jit(solution)/shard_map/ppermute | solution.py:27
  127.6 49.8 %collective-permute-start.9 = (bf16[2,512,384]{1,2,0:T(8,128)(2,1)S(1)}, bf16[2,512,384]{1,2,0:T(8,128)(2,1)S(1)}, u32[]{:S(2)}, u32[]{:S(2)}) collective-permute-start(bf16[2,512,384]{1,2,0:T(8,128)(2,1)S(1)} %pad_maximum_fusion), channel_id=1, source_target_pairs={{0,8},{8,0},{1,9},{9,1},{2,10},{10,2},{3,11},{11,3},{4,12},{12,4},... | collective-permute-start | bytes 2359304 | tf_op jit(solution)/shard_map/ppermute | solution.py:31
  181.0 2.4 collective-permute-start.12
  183.4 11.0 %collective-permute-done.5 = bf16[2,512,384]{1,2,0:T(8,128)(2,1)S(1)} collective-permute-done((bf16[2,512,384]{1,2,0:T(8,128)(2,1)S(1)}, bf16[2,512,384]{1,2,0:T(8,128)(2,1)S(1)}, u32[]{:S(2)}, u32[]{:S(2)}) %collective-permute-start.5) | collective-permute-done | bytes 786464 | tf_op jit(solution)/shard_map/ppermute | solution.py:27
  194.4 4.3 %collective-permute-start.13 = (bf16[2,512,384]{1,2,0:T(8,128)(2,1)S(1)}, bf16[2,512,384]{1,2,0:T(8,128)(2,1)S(1)}, u32[]{:S(2)}, u32[]{:S(2)}) collective-permute-start(bf16[2,512,384]{1,2,0:T(8,128)(2,1)S(1)} %get-tuple-element.77), channel_id=1, source_target_pairs={{0,8},{8,0},{1,9},{9,1},{2,10},{10,2},{3,11},{11,3},{4,12},{12,4},... | collective-permute-start | bytes 2359304 | tf_op jit(solution)/shard_map/ppermute | solution.py:31
  200.9 2.6 collective-permute-start.14
  225.7 7.9 %collective-permute-start.15 = (bf16[256,384]{0,1:T(8,128)(2,1)S(1)}, bf16[256,384]{0,1:T(8,128)(2,1)S(1)}, u32[]{:S(2)}, u32[]{:S(2)}) collective-permute-start(bf16[256,384]{0,1:T(8,128)(2,1)S(1)} %bitcast.458), channel_id=1, source_target_pairs={{0,4},{4,0},{1,5},{5,1},{2,6},{6,2},{3,7},{7,3},{8,12},{12,8},{9,1... | collective-permute-start | bytes 589832 | tf_op jit(solution)/shard_map/ppermute | solution.py:156
  234.2 2.2 collective-permute-start.19
  236.4 5.5 %collective-permute-done.15 = bf16[256,384]{0,1:T(8,128)(2,1)S(1)} collective-permute-done((bf16[256,384]{0,1:T(8,128)(2,1)S(1)}, bf16[256,384]{0,1:T(8,128)(2,1)S(1)}, u32[]{:S(2)}, u32[]{:S(2)}) %collective-permute-start.15) | collective-permute-done | bytes 196640 | tf_op jit(solution)/shard_map/ppermute | solution.py:156
  242.0 3.1 %collective-permute-start.16 = (bf16[256,768]{0,1:T(8,128)(2,1)S(1)}, bf16[256,768]{0,1:T(8,128)(2,1)S(1)}, u32[]{:S(2)}, u32[]{:S(2)}) collective-permute-start(bf16[256,768]{0,1:T(8,128)(2,1)S(1)} %maximum_select_fusion.1), channel_id=1, source_target_pairs={{0,1},{1,2},{2,3},{3,0},{4,5},{5,6},{6,7},{7,4},{8,9},{9,10},{10,1... | collective-permute-start | bytes 1179656 | tf_op jit(solution)/shard_map/ppermute | solution.py:27
  245.1 2.7 collective-permute-start.17
  247.9 3.8 %collective-permute-start.18 = (bf16[256,768]{0,1:T(8,128)(2,1)S(1)}, bf16[256,768]{0,1:T(8,128)(2,1)S(1)}, u32[]{:S(2)}, u32[]{:S(2)}) collective-permute-start(bf16[256,768]{0,1:T(8,128)(2,1)S(1)} %maximum_select_fusion.1), channel_id=1, source_target_pairs={{0,3},{1,0},{2,1},{3,2},{4,7},{5,4},{6,5},{7,6},{8,11},{9,8},{10,9... | collective-permute-start | bytes 1179656 | tf_op jit(solution)/shard_map/ppermute | solution.py:27
  254.0 4.3 %collective-permute-done.17 = bf16[256,768]{0,1:T(8,128)(2,1)S(1)} collective-permute-done((bf16[256,768]{0,1:T(8,128)(2,1)S(1)}, bf16[256,768]{0,1:T(8,128)(2,1)S(1)}, u32[]{:S(2)}, u32[]{:S(2)}) %collective-permute-start.17) | collective-permute-done | bytes 393248 | tf_op jit(solution)/shard_map/ppermute | solution.py:27
  258.3 9.7 %collective-permute-done.18 = bf16[256,768]{0,1:T(8,128)(2,1)S(1)} collective-permute-done((bf16[256,768]{0,1:T(8,128)(2,1)S(1)}, bf16[256,768]{0,1:T(8,128)(2,1)S(1)}, u32[]{:S(2)}, u32[]{:S(2)}) %collective-permute-start.18) | collective-permute-done | bytes 393248 | tf_op jit(solution)/shard_map/ppermute | solution.py:27
  269.0 2.1 fusion.27
  (240 shorter events, 78.9 us)
Async XLA Ops:
  6.5 61.2 %copy-start = (f32[1000,640]{1,0:T(8,128)S(1)}, f32[1000,640]{1,0:T(8,128)}, u32[]{:S(2)}) copy-start(f32[1000,640]{1,0:T(8,128)} %param.19) | copy-start | bytes 7680004
  6.5 19.6 %copy-start.21 = (bf16[48,640]{1,0:T(8,128)(2,1)S(1)}, bf16[48,640]{1,0:T(8,128)(2,1)}, u32[]{:S(2)}) copy-start(bf16[48,640]{1,0:T(8,128)(2,1)} %param.18) | copy-start | bytes 184324
  6.5 227.6 %all-gather.3.cloned.1.call-start = ((), (), s32[]{:S(2)}) async-start(), calls=%async_computation | async-start | bytes 2211840 | tf_op jit(solution)/shard_map/all_gather | solution.py:218
  6.6 45.1 %collective-permute-start = (bf16[48,640]{1,0:T(8,128)(2,1)}, bf16[48,640]{1,0:T(8,128)(2,1)}, u32[]{:S(2)}, u32[]{:S(2)}) collective-permute-start(bf16[48,640]{1,0:T(8,128)(2,1)} %param.18), channel_id=1, source_target_pairs={{0,16},{16,32},{32,48},{48,0},{1,17},{17,33},{33,49},{49,1},{2,18}... | collective-permute-start | bytes 184328 | tf_op jit(solution)/shard_map/ppermute | solution.py:27
  10.9 42.3 %collective-permute-start.1 = (bf16[48,640]{1,0:T(8,128)(2,1)}, bf16[48,640]{1,0:T(8,128)(2,1)}, u32[]{:S(2)}, u32[]{:S(2)}) collective-permute-start(bf16[48,640]{1,0:T(8,128)(2,1)} %param.18), channel_id=1, source_target_pairs={{0,32},{16,48},{32,0},{48,16},{1,33},{17,49},{33,1},{49,17},{2,34}... | collective-permute-start | bytes 184328 | tf_op jit(solution)/shard_map/ppermute | solution.py:27
  16.7 38.0 %collective-permute-start.2 = (bf16[48,640]{1,0:T(8,128)(2,1)}, bf16[48,640]{1,0:T(8,128)(2,1)}, u32[]{:S(2)}, u32[]{:S(2)}) collective-permute-start(bf16[48,640]{1,0:T(8,128)(2,1)} %param.18), channel_id=1, source_target_pairs={{0,48},{16,0},{32,16},{48,32},{1,49},{17,1},{33,17},{49,33},{2,50}... | collective-permute-start | bytes 184328 | tf_op jit(solution)/shard_map/ppermute | solution.py:27
  56.1 54.2 %collective-permute-start.3 = (bf16[2,512,384]{1,2,0:T(8,128)(2,1)S(1)}, bf16[2,512,384]{1,2,0:T(8,128)(2,1)}, u32[]{:S(2)}, u32[]{:S(2)}) collective-permute-start(bf16[2,512,384]{1,2,0:T(8,128)(2,1)S(1)} %pad_maximum_fusion), channel_id=1, source_target_pairs={{16,0},{32,16},{48,32},{64,48},{80,64},{96,80},{112,96},{128,112},... | collective-permute-start | bytes 2359304 | tf_op jit(solution)/shard_map/ppermute | solution.py:27
  65.1 62.5 %collective-permute-start.4 = (bf16[2,512,384]{1,2,0:T(8,128)(2,1)S(1)}, bf16[2,512,384]{1,2,0:T(8,128)(2,1)}, u32[]{:S(2)}, u32[]{:S(2)}) collective-permute-start(bf16[2,512,384]{1,2,0:T(8,128)(2,1)S(1)} %pad_maximum_fusion), channel_id=1, source_target_pairs={{0,16},{16,32},{32,48},{48,64},{64,80},{80,96},{96,112},{112,128},... | collective-permute-start | bytes 2359304 | tf_op jit(solution)/shard_map/ppermute | solution.py:27
  69.9 42.4 %copy-start.15 = (pred[256,512]{0,1:T(8,128)(4,1)S(1)}, pred[256,512]{0,1:T(8,128)(4,1)}, u32[]{:S(2)}) copy-start(pred[256,512]{0,1:T(8,128)(4,1)} %pad_add_fusion) | copy-start | bytes 393220
  69.9 109.0 %collective-permute-start.7 = (bf16[2,512,384]{1,2,0:T(8,128)(2,1)S(1)}, bf16[2,512,384]{1,2,0:T(8,128)(2,1)S(1)}, u32[]{:S(2)}, u32[]{:S(2)}) collective-permute-start(bf16[2,512,384]{1,2,0:T(8,128)(2,1)S(1)} %pad_maximum_fusion), channel_id=1, source_target_pairs={{48,0},{64,16},{80,32},{96,48},{112,64},{128,80},{144,96},{160,112... | collective-permute-start | bytes 2359304 | tf_op jit(solution)/shard_map/ppermute | solution.py:27
  73.1 107.8 %collective-permute-start.8 = (bf16[2,512,384]{1,2,0:T(8,128)(2,1)S(1)}, bf16[2,512,384]{1,2,0:T(8,128)(2,1)S(1)}, u32[]{:S(2)}, u32[]{:S(2)}) collective-permute-start(bf16[2,512,384]{1,2,0:T(8,128)(2,1)S(1)} %pad_maximum_fusion), channel_id=1, source_target_pairs={{0,48},{16,64},{32,80},{48,96},{64,112},{80,128},{96,144},{112,160... | collective-permute-start | bytes 2359304 | tf_op jit(solution)/shard_map/ppermute | solution.py:27
  77.5 116.9 %collective-permute-start.5 = (bf16[2,512,384]{1,2,0:T(8,128)(2,1)S(1)}, bf16[2,512,384]{1,2,0:T(8,128)(2,1)S(1)}, u32[]{:S(2)}, u32[]{:S(2)}) collective-permute-start(bf16[2,512,384]{1,2,0:T(8,128)(2,1)S(1)} %pad_maximum_fusion), channel_id=1, source_target_pairs={{32,0},{48,16},{64,32},{80,48},{96,64},{112,80},{128,96},{144,112}... | collective-permute-start | bytes 2359304 | tf_op jit(solution)/shard_map/ppermute | solution.py:27
  110.3 88.5 %collective-permute-start.6 = (bf16[2,512,384]{1,2,0:T(8,128)(2,1)S(1)}, bf16[2,512,384]{1,2,0:T(8,128)(2,1)S(1)}, u32[]{:S(2)}, u32[]{:S(2)}) collective-permute-start(bf16[2,512,384]{1,2,0:T(8,128)(2,1)S(1)} %pad_maximum_fusion), channel_id=1, source_target_pairs={{0,32},{16,48},{32,64},{48,80},{64,96},{80,112},{96,128},{112,144}... | collective-permute-start | bytes 2359304 | tf_op jit(solution)/shard_map/ppermute | solution.py:27
  127.6 73.3 %collective-permute-start.9 = (bf16[2,512,384]{1,2,0:T(8,128)(2,1)S(1)}, bf16[2,512,384]{1,2,0:T(8,128)(2,1)S(1)}, u32[]{:S(2)}, u32[]{:S(2)}) collective-permute-start(bf16[2,512,384]{1,2,0:T(8,128)(2,1)S(1)} %pad_maximum_fusion), channel_id=1, source_target_pairs={{0,8},{8,0},{1,9},{9,1},{2,10},{10,2},{3,11},{11,3},{4,12},{12,4},... | collective-permute-start | bytes 2359304 | tf_op jit(solution)/shard_map/ppermute | solution.py:31
  179.0 32.1 %collective-permute-start.10 = (bf16[2,512,384]{1,2,0:T(8,128)(2,1)S(1)}, bf16[2,512,384]{1,2,0:T(8,128)(2,1)S(1)}, u32[]{:S(2)}, u32[]{:S(2)}) collective-permute-start(bf16[2,512,384]{1,2,0:T(8,128)(2,1)S(1)} %get-tuple-element.76), channel_id=1, source_target_pairs={{0,8},{8,0},{1,9},{9,1},{2,10},{10,2},{3,11},{11,3},{4,12},{12,4},... | collective-permute-start | bytes 2359304 | tf_op jit(solution)/shard_map/ppermute | solution.py:31
  181.0 30.2 %collective-permute-start.12 = (bf16[2,512,384]{1,2,0:T(8,128)(2,1)S(1)}, bf16[2,512,384]{1,2,0:T(8,128)(2,1)S(1)}, u32[]{:S(2)}, u32[]{:S(2)}) collective-permute-start(bf16[2,512,384]{1,2,0:T(8,128)(2,1)S(1)} %broadcast_select_fusion.2), channel_id=1, source_target_pairs={{0,8},{8,0},{1,9},{9,1},{2,10},{10,2},{3,11},{11,3},{4,12},{12,4},... | collective-permute-start | bytes 2359304 | tf_op jit(solution)/shard_map/ppermute | solution.py:31
  194.4 16.8 %collective-permute-start.13 = (bf16[2,512,384]{1,2,0:T(8,128)(2,1)S(1)}, bf16[2,512,384]{1,2,0:T(8,128)(2,1)S(1)}, u32[]{:S(2)}, u32[]{:S(2)}) collective-permute-start(bf16[2,512,384]{1,2,0:T(8,128)(2,1)S(1)} %get-tuple-element.77), channel_id=1, source_target_pairs={{0,8},{8,0},{1,9},{9,1},{2,10},{10,2},{3,11},{11,3},{4,12},{12,4},... | collective-permute-start | bytes 2359304 | tf_op jit(solution)/shard_map/ppermute | solution.py:31
  198.9 14.2 %collective-permute-start.11 = (bf16[2,512,384]{1,2,0:T(8,128)(2,1)S(1)}, bf16[2,512,384]{1,2,0:T(8,128)(2,1)S(1)}, u32[]{:S(2)}, u32[]{:S(2)}) collective-permute-start(bf16[2,512,384]{1,2,0:T(8,128)(2,1)S(1)} %get-tuple-element.78), channel_id=1, source_target_pairs={{0,8},{8,0},{1,9},{9,1},{2,10},{10,2},{3,11},{11,3},{4,12},{12,4},... | collective-permute-start | bytes 2359304 | tf_op jit(solution)/shard_map/ppermute | solution.py:31
  200.9 13.5 %collective-permute-start.14 = (bf16[2,512,384]{1,2,0:T(8,128)(2,1)S(1)}, bf16[2,512,384]{1,2,0:T(8,128)(2,1)S(1)}, u32[]{:S(2)}, u32[]{:S(2)}) collective-permute-start(bf16[2,512,384]{1,2,0:T(8,128)(2,1)S(1)} %get-tuple-element.79), channel_id=1, source_target_pairs={{0,8},{8,0},{1,9},{9,1},{2,10},{10,2},{3,11},{11,3},{4,12},{12,4},... | collective-permute-start | bytes 2359304 | tf_op jit(solution)/shard_map/ppermute | solution.py:31
  225.7 16.1 %collective-permute-start.15 = (bf16[256,384]{0,1:T(8,128)(2,1)S(1)}, bf16[256,384]{0,1:T(8,128)(2,1)S(1)}, u32[]{:S(2)}, u32[]{:S(2)}) collective-permute-start(bf16[256,384]{0,1:T(8,128)(2,1)S(1)} %bitcast.458), channel_id=1, source_target_pairs={{0,4},{4,0},{1,5},{5,1},{2,6},{6,2},{3,7},{7,3},{8,12},{12,8},{9,1... | collective-permute-start | bytes 589832 | tf_op jit(solution)/shard_map/ppermute | solution.py:156
  234.2 33.9 %collective-permute-start.19 = (bf16[8,4,48,640]{3,2,1,0:T(8,128)(2,1)}, bf16[8,4,48,640]{3,2,1,0:T(8,128)(2,1)S(1)}, u32[]{:S(2)}, u32[]{:S(2)}) collective-permute-start(bf16[8,4,48,640]{3,2,1,0:T(8,128)(2,1)} %bitcast.414), channel_id=1, source_target_pairs={{0,8},{8,0},{1,9},{9,1},{2,10},{10,2},{3,11},{11,3},{4,12},{12,4},... | collective-permute-start | bytes 5898248 | tf_op jit(solution)/shard_map/ppermute | solution.py:31
  242.0 11.9 %collective-permute-start.16 = (bf16[256,768]{0,1:T(8,128)(2,1)S(1)}, bf16[256,768]{0,1:T(8,128)(2,1)S(1)}, u32[]{:S(2)}, u32[]{:S(2)}) collective-permute-start(bf16[256,768]{0,1:T(8,128)(2,1)S(1)} %maximum_select_fusion.1), channel_id=1, source_target_pairs={{0,1},{1,2},{2,3},{3,0},{4,5},{5,6},{6,7},{7,4},{8,9},{9,10},{10,1... | collective-permute-start | bytes 1179656 | tf_op jit(solution)/shard_map/ppermute | solution.py:27
  245.1 13.2 %collective-permute-start.17 = (bf16[256,768]{0,1:T(8,128)(2,1)S(1)}, bf16[256,768]{0,1:T(8,128)(2,1)S(1)}, u32[]{:S(2)}, u32[]{:S(2)}) collective-permute-start(bf16[256,768]{0,1:T(8,128)(2,1)S(1)} %maximum_select_fusion.1), channel_id=1, source_target_pairs={{0,2},{1,3},{2,0},{3,1},{4,6},{5,7},{6,4},{7,5},{8,10},{9,11},{10,... | collective-permute-start | bytes 1179656 | tf_op jit(solution)/shard_map/ppermute | solution.py:27
  247.9 20.1 %collective-permute-start.18 = (bf16[256,768]{0,1:T(8,128)(2,1)S(1)}, bf16[256,768]{0,1:T(8,128)(2,1)S(1)}, u32[]{:S(2)}, u32[]{:S(2)}) collective-permute-start(bf16[256,768]{0,1:T(8,128)(2,1)S(1)} %maximum_select_fusion.1), channel_id=1, source_target_pairs={{0,3},{1,0},{2,1},{3,2},{4,7},{5,4},{6,5},{7,6},{8,11},{9,8},{10,9... | collective-permute-start | bytes 1179656 | tf_op jit(solution)/shard_map/ppermute | solution.py:27
  (34 other events, 170.1 us)
Sparse Core Ops, SparseCore 0:
  79.6 57.5 all-gather.2

commit v7 on v6

--- a/solution.py
+++ b/solution.py
@@ -213,12 +213,10 @@
                 jnp.concatenate([value_tiles, cache_values.reshape(-1, tile_width)], axis=0),
             ]
         )
-        row_part = gather_row_weight(out_weight, sizes)
-        packed, row_part = lax.optimization_barrier((packed, row_part))
-        column = lax.all_gather(row_part, "y", axis=0)
+        column = lax.all_gather(out_weight, CHIP, axis=0)
         other = swap_cores(column)
         weight_full = jnp.where(
-            is_first, jnp.stack([column, other], axis=2), jnp.stack([other, column], axis=2)
+            is_first, jnp.stack([column, other], axis=1), jnp.stack([other, column], axis=1)
         ).reshape(-1, out_weight.shape[1])
 
         carry_state = visit_block(

time: 280 us -> 315 us (1.12)
  the two profiles are of different devices: /device:TPU:11 before, /device:TPU:35 now
where the time goes in v7:
time: 315 us; the launch traced here: 314 us
  waiting for transfers between devices  132 us (42%)
  starting transfers between devices  82.8 us (26%)
  other arithmetic  40.4 us (13%)
  local copies, waits for them, and re-layouts  27.3 us (9%)
  matrix products  16.5 us (5%)
  between operations  14.5 us (5%)
    ppermute x9, waiting for transfers between devices, shifted(): return lax.ppermute(block, axes, route)  92.4 us
    all_gather x1, waiting for transfers between devices, local(): column = lax.all_gather(out_weight, CHIP, axis=0)  39.9 us
    ppermute x7, starting transfers between devices, swap_cores(): return lax.ppermute(block, 'c', [(0, 1), (1, 0)])  38.5 us
    ppermute x9, starting transfers between devices, shifted(): return lax.ppermute(block, axes, route)  33.8 us
    and x13, other arithmetic, allowed_keys(): page_ok = jnp.any(member[:, :, None] & named_pages[None], axis=1) & in_range  10.9 us
    ppermute x1, starting transfers between devices, gather_attention(): partner = lax.ppermute(attention_local, 'zh', [(0, 1), (1, 0)])  10.5 us
    concatenate x13, other arithmetic, allowed_keys(): return jnp.concatenate([same_clip, page_ok], axis=1)  8.94 us
    unnamed x62, local copies, waits for them, and re-layouts  8.18 us
  transfers between devices with their start and end apart: 18, of which 5 were waited for; matrix products, arithmetic and copies ran while one was open for 22% of the time, Pallas kernels for 0%

profile of v7, /device:TPU:35, one launch (start us, length us, event | category | flops | bytes accessed | tf_op | source)
XLA Modules:
  0.0 313.8 jit_solution(9596054420308710429)
XLA Ops:
  14.6 7.5 %collective-permute-start = (bf16[2,512,384]{1,2,0:T(8,128)(2,1)}, bf16[2,512,384]{1,2,0:T(8,128)(2,1)}, u32[]{:S(2)}, u32[]{:S(2)}) collective-permute-start(bf16[2,512,384]{1,2,0:T(8,128)(2,1)} %pad_maximum_fusion), channel_id=1, source_target_pairs={{16,0},{32,16},{48,32},{64,48},{80,64},{96,80},{112,96},{128,112},... | collective-permute-start | bytes 2359304 | tf_op jit(solution)/shard_map/ppermute | solution.py:27
  22.1 1.9 collective-permute-start.1
  24.0 2.2 collective-permute-start.2
  26.2 4.0 %collective-permute-start.3 = (bf16[2,512,384]{1,2,0:T(8,128)(2,1)}, bf16[2,512,384]{1,2,0:T(8,128)(2,1)}, u32[]{:S(2)}, u32[]{:S(2)}) collective-permute-start(bf16[2,512,384]{1,2,0:T(8,128)(2,1)} %pad_maximum_fusion), channel_id=1, source_target_pairs={{0,32},{16,48},{32,64},{48,80},{64,96},{80,112},{96,128},{112,144}... | collective-permute-start | bytes 2359304 | tf_op jit(solution)/shard_map/ppermute | solution.py:27
  30.2 5.2 %collective-permute-start.4 = (bf16[2,512,384]{1,2,0:T(8,128)(2,1)}, bf16[2,512,384]{1,2,0:T(8,128)(2,1)S(1)}, u32[]{:S(2)}, u32[]{:S(2)}) collective-permute-start(bf16[2,512,384]{1,2,0:T(8,128)(2,1)} %pad_maximum_fusion), channel_id=1, source_target_pairs={{48,0},{64,16},{80,32},{96,48},{112,64},{128,80},{144,96},{160,112... | collective-permute-start | bytes 2359304 | tf_op jit(solution)/shard_map/ppermute | solution.py:27
  59.1 2.0 compare_and_fusion.10
  81.2 3.8 %collective-permute-start.5 = (bf16[2,512,384]{1,2,0:T(8,128)(2,1)}, bf16[2,512,384]{1,2,0:T(8,128)(2,1)S(1)}, u32[]{:S(2)}, u32[]{:S(2)}) collective-permute-start(bf16[2,512,384]{1,2,0:T(8,128)(2,1)} %pad_maximum_fusion), channel_id=1, source_target_pairs={{0,48},{16,64},{32,80},{48,96},{64,112},{80,128},{96,144},{112,160... | collective-permute-start | bytes 2359304 | tf_op jit(solution)/shard_map/ppermute | solution.py:27
  85.1 4.8 %collective-permute-start.6 = (bf16[2,512,384]{1,2,0:T(8,128)(2,1)}, bf16[2,512,384]{1,2,0:T(8,128)(2,1)S(1)}, u32[]{:S(2)}, u32[]{:S(2)}) collective-permute-start(bf16[2,512,384]{1,2,0:T(8,128)(2,1)} %pad_maximum_fusion), channel_id=1, source_target_pairs={{0,8},{8,0},{1,9},{9,1},{2,10},{10,2},{3,11},{11,3},{4,12},{12,4},... | collective-permute-start | bytes 2359304 | tf_op jit(solution)/shard_map/ppermute | solution.py:31
  91.4 76.3 %collective-permute-done.2 = bf16[2,512,384]{1,2,0:T(8,128)(2,1)} collective-permute-done((bf16[2,512,384]{1,2,0:T(8,128)(2,1)}, bf16[2,512,384]{1,2,0:T(8,128)(2,1)}, u32[]{:S(2)}, u32[]{:S(2)}) %collective-permute-start.2) | collective-permute-done | bytes 786464 | tf_op jit(solution)/shard_map/ppermute | solution.py:27
  167.7 3.2 %collective-permute-start.7 = (bf16[2,512,384]{1,2,0:T(8,128)(2,1)S(1)}, bf16[2,512,384]{1,2,0:T(8,128)(2,1)S(1)}, u32[]{:S(2)}, u32[]{:S(2)}) collective-permute-start(bf16[2,512,384]{1,2,0:T(8,128)(2,1)S(1)} %get-tuple-element.72), channel_id=1, source_target_pairs={{0,8},{8,0},{1,9},{9,1},{2,10},{10,2},{3,11},{11,3},{4,12},{12,4},... | collective-permute-start | bytes 2359304 | tf_op jit(solution)/shard_map/ppermute | solution.py:31
  172.4 2.1 collective-permute-start.8
  174.6 2.4 collective-permute-start.9
  177.0 1.9 collective-permute-start.10
  179.0 2.6 collective-permute-start.11
  205.7 10.5 %collective-permute-start.12 = (bf16[256,384]{0,1:T(8,128)(2,1)S(1)}, bf16[256,384]{0,1:T(8,128)(2,1)S(1)}, u32[]{:S(2)}, u32[]{:S(2)}) collective-permute-start(bf16[256,384]{0,1:T(8,128)(2,1)S(1)} %bitcast.450), channel_id=1, source_target_pairs={{0,4},{4,0},{1,5},{5,1},{2,6},{6,2},{3,7},{7,3},{8,12},{12,8},{9,1... | collective-permute-start | bytes 589832 | tf_op jit(solution)/shard_map/ppermute | solution.py:156
  216.7 39.9 %all-gather.3.cloned.1.call-done = bf16[1536,640]{1,0:T(8,128)(2,1)} async-done(((bf16[48,640]{1,0:T(8,128)(2,1)}), bf16[1536,640]{1,0:T(8,128)(2,1)}) %all-gather.3.cloned.1.call-update) | async-done | bytes 1966096 | tf_op jit(solution)/shard_map/all_gather | solution.py:216
  256.5 21.5 %collective-permute-start.16 = (bf16[32,48,640]{2,1,0:T(8,128)(2,1)}, bf16[32,48,640]{2,1,0:T(8,128)(2,1)S(1)}, u32[]{:S(2)}, u32[]{:S(2)}) collective-permute-start(bf16[32,48,640]{2,1,0:T(8,128)(2,1)} %bitcast.406), channel_id=1, source_target_pairs={{0,8},{8,0},{1,9},{9,1},{2,10},{10,2},{3,11},{11,3},{4,12},{12,4},... | collective-permute-start | bytes 5898248 | tf_op jit(solution)/shard_map/ppermute | solution.py:31
  278.2 2.7 collective-permute-start.13
  280.9 2.8 collective-permute-start.14
  283.8 3.7 %collective-permute-start.15 = (bf16[256,768]{0,1:T(8,128)(2,1)S(1)}, bf16[256,768]{0,1:T(8,128)(2,1)S(1)}, u32[]{:S(2)}, u32[]{:S(2)}) collective-permute-start(bf16[256,768]{0,1:T(8,128)(2,1)S(1)} %maximum_select_fusion.1), channel_id=1, source_target_pairs={{0,3},{1,0},{2,1},{3,2},{4,7},{5,4},{6,5},{7,6},{8,11},{9,8},{10,9... | collective-permute-start | bytes 1179656 | tf_op jit(solution)/shard_map/ppermute | solution.py:27
  287.7 3.2 %collective-permute-done.13 = bf16[256,768]{0,1:T(8,128)(2,1)S(1)} collective-permute-done((bf16[256,768]{0,1:T(8,128)(2,1)S(1)}, bf16[256,768]{0,1:T(8,128)(2,1)S(1)}, u32[]{:S(2)}, u32[]{:S(2)}) %collective-permute-start.13) | collective-permute-done | bytes 393248 | tf_op jit(solution)/shard_map/ppermute | solution.py:27
  290.9 3.9 %collective-permute-done.14 = bf16[256,768]{0,1:T(8,128)(2,1)S(1)} collective-permute-done((bf16[256,768]{0,1:T(8,128)(2,1)S(1)}, bf16[256,768]{0,1:T(8,128)(2,1)S(1)}, u32[]{:S(2)}, u32[]{:S(2)}) %collective-permute-start.14) | collective-permute-done | bytes 393248 | tf_op jit(solution)/shard_map/ppermute | solution.py:27
  294.8 9.0 %collective-permute-done.15 = bf16[256,768]{0,1:T(8,128)(2,1)S(1)} collective-permute-done((bf16[256,768]{0,1:T(8,128)(2,1)S(1)}, bf16[256,768]{0,1:T(8,128)(2,1)S(1)}, u32[]{:S(2)}, u32[]{:S(2)}) %collective-permute-start.15) | collective-permute-done | bytes 393248 | tf_op jit(solution)/shard_map/ppermute | solution.py:27
  304.8 2.2 fusion.27
  (217 shorter events, 80.2 us)
Async XLA Ops:
  6.5 72.6 %copy-start = (f32[1000,640]{1,0:T(8,128)S(1)}, f32[1000,640]{1,0:T(8,128)}, u32[]{:S(2)}) copy-start(f32[1000,640]{1,0:T(8,128)} %param.19) | copy-start | bytes 7680004
  6.5 250.0 %all-gather.3.cloned.1.call-start = ((), (), s32[]{:S(2)}) async-start(), calls=%async_computation | async-start | bytes 2027520 | tf_op jit(solution)/shard_map/all_gather | solution.py:216
  12.5 23.1 %copy-start.14 = (bf16[2,128,384]{2,1,0:T(8,128)(2,1)S(1)}, bf16[2,128,384]{2,1,0:T(8,128)(2,1)}, u32[]{:S(2)}) copy-start(bf16[2,128,384]{2,1,0:T(8,128)(2,1)} %param.15) | copy-start | bytes 589828
  13.6 25.1 %copy-start.28 = (s32[16]{0:T(128)S(1)}, s32[16]{0:T(128)}, u32[]{:S(2)}) copy-start(s32[16]{0:T(128)} %param.22) | copy-start | bytes 196
  13.6 25.6 %copy-start.26 = (s32[16]{0:T(128)S(1)}, s32[16]{0:T(128)}, u32[]{:S(2)}) copy-start(s32[16]{0:T(128)} %param.20) | copy-start | bytes 196
  14.6 66.6 %collective-permute-start = (bf16[2,512,384]{1,2,0:T(8,128)(2,1)}, bf16[2,512,384]{1,2,0:T(8,128)(2,1)}, u32[]{:S(2)}, u32[]{:S(2)}) collective-permute-start(bf16[2,512,384]{1,2,0:T(8,128)(2,1)} %pad_maximum_fusion), channel_id=1, source_target_pairs={{16,0},{32,16},{48,32},{64,48},{80,64},{96,80},{112,96},{128,112},... | collective-permute-start | bytes 2359304 | tf_op jit(solution)/shard_map/ppermute | solution.py:27
  22.1 63.0 %collective-permute-start.1 = (bf16[2,512,384]{1,2,0:T(8,128)(2,1)}, bf16[2,512,384]{1,2,0:T(8,128)(2,1)}, u32[]{:S(2)}, u32[]{:S(2)}) collective-permute-start(bf16[2,512,384]{1,2,0:T(8,128)(2,1)} %pad_maximum_fusion), channel_id=1, source_target_pairs={{0,16},{16,32},{32,48},{48,64},{64,80},{80,96},{96,112},{112,128},... | collective-permute-start | bytes 2359304 | tf_op jit(solution)/shard_map/ppermute | solution.py:27
  24.0 143.7 %collective-permute-start.2 = (bf16[2,512,384]{1,2,0:T(8,128)(2,1)}, bf16[2,512,384]{1,2,0:T(8,128)(2,1)}, u32[]{:S(2)}, u32[]{:S(2)}) collective-permute-start(bf16[2,512,384]{1,2,0:T(8,128)(2,1)} %pad_maximum_fusion), channel_id=1, source_target_pairs={{32,0},{48,16},{64,32},{80,48},{96,64},{112,80},{128,96},{144,112}... | collective-permute-start | bytes 2359304 | tf_op jit(solution)/shard_map/ppermute | solution.py:27
  26.2 144.7 %collective-permute-start.3 = (bf16[2,512,384]{1,2,0:T(8,128)(2,1)}, bf16[2,512,384]{1,2,0:T(8,128)(2,1)}, u32[]{:S(2)}, u32[]{:S(2)}) collective-permute-start(bf16[2,512,384]{1,2,0:T(8,128)(2,1)} %pad_maximum_fusion), channel_id=1, source_target_pairs={{0,32},{16,48},{32,64},{48,80},{64,96},{80,112},{96,128},{112,144}... | collective-permute-start | bytes 2359304 | tf_op jit(solution)/shard_map/ppermute | solution.py:27
  30.2 144.3 %collective-permute-start.4 = (bf16[2,512,384]{1,2,0:T(8,128)(2,1)}, bf16[2,512,384]{1,2,0:T(8,128)(2,1)S(1)}, u32[]{:S(2)}, u32[]{:S(2)}) collective-permute-start(bf16[2,512,384]{1,2,0:T(8,128)(2,1)} %pad_maximum_fusion), channel_id=1, source_target_pairs={{48,0},{64,16},{80,32},{96,48},{112,64},{128,80},{144,96},{160,112... | collective-permute-start | bytes 2359304 | tf_op jit(solution)/shard_map/ppermute | solution.py:27
  65.0 12.0 %copy-start.20 = (pred[256,256]{0,1:T(8,128)(4,1)S(1)}, pred[256,256]{0,1:T(8,128)(4,1)}, u32[]{:S(2)}) copy-start(pred[256,256]{0,1:T(8,128)(4,1)} %get-tuple-element.104) | copy-start | bytes 196612
  81.2 93.3 %collective-permute-start.5 = (bf16[2,512,384]{1,2,0:T(8,128)(2,1)}, bf16[2,512,384]{1,2,0:T(8,128)(2,1)S(1)}, u32[]{:S(2)}, u32[]{:S(2)}) collective-permute-start(bf16[2,512,384]{1,2,0:T(8,128)(2,1)} %pad_maximum_fusion), channel_id=1, source_target_pairs={{0,48},{16,64},{32,80},{48,96},{64,112},{80,128},{96,144},{112,160... | collective-permute-start | bytes 2359304 | tf_op jit(solution)/shard_map/ppermute | solution.py:27
  85.1 93.9 %collective-permute-start.6 = (bf16[2,512,384]{1,2,0:T(8,128)(2,1)}, bf16[2,512,384]{1,2,0:T(8,128)(2,1)S(1)}, u32[]{:S(2)}, u32[]{:S(2)}) collective-permute-start(bf16[2,512,384]{1,2,0:T(8,128)(2,1)} %pad_maximum_fusion), channel_id=1, source_target_pairs={{0,8},{8,0},{1,9},{9,1},{2,10},{10,2},{3,11},{11,3},{4,12},{12,4},... | collective-permute-start | bytes 2359304 | tf_op jit(solution)/shard_map/ppermute | solution.py:31
  167.7 22.9 %collective-permute-start.7 = (bf16[2,512,384]{1,2,0:T(8,128)(2,1)S(1)}, bf16[2,512,384]{1,2,0:T(8,128)(2,1)S(1)}, u32[]{:S(2)}, u32[]{:S(2)}) collective-permute-start(bf16[2,512,384]{1,2,0:T(8,128)(2,1)S(1)} %get-tuple-element.72), channel_id=1, source_target_pairs={{0,8},{8,0},{1,9},{9,1},{2,10},{10,2},{3,11},{11,3},{4,12},{12,4},... | collective-permute-start | bytes 2359304 | tf_op jit(solution)/shard_map/ppermute | solution.py:31
  172.4 18.3 %collective-permute-start.8 = (bf16[2,512,384]{1,2,0:T(8,128)(2,1)S(1)}, bf16[2,512,384]{1,2,0:T(8,128)(2,1)S(1)}, u32[]{:S(2)}, u32[]{:S(2)}) collective-permute-start(bf16[2,512,384]{1,2,0:T(8,128)(2,1)S(1)} %get-tuple-element.74), channel_id=1, source_target_pairs={{0,8},{8,0},{1,9},{9,1},{2,10},{10,2},{3,11},{11,3},{4,12},{12,4},... | collective-permute-start | bytes 2359304 | tf_op jit(solution)/shard_map/ppermute | solution.py:31
  174.6 16.2 %collective-permute-start.9 = (bf16[2,512,384]{1,2,0:T(8,128)(2,1)S(1)}, bf16[2,512,384]{1,2,0:T(8,128)(2,1)S(1)}, u32[]{:S(2)}, u32[]{:S(2)}) collective-permute-start(bf16[2,512,384]{1,2,0:T(8,128)(2,1)S(1)} %broadcast_select_fusion.2), channel_id=1, source_target_pairs={{0,8},{8,0},{1,9},{9,1},{2,10},{10,2},{3,11},{11,3},{4,12},{12,4},... | collective-permute-start | bytes 2359304 | tf_op jit(solution)/shard_map/ppermute | solution.py:31
  177.0 15.6 %collective-permute-start.10 = (bf16[2,512,384]{1,2,0:T(8,128)(2,1)S(1)}, bf16[2,512,384]{1,2,0:T(8,128)(2,1)S(1)}, u32[]{:S(2)}, u32[]{:S(2)}) collective-permute-start(bf16[2,512,384]{1,2,0:T(8,128)(2,1)S(1)} %get-tuple-element.73), channel_id=1, source_target_pairs={{0,8},{8,0},{1,9},{9,1},{2,10},{10,2},{3,11},{11,3},{4,12},{12,4},... | collective-permute-start | bytes 2359304 | tf_op jit(solution)/shard_map/ppermute | solution.py:31
  179.0 15.0 %collective-permute-start.11 = (bf16[2,512,384]{1,2,0:T(8,128)(2,1)S(1)}, bf16[2,512,384]{1,2,0:T(8,128)(2,1)S(1)}, u32[]{:S(2)}, u32[]{:S(2)}) collective-permute-start(bf16[2,512,384]{1,2,0:T(8,128)(2,1)S(1)} %get-tuple-element.75), channel_id=1, source_target_pairs={{0,8},{8,0},{1,9},{9,1},{2,10},{10,2},{3,11},{11,3},{4,12},{12,4},... | collective-permute-start | bytes 2359304 | tf_op jit(solution)/shard_map/ppermute | solution.py:31
  205.7 72.4 %collective-permute-start.12 = (bf16[256,384]{0,1:T(8,128)(2,1)S(1)}, bf16[256,384]{0,1:T(8,128)(2,1)S(1)}, u32[]{:S(2)}, u32[]{:S(2)}) collective-permute-start(bf16[256,384]{0,1:T(8,128)(2,1)S(1)} %bitcast.450), channel_id=1, source_target_pairs={{0,4},{4,0},{1,5},{5,1},{2,6},{6,2},{3,7},{7,3},{8,12},{12,8},{9,1... | collective-permute-start | bytes 589832 | tf_op jit(solution)/shard_map/ppermute | solution.py:156
  256.5 47.3 %collective-permute-start.16 = (bf16[32,48,640]{2,1,0:T(8,128)(2,1)}, bf16[32,48,640]{2,1,0:T(8,128)(2,1)S(1)}, u32[]{:S(2)}, u32[]{:S(2)}) collective-permute-start(bf16[32,48,640]{2,1,0:T(8,128)(2,1)} %bitcast.406), channel_id=1, source_target_pairs={{0,8},{8,0},{1,9},{9,1},{2,10},{10,2},{3,11},{11,3},{4,12},{12,4},... | collective-permute-start | bytes 5898248 | tf_op jit(solution)/shard_map/ppermute | solution.py:31
  278.2 12.6 %collective-permute-start.13 = (bf16[256,768]{0,1:T(8,128)(2,1)S(1)}, bf16[256,768]{0,1:T(8,128)(2,1)S(1)}, u32[]{:S(2)}, u32[]{:S(2)}) collective-permute-start(bf16[256,768]{0,1:T(8,128)(2,1)S(1)} %maximum_select_fusion.1), channel_id=1, source_target_pairs={{0,1},{1,2},{2,3},{3,0},{4,5},{5,6},{6,7},{7,4},{8,9},{9,10},{10,1... | collective-permute-start | bytes 1179656 | tf_op jit(solution)/shard_map/ppermute | solution.py:27
  280.9 13.9 %collective-permute-start.14 = (bf16[256,768]{0,1:T(8,128)(2,1)S(1)}, bf16[256,768]{0,1:T(8,128)(2,1)S(1)}, u32[]{:S(2)}, u32[]{:S(2)}) collective-permute-start(bf16[256,768]{0,1:T(8,128)(2,1)S(1)} %maximum_select_fusion.1), channel_id=1, source_target_pairs={{0,2},{1,3},{2,0},{3,1},{4,6},{5,7},{6,4},{7,5},{8,10},{9,11},{10,... | collective-permute-start | bytes 1179656 | tf_op jit(solution)/shard_map/ppermute | solution.py:27
  283.8 20.0 %collective-permute-start.15 = (bf16[256,768]{0,1:T(8,128)(2,1)S(1)}, bf16[256,768]{0,1:T(8,128)(2,1)S(1)}, u32[]{:S(2)}, u32[]{:S(2)}) collective-permute-start(bf16[256,768]{0,1:T(8,128)(2,1)S(1)} %maximum_select_fusion.1), channel_id=1, source_target_pairs={{0,3},{1,0},{2,1},{3,2},{4,7},{5,4},{6,5},{7,6},{8,11},{9,8},{10,9... | collective-permute-start | bytes 1179656 | tf_op jit(solution)/shard_map/ppermute | solution.py:27
  287.6 16.3 %copy-start.11 = (bf16[1536,640]{1,0:T(8,128)(2,1)S(1)}, bf16[1536,640]{1,0:T(8,128)(2,1)}, u32[]{:S(2)}) copy-start(bf16[1536,640]{1,0:T(8,128)(2,1)} %all-gather.3.cloned.1.call-done) | copy-start | bytes 5898244
  (23 other events, 73.9 us)
Sparse Core Ops, SparseCore 0:
  35.6 220.9 all-gather.2

commit v8 on v3

--- a/solution.py
+++ b/solution.py
@@ -221,18 +221,19 @@
                 carry_state, below[d], seq_index - 2 * d, query_heads, query_clip, context
             )
         sign = 1 - 2 * core
-        outgoing = [
-            (packed, 1),
-            (jnp.where(is_first, above[1], below[1]), -1),
-            (jnp.where(is_first, above[2], below[2]), -3),
-            (jnp.where(is_first, above[3], below[3]), -5),
-            (jnp.where(is_first, below[1], above[1]), 3),
-            (jnp.where(is_first, below[2], above[2]), 5),
-        ]
-        for block, offset in outgoing:
-            got = swap_cores(block)
+        got = swap_cores(packed)
+        carry_state = visit_block(
+            carry_state, got, seq_index + sign, query_heads, query_clip, context
+        )
+        selected = jnp.where(
+            is_first,
+            jnp.stack([above[1], above[2], above[3], below[1], below[2]]),
+            jnp.stack([below[1], below[2], below[3], above[1], above[2]]),
+        )
+        traded = swap_cores(selected)
+        for slot, offset in enumerate((-1, -3, -5, 3, 5)):
             carry_state = visit_block(
-                carry_state, got, seq_index + sign * offset, query_heads, query_clip, context
+                carry_state, traded[slot], seq_index + sign * offset, query_heads, query_clip, context
             )
         running_max, totals, accumulated = carry_state
         result = accumulated / totals[:, :, None]

time: 275 us -> 268 us (0.975)
  the two profiles are of different devices: /device:TPU:147 before, /device:TPU:19 now
where the time goes in v8:
time: 268 us; the launch traced here: 267 us
  starting transfers between devices  151 us (56%)
  waiting for transfers between devices  76.9 us (29%)
  matrix products  17.6 us (7%)
  local copies, waits for them, and re-layouts  10.3 us (4%)
  other arithmetic  9.55 us (4%)
    ppermute x4, starting transfers between devices, swap_cores(): return lax.ppermute(block, 'c', [(0, 1), (1, 0)])  92.9 us
    ppermute x12, waiting for transfers between devices, shifted(): return lax.ppermute(block, axes, route)  46.3 us
    ppermute x12, starting transfers between devices, shifted(): return lax.ppermute(block, axes, route)  38.2 us
    ppermute x4, waiting for transfers between devices, spread_weight(): received.append(lax.ppermute(row_block, ('y', 'c'), route))  23.6 us
    ppermute x4, starting transfers between devices, spread_weight(): received.append(lax.ppermute(row_block, ('y', 'c'), route))  12.3 us
    ppermute x1, starting transfers between devices, gather_attention(): partner = lax.ppermute(attention_local, 'zh', [(0, 1), (1, 0)])  7.68 us
    ppermute x1, waiting for transfers between devices, gather_attention(): partner = lax.ppermute(attention_local, 'zh', [(0, 1), (1, 0)])  6.97 us
    dot_general x13, matrix products, attend(): jnp.einsum('qhd,khd->hqk', query_heads, key_heads, preferred_element_type...  6.3 us
  transfers between devices with their start and end apart: 21, of which 10 were waited for; matrix products, arithmetic and copies ran while one was open for 8% of the time, Pallas kernels for 0%

profile of v8, /device:TPU:19, one launch (start us, length us, event | category | flops | bytes accessed | tf_op | source)
XLA Modules:
  0.0 267.2 jit_solution(1376874002201074891)
XLA Ops:
  0.0 2.8 %collective-permute-start = (bf16[48,640]{1,0:T(8,128)(2,1)}, bf16[48,640]{1,0:T(8,128)(2,1)S(1)}, u32[]{:S(2)}, u32[]{:S(2)}) collective-permute-start(bf16[48,640]{1,0:T(8,128)(2,1)} %param.18), channel_id=1, source_target_pairs={{0,8},{8,0},{1,9},{9,1},{2,10},{10,2},{3,11},{11,3},{4,12},{12,4},... | collective-permute-start | bytes 184328 | tf_op jit(solution)/shard_map/ppermute | solution.py:31
  11.1 4.0 %collective-permute-start.1 = (bf16[96,640]{1,0:T(8,128)(2,1)S(1)}, bf16[96,640]{1,0:T(8,128)(2,1)S(1)}, u32[]{:S(2)}, u32[]{:S(2)}) collective-permute-start(bf16[96,640]{1,0:T(8,128)(2,1)S(1)} %maximum_select_fusion.2), channel_id=1, source_target_pairs={{0,16},{16,32},{32,48},{48,0},{1,17},{17,33},{33,49},{49,1},{2,18}... | collective-permute-start | bytes 368648 | tf_op jit(solution)/shard_map/ppermute | solution.py:27
  15.5 5.8 %collective-permute-start.2 = (bf16[96,640]{1,0:T(8,128)(2,1)S(1)}, bf16[96,640]{1,0:T(8,128)(2,1)S(1)}, u32[]{:S(2)}, u32[]{:S(2)}) collective-permute-start(bf16[96,640]{1,0:T(8,128)(2,1)S(1)} %maximum_select_fusion.2), channel_id=1, source_target_pairs={{0,32},{16,48},{32,0},{48,16},{1,33},{17,49},{33,1},{49,17},{2,34}... | collective-permute-start | bytes 368648 | tf_op jit(solution)/shard_map/ppermute | solution.py:27
  21.3 2.2 collective-permute-start.3
  23.6 4.0 %collective-permute-done.2 = bf16[96,640]{1,0:T(8,128)(2,1)S(1)} collective-permute-done((bf16[96,640]{1,0:T(8,128)(2,1)S(1)}, bf16[96,640]{1,0:T(8,128)(2,1)S(1)}, u32[]{:S(2)}, u32[]{:S(2)}) %collective-permute-start.2) | collective-permute-done | bytes 122912 | tf_op jit(solution)/shard_map/ppermute | solution.py:27
  27.7 2.7 %collective-permute-done.3 = bf16[96,640]{1,0:T(8,128)(2,1)S(1)} collective-permute-done((bf16[96,640]{1,0:T(8,128)(2,1)S(1)}, bf16[96,640]{1,0:T(8,128)(2,1)S(1)}, u32[]{:S(2)}, u32[]{:S(2)}) %collective-permute-start.3) | collective-permute-done | bytes 122912 | tf_op jit(solution)/shard_map/ppermute | solution.py:27
  33.2 5.8 %collective-permute-start.18 = (bf16[384,640]{1,0:T(8,128)(2,1)S(1)}, bf16[384,640]{1,0:T(8,128)(2,1)S(1)}, u32[]{:S(2)}, u32[]{:S(2)}) collective-permute-start(bf16[384,640]{1,0:T(8,128)(2,1)S(1)} %bitcast.454), channel_id=1, source_target_pairs={{0,192},{64,256},{128,320},{192,384},{256,448},{320,0},{384,64},{4... | collective-permute-start | bytes 1474568 | tf_op jit(solution)/shard_map/ppermute | solution.py:124
  39.0 3.8 %collective-permute-start.17 = (bf16[384,640]{1,0:T(8,128)(2,1)S(1)}, bf16[384,640]{1,0:T(8,128)(2,1)S(1)}, u32[]{:S(2)}, u32[]{:S(2)}) collective-permute-start(bf16[384,640]{1,0:T(8,128)(2,1)S(1)} %bitcast.455), channel_id=1, source_target_pairs={{0,128},{64,192},{128,256},{192,320},{256,384},{320,448},{384,0},{... | collective-permute-start | bytes 1474568 | tf_op jit(solution)/shard_map/ppermute | solution.py:124
  46.1 3.8 %collective-permute-start.7 = (bf16[2,512,384]{1,2,0:T(8,128)(2,1)S(1)}, bf16[2,512,384]{1,2,0:T(8,128)(2,1)S(1)}, u32[]{:S(2)}, u32[]{:S(2)}) collective-permute-start(bf16[2,512,384]{1,2,0:T(8,128)(2,1)S(1)} %pad_maximum_fusion.1), channel_id=1, source_target_pairs={{0,32},{16,48},{32,64},{48,80},{64,96},{80,112},{96,128},{112,144}... | collective-permute-start | bytes 2359304 | tf_op jit(solution)/shard_map/ppermute | solution.py:27
  50.3 3.2 %collective-permute-start.9 = (bf16[2,512,384]{1,2,0:T(8,128)(2,1)S(1)}, bf16[2,512,384]{1,2,0:T(8,128)(2,1)S(1)}, u32[]{:S(2)}, u32[]{:S(2)}) collective-permute-start(bf16[2,512,384]{1,2,0:T(8,128)(2,1)S(1)} %pad_maximum_fusion.1), channel_id=1, source_target_pairs={{0,48},{16,64},{32,80},{48,96},{64,112},{80,128},{96,144},{112,160... | collective-permute-start | bytes 2359304 | tf_op jit(solution)/shard_map/ppermute | solution.py:27
  53.6 15.1 %collective-permute-done.18 = bf16[384,640]{1,0:T(8,128)(2,1)S(1)} collective-permute-done((bf16[384,640]{1,0:T(8,128)(2,1)S(1)}, bf16[384,640]{1,0:T(8,128)(2,1)S(1)}, u32[]{:S(2)}, u32[]{:S(2)}) %collective-permute-start.18) | collective-permute-done | bytes 491552 | tf_op jit(solution)/shard_map/ppermute | solution.py:124
  70.6 8.5 %collective-permute-done.17 = bf16[384,640]{1,0:T(8,128)(2,1)S(1)} collective-permute-done((bf16[384,640]{1,0:T(8,128)(2,1)S(1)}, bf16[384,640]{1,0:T(8,128)(2,1)S(1)}, u32[]{:S(2)}, u32[]{:S(2)}) %collective-permute-start.17) | collective-permute-done | bytes 491552 | tf_op jit(solution)/shard_map/ppermute | solution.py:124
  82.8 3.7 %collective-permute-start.8 = (bf16[2,512,384]{1,2,0:T(8,128)(2,1)S(1)}, bf16[2,512,384]{1,2,0:T(8,128)(2,1)S(1)}, u32[]{:S(2)}, u32[]{:S(2)}) collective-permute-start(bf16[2,512,384]{1,2,0:T(8,128)(2,1)S(1)} %pad_maximum_fusion.1), channel_id=1, source_target_pairs={{48,0},{64,16},{80,32},{96,48},{112,64},{128,80},{144,96},{160,112... | collective-permute-start | bytes 2359304 | tf_op jit(solution)/shard_map/ppermute | solution.py:27
  86.5 82.8 %collective-permute-start.10 = (bf16[2,512,384]{1,2,0:T(8,128)(2,1)S(1)}, bf16[2,512,384]{1,2,0:T(8,128)(2,1)}, u32[]{:S(2)}, u32[]{:S(2)}) collective-permute-start(bf16[2,512,384]{1,2,0:T(8,128)(2,1)S(1)} %pad_maximum_fusion.1), channel_id=1, source_target_pairs={{0,8},{8,0},{1,9},{9,1},{2,10},{10,2},{3,11},{11,3},{4,12},{12,4},... | collective-permute-start | bytes 2359304 | tf_op jit(solution)/shard_map/ppermute | solution.py:31
  171.5 23.4 %collective-permute-done.6 = bf16[2,512,384]{1,2,0:T(8,128)(2,1)S(1)} collective-permute-done((bf16[2,512,384]{1,2,0:T(8,128)(2,1)S(1)}, bf16[2,512,384]{1,2,0:T(8,128)(2,1)S(1)}, u32[]{:S(2)}, u32[]{:S(2)}) %collective-permute-start.6) | collective-permute-done | bytes 786464 | tf_op jit(solution)/shard_map/ppermute | solution.py:27
  195.7 5.3 %collective-permute-start.11 = (bf16[5,2,512,384]{2,3,1,0:T(8,128)(2,1)S(1)}, bf16[5,2,512,384]{2,3,1,0:T(8,128)(2,1)S(1)}, u32[]{:S(2)}, u32[]{:S(2)}) collective-permute-start(bf16[5,2,512,384]{2,3,1,0:T(8,128)(2,1)S(1)} %broadcast_select_fusion), channel_id=1, source_target_pairs={{0,8},{8,0},{1,9},{9,1},{2,10},{10,2},{3,11},{11,3},{4,12},{12,4},... | collective-permute-start | bytes 11796488 | tf_op jit(solution)/shard_map/ppermute | solution.py:31
  222.9 7.7 %collective-permute-start.12 = (bf16[256,384]{0,1:T(8,128)(2,1)S(1)}, bf16[256,384]{0,1:T(8,128)(2,1)S(1)}, u32[]{:S(2)}, u32[]{:S(2)}) collective-permute-start(bf16[256,384]{0,1:T(8,128)(2,1)S(1)} %bitcast.501), channel_id=1, source_target_pairs={{0,4},{4,0},{1,5},{5,1},{2,6},{6,2},{3,7},{7,3},{8,12},{12,8},{9,1... | collective-permute-start | bytes 589832 | tf_op jit(solution)/shard_map/ppermute | solution.py:145
  231.8 7.0 %collective-permute-done.12 = bf16[256,384]{0,1:T(8,128)(2,1)S(1)} collective-permute-done((bf16[256,384]{0,1:T(8,128)(2,1)S(1)}, bf16[256,384]{0,1:T(8,128)(2,1)S(1)}, u32[]{:S(2)}, u32[]{:S(2)}) %collective-permute-start.12) | collective-permute-done | bytes 196640 | tf_op jit(solution)/shard_map/ppermute | solution.py:145
  238.9 3.1 %collective-permute-start.13 = (bf16[256,768]{0,1:T(8,128)(2,1)S(1)}, bf16[256,768]{0,1:T(8,128)(2,1)S(1)}, u32[]{:S(2)}, u32[]{:S(2)}) collective-permute-start(bf16[256,768]{0,1:T(8,128)(2,1)S(1)} %maximum_select_fusion), channel_id=1, source_target_pairs={{0,1},{1,2},{2,3},{3,0},{4,5},{5,6},{6,7},{7,4},{8,9},{9,10},{10,1... | collective-permute-start | bytes 1179656 | tf_op jit(solution)/shard_map/ppermute | solution.py:27
  242.1 2.7 %collective-permute-start.14 = (bf16[256,768]{0,1:T(8,128)(2,1)S(1)}, bf16[256,768]{0,1:T(8,128)(2,1)S(1)}, u32[]{:S(2)}, u32[]{:S(2)}) collective-permute-start(bf16[256,768]{0,1:T(8,128)(2,1)S(1)} %maximum_select_fusion), channel_id=1, source_target_pairs={{0,2},{1,3},{2,0},{3,1},{4,6},{5,7},{6,4},{7,5},{8,10},{9,11},{10,... | collective-permute-start | bytes 1179656 | tf_op jit(solution)/shard_map/ppermute | solution.py:27
  244.8 3.8 %collective-permute-start.15 = (bf16[256,768]{0,1:T(8,128)(2,1)S(1)}, bf16[256,768]{0,1:T(8,128)(2,1)S(1)}, u32[]{:S(2)}, u32[]{:S(2)}) collective-permute-start(bf16[256,768]{0,1:T(8,128)(2,1)S(1)} %maximum_select_fusion), channel_id=1, source_target_pairs={{0,3},{1,0},{2,1},{3,2},{4,7},{5,4},{6,5},{7,6},{8,11},{9,8},{10,9... | collective-permute-start | bytes 1179656 | tf_op jit(solution)/shard_map/ppermute | solution.py:27
  250.9 4.3 %collective-permute-done.14 = bf16[256,768]{0,1:T(8,128)(2,1)S(1)} collective-permute-done((bf16[256,768]{0,1:T(8,128)(2,1)S(1)}, bf16[256,768]{0,1:T(8,128)(2,1)S(1)}, u32[]{:S(2)}, u32[]{:S(2)}) %collective-permute-start.14) | collective-permute-done | bytes 393248 | tf_op jit(solution)/shard_map/ppermute | solution.py:27
  255.3 9.7 %collective-permute-done.15 = bf16[256,768]{0,1:T(8,128)(2,1)S(1)} collective-permute-done((bf16[256,768]{0,1:T(8,128)(2,1)S(1)}, bf16[256,768]{0,1:T(8,128)(2,1)S(1)}, u32[]{:S(2)}, u32[]{:S(2)}) %collective-permute-start.15) | collective-permute-done | bytes 393248 | tf_op jit(solution)/shard_map/ppermute | solution.py:27
  265.0 2.2 fusion.27
  (207 shorter events, 48.1 us)
Async XLA Ops:
  0.0 10.7 %collective-permute-start = (bf16[48,640]{1,0:T(8,128)(2,1)}, bf16[48,640]{1,0:T(8,128)(2,1)S(1)}, u32[]{:S(2)}, u32[]{:S(2)}) collective-permute-start(bf16[48,640]{1,0:T(8,128)(2,1)} %param.18), channel_id=1, source_target_pairs={{0,8},{8,0},{1,9},{9,1},{2,10},{10,2},{3,11},{11,3},{4,12},{12,4},... | collective-permute-start | bytes 184328 | tf_op jit(solution)/shard_map/ppermute | solution.py:31
  11.1 12.5 %collective-permute-start.1 = (bf16[96,640]{1,0:T(8,128)(2,1)S(1)}, bf16[96,640]{1,0:T(8,128)(2,1)S(1)}, u32[]{:S(2)}, u32[]{:S(2)}) collective-permute-start(bf16[96,640]{1,0:T(8,128)(2,1)S(1)} %maximum_select_fusion.2), channel_id=1, source_target_pairs={{0,16},{16,32},{32,48},{48,0},{1,17},{17,33},{33,49},{49,1},{2,18}... | collective-permute-start | bytes 368648 | tf_op jit(solution)/shard_map/ppermute | solution.py:27
  15.5 12.2 %collective-permute-start.2 = (bf16[96,640]{1,0:T(8,128)(2,1)S(1)}, bf16[96,640]{1,0:T(8,128)(2,1)S(1)}, u32[]{:S(2)}, u32[]{:S(2)}) collective-permute-start(bf16[96,640]{1,0:T(8,128)(2,1)S(1)} %maximum_select_fusion.2), channel_id=1, source_target_pairs={{0,32},{16,48},{32,0},{48,16},{1,33},{17,49},{33,1},{49,17},{2,34}... | collective-permute-start | bytes 368648 | tf_op jit(solution)/shard_map/ppermute | solution.py:27
  21.3 9.1 %collective-permute-start.3 = (bf16[96,640]{1,0:T(8,128)(2,1)S(1)}, bf16[96,640]{1,0:T(8,128)(2,1)S(1)}, u32[]{:S(2)}, u32[]{:S(2)}) collective-permute-start(bf16[96,640]{1,0:T(8,128)(2,1)S(1)} %maximum_select_fusion.2), channel_id=1, source_target_pairs={{0,48},{16,0},{32,16},{48,32},{1,49},{17,1},{33,17},{49,33},{2,50}... | collective-permute-start | bytes 368648 | tf_op jit(solution)/shard_map/ppermute | solution.py:27
  30.4 15.7 %collective-permute-start.16 = (bf16[384,640]{1,0:T(8,128)(2,1)S(1)}, bf16[384,640]{1,0:T(8,128)(2,1)S(1)}, u32[]{:S(2)}, u32[]{:S(2)}) collective-permute-start(bf16[384,640]{1,0:T(8,128)(2,1)S(1)} %bitcast.452), channel_id=1, source_target_pairs={{0,64},{64,128},{128,192},{192,256},{256,320},{320,384},{384,448},... | collective-permute-start | bytes 1474568 | tf_op jit(solution)/shard_map/ppermute | solution.py:124
  32.5 17.8 %collective-permute-start.19 = (bf16[384,640]{1,0:T(8,128)(2,1)S(1)}, bf16[384,640]{1,0:T(8,128)(2,1)S(1)}, u32[]{:S(2)}, u32[]{:S(2)}) collective-permute-start(bf16[384,640]{1,0:T(8,128)(2,1)S(1)} %bitcast.453), channel_id=1, source_target_pairs={{0,256},{64,320},{128,384},{192,448},{256,0},{320,64},{384,128},{4... | collective-permute-start | bytes 1474568 | tf_op jit(solution)/shard_map/ppermute | solution.py:124
  33.2 35.5 %collective-permute-start.18 = (bf16[384,640]{1,0:T(8,128)(2,1)S(1)}, bf16[384,640]{1,0:T(8,128)(2,1)S(1)}, u32[]{:S(2)}, u32[]{:S(2)}) collective-permute-start(bf16[384,640]{1,0:T(8,128)(2,1)S(1)} %bitcast.454), channel_id=1, source_target_pairs={{0,192},{64,256},{128,320},{192,384},{256,448},{320,0},{384,64},{4... | collective-permute-start | bytes 1474568 | tf_op jit(solution)/shard_map/ppermute | solution.py:124
  39.0 40.1 %collective-permute-start.17 = (bf16[384,640]{1,0:T(8,128)(2,1)S(1)}, bf16[384,640]{1,0:T(8,128)(2,1)S(1)}, u32[]{:S(2)}, u32[]{:S(2)}) collective-permute-start(bf16[384,640]{1,0:T(8,128)(2,1)S(1)} %bitcast.455), channel_id=1, source_target_pairs={{0,128},{64,192},{128,256},{192,320},{256,384},{320,448},{384,0},{... | collective-permute-start | bytes 1474568 | tf_op jit(solution)/shard_map/ppermute | solution.py:124
  42.7 40.0 %collective-permute-start.5 = (bf16[2,512,384]{1,2,0:T(8,128)(2,1)S(1)}, bf16[2,512,384]{1,2,0:T(8,128)(2,1)S(1)}, u32[]{:S(2)}, u32[]{:S(2)}) collective-permute-start(bf16[2,512,384]{1,2,0:T(8,128)(2,1)S(1)} %pad_maximum_fusion.1), channel_id=1, source_target_pairs={{0,16},{16,32},{32,48},{48,64},{64,80},{80,96},{96,112},{112,128},... | collective-permute-start | bytes 2359304 | tf_op jit(solution)/shard_map/ppermute | solution.py:27
  46.1 40.3 %collective-permute-start.7 = (bf16[2,512,384]{1,2,0:T(8,128)(2,1)S(1)}, bf16[2,512,384]{1,2,0:T(8,128)(2,1)S(1)}, u32[]{:S(2)}, u32[]{:S(2)}) collective-permute-start(bf16[2,512,384]{1,2,0:T(8,128)(2,1)S(1)} %pad_maximum_fusion.1), channel_id=1, source_target_pairs={{0,32},{16,48},{32,64},{48,80},{64,96},{80,112},{96,128},{112,144}... | collective-permute-start | bytes 2359304 | tf_op jit(solution)/shard_map/ppermute | solution.py:27
  50.3 32.3 %copy-start.2 = (bf16[384,640]{1,0:T(8,128)(2,1)}, bf16[384,640]{1,0:T(8,128)(2,1)S(1)}, u32[]{:S(2)}) copy-start(bf16[384,640]{1,0:T(8,128)(2,1)S(1)} %collective-permute-done.19) | copy-start | bytes 1474564
  50.3 119.1 %collective-permute-start.9 = (bf16[2,512,384]{1,2,0:T(8,128)(2,1)S(1)}, bf16[2,512,384]{1,2,0:T(8,128)(2,1)S(1)}, u32[]{:S(2)}, u32[]{:S(2)}) collective-permute-start(bf16[2,512,384]{1,2,0:T(8,128)(2,1)S(1)} %pad_maximum_fusion.1), channel_id=1, source_target_pairs={{0,48},{16,64},{32,80},{48,96},{64,112},{80,128},{96,144},{112,160... | collective-permute-start | bytes 2359304 | tf_op jit(solution)/shard_map/ppermute | solution.py:27
  68.7 102.7 %collective-permute-start.4 = (bf16[2,512,384]{1,2,0:T(8,128)(2,1)S(1)}, bf16[2,512,384]{1,2,0:T(8,128)(2,1)S(1)}, u32[]{:S(2)}, u32[]{:S(2)}) collective-permute-start(bf16[2,512,384]{1,2,0:T(8,128)(2,1)S(1)} %pad_maximum_fusion.1), channel_id=1, source_target_pairs={{16,0},{32,16},{48,32},{64,48},{80,64},{96,80},{112,96},{128,112},... | collective-permute-start | bytes 2359304 | tf_op jit(solution)/shard_map/ppermute | solution.py:27
  79.1 115.8 %collective-permute-start.6 = (bf16[2,512,384]{1,2,0:T(8,128)(2,1)S(1)}, bf16[2,512,384]{1,2,0:T(8,128)(2,1)S(1)}, u32[]{:S(2)}, u32[]{:S(2)}) collective-permute-start(bf16[2,512,384]{1,2,0:T(8,128)(2,1)S(1)} %pad_maximum_fusion.1), channel_id=1, source_target_pairs={{32,0},{48,16},{64,32},{80,48},{96,64},{112,80},{128,96},{144,112}... | collective-permute-start | bytes 2359304 | tf_op jit(solution)/shard_map/ppermute | solution.py:27
  82.8 112.3 %collective-permute-start.8 = (bf16[2,512,384]{1,2,0:T(8,128)(2,1)S(1)}, bf16[2,512,384]{1,2,0:T(8,128)(2,1)S(1)}, u32[]{:S(2)}, u32[]{:S(2)}) collective-permute-start(bf16[2,512,384]{1,2,0:T(8,128)(2,1)S(1)} %pad_maximum_fusion.1), channel_id=1, source_target_pairs={{48,0},{64,16},{80,32},{96,48},{112,64},{128,80},{144,96},{160,112... | collective-permute-start | bytes 2359304 | tf_op jit(solution)/shard_map/ppermute | solution.py:27
  86.5 114.8 %collective-permute-start.10 = (bf16[2,512,384]{1,2,0:T(8,128)(2,1)S(1)}, bf16[2,512,384]{1,2,0:T(8,128)(2,1)}, u32[]{:S(2)}, u32[]{:S(2)}) collective-permute-start(bf16[2,512,384]{1,2,0:T(8,128)(2,1)S(1)} %pad_maximum_fusion.1), channel_id=1, source_target_pairs={{0,8},{8,0},{1,9},{9,1},{2,10},{10,2},{3,11},{11,3},{4,12},{12,4},... | collective-permute-start | bytes 2359304 | tf_op jit(solution)/shard_map/ppermute | solution.py:31
  169.4 36.5 %collective-permute-start.20 = (bf16[4,384,640]{2,1,0:T(8,128)(2,1)}, bf16[4,384,640]{2,1,0:T(8,128)(2,1)}, u32[]{:S(2)}, u32[]{:S(2)}) collective-permute-start(bf16[4,384,640]{2,1,0:T(8,128)(2,1)} %pad_maximum_fusion), channel_id=1, source_target_pairs={{0,8},{8,0},{1,9},{9,1},{2,10},{10,2},{3,11},{11,3},{4,12},{12,4},... | collective-permute-start | bytes 5898248 | tf_op jit(solution)/shard_map/ppermute | solution.py:31
  195.7 13.7 %collective-permute-start.11 = (bf16[5,2,512,384]{2,3,1,0:T(8,128)(2,1)S(1)}, bf16[5,2,512,384]{2,3,1,0:T(8,128)(2,1)S(1)}, u32[]{:S(2)}, u32[]{:S(2)}) collective-permute-start(bf16[5,2,512,384]{2,3,1,0:T(8,128)(2,1)S(1)} %broadcast_select_fusion), channel_id=1, source_target_pairs={{0,8},{8,0},{1,9},{9,1},{2,10},{10,2},{3,11},{11,3},{4,12},{12,4},... | collective-permute-start | bytes 11796488 | tf_op jit(solution)/shard_map/ppermute | solution.py:31
  222.9 15.9 %collective-permute-start.12 = (bf16[256,384]{0,1:T(8,128)(2,1)S(1)}, bf16[256,384]{0,1:T(8,128)(2,1)S(1)}, u32[]{:S(2)}, u32[]{:S(2)}) collective-permute-start(bf16[256,384]{0,1:T(8,128)(2,1)S(1)} %bitcast.501), channel_id=1, source_target_pairs={{0,4},{4,0},{1,5},{5,1},{2,6},{6,2},{3,7},{7,3},{8,12},{12,8},{9,1... | collective-permute-start | bytes 589832 | tf_op jit(solution)/shard_map/ppermute | solution.py:145
  238.9 11.9 %collective-permute-start.13 = (bf16[256,768]{0,1:T(8,128)(2,1)S(1)}, bf16[256,768]{0,1:T(8,128)(2,1)S(1)}, u32[]{:S(2)}, u32[]{:S(2)}) collective-permute-start(bf16[256,768]{0,1:T(8,128)(2,1)S(1)} %maximum_select_fusion), channel_id=1, source_target_pairs={{0,1},{1,2},{2,3},{3,0},{4,5},{5,6},{6,7},{7,4},{8,9},{9,10},{10,1... | collective-permute-start | bytes 1179656 | tf_op jit(solution)/shard_map/ppermute | solution.py:27
  242.1 13.2 %collective-permute-start.14 = (bf16[256,768]{0,1:T(8,128)(2,1)S(1)}, bf16[256,768]{0,1:T(8,128)(2,1)S(1)}, u32[]{:S(2)}, u32[]{:S(2)}) collective-permute-start(bf16[256,768]{0,1:T(8,128)(2,1)S(1)} %maximum_select_fusion), channel_id=1, source_target_pairs={{0,2},{1,3},{2,0},{3,1},{4,6},{5,7},{6,4},{7,5},{8,10},{9,11},{10,... | collective-permute-start | bytes 1179656 | tf_op jit(solution)/shard_map/ppermute | solution.py:27
  244.8 20.1 %collective-permute-start.15 = (bf16[256,768]{0,1:T(8,128)(2,1)S(1)}, bf16[256,768]{0,1:T(8,128)(2,1)S(1)}, u32[]{:S(2)}, u32[]{:S(2)}) collective-permute-start(bf16[256,768]{0,1:T(8,128)(2,1)S(1)} %maximum_select_fusion), channel_id=1, source_target_pairs={{0,3},{1,0},{2,1},{3,2},{4,7},{5,4},{6,5},{7,6},{8,11},{9,8},{10,9... | collective-permute-start | bytes 1179656 | tf_op jit(solution)/shard_map/ppermute | solution.py:27
  248.7 16.3 %copy-start.4 = (f32[256,640]{1,0:T(8,128)S(1)}, f32[256,640]{1,0:T(8,128)}, u32[]{:S(2)}) copy-start(f32[256,640]{1,0:T(8,128)} %fusion.142) | copy-start | bytes 1966084
  248.7 16.3 %copy-start.13 = (bf16[256,640]{1,0:T(8,128)(2,1)S(1)}, bf16[256,640]{1,0:T(8,128)(2,1)}, u32[]{:S(2)}) copy-start(bf16[256,640]{1,0:T(8,128)(2,1)} %param.17) | copy-start | bytes 983044
  (12 other events, 35.3 us)

commit v9 on v8

--- a/solution.py
+++ b/solution.py
@@ -88,6 +88,17 @@
     key_heads = packed[0].reshape(-1, head_count, HD)
     value_heads = packed[1].reshape(-1, head_count, HD)
     return attend(carry_state, query_heads, key_heads, value_heads, allowed)
+
+
+def gather_row_weight(out_weight, sizes):
+    n_zl = sizes["zl"]
+    zl = lax.axis_index("zl")
+    row_part = jnp.zeros((n_zl,) + out_weight.shape, out_weight.dtype)
+    row_part = lax.dynamic_update_index_in_dim(row_part, out_weight, zl, 0)
+    for d in range(1, n_zl):
+        got = shifted(out_weight, "zl", n_zl, d, wrap=True)
+        row_part = lax.dynamic_update_index_in_dim(row_part, got, (zl - d) % n_zl, 0)
+    return row_part
 
 
 def gather_weight(out_weight, sizes, is_first):
@@ -202,9 +213,13 @@
                 jnp.concatenate([value_tiles, cache_values.reshape(-1, tile_width)], axis=0),
             ]
         )
-        row_block = gather_weight(out_weight, sizes, is_first)
-        packed, row_block = lax.optimization_barrier((packed, row_block))
-        weight_full = spread_weight(row_block, sizes, is_first)
+        row_part = gather_row_weight(out_weight, sizes)
+        packed, row_part = lax.optimization_barrier((packed, row_part))
+        column = lax.all_gather(row_part, "y", axis=0)
+        other = swap_cores(column)
+        weight_full = jnp.where(
+            is_first, jnp.stack([column, other], axis=2), jnp.stack([other, column], axis=2)
+        ).reshape(-1, out_weight.shape[1])
 
         carry_state = visit_block(
             empty_state(head_count, row_count), packed, seq_index, query_heads, query_clip, context

time: 268 us -> 278 us (1.037)
  the two profiles are of different devices: /device:TPU:19 before, /device:TPU:211 now
where the time goes in v9:
time: 278 us; the launch traced here: 277 us
  waiting for transfers between devices  136 us (49%)
  starting transfers between devices  59.1 us (21%)
  other arithmetic  25.3 us (9%)
  local copies, waits for them, and re-layouts  24.5 us (9%)
  matrix products  17.2 us (6%)
  between operations  14.6 us (5%)
    ppermute x12, waiting for transfers between devices, shifted(): return lax.ppermute(block, axes, route)  129 us
    ppermute x12, starting transfers between devices, shifted(): return lax.ppermute(block, axes, route)  44.3 us
    concatenate x13, other arithmetic, allowed_keys(): return jnp.concatenate([same_clip, page_ok], axis=1)  11.2 us
    ppermute x3, starting transfers between devices, swap_cores(): return lax.ppermute(block, 'c', [(0, 1), (1, 0)])  8.84 us
    unnamed x57, local copies, waits for them, and re-layouts  7.92 us
    ppermute x1, waiting for transfers between devices, gather_attention(): partner = lax.ppermute(attention_local, 'zh', [(0, 1), (1, 0)])  6.87 us
    dot_general x13, matrix products, attend(): jnp.einsum('qhd,khd->hqk', query_heads, key_heads, preferred_element_type...  6.26 us
    dot_general x13, matrix products, attend(): jnp.einsum('hqk,khd->hqd', weights.astype(jnp.bfloat16), value_heads, pre...  6.05 us
  transfers between devices with their start and end apart: 17, of which 6 were waited for; matrix products, arithmetic and copies ran while one was open for 22% of the time, Pallas kernels for 0%

profile of v9, /device:TPU:211, one launch (start us, length us, event | category | flops | bytes accessed | tf_op | source)
XLA Modules:
  0.0 276.7 jit_solution(3824215337337404278)
XLA Ops:
  6.6 2.2 collective-permute-start
  8.8 2.5 collective-permute-start.1
  11.2 2.8 %collective-permute-start.2 = (bf16[48,640]{1,0:T(8,128)(2,1)}, bf16[48,640]{1,0:T(8,128)(2,1)}, u32[]{:S(2)}, u32[]{:S(2)}) collective-permute-start(bf16[48,640]{1,0:T(8,128)(2,1)} %param.18), channel_id=1, source_target_pairs={{0,48},{16,0},{32,16},{48,32},{1,49},{17,1},{33,17},{49,33},{2,50}... | collective-permute-start | bytes 184328 | tf_op jit(solution)/shard_map/ppermute | solution.py:27
  32.7 1.5 pad_add_fusion.7
  39.1 2.2 fusion.107
  46.4 5.3 %collective-permute-start.4 = (bf16[2,512,384]{1,2,0:T(8,128)(2,1)S(1)}, bf16[2,512,384]{1,2,0:T(8,128)(2,1)S(1)}, u32[]{:S(2)}, u32[]{:S(2)}) collective-permute-start(bf16[2,512,384]{1,2,0:T(8,128)(2,1)S(1)} %pad_maximum_fusion), channel_id=1, source_target_pairs={{0,16},{16,32},{32,48},{48,64},{64,80},{80,96},{96,112},{112,128},... | collective-permute-start | bytes 2359304 | tf_op jit(solution)/shard_map/ppermute | solution.py:27
  52.3 1.9 collective-permute-start.6
  58.0 5.6 %collective-permute-start.8 = (bf16[2,512,384]{1,2,0:T(8,128)(2,1)S(1)}, bf16[2,512,384]{1,2,0:T(8,128)(2,1)S(1)}, u32[]{:S(2)}, u32[]{:S(2)}) collective-permute-start(bf16[2,512,384]{1,2,0:T(8,128)(2,1)S(1)} %pad_maximum_fusion), channel_id=1, source_target_pairs={{0,48},{16,64},{32,80},{48,96},{64,112},{80,128},{96,144},{112,160... | collective-permute-start | bytes 2359304 | tf_op jit(solution)/shard_map/ppermute | solution.py:27
  65.3 3.1 %collective-permute-start.3 = (bf16[2,512,384]{1,2,0:T(8,128)(2,1)S(1)}, bf16[2,512,384]{1,2,0:T(8,128)(2,1)}, u32[]{:S(2)}, u32[]{:S(2)}) collective-permute-start(bf16[2,512,384]{1,2,0:T(8,128)(2,1)S(1)} %pad_maximum_fusion), channel_id=1, source_target_pairs={{16,0},{32,16},{48,32},{64,48},{80,64},{96,80},{112,96},{128,112},... | collective-permute-start | bytes 2359304 | tf_op jit(solution)/shard_map/ppermute | solution.py:27
  68.4 1.9 collective-permute-start.5
  70.4 10.5 %collective-permute-done.4 = bf16[2,512,384]{1,2,0:T(8,128)(2,1)S(1)} collective-permute-done((bf16[2,512,384]{1,2,0:T(8,128)(2,1)S(1)}, bf16[2,512,384]{1,2,0:T(8,128)(2,1)S(1)}, u32[]{:S(2)}, u32[]{:S(2)}) %collective-permute-start.4) | collective-permute-done | bytes 786464 | tf_op jit(solution)/shard_map/ppermute | solution.py:27
  81.0 9.4 %collective-permute-start.7 = (bf16[2,512,384]{1,2,0:T(8,128)(2,1)S(1)}, bf16[2,512,384]{1,2,0:T(8,128)(2,1)S(1)}, u32[]{:S(2)}, u32[]{:S(2)}) collective-permute-start(bf16[2,512,384]{1,2,0:T(8,128)(2,1)S(1)} %pad_maximum_fusion), channel_id=1, source_target_pairs={{48,0},{64,16},{80,32},{96,48},{112,64},{128,80},{144,96},{160,112... | collective-permute-start | bytes 2359304 | tf_op jit(solution)/shard_map/ppermute | solution.py:27
  90.5 102.5 %collective-permute-done.6 = bf16[2,512,384]{1,2,0:T(8,128)(2,1)S(1)} collective-permute-done((bf16[2,512,384]{1,2,0:T(8,128)(2,1)S(1)}, bf16[2,512,384]{1,2,0:T(8,128)(2,1)S(1)}, u32[]{:S(2)}, u32[]{:S(2)}) %collective-permute-start.6) | collective-permute-done | bytes 786464 | tf_op jit(solution)/shard_map/ppermute | solution.py:27
  192.9 4.1 %collective-permute-start.9 = (bf16[2,512,384]{1,2,0:T(8,128)(2,1)S(1)}, bf16[2,512,384]{1,2,0:T(8,128)(2,1)S(1)}, u32[]{:S(2)}, u32[]{:S(2)}) collective-permute-start(bf16[2,512,384]{1,2,0:T(8,128)(2,1)S(1)} %pad_maximum_fusion), channel_id=1, source_target_pairs={{0,8},{8,0},{1,9},{9,1},{2,10},{10,2},{3,11},{11,3},{4,12},{12,4},... | collective-permute-start | bytes 2359304 | tf_op jit(solution)/shard_map/ppermute | solution.py:31
  200.3 2.1 collective-permute-start.10
  224.5 5.9 %collective-permute-start.11 = (bf16[256,384]{0,1:T(8,128)(2,1)S(1)}, bf16[256,384]{0,1:T(8,128)(2,1)S(1)}, u32[]{:S(2)}, u32[]{:S(2)}) collective-permute-start(bf16[256,384]{0,1:T(8,128)(2,1)S(1)} %bitcast.474), channel_id=1, source_target_pairs={{0,4},{4,0},{1,5},{5,1},{2,6},{6,2},{3,7},{7,3},{8,12},{12,8},{9,1... | collective-permute-start | bytes 589832 | tf_op jit(solution)/shard_map/ppermute | solution.py:156
  230.9 2.7 collective-permute-start.15
  233.6 6.9 %collective-permute-done.11 = bf16[256,384]{0,1:T(8,128)(2,1)S(1)} collective-permute-done((bf16[256,384]{0,1:T(8,128)(2,1)S(1)}, bf16[256,384]{0,1:T(8,128)(2,1)S(1)}, u32[]{:S(2)}, u32[]{:S(2)}) %collective-permute-start.11) | collective-permute-done | bytes 196640 | tf_op jit(solution)/shard_map/ppermute | solution.py:156
  240.6 3.1 %collective-permute-start.12 = (bf16[256,768]{0,1:T(8,128)(2,1)S(1)}, bf16[256,768]{0,1:T(8,128)(2,1)S(1)}, u32[]{:S(2)}, u32[]{:S(2)}) collective-permute-start(bf16[256,768]{0,1:T(8,128)(2,1)S(1)} %maximum_select_fusion.1), channel_id=1, source_target_pairs={{0,1},{1,2},{2,3},{3,0},{4,5},{5,6},{6,7},{7,4},{8,9},{9,10},{10,1... | collective-permute-start | bytes 1179656 | tf_op jit(solution)/shard_map/ppermute | solution.py:27
  243.8 2.8 collective-permute-start.13
  246.5 3.7 %collective-permute-start.14 = (bf16[256,768]{0,1:T(8,128)(2,1)S(1)}, bf16[256,768]{0,1:T(8,128)(2,1)S(1)}, u32[]{:S(2)}, u32[]{:S(2)}) collective-permute-start(bf16[256,768]{0,1:T(8,128)(2,1)S(1)} %maximum_select_fusion.1), channel_id=1, source_target_pairs={{0,3},{1,0},{2,1},{3,2},{4,7},{5,4},{6,5},{7,6},{8,11},{9,8},{10,9... | collective-permute-start | bytes 1179656 | tf_op jit(solution)/shard_map/ppermute | solution.py:27
  251.8 4.4 %collective-permute-done.13 = bf16[256,768]{0,1:T(8,128)(2,1)S(1)} collective-permute-done((bf16[256,768]{0,1:T(8,128)(2,1)S(1)}, bf16[256,768]{0,1:T(8,128)(2,1)S(1)}, u32[]{:S(2)}, u32[]{:S(2)}) %collective-permute-start.13) | collective-permute-done | bytes 393248 | tf_op jit(solution)/shard_map/ppermute | solution.py:27
  256.2 10.4 %collective-permute-done.14 = bf16[256,768]{0,1:T(8,128)(2,1)S(1)} collective-permute-done((bf16[256,768]{0,1:T(8,128)(2,1)S(1)}, bf16[256,768]{0,1:T(8,128)(2,1)S(1)}, u32[]{:S(2)}, u32[]{:S(2)}) %collective-permute-start.14) | collective-permute-done | bytes 393248 | tf_op jit(solution)/shard_map/ppermute | solution.py:27
  267.7 2.1 fusion.27
  (208 shorter events, 62.5 us)
Async XLA Ops:
  6.5 32.5 %copy-start = (f32[1000,640]{1,0:T(8,128)S(1)}, f32[1000,640]{1,0:T(8,128)}, u32[]{:S(2)}) copy-start(f32[1000,640]{1,0:T(8,128)} %param.19) | copy-start | bytes 7680004
  6.5 13.8 %copy-start.19 = (bf16[48,640]{1,0:T(8,128)(2,1)S(1)}, bf16[48,640]{1,0:T(8,128)(2,1)}, u32[]{:S(2)}) copy-start(bf16[48,640]{1,0:T(8,128)(2,1)} %param.18) | copy-start | bytes 184324
  6.5 12.0 %copy-start.23 = (s32[16]{0:T(128)S(1)}, s32[16]{0:T(128)}, u32[]{:S(2)}) copy-start(s32[16]{0:T(128)} %param.22) | copy-start | bytes 196
  6.5 12.0 %copy-start.21 = (s32[16]{0:T(128)S(1)}, s32[16]{0:T(128)}, u32[]{:S(2)}) copy-start(s32[16]{0:T(128)} %param.20) | copy-start | bytes 196
  6.5 224.4 %all-gather.3.cloned.1.call-start = ((), (), s32[]{:S(2)}) async-start(), calls=%async_computation | async-start | bytes 2211840 | tf_op jit(solution)/shard_map/all_gather | solution.py:218
  6.6 35.4 %collective-permute-start = (bf16[48,640]{1,0:T(8,128)(2,1)}, bf16[48,640]{1,0:T(8,128)(2,1)}, u32[]{:S(2)}, u32[]{:S(2)}) collective-permute-start(bf16[48,640]{1,0:T(8,128)(2,1)} %param.18), channel_id=1, source_target_pairs={{0,16},{16,32},{32,48},{48,0},{1,17},{17,33},{33,49},{49,1},{2,18}... | collective-permute-start | bytes 184328 | tf_op jit(solution)/shard_map/ppermute | solution.py:27
  8.8 34.7 %collective-permute-start.1 = (bf16[48,640]{1,0:T(8,128)(2,1)}, bf16[48,640]{1,0:T(8,128)(2,1)}, u32[]{:S(2)}, u32[]{:S(2)}) collective-permute-start(bf16[48,640]{1,0:T(8,128)(2,1)} %param.18), channel_id=1, source_target_pairs={{0,32},{16,48},{32,0},{48,16},{1,33},{17,49},{33,1},{49,17},{2,34}... | collective-permute-start | bytes 184328 | tf_op jit(solution)/shard_map/ppermute | solution.py:27
  11.2 33.7 %collective-permute-start.2 = (bf16[48,640]{1,0:T(8,128)(2,1)}, bf16[48,640]{1,0:T(8,128)(2,1)}, u32[]{:S(2)}, u32[]{:S(2)}) collective-permute-start(bf16[48,640]{1,0:T(8,128)(2,1)} %param.18), channel_id=1, source_target_pairs={{0,48},{16,0},{32,16},{48,32},{1,49},{17,1},{33,17},{49,33},{2,50}... | collective-permute-start | bytes 184328 | tf_op jit(solution)/shard_map/ppermute | solution.py:27
  27.9 9.1 %copy-start.17 = (pred[256,256]{0,1:T(8,128)(4,1)S(1)}, pred[256,256]{0,1:T(8,128)(4,1)}, u32[]{:S(2)}) copy-start(pred[256,256]{0,1:T(8,128)(4,1)} %get-tuple-element.112) | copy-start | bytes 196612
  27.9 10.5 %copy-start.16 = (pred[256,256]{0,1:T(8,128)(4,1)S(1)}, pred[256,256]{0,1:T(8,128)(4,1)}, u32[]{:S(2)}) copy-start(pred[256,256]{0,1:T(8,128)(4,1)} %get-tuple-element.111) | copy-start | bytes 196612
  46.4 34.6 %collective-permute-start.4 = (bf16[2,512,384]{1,2,0:T(8,128)(2,1)S(1)}, bf16[2,512,384]{1,2,0:T(8,128)(2,1)S(1)}, u32[]{:S(2)}, u32[]{:S(2)}) collective-permute-start(bf16[2,512,384]{1,2,0:T(8,128)(2,1)S(1)} %pad_maximum_fusion), channel_id=1, source_target_pairs={{0,16},{16,32},{32,48},{48,64},{64,80},{80,96},{96,112},{112,128},... | collective-permute-start | bytes 2359304 | tf_op jit(solution)/shard_map/ppermute | solution.py:27
  52.3 140.6 %collective-permute-start.6 = (bf16[2,512,384]{1,2,0:T(8,128)(2,1)S(1)}, bf16[2,512,384]{1,2,0:T(8,128)(2,1)S(1)}, u32[]{:S(2)}, u32[]{:S(2)}) collective-permute-start(bf16[2,512,384]{1,2,0:T(8,128)(2,1)S(1)} %pad_maximum_fusion), channel_id=1, source_target_pairs={{0,32},{16,48},{32,64},{48,80},{64,96},{80,112},{96,128},{112,144}... | collective-permute-start | bytes 2359304 | tf_op jit(solution)/shard_map/ppermute | solution.py:27
  58.0 139.1 %collective-permute-start.8 = (bf16[2,512,384]{1,2,0:T(8,128)(2,1)S(1)}, bf16[2,512,384]{1,2,0:T(8,128)(2,1)S(1)}, u32[]{:S(2)}, u32[]{:S(2)}) collective-permute-start(bf16[2,512,384]{1,2,0:T(8,128)(2,1)S(1)} %pad_maximum_fusion), channel_id=1, source_target_pairs={{0,48},{16,64},{32,80},{48,96},{64,112},{80,128},{96,144},{112,160... | collective-permute-start | bytes 2359304 | tf_op jit(solution)/shard_map/ppermute | solution.py:27
  65.3 131.8 %collective-permute-start.3 = (bf16[2,512,384]{1,2,0:T(8,128)(2,1)S(1)}, bf16[2,512,384]{1,2,0:T(8,128)(2,1)}, u32[]{:S(2)}, u32[]{:S(2)}) collective-permute-start(bf16[2,512,384]{1,2,0:T(8,128)(2,1)S(1)} %pad_maximum_fusion), channel_id=1, source_target_pairs={{16,0},{32,16},{48,32},{64,48},{80,64},{96,80},{112,96},{128,112},... | collective-permute-start | bytes 2359304 | tf_op jit(solution)/shard_map/ppermute | solution.py:27
  68.4 130.0 %collective-permute-start.5 = (bf16[2,512,384]{1,2,0:T(8,128)(2,1)S(1)}, bf16[2,512,384]{1,2,0:T(8,128)(2,1)}, u32[]{:S(2)}, u32[]{:S(2)}) collective-permute-start(bf16[2,512,384]{1,2,0:T(8,128)(2,1)S(1)} %pad_maximum_fusion), channel_id=1, source_target_pairs={{32,0},{48,16},{64,32},{80,48},{96,64},{112,80},{128,96},{144,112}... | collective-permute-start | bytes 2359304 | tf_op jit(solution)/shard_map/ppermute | solution.py:27
  81.0 118.7 %collective-permute-start.7 = (bf16[2,512,384]{1,2,0:T(8,128)(2,1)S(1)}, bf16[2,512,384]{1,2,0:T(8,128)(2,1)S(1)}, u32[]{:S(2)}, u32[]{:S(2)}) collective-permute-start(bf16[2,512,384]{1,2,0:T(8,128)(2,1)S(1)} %pad_maximum_fusion), channel_id=1, source_target_pairs={{48,0},{64,16},{80,32},{96,48},{112,64},{128,80},{144,96},{160,112... | collective-permute-start | bytes 2359304 | tf_op jit(solution)/shard_map/ppermute | solution.py:27
  192.9 12.6 %collective-permute-start.9 = (bf16[2,512,384]{1,2,0:T(8,128)(2,1)S(1)}, bf16[2,512,384]{1,2,0:T(8,128)(2,1)S(1)}, u32[]{:S(2)}, u32[]{:S(2)}) collective-permute-start(bf16[2,512,384]{1,2,0:T(8,128)(2,1)S(1)} %pad_maximum_fusion), channel_id=1, source_target_pairs={{0,8},{8,0},{1,9},{9,1},{2,10},{10,2},{3,11},{11,3},{4,12},{12,4},... | collective-permute-start | bytes 2359304 | tf_op jit(solution)/shard_map/ppermute | solution.py:31
  200.3 10.0 %collective-permute-start.10 = (bf16[5,2,512,384]{2,3,1,0:T(8,128)(2,1)S(1)}, bf16[5,2,512,384]{2,3,1,0:T(8,128)(2,1)S(1)}, u32[]{:S(2)}, u32[]{:S(2)}) collective-permute-start(bf16[5,2,512,384]{2,3,1,0:T(8,128)(2,1)S(1)} %broadcast_select_fusion), channel_id=1, source_target_pairs={{0,8},{8,0},{1,9},{9,1},{2,10},{10,2},{3,11},{11,3},{4,12},{12,4},... | collective-permute-start | bytes 11796488 | tf_op jit(solution)/shard_map/ppermute | solution.py:31
  224.5 16.0 %collective-permute-start.11 = (bf16[256,384]{0,1:T(8,128)(2,1)S(1)}, bf16[256,384]{0,1:T(8,128)(2,1)S(1)}, u32[]{:S(2)}, u32[]{:S(2)}) collective-permute-start(bf16[256,384]{0,1:T(8,128)(2,1)S(1)} %bitcast.474), channel_id=1, source_target_pairs={{0,4},{4,0},{1,5},{5,1},{2,6},{6,2},{3,7},{7,3},{8,12},{12,8},{9,1... | collective-permute-start | bytes 589832 | tf_op jit(solution)/shard_map/ppermute | solution.py:156
  230.9 35.8 %collective-permute-start.15 = (bf16[8,4,48,640]{3,2,1,0:T(8,128)(2,1)}, bf16[8,4,48,640]{3,2,1,0:T(8,128)(2,1)S(1)}, u32[]{:S(2)}, u32[]{:S(2)}) collective-permute-start(bf16[8,4,48,640]{3,2,1,0:T(8,128)(2,1)} %bitcast.430), channel_id=1, source_target_pairs={{0,8},{8,0},{1,9},{9,1},{2,10},{10,2},{3,11},{11,3},{4,12},{12,4},... | collective-permute-start | bytes 5898248 | tf_op jit(solution)/shard_map/ppermute | solution.py:31
  240.6 11.1 %collective-permute-start.12 = (bf16[256,768]{0,1:T(8,128)(2,1)S(1)}, bf16[256,768]{0,1:T(8,128)(2,1)S(1)}, u32[]{:S(2)}, u32[]{:S(2)}) collective-permute-start(bf16[256,768]{0,1:T(8,128)(2,1)S(1)} %maximum_select_fusion.1), channel_id=1, source_target_pairs={{0,1},{1,2},{2,3},{3,0},{4,5},{5,6},{6,7},{7,4},{8,9},{9,10},{10,1... | collective-permute-start | bytes 1179656 | tf_op jit(solution)/shard_map/ppermute | solution.py:27
  243.8 12.4 %collective-permute-start.13 = (bf16[256,768]{0,1:T(8,128)(2,1)S(1)}, bf16[256,768]{0,1:T(8,128)(2,1)S(1)}, u32[]{:S(2)}, u32[]{:S(2)}) collective-permute-start(bf16[256,768]{0,1:T(8,128)(2,1)S(1)} %maximum_select_fusion.1), channel_id=1, source_target_pairs={{0,2},{1,3},{2,0},{3,1},{4,6},{5,7},{6,4},{7,5},{8,10},{9,11},{10,... | collective-permute-start | bytes 1179656 | tf_op jit(solution)/shard_map/ppermute | solution.py:27
  246.5 20.1 %collective-permute-start.14 = (bf16[256,768]{0,1:T(8,128)(2,1)S(1)}, bf16[256,768]{0,1:T(8,128)(2,1)S(1)}, u32[]{:S(2)}, u32[]{:S(2)}) collective-permute-start(bf16[256,768]{0,1:T(8,128)(2,1)S(1)} %maximum_select_fusion.1), channel_id=1, source_target_pairs={{0,3},{1,0},{2,1},{3,2},{4,7},{5,4},{6,5},{7,6},{8,11},{9,8},{10,9... | collective-permute-start | bytes 1179656 | tf_op jit(solution)/shard_map/ppermute | solution.py:27
  250.4 16.3 %copy-start.12 = (bf16[32,48,640]{2,1,0:T(8,128)(2,1)S(1)}, bf16[32,48,640]{2,1,0:T(8,128)(2,1)}, u32[]{:S(2)}) copy-start(bf16[32,48,640]{2,1,0:T(8,128)(2,1)} %all-gather.3.cloned.1.call-done) | copy-start | bytes 5898244
  (17 other events, 27.7 us)
Sparse Core Ops, SparseCore 0:
  70.5 59.6 all-gather.2

commit v10 on v8

--- a/solution.py
+++ b/solution.py
@@ -204,7 +204,6 @@
         )
         row_block = gather_weight(out_weight, sizes, is_first)
         packed, row_block = lax.optimization_barrier((packed, row_block))
-        weight_full = spread_weight(row_block, sizes, is_first)
 
         carry_state = visit_block(
             empty_state(head_count, row_count), packed, seq_index, query_heads, query_clip, context
@@ -221,6 +220,13 @@
                 carry_state, below[d], seq_index - 2 * d, query_heads, query_clip, context
             )
         sign = 1 - 2 * core
+        gated = lax.optimization_barrier(
+            (row_block, above[1], above[2], above[3], below[1], below[2], below[3])
+        )
+        row_block = gated[0]
+        above = dict(zip((1, 2, 3), gated[1:4]))
+        below = dict(zip((1, 2, 3), gated[4:7]))
+        weight_full = spread_weight(row_block, sizes, is_first)
         got = swap_cores(packed)
         carry_state = visit_block(
             carry_state, got, seq_index + sign, query_heads, query_clip, context

time: 268 us -> 317 us (1.18)
  the two profiles are of different devices: /device:TPU:19 before, /device:TPU:43 now
where the time goes in v10:
time: 317 us; the launch traced here: 316 us
  waiting for transfers between devices  157 us (50%)
  starting transfers between devices  91.4 us (29%)
  other arithmetic  28.4 us (9%)
  local copies, waits for them, and re-layouts  21.3 us (7%)
  matrix products  16.5 us (5%)
    ppermute x12, waiting for transfers between devices, shifted(): return lax.ppermute(block, axes, route)  131 us
    ppermute x12, starting transfers between devices, shifted(): return lax.ppermute(block, axes, route)  47.2 us
    ppermute x4, starting transfers between devices, swap_cores(): return lax.ppermute(block, 'c', [(0, 1), (1, 0)])  23.1 us
    ppermute x4, waiting for transfers between devices, spread_weight(): received.append(lax.ppermute(row_block, ('y', 'c'), route))  17.4 us
    ppermute x4, starting transfers between devices, spread_weight(): received.append(lax.ppermute(row_block, ('y', 'c'), route))  13.1 us
    unnamed x51, local copies, waits for them, and re-layouts  10.1 us
    concatenate x13, other arithmetic, allowed_keys(): return jnp.concatenate([same_clip, page_ok], axis=1)  8.75 us
    ppermute x1, waiting for transfers between devices, gather_attention(): partner = lax.ppermute(attention_local, 'zh', [(0, 1), (1, 0)])  8.13 us
  transfers between devices with their start and end apart: 21, of which 10 were waited for; matrix products, arithmetic and copies ran while one was open for 14% of the time, Pallas kernels for 0%

profile of v10, /device:TPU:43, one launch (start us, length us, event | category | flops | bytes accessed | tf_op | source)
XLA Modules:
  0.0 315.8 jit_solution(11885340196008046274)
XLA Ops:
  0.0 2.8 collective-permute-start
  27.7 4.0 %collective-permute-start.1 = (bf16[96,640]{1,0:T(8,128)(2,1)}, bf16[96,640]{1,0:T(8,128)(2,1)}, u32[]{:S(2)}, u32[]{:S(2)}) collective-permute-start(bf16[96,640]{1,0:T(8,128)(2,1)} %maximum_select_fusion.2), channel_id=1, source_target_pairs={{0,16},{16,32},{32,48},{48,0},{1,17},{17,33},{33,49},{49,1},{2,18}... | collective-permute-start | bytes 368648 | tf_op jit(solution)/shard_map/ppermute | solution.py:27
  32.4 5.9 %collective-permute-start.2 = (bf16[96,640]{1,0:T(8,128)(2,1)}, bf16[96,640]{1,0:T(8,128)(2,1)S(1)}, u32[]{:S(2)}, u32[]{:S(2)}) collective-permute-start(bf16[96,640]{1,0:T(8,128)(2,1)} %maximum_select_fusion.2), channel_id=1, source_target_pairs={{0,32},{16,48},{32,0},{48,16},{1,33},{17,49},{33,1},{49,17},{2,34}... | collective-permute-start | bytes 368648 | tf_op jit(solution)/shard_map/ppermute | solution.py:27
  42.5 2.3 collective-permute-done.2
  44.8 2.8 collective-permute-done.3
  48.4 4.5 %collective-permute-start.4 = (bf16[2,512,384]{1,2,0:T(8,128)(2,1)S(1)}, bf16[2,512,384]{1,2,0:T(8,128)(2,1)}, u32[]{:S(2)}, u32[]{:S(2)}) collective-permute-start(bf16[2,512,384]{1,2,0:T(8,128)(2,1)S(1)} %pad_maximum_fusion.1), channel_id=1, source_target_pairs={{16,0},{32,16},{48,32},{64,48},{80,64},{96,80},{112,96},{128,112},... | collective-permute-start | bytes 2359304 | tf_op jit(solution)/shard_map/ppermute | solution.py:27
  62.1 4.3 %collective-permute-start.5 = (bf16[2,512,384]{1,2,0:T(8,128)(2,1)S(1)}, bf16[2,512,384]{1,2,0:T(8,128)(2,1)S(1)}, u32[]{:S(2)}, u32[]{:S(2)}) collective-permute-start(bf16[2,512,384]{1,2,0:T(8,128)(2,1)S(1)} %pad_maximum_fusion.1), channel_id=1, source_target_pairs={{0,16},{16,32},{32,48},{48,64},{64,80},{80,96},{96,112},{112,128},... | collective-permute-start | bytes 2359304 | tf_op jit(solution)/shard_map/ppermute | solution.py:27
  66.3 2.9 collective-permute-start.7
  69.3 10.5 %collective-permute-done.4 = bf16[2,512,384]{1,2,0:T(8,128)(2,1)} collective-permute-done((bf16[2,512,384]{1,2,0:T(8,128)(2,1)S(1)}, bf16[2,512,384]{1,2,0:T(8,128)(2,1)}, u32[]{:S(2)}, u32[]{:S(2)}) %collective-permute-start.4) | collective-permute-done | bytes 786464 | tf_op jit(solution)/shard_map/ppermute | solution.py:27
  79.8 9.8 %collective-permute-start.9 = (bf16[2,512,384]{1,2,0:T(8,128)(2,1)S(1)}, bf16[2,512,384]{1,2,0:T(8,128)(2,1)}, u32[]{:S(2)}, u32[]{:S(2)}) collective-permute-start(bf16[2,512,384]{1,2,0:T(8,128)(2,1)S(1)} %pad_maximum_fusion.1), channel_id=1, source_target_pairs={{0,48},{16,64},{32,80},{48,96},{64,112},{80,128},{96,144},{112,160... | collective-permute-start | bytes 2359304 | tf_op jit(solution)/shard_map/ppermute | solution.py:27
  92.3 99.5 %collective-permute-done.6 = bf16[2,512,384]{1,2,0:T(8,128)(2,1)} collective-permute-done((bf16[2,512,384]{1,2,0:T(8,128)(2,1)S(1)}, bf16[2,512,384]{1,2,0:T(8,128)(2,1)}, u32[]{:S(2)}, u32[]{:S(2)}) %collective-permute-start.6) | collective-permute-done | bytes 786464 | tf_op jit(solution)/shard_map/ppermute | solution.py:27
  191.8 3.4 %collective-permute-start.10 = (bf16[2,512,384]{1,2,0:T(8,128)(2,1)S(1)}, bf16[2,512,384]{1,2,0:T(8,128)(2,1)S(1)}, u32[]{:S(2)}, u32[]{:S(2)}) collective-permute-start(bf16[2,512,384]{1,2,0:T(8,128)(2,1)S(1)} %pad_maximum_fusion.1), channel_id=1, source_target_pairs={{0,8},{8,0},{1,9},{9,1},{2,10},{10,2},{3,11},{11,3},{4,12},{12,4},... | collective-permute-start | bytes 2359304 | tf_op jit(solution)/shard_map/ppermute | solution.py:31
  195.3 8.6 %collective-permute-start.16 = (bf16[384,640]{1,0:T(8,128)(2,1)S(1)}, bf16[384,640]{1,0:T(8,128)(2,1)S(1)}, u32[]{:S(2)}, u32[]{:S(2)}) collective-permute-start(bf16[384,640]{1,0:T(8,128)(2,1)S(1)} %bitcast.452), channel_id=1, source_target_pairs={{0,64},{64,128},{128,192},{192,256},{256,320},{320,384},{384,448},... | collective-permute-start | bytes 1474568 | tf_op jit(solution)/shard_map/ppermute | solution.py:124
  216.6 8.6 %collective-permute-start.11 = (bf16[5,2,512,384]{2,3,1,0:T(8,128)(2,1)S(1)}, bf16[5,2,512,384]{2,3,1,0:T(8,128)(2,1)S(1)}, u32[]{:S(2)}, u32[]{:S(2)}) collective-permute-start(bf16[5,2,512,384]{2,3,1,0:T(8,128)(2,1)S(1)} %broadcast_select_fusion), channel_id=1, source_target_pairs={{0,8},{8,0},{1,9},{9,1},{2,10},{10,2},{3,11},{11,3},{4,12},{12,4},... | collective-permute-start | bytes 11796488 | tf_op jit(solution)/shard_map/ppermute | solution.py:31
  225.8 14.2 %collective-permute-done.18 = bf16[384,640]{1,0:T(8,128)(2,1)S(1)} collective-permute-done((bf16[384,640]{1,0:T(8,128)(2,1)S(1)}, bf16[384,640]{1,0:T(8,128)(2,1)S(1)}, u32[]{:S(2)}, u32[]{:S(2)}) %collective-permute-start.18) | collective-permute-done | bytes 491552 | tf_op jit(solution)/shard_map/ppermute | solution.py:124
  239.9 3.2 %collective-permute-done.17 = bf16[384,640]{1,0:T(8,128)(2,1)S(1)} collective-permute-done((bf16[384,640]{1,0:T(8,128)(2,1)S(1)}, bf16[384,640]{1,0:T(8,128)(2,1)S(1)}, u32[]{:S(2)}, u32[]{:S(2)}) %collective-permute-start.17) | collective-permute-done | bytes 491552 | tf_op jit(solution)/shard_map/ppermute | solution.py:124
  243.4 8.3 %collective-permute-start.20 = (bf16[4,384,640]{2,1,0:T(8,128)(2,1)S(1)}, bf16[4,384,640]{2,1,0:T(8,128)(2,1)S(1)}, u32[]{:S(2)}, u32[]{:S(2)}) collective-permute-start(bf16[4,384,640]{2,1,0:T(8,128)(2,1)S(1)} %pad_maximum_fusion), channel_id=1, source_target_pairs={{0,8},{8,0},{1,9},{9,1},{2,10},{10,2},{3,11},{11,3},{4,12},{12,4},... | collective-permute-start | bytes 5898248 | tf_op jit(solution)/shard_map/ppermute | solution.py:31
  271.2 8.0 %collective-permute-start.12 = (bf16[256,384]{0,1:T(8,128)(2,1)S(1)}, bf16[256,384]{0,1:T(8,128)(2,1)S(1)}, u32[]{:S(2)}, u32[]{:S(2)}) collective-permute-start(bf16[256,384]{0,1:T(8,128)(2,1)S(1)} %bitcast.500), channel_id=1, source_target_pairs={{0,4},{4,0},{1,5},{5,1},{2,6},{6,2},{3,7},{7,3},{8,12},{12,8},{9,1... | collective-permute-start | bytes 589832 | tf_op jit(solution)/shard_map/ppermute | solution.py:145
  279.3 8.1 %collective-permute-done.12 = bf16[256,384]{0,1:T(8,128)(2,1)S(1)} collective-permute-done((bf16[256,384]{0,1:T(8,128)(2,1)S(1)}, bf16[256,384]{0,1:T(8,128)(2,1)S(1)}, u32[]{:S(2)}, u32[]{:S(2)}) %collective-permute-start.12) | collective-permute-done | bytes 196640 | tf_op jit(solution)/shard_map/ppermute | solution.py:145
  287.6 3.1 collective-permute-start.13
  290.7 2.7 collective-permute-start.14
  293.4 3.8 %collective-permute-start.15 = (bf16[256,768]{0,1:T(8,128)(2,1)S(1)}, bf16[256,768]{0,1:T(8,128)(2,1)S(1)}, u32[]{:S(2)}, u32[]{:S(2)}) collective-permute-start(bf16[256,768]{0,1:T(8,128)(2,1)S(1)} %maximum_select_fusion), channel_id=1, source_target_pairs={{0,3},{1,0},{2,1},{3,2},{4,7},{5,4},{6,5},{7,6},{8,11},{9,8},{10,9... | collective-permute-start | bytes 1179656 | tf_op jit(solution)/shard_map/ppermute | solution.py:27
  299.5 4.3 %collective-permute-done.14 = bf16[256,768]{0,1:T(8,128)(2,1)S(1)} collective-permute-done((bf16[256,768]{0,1:T(8,128)(2,1)S(1)}, bf16[256,768]{0,1:T(8,128)(2,1)S(1)}, u32[]{:S(2)}, u32[]{:S(2)}) %collective-permute-start.14) | collective-permute-done | bytes 393248 | tf_op jit(solution)/shard_map/ppermute | solution.py:27
  303.9 9.7 %collective-permute-done.15 = bf16[256,768]{0,1:T(8,128)(2,1)S(1)} collective-permute-done((bf16[256,768]{0,1:T(8,128)(2,1)S(1)}, bf16[256,768]{0,1:T(8,128)(2,1)S(1)}, u32[]{:S(2)}, u32[]{:S(2)}) %collective-permute-start.15) | collective-permute-done | bytes 393248 | tf_op jit(solution)/shard_map/ppermute | solution.py:27
  (219 shorter events, 79.0 us)
Async XLA Ops:
  0.0 56.4 %copy-start = (f32[1000,640]{1,0:T(8,128)S(1)}, f32[1000,640]{1,0:T(8,128)}, u32[]{:S(2)}) copy-start(f32[1000,640]{1,0:T(8,128)} %param.19) | copy-start | bytes 7680004
  0.0 26.1 %collective-permute-start = (bf16[48,640]{1,0:T(8,128)(2,1)}, bf16[48,640]{1,0:T(8,128)(2,1)}, u32[]{:S(2)}, u32[]{:S(2)}) collective-permute-start(bf16[48,640]{1,0:T(8,128)(2,1)} %param.18), channel_id=1, source_target_pairs={{0,8},{8,0},{1,9},{9,1},{2,10},{10,2},{3,11},{11,3},{4,12},{12,4},... | collective-permute-start | bytes 184328 | tf_op jit(solution)/shard_map/ppermute | solution.py:31
  27.7 13.8 %collective-permute-start.1 = (bf16[96,640]{1,0:T(8,128)(2,1)}, bf16[96,640]{1,0:T(8,128)(2,1)}, u32[]{:S(2)}, u32[]{:S(2)}) collective-permute-start(bf16[96,640]{1,0:T(8,128)(2,1)} %maximum_select_fusion.2), channel_id=1, source_target_pairs={{0,16},{16,32},{32,48},{48,0},{1,17},{17,33},{33,49},{49,1},{2,18}... | collective-permute-start | bytes 368648 | tf_op jit(solution)/shard_map/ppermute | solution.py:27
  32.4 20.5 %copy-start.16 = (pred[256,256]{0,1:T(8,128)(4,1)S(1)}, pred[256,256]{0,1:T(8,128)(4,1)}, u32[]{:S(2)}) copy-start(pred[256,256]{0,1:T(8,128)(4,1)} %get-tuple-element.124) | copy-start | bytes 196612
  32.4 12.4 %collective-permute-start.2 = (bf16[96,640]{1,0:T(8,128)(2,1)}, bf16[96,640]{1,0:T(8,128)(2,1)S(1)}, u32[]{:S(2)}, u32[]{:S(2)}) collective-permute-start(bf16[96,640]{1,0:T(8,128)(2,1)} %maximum_select_fusion.2), channel_id=1, source_target_pairs={{0,32},{16,48},{32,0},{48,16},{1,33},{17,49},{33,1},{49,17},{2,34}... | collective-permute-start | bytes 368648 | tf_op jit(solution)/shard_map/ppermute | solution.py:27
  38.3 9.2 %collective-permute-start.3 = (bf16[96,640]{1,0:T(8,128)(2,1)}, bf16[96,640]{1,0:T(8,128)(2,1)S(1)}, u32[]{:S(2)}, u32[]{:S(2)}) collective-permute-start(bf16[96,640]{1,0:T(8,128)(2,1)} %maximum_select_fusion.2), channel_id=1, source_target_pairs={{0,48},{16,0},{32,16},{48,32},{1,49},{17,1},{33,17},{49,33},{2,50}... | collective-permute-start | bytes 368648 | tf_op jit(solution)/shard_map/ppermute | solution.py:27
  48.4 31.4 %collective-permute-start.4 = (bf16[2,512,384]{1,2,0:T(8,128)(2,1)S(1)}, bf16[2,512,384]{1,2,0:T(8,128)(2,1)}, u32[]{:S(2)}, u32[]{:S(2)}) collective-permute-start(bf16[2,512,384]{1,2,0:T(8,128)(2,1)S(1)} %pad_maximum_fusion.1), channel_id=1, source_target_pairs={{16,0},{32,16},{48,32},{64,48},{80,64},{96,80},{112,96},{128,112},... | collective-permute-start | bytes 2359304 | tf_op jit(solution)/shard_map/ppermute | solution.py:27
  58.0 133.7 %collective-permute-start.6 = (bf16[2,512,384]{1,2,0:T(8,128)(2,1)S(1)}, bf16[2,512,384]{1,2,0:T(8,128)(2,1)}, u32[]{:S(2)}, u32[]{:S(2)}) collective-permute-start(bf16[2,512,384]{1,2,0:T(8,128)(2,1)S(1)} %pad_maximum_fusion.1), channel_id=1, source_target_pairs={{32,0},{48,16},{64,32},{80,48},{96,64},{112,80},{128,96},{144,112}... | collective-permute-start | bytes 2359304 | tf_op jit(solution)/shard_map/ppermute | solution.py:27
  60.0 135.3 %collective-permute-start.8 = (bf16[2,512,384]{1,2,0:T(8,128)(2,1)S(1)}, bf16[2,512,384]{1,2,0:T(8,128)(2,1)S(1)}, u32[]{:S(2)}, u32[]{:S(2)}) collective-permute-start(bf16[2,512,384]{1,2,0:T(8,128)(2,1)S(1)} %pad_maximum_fusion.1), channel_id=1, source_target_pairs={{48,0},{64,16},{80,32},{96,48},{112,64},{128,80},{144,96},{160,112... | collective-permute-start | bytes 2359304 | tf_op jit(solution)/shard_map/ppermute | solution.py:27
  62.1 133.2 %collective-permute-start.5 = (bf16[2,512,384]{1,2,0:T(8,128)(2,1)S(1)}, bf16[2,512,384]{1,2,0:T(8,128)(2,1)S(1)}, u32[]{:S(2)}, u32[]{:S(2)}) collective-permute-start(bf16[2,512,384]{1,2,0:T(8,128)(2,1)S(1)} %pad_maximum_fusion.1), channel_id=1, source_target_pairs={{0,16},{16,32},{32,48},{48,64},{64,80},{80,96},{96,112},{112,128},... | collective-permute-start | bytes 2359304 | tf_op jit(solution)/shard_map/ppermute | solution.py:27
  66.3 128.9 %collective-permute-start.7 = (bf16[2,512,384]{1,2,0:T(8,128)(2,1)S(1)}, bf16[2,512,384]{1,2,0:T(8,128)(2,1)S(1)}, u32[]{:S(2)}, u32[]{:S(2)}) collective-permute-start(bf16[2,512,384]{1,2,0:T(8,128)(2,1)S(1)} %pad_maximum_fusion.1), channel_id=1, source_target_pairs={{0,32},{16,48},{32,64},{48,80},{64,96},{80,112},{96,128},{112,144}... | collective-permute-start | bytes 2359304 | tf_op jit(solution)/shard_map/ppermute | solution.py:27
  79.8 115.5 %collective-permute-start.9 = (bf16[2,512,384]{1,2,0:T(8,128)(2,1)S(1)}, bf16[2,512,384]{1,2,0:T(8,128)(2,1)}, u32[]{:S(2)}, u32[]{:S(2)}) collective-permute-start(bf16[2,512,384]{1,2,0:T(8,128)(2,1)S(1)} %pad_maximum_fusion.1), channel_id=1, source_target_pairs={{0,48},{16,64},{32,80},{48,96},{64,112},{80,128},{96,144},{112,160... | collective-permute-start | bytes 2359304 | tf_op jit(solution)/shard_map/ppermute | solution.py:27
  91.4 103.9 %copy-start.13 = (bf16[4,96,640]{2,1,0:T(8,128)(2,1)S(1)}, bf16[4,96,640]{2,1,0:T(8,128)(2,1)}, u32[]{:S(2)}) copy-start(bf16[4,96,640]{2,1,0:T(8,128)(2,1)} %copy-done.12) | copy-start | bytes 1474564
  191.8 24.8 %collective-permute-start.10 = (bf16[2,512,384]{1,2,0:T(8,128)(2,1)S(1)}, bf16[2,512,384]{1,2,0:T(8,128)(2,1)S(1)}, u32[]{:S(2)}, u32[]{:S(2)}) collective-permute-start(bf16[2,512,384]{1,2,0:T(8,128)(2,1)S(1)} %pad_maximum_fusion.1), channel_id=1, source_target_pairs={{0,8},{8,0},{1,9},{9,1},{2,10},{10,2},{3,11},{11,3},{4,12},{12,4},... | collective-permute-start | bytes 2359304 | tf_op jit(solution)/shard_map/ppermute | solution.py:31
  195.3 30.5 %collective-permute-start.16 = (bf16[384,640]{1,0:T(8,128)(2,1)S(1)}, bf16[384,640]{1,0:T(8,128)(2,1)S(1)}, u32[]{:S(2)}, u32[]{:S(2)}) collective-permute-start(bf16[384,640]{1,0:T(8,128)(2,1)S(1)} %bitcast.452), channel_id=1, source_target_pairs={{0,64},{64,128},{128,192},{192,256},{256,320},{320,384},{384,448},... | collective-permute-start | bytes 1474568 | tf_op jit(solution)/shard_map/ppermute | solution.py:124
  203.9 21.9 %collective-permute-start.19 = (bf16[384,640]{1,0:T(8,128)(2,1)S(1)}, bf16[384,640]{1,0:T(8,128)(2,1)S(1)}, u32[]{:S(2)}, u32[]{:S(2)}) collective-permute-start(bf16[384,640]{1,0:T(8,128)(2,1)S(1)} %bitcast.453), channel_id=1, source_target_pairs={{0,256},{64,320},{128,384},{192,448},{256,0},{320,64},{384,128},{4... | collective-permute-start | bytes 1474568 | tf_op jit(solution)/shard_map/ppermute | solution.py:124
  204.6 35.3 %collective-permute-start.18 = (bf16[384,640]{1,0:T(8,128)(2,1)S(1)}, bf16[384,640]{1,0:T(8,128)(2,1)S(1)}, u32[]{:S(2)}, u32[]{:S(2)}) collective-permute-start(bf16[384,640]{1,0:T(8,128)(2,1)S(1)} %bitcast.454), channel_id=1, source_target_pairs={{0,192},{64,256},{128,320},{192,384},{256,448},{320,0},{384,64},{4... | collective-permute-start | bytes 1474568 | tf_op jit(solution)/shard_map/ppermute | solution.py:124
  206.5 36.6 %collective-permute-start.17 = (bf16[384,640]{1,0:T(8,128)(2,1)S(1)}, bf16[384,640]{1,0:T(8,128)(2,1)S(1)}, u32[]{:S(2)}, u32[]{:S(2)}) collective-permute-start(bf16[384,640]{1,0:T(8,128)(2,1)S(1)} %bitcast.455), channel_id=1, source_target_pairs={{0,128},{64,192},{128,256},{192,320},{256,384},{320,448},{384,0},{... | collective-permute-start | bytes 1474568 | tf_op jit(solution)/shard_map/ppermute | solution.py:124
  216.6 40.1 %collective-permute-start.11 = (bf16[5,2,512,384]{2,3,1,0:T(8,128)(2,1)S(1)}, bf16[5,2,512,384]{2,3,1,0:T(8,128)(2,1)S(1)}, u32[]{:S(2)}, u32[]{:S(2)}) collective-permute-start(bf16[5,2,512,384]{2,3,1,0:T(8,128)(2,1)S(1)} %broadcast_select_fusion), channel_id=1, source_target_pairs={{0,8},{8,0},{1,9},{9,1},{2,10},{10,2},{3,11},{11,3},{4,12},{12,4},... | collective-permute-start | bytes 11796488 | tf_op jit(solution)/shard_map/ppermute | solution.py:31
  243.4 12.9 %collective-permute-start.20 = (bf16[4,384,640]{2,1,0:T(8,128)(2,1)S(1)}, bf16[4,384,640]{2,1,0:T(8,128)(2,1)S(1)}, u32[]{:S(2)}, u32[]{:S(2)}) collective-permute-start(bf16[4,384,640]{2,1,0:T(8,128)(2,1)S(1)} %pad_maximum_fusion), channel_id=1, source_target_pairs={{0,8},{8,0},{1,9},{9,1},{2,10},{10,2},{3,11},{11,3},{4,12},{12,4},... | collective-permute-start | bytes 5898248 | tf_op jit(solution)/shard_map/ppermute | solution.py:31
  271.2 16.2 %collective-permute-start.12 = (bf16[256,384]{0,1:T(8,128)(2,1)S(1)}, bf16[256,384]{0,1:T(8,128)(2,1)S(1)}, u32[]{:S(2)}, u32[]{:S(2)}) collective-permute-start(bf16[256,384]{0,1:T(8,128)(2,1)S(1)} %bitcast.500), channel_id=1, source_target_pairs={{0,4},{4,0},{1,5},{5,1},{2,6},{6,2},{3,7},{7,3},{8,12},{12,8},{9,1... | collective-permute-start | bytes 589832 | tf_op jit(solution)/shard_map/ppermute | solution.py:145
  287.6 11.9 %collective-permute-start.13 = (bf16[256,768]{0,1:T(8,128)(2,1)S(1)}, bf16[256,768]{0,1:T(8,128)(2,1)S(1)}, u32[]{:S(2)}, u32[]{:S(2)}) collective-permute-start(bf16[256,768]{0,1:T(8,128)(2,1)S(1)} %maximum_select_fusion), channel_id=1, source_target_pairs={{0,1},{1,2},{2,3},{3,0},{4,5},{5,6},{6,7},{7,4},{8,9},{9,10},{10,1... | collective-permute-start | bytes 1179656 | tf_op jit(solution)/shard_map/ppermute | solution.py:27
  290.7 13.2 %collective-permute-start.14 = (bf16[256,768]{0,1:T(8,128)(2,1)S(1)}, bf16[256,768]{0,1:T(8,128)(2,1)S(1)}, u32[]{:S(2)}, u32[]{:S(2)}) collective-permute-start(bf16[256,768]{0,1:T(8,128)(2,1)S(1)} %maximum_select_fusion), channel_id=1, source_target_pairs={{0,2},{1,3},{2,0},{3,1},{4,6},{5,7},{6,4},{7,5},{8,10},{9,11},{10,... | collective-permute-start | bytes 1179656 | tf_op jit(solution)/shard_map/ppermute | solution.py:27
  293.4 20.1 %collective-permute-start.15 = (bf16[256,768]{0,1:T(8,128)(2,1)S(1)}, bf16[256,768]{0,1:T(8,128)(2,1)S(1)}, u32[]{:S(2)}, u32[]{:S(2)}) collective-permute-start(bf16[256,768]{0,1:T(8,128)(2,1)S(1)} %maximum_select_fusion), channel_id=1, source_target_pairs={{0,3},{1,0},{2,1},{3,2},{4,7},{5,4},{6,5},{7,6},{8,11},{9,8},{10,9... | collective-permute-start | bytes 1179656 | tf_op jit(solution)/shard_map/ppermute | solution.py:27
  (18 other events, 66.4 us)

commit v11 on v8

--- a/solution.py
+++ b/solution.py
@@ -202,12 +202,17 @@
                 jnp.concatenate([value_tiles, cache_values.reshape(-1, tile_width)], axis=0),
             ]
         )
+        sign = 1 - 2 * core
+        own_pair = swap_cores(packed)
         row_block = gather_weight(out_weight, sizes, is_first)
-        packed, row_block = lax.optimization_barrier((packed, row_block))
+        packed, row_block, own_pair = lax.optimization_barrier((packed, row_block, own_pair))
         weight_full = spread_weight(row_block, sizes, is_first)
 
         carry_state = visit_block(
             empty_state(head_count, row_count), packed, seq_index, query_heads, query_clip, context
+        )
+        carry_state = visit_block(
+            carry_state, own_pair, seq_index + sign, query_heads, query_clip, context
         )
         above = {}
         below = {}
@@ -220,11 +225,6 @@
             carry_state = visit_block(
                 carry_state, below[d], seq_index - 2 * d, query_heads, query_clip, context
             )
-        sign = 1 - 2 * core
-        got = swap_cores(packed)
-        carry_state = visit_block(
-            carry_state, got, seq_index + sign, query_heads, query_clip, context
-        )
         selected = jnp.where(
             is_first,
             jnp.stack([above[1], above[2], above[3], below[1], below[2]]),

time: 268 us -> 260 us (0.970)
  the two profiles are of different devices: /device:TPU:19 before, /device:TPU:15 now
where the time goes in v11:
time: 260 us; the launch traced here: 259 us
  starting transfers between devices  117 us (45%)
  waiting for transfers between devices  96.6 us (37%)
  matrix products  16.7 us (6%)
  local copies, waits for them, and re-layouts  15.2 us (6%)
  other arithmetic  12.1 us (5%)
    ppermute x12, waiting for transfers between devices, shifted(): return lax.ppermute(block, axes, route)  74.4 us
    ppermute x4, starting transfers between devices, swap_cores(): return lax.ppermute(block, 'c', [(0, 1), (1, 0)])  52.2 us
    ppermute x12, starting transfers between devices, shifted(): return lax.ppermute(block, axes, route)  45.5 us
    ppermute x4, waiting for transfers between devices, spread_weight(): received.append(lax.ppermute(row_block, ('y', 'c'), route))  14.7 us
    ppermute x4, starting transfers between devices, spread_weight(): received.append(lax.ppermute(row_block, ('y', 'c'), route))  12.3 us
    ppermute x1, waiting for transfers between devices, gather_attention(): partner = lax.ppermute(attention_local, 'zh', [(0, 1), (1, 0)])  7.46 us
    ppermute x1, starting transfers between devices, gather_attention(): partner = lax.ppermute(attention_local, 'zh', [(0, 1), (1, 0)])  6.84 us
    dot_general x13, matrix products, attend(): jnp.einsum('qhd,khd->hqk', query_heads, key_heads, preferred_element_type...  6.27 us
  transfers between devices with their start and end apart: 21, of which 10 were waited for; matrix products, arithmetic and copies ran while one was open for 10% of the time, Pallas kernels for 0%

profile of v11, /device:TPU:15, one launch (start us, length us, event | category | flops | bytes accessed | tf_op | source)
XLA Modules:
  0.0 259.3 jit_solution(6240923816056694310)
XLA Ops:
  0.0 2.8 %collective-permute-start = (bf16[48,640]{1,0:T(8,128)(2,1)}, bf16[48,640]{1,0:T(8,128)(2,1)S(1)}, u32[]{:S(2)}, u32[]{:S(2)}) collective-permute-start(bf16[48,640]{1,0:T(8,128)(2,1)} %param.18), channel_id=1, source_target_pairs={{0,8},{8,0},{1,9},{9,1},{2,10},{10,2},{3,11},{11,3},{4,12},{12,4},... | collective-permute-start | bytes 184328 | tf_op jit(solution)/shard_map/ppermute | solution.py:31
  17.1 4.0 %collective-permute-start.1 = (bf16[96,640]{1,0:T(8,128)(2,1)S(1)}, bf16[96,640]{1,0:T(8,128)(2,1)S(1)}, u32[]{:S(2)}, u32[]{:S(2)}) collective-permute-start(bf16[96,640]{1,0:T(8,128)(2,1)S(1)} %maximum_select_fusion.2), channel_id=1, source_target_pairs={{0,16},{16,32},{32,48},{48,0},{1,17},{17,33},{33,49},{49,1},{2,18}... | collective-permute-start | bytes 368648 | tf_op jit(solution)/shard_map/ppermute | solution.py:27
  21.5 5.8 %collective-permute-start.2 = (bf16[96,640]{1,0:T(8,128)(2,1)S(1)}, bf16[96,640]{1,0:T(8,128)(2,1)S(1)}, u32[]{:S(2)}, u32[]{:S(2)}) collective-permute-start(bf16[96,640]{1,0:T(8,128)(2,1)S(1)} %maximum_select_fusion.2), channel_id=1, source_target_pairs={{0,32},{16,48},{32,0},{48,16},{1,33},{17,49},{33,1},{49,17},{2,34}... | collective-permute-start | bytes 368648 | tf_op jit(solution)/shard_map/ppermute | solution.py:27
  27.3 2.2 collective-permute-start.3
  29.6 4.0 %collective-permute-done.2 = bf16[96,640]{1,0:T(8,128)(2,1)S(1)} collective-permute-done((bf16[96,640]{1,0:T(8,128)(2,1)S(1)}, bf16[96,640]{1,0:T(8,128)(2,1)S(1)}, u32[]{:S(2)}, u32[]{:S(2)}) %collective-permute-start.2) | collective-permute-done | bytes 122912 | tf_op jit(solution)/shard_map/ppermute | solution.py:27
  33.7 2.7 %collective-permute-done.3 = bf16[96,640]{1,0:T(8,128)(2,1)S(1)} collective-permute-done((bf16[96,640]{1,0:T(8,128)(2,1)S(1)}, bf16[96,640]{1,0:T(8,128)(2,1)S(1)}, u32[]{:S(2)}, u32[]{:S(2)}) %collective-permute-start.3) | collective-permute-done | bytes 122912 | tf_op jit(solution)/shard_map/ppermute | solution.py:27
  42.1 6.6 %collective-permute-start.18 = (bf16[384,640]{1,0:T(8,128)(2,1)S(1)}, bf16[384,640]{1,0:T(8,128)(2,1)S(1)}, u32[]{:S(2)}, u32[]{:S(2)}) collective-permute-start(bf16[384,640]{1,0:T(8,128)(2,1)S(1)} %bitcast.454), channel_id=1, source_target_pairs={{0,192},{64,256},{128,320},{192,384},{256,448},{320,0},{384,64},{4... | collective-permute-start | bytes 1474568 | tf_op jit(solution)/shard_map/ppermute | solution.py:124
  48.8 2.9 %collective-permute-start.17 = (bf16[384,640]{1,0:T(8,128)(2,1)S(1)}, bf16[384,640]{1,0:T(8,128)(2,1)S(1)}, u32[]{:S(2)}, u32[]{:S(2)}) collective-permute-start(bf16[384,640]{1,0:T(8,128)(2,1)S(1)} %bitcast.455), channel_id=1, source_target_pairs={{0,128},{64,192},{128,256},{192,320},{256,384},{320,448},{384,0},{... | collective-permute-start | bytes 1474568 | tf_op jit(solution)/shard_map/ppermute | solution.py:124
  54.6 3.2 %collective-permute-start.8 = (bf16[2,512,384]{1,2,0:T(8,128)(2,1)S(1)}, bf16[2,512,384]{1,2,0:T(8,128)(2,1)S(1)}, u32[]{:S(2)}, u32[]{:S(2)}) collective-permute-start(bf16[2,512,384]{1,2,0:T(8,128)(2,1)S(1)} %pad_maximum_fusion.1), channel_id=1, source_target_pairs={{0,32},{16,48},{32,64},{48,80},{64,96},{80,112},{96,128},{112,144}... | collective-permute-start | bytes 2359304 | tf_op jit(solution)/shard_map/ppermute | solution.py:27
  58.2 5.9 %collective-permute-start.10 = (bf16[2,512,384]{1,2,0:T(8,128)(2,1)S(1)}, bf16[2,512,384]{1,2,0:T(8,128)(2,1)S(1)}, u32[]{:S(2)}, u32[]{:S(2)}) collective-permute-start(bf16[2,512,384]{1,2,0:T(8,128)(2,1)S(1)} %pad_maximum_fusion.1), channel_id=1, source_target_pairs={{0,48},{16,64},{32,80},{48,96},{64,112},{80,128},{96,144},{112,160... | collective-permute-start | bytes 2359304 | tf_op jit(solution)/shard_map/ppermute | solution.py:27
  64.1 9.4 %collective-permute-done.18 = bf16[384,640]{1,0:T(8,128)(2,1)S(1)} collective-permute-done((bf16[384,640]{1,0:T(8,128)(2,1)S(1)}, bf16[384,640]{1,0:T(8,128)(2,1)S(1)}, u32[]{:S(2)}, u32[]{:S(2)}) %collective-permute-start.18) | collective-permute-done | bytes 491552 | tf_op jit(solution)/shard_map/ppermute | solution.py:124
  73.5 5.8 %collective-permute-start.5 = (bf16[2,512,384]{1,2,0:T(8,128)(2,1)S(1)}, bf16[2,512,384]{1,2,0:T(8,128)(2,1)S(1)}, u32[]{:S(2)}, u32[]{:S(2)}) collective-permute-start(bf16[2,512,384]{1,2,0:T(8,128)(2,1)S(1)} %pad_maximum_fusion.1), channel_id=1, source_target_pairs={{16,0},{32,16},{48,32},{64,48},{80,64},{96,80},{112,96},{128,112},... | collective-permute-start | bytes 2359304 | tf_op jit(solution)/shard_map/ppermute | solution.py:27
  79.3 5.3 %collective-permute-done.17 = bf16[384,640]{1,0:T(8,128)(2,1)S(1)} collective-permute-done((bf16[384,640]{1,0:T(8,128)(2,1)S(1)}, bf16[384,640]{1,0:T(8,128)(2,1)S(1)}, u32[]{:S(2)}, u32[]{:S(2)}) %collective-permute-start.17) | collective-permute-done | bytes 491552 | tf_op jit(solution)/shard_map/ppermute | solution.py:124
  84.6 6.5 %collective-permute-start.7 = (bf16[2,512,384]{1,2,0:T(8,128)(2,1)S(1)}, bf16[2,512,384]{1,2,0:T(8,128)(2,1)S(1)}, u32[]{:S(2)}, u32[]{:S(2)}) collective-permute-start(bf16[2,512,384]{1,2,0:T(8,128)(2,1)S(1)} %pad_maximum_fusion.1), channel_id=1, source_target_pairs={{32,0},{48,16},{64,32},{80,48},{96,64},{112,80},{128,96},{144,112}... | collective-permute-start | bytes 2359304 | tf_op jit(solution)/shard_map/ppermute | solution.py:27
  95.1 37.1 %collective-permute-start.20 = (bf16[4,384,640]{2,1,0:T(8,128)(2,1)}, bf16[4,384,640]{2,1,0:T(8,128)(2,1)}, u32[]{:S(2)}, u32[]{:S(2)}) collective-permute-start(bf16[4,384,640]{2,1,0:T(8,128)(2,1)} %pad_maximum_fusion), channel_id=1, source_target_pairs={{0,8},{8,0},{1,9},{9,1},{2,10},{10,2},{3,11},{11,3},{4,12},{12,4},... | collective-permute-start | bytes 5898248 | tf_op jit(solution)/shard_map/ppermute | solution.py:31
  132.5 49.5 %collective-permute-done.7 = bf16[2,512,384]{1,2,0:T(8,128)(2,1)S(1)} collective-permute-done((bf16[2,512,384]{1,2,0:T(8,128)(2,1)S(1)}, bf16[2,512,384]{1,2,0:T(8,128)(2,1)S(1)}, u32[]{:S(2)}, u32[]{:S(2)}) %collective-permute-start.7) | collective-permute-done | bytes 786464 | tf_op jit(solution)/shard_map/ppermute | solution.py:27
  182.8 10.3 %collective-permute-start.11 = (bf16[5,2,512,384]{2,3,1,0:T(8,128)(2,1)S(1)}, bf16[5,2,512,384]{2,3,1,0:T(8,128)(2,1)S(1)}, u32[]{:S(2)}, u32[]{:S(2)}) collective-permute-start(bf16[5,2,512,384]{2,3,1,0:T(8,128)(2,1)S(1)} %broadcast_select_fusion), channel_id=1, source_target_pairs={{0,8},{8,0},{1,9},{9,1},{2,10},{10,2},{3,11},{11,3},{4,12},{12,4},... | collective-permute-start | bytes 11796488 | tf_op jit(solution)/shard_map/ppermute | solution.py:31
  215.2 6.8 %collective-permute-start.12 = (bf16[256,384]{0,1:T(8,128)(2,1)S(1)}, bf16[256,384]{0,1:T(8,128)(2,1)S(1)}, u32[]{:S(2)}, u32[]{:S(2)}) collective-permute-start(bf16[256,384]{0,1:T(8,128)(2,1)S(1)} %bitcast.501), channel_id=1, source_target_pairs={{0,4},{4,0},{1,5},{5,1},{2,6},{6,2},{3,7},{7,3},{8,12},{12,8},{9,1... | collective-permute-start | bytes 589832 | tf_op jit(solution)/shard_map/ppermute | solution.py:145
  223.2 7.5 %collective-permute-done.12 = bf16[256,384]{0,1:T(8,128)(2,1)S(1)} collective-permute-done((bf16[256,384]{0,1:T(8,128)(2,1)S(1)}, bf16[256,384]{0,1:T(8,128)(2,1)S(1)}, u32[]{:S(2)}, u32[]{:S(2)}) %collective-permute-start.12) | collective-permute-done | bytes 196640 | tf_op jit(solution)/shard_map/ppermute | solution.py:145
  230.8 3.4 %collective-permute-start.13 = (bf16[256,768]{0,1:T(8,128)(2,1)S(1)}, bf16[256,768]{0,1:T(8,128)(2,1)S(1)}, u32[]{:S(2)}, u32[]{:S(2)}) collective-permute-start(bf16[256,768]{0,1:T(8,128)(2,1)S(1)} %maximum_select_fusion), channel_id=1, source_target_pairs={{0,1},{1,2},{2,3},{3,0},{4,5},{5,6},{6,7},{7,4},{8,9},{9,10},{10,1... | collective-permute-start | bytes 1179656 | tf_op jit(solution)/shard_map/ppermute | solution.py:27
  234.2 2.8 %collective-permute-start.14 = (bf16[256,768]{0,1:T(8,128)(2,1)S(1)}, bf16[256,768]{0,1:T(8,128)(2,1)S(1)}, u32[]{:S(2)}, u32[]{:S(2)}) collective-permute-start(bf16[256,768]{0,1:T(8,128)(2,1)S(1)} %maximum_select_fusion), channel_id=1, source_target_pairs={{0,2},{1,3},{2,0},{3,1},{4,6},{5,7},{6,4},{7,5},{8,10},{9,11},{10,... | collective-permute-start | bytes 1179656 | tf_op jit(solution)/shard_map/ppermute | solution.py:27
  239.1 3.5 %collective-permute-done.13 = bf16[256,768]{0,1:T(8,128)(2,1)S(1)} collective-permute-done((bf16[256,768]{0,1:T(8,128)(2,1)S(1)}, bf16[256,768]{0,1:T(8,128)(2,1)S(1)}, u32[]{:S(2)}, u32[]{:S(2)}) %collective-permute-start.13) | collective-permute-done | bytes 393248 | tf_op jit(solution)/shard_map/ppermute | solution.py:27
  242.7 4.5 %collective-permute-done.14 = bf16[256,768]{0,1:T(8,128)(2,1)S(1)} collective-permute-done((bf16[256,768]{0,1:T(8,128)(2,1)S(1)}, bf16[256,768]{0,1:T(8,128)(2,1)S(1)}, u32[]{:S(2)}, u32[]{:S(2)}) %collective-permute-start.14) | collective-permute-done | bytes 393248 | tf_op jit(solution)/shard_map/ppermute | solution.py:27
  247.2 9.9 %collective-permute-done.15 = bf16[256,768]{0,1:T(8,128)(2,1)S(1)} collective-permute-done((bf16[256,768]{0,1:T(8,128)(2,1)S(1)}, bf16[256,768]{0,1:T(8,128)(2,1)S(1)}, u32[]{:S(2)}, u32[]{:S(2)}) %collective-permute-start.15) | collective-permute-done | bytes 393248 | tf_op jit(solution)/shard_map/ppermute | solution.py:27
  (229 shorter events, 55.1 us)
Async XLA Ops:
  0.0 17.1 %collective-permute-start = (bf16[48,640]{1,0:T(8,128)(2,1)}, bf16[48,640]{1,0:T(8,128)(2,1)S(1)}, u32[]{:S(2)}, u32[]{:S(2)}) collective-permute-start(bf16[48,640]{1,0:T(8,128)(2,1)} %param.18), channel_id=1, source_target_pairs={{0,8},{8,0},{1,9},{9,1},{2,10},{10,2},{3,11},{11,3},{4,12},{12,4},... | collective-permute-start | bytes 184328 | tf_op jit(solution)/shard_map/ppermute | solution.py:31
  7.3 29.1 %collective-permute-start.4 = (bf16[2,512,384]{1,2,0:T(8,128)(2,1)S(1)}, bf16[2,512,384]{1,2,0:T(8,128)(2,1)}, u32[]{:S(2)}, u32[]{:S(2)}) collective-permute-start(bf16[2,512,384]{1,2,0:T(8,128)(2,1)S(1)} %pad_maximum_fusion.1), channel_id=1, source_target_pairs={{0,8},{8,0},{1,9},{9,1},{2,10},{10,2},{3,11},{11,3},{4,12},{12,4},... | collective-permute-start | bytes 2359304 | tf_op jit(solution)/shard_map/ppermute | solution.py:31
  13.1 38.6 %copy-start.15 = (pred[256,512]{0,1:T(8,128)(4,1)}, pred[256,512]{0,1:T(8,128)(4,1)S(1)}, u32[]{:S(2)}) copy-start(pred[256,512]{0,1:T(8,128)(4,1)S(1)} %pad_add_fusion) | copy-start | bytes 393220
  17.0 37.0 %copy-start.5 = (pred[256,512]{0,1:T(8,128)(4,1)}, pred[256,512]{0,1:T(8,128)(4,1)S(1)}, u32[]{:S(2)}) copy-start(pred[256,512]{0,1:T(8,128)(4,1)S(1)} %pad_add_fusion.1) | copy-start | bytes 393220
  17.1 12.5 %collective-permute-start.1 = (bf16[96,640]{1,0:T(8,128)(2,1)S(1)}, bf16[96,640]{1,0:T(8,128)(2,1)S(1)}, u32[]{:S(2)}, u32[]{:S(2)}) collective-permute-start(bf16[96,640]{1,0:T(8,128)(2,1)S(1)} %maximum_select_fusion.2), channel_id=1, source_target_pairs={{0,16},{16,32},{32,48},{48,0},{1,17},{17,33},{33,49},{49,1},{2,18}... | collective-permute-start | bytes 368648 | tf_op jit(solution)/shard_map/ppermute | solution.py:27
  21.5 12.2 %collective-permute-start.2 = (bf16[96,640]{1,0:T(8,128)(2,1)S(1)}, bf16[96,640]{1,0:T(8,128)(2,1)S(1)}, u32[]{:S(2)}, u32[]{:S(2)}) collective-permute-start(bf16[96,640]{1,0:T(8,128)(2,1)S(1)} %maximum_select_fusion.2), channel_id=1, source_target_pairs={{0,32},{16,48},{32,0},{48,16},{1,33},{17,49},{33,1},{49,17},{2,34}... | collective-permute-start | bytes 368648 | tf_op jit(solution)/shard_map/ppermute | solution.py:27
  27.3 9.1 %collective-permute-start.3 = (bf16[96,640]{1,0:T(8,128)(2,1)S(1)}, bf16[96,640]{1,0:T(8,128)(2,1)S(1)}, u32[]{:S(2)}, u32[]{:S(2)}) collective-permute-start(bf16[96,640]{1,0:T(8,128)(2,1)S(1)} %maximum_select_fusion.2), channel_id=1, source_target_pairs={{0,48},{16,0},{32,16},{48,32},{1,49},{17,1},{33,17},{49,33},{2,50}... | collective-permute-start | bytes 368648 | tf_op jit(solution)/shard_map/ppermute | solution.py:27
  37.2 55.6 %collective-permute-start.6 = (bf16[2,512,384]{1,2,0:T(8,128)(2,1)S(1)}, bf16[2,512,384]{1,2,0:T(8,128)(2,1)S(1)}, u32[]{:S(2)}, u32[]{:S(2)}) collective-permute-start(bf16[2,512,384]{1,2,0:T(8,128)(2,1)S(1)} %pad_maximum_fusion.1), channel_id=1, source_target_pairs={{0,16},{16,32},{32,48},{48,64},{64,80},{80,96},{96,112},{112,128},... | collective-permute-start | bytes 2359304 | tf_op jit(solution)/shard_map/ppermute | solution.py:27
  39.3 15.2 %collective-permute-start.16 = (bf16[384,640]{1,0:T(8,128)(2,1)S(1)}, bf16[384,640]{1,0:T(8,128)(2,1)S(1)}, u32[]{:S(2)}, u32[]{:S(2)}) collective-permute-start(bf16[384,640]{1,0:T(8,128)(2,1)S(1)} %bitcast.452), channel_id=1, source_target_pairs={{0,64},{64,128},{128,192},{192,256},{256,320},{320,384},{384,448},... | collective-permute-start | bytes 1474568 | tf_op jit(solution)/shard_map/ppermute | solution.py:124
  41.4 16.7 %collective-permute-start.19 = (bf16[384,640]{1,0:T(8,128)(2,1)S(1)}, bf16[384,640]{1,0:T(8,128)(2,1)S(1)}, u32[]{:S(2)}, u32[]{:S(2)}) collective-permute-start(bf16[384,640]{1,0:T(8,128)(2,1)S(1)} %bitcast.453), channel_id=1, source_target_pairs={{0,256},{64,320},{128,384},{192,448},{256,0},{320,64},{384,128},{4... | collective-permute-start | bytes 1474568 | tf_op jit(solution)/shard_map/ppermute | solution.py:124
  42.1 31.4 %collective-permute-start.18 = (bf16[384,640]{1,0:T(8,128)(2,1)S(1)}, bf16[384,640]{1,0:T(8,128)(2,1)S(1)}, u32[]{:S(2)}, u32[]{:S(2)}) collective-permute-start(bf16[384,640]{1,0:T(8,128)(2,1)S(1)} %bitcast.454), channel_id=1, source_target_pairs={{0,192},{64,256},{128,320},{192,384},{256,448},{320,0},{384,64},{4... | collective-permute-start | bytes 1474568 | tf_op jit(solution)/shard_map/ppermute | solution.py:124
  48.8 35.8 %collective-permute-start.17 = (bf16[384,640]{1,0:T(8,128)(2,1)S(1)}, bf16[384,640]{1,0:T(8,128)(2,1)S(1)}, u32[]{:S(2)}, u32[]{:S(2)}) collective-permute-start(bf16[384,640]{1,0:T(8,128)(2,1)S(1)} %bitcast.455), channel_id=1, source_target_pairs={{0,128},{64,192},{128,256},{192,320},{256,384},{320,448},{384,0},{... | collective-permute-start | bytes 1474568 | tf_op jit(solution)/shard_map/ppermute | solution.py:124
  54.6 40.5 %collective-permute-start.8 = (bf16[2,512,384]{1,2,0:T(8,128)(2,1)S(1)}, bf16[2,512,384]{1,2,0:T(8,128)(2,1)S(1)}, u32[]{:S(2)}, u32[]{:S(2)}) collective-permute-start(bf16[2,512,384]{1,2,0:T(8,128)(2,1)S(1)} %pad_maximum_fusion.1), channel_id=1, source_target_pairs={{0,32},{16,48},{32,64},{48,80},{64,96},{80,112},{96,128},{112,144}... | collective-permute-start | bytes 2359304 | tf_op jit(solution)/shard_map/ppermute | solution.py:27
  58.2 34.5 %copy-start.11 = (bf16[384,640]{1,0:T(8,128)(2,1)}, bf16[384,640]{1,0:T(8,128)(2,1)S(1)}, u32[]{:S(2)}) copy-start(bf16[384,640]{1,0:T(8,128)(2,1)S(1)} %collective-permute-done.19) | copy-start | bytes 1474564
  58.2 74.1 %collective-permute-start.10 = (bf16[2,512,384]{1,2,0:T(8,128)(2,1)S(1)}, bf16[2,512,384]{1,2,0:T(8,128)(2,1)S(1)}, u32[]{:S(2)}, u32[]{:S(2)}) collective-permute-start(bf16[2,512,384]{1,2,0:T(8,128)(2,1)S(1)} %pad_maximum_fusion.1), channel_id=1, source_target_pairs={{0,48},{16,64},{32,80},{48,96},{64,112},{80,128},{96,144},{112,160... | collective-permute-start | bytes 2359304 | tf_op jit(solution)/shard_map/ppermute | solution.py:27
  73.5 58.9 %collective-permute-start.5 = (bf16[2,512,384]{1,2,0:T(8,128)(2,1)S(1)}, bf16[2,512,384]{1,2,0:T(8,128)(2,1)S(1)}, u32[]{:S(2)}, u32[]{:S(2)}) collective-permute-start(bf16[2,512,384]{1,2,0:T(8,128)(2,1)S(1)} %pad_maximum_fusion.1), channel_id=1, source_target_pairs={{16,0},{32,16},{48,32},{64,48},{80,64},{96,80},{112,96},{128,112},... | collective-permute-start | bytes 2359304 | tf_op jit(solution)/shard_map/ppermute | solution.py:27
  84.6 97.4 %collective-permute-start.7 = (bf16[2,512,384]{1,2,0:T(8,128)(2,1)S(1)}, bf16[2,512,384]{1,2,0:T(8,128)(2,1)S(1)}, u32[]{:S(2)}, u32[]{:S(2)}) collective-permute-start(bf16[2,512,384]{1,2,0:T(8,128)(2,1)S(1)} %pad_maximum_fusion.1), channel_id=1, source_target_pairs={{32,0},{48,16},{64,32},{80,48},{96,64},{112,80},{128,96},{144,112}... | collective-permute-start | bytes 2359304 | tf_op jit(solution)/shard_map/ppermute | solution.py:27
  92.8 89.4 %collective-permute-start.9 = (bf16[2,512,384]{1,2,0:T(8,128)(2,1)S(1)}, bf16[2,512,384]{1,2,0:T(8,128)(2,1)S(1)}, u32[]{:S(2)}, u32[]{:S(2)}) collective-permute-start(bf16[2,512,384]{1,2,0:T(8,128)(2,1)S(1)} %pad_maximum_fusion.1), channel_id=1, source_target_pairs={{48,0},{64,16},{80,32},{96,48},{112,64},{128,80},{144,96},{160,112... | collective-permute-start | bytes 2359304 | tf_op jit(solution)/shard_map/ppermute | solution.py:27
  95.1 102.1 %collective-permute-start.20 = (bf16[4,384,640]{2,1,0:T(8,128)(2,1)}, bf16[4,384,640]{2,1,0:T(8,128)(2,1)}, u32[]{:S(2)}, u32[]{:S(2)}) collective-permute-start(bf16[4,384,640]{2,1,0:T(8,128)(2,1)} %pad_maximum_fusion), channel_id=1, source_target_pairs={{0,8},{8,0},{1,9},{9,1},{2,10},{10,2},{3,11},{11,3},{4,12},{12,4},... | collective-permute-start | bytes 5898248 | tf_op jit(solution)/shard_map/ppermute | solution.py:31
  182.8 18.0 %collective-permute-start.11 = (bf16[5,2,512,384]{2,3,1,0:T(8,128)(2,1)S(1)}, bf16[5,2,512,384]{2,3,1,0:T(8,128)(2,1)S(1)}, u32[]{:S(2)}, u32[]{:S(2)}) collective-permute-start(bf16[5,2,512,384]{2,3,1,0:T(8,128)(2,1)S(1)} %broadcast_select_fusion), channel_id=1, source_target_pairs={{0,8},{8,0},{1,9},{9,1},{2,10},{10,2},{3,11},{11,3},{4,12},{12,4},... | collective-permute-start | bytes 11796488 | tf_op jit(solution)/shard_map/ppermute | solution.py:31
  215.2 15.5 %collective-permute-start.12 = (bf16[256,384]{0,1:T(8,128)(2,1)S(1)}, bf16[256,384]{0,1:T(8,128)(2,1)S(1)}, u32[]{:S(2)}, u32[]{:S(2)}) collective-permute-start(bf16[256,384]{0,1:T(8,128)(2,1)S(1)} %bitcast.501), channel_id=1, source_target_pairs={{0,4},{4,0},{1,5},{5,1},{2,6},{6,2},{3,7},{7,3},{8,12},{12,8},{9,1... | collective-permute-start | bytes 589832 | tf_op jit(solution)/shard_map/ppermute | solution.py:145
  230.8 11.8 %collective-permute-start.13 = (bf16[256,768]{0,1:T(8,128)(2,1)S(1)}, bf16[256,768]{0,1:T(8,128)(2,1)S(1)}, u32[]{:S(2)}, u32[]{:S(2)}) collective-permute-start(bf16[256,768]{0,1:T(8,128)(2,1)S(1)} %maximum_select_fusion), channel_id=1, source_target_pairs={{0,1},{1,2},{2,3},{3,0},{4,5},{5,6},{6,7},{7,4},{8,9},{9,10},{10,1... | collective-permute-start | bytes 1179656 | tf_op jit(solution)/shard_map/ppermute | solution.py:27
  234.2 12.9 %collective-permute-start.14 = (bf16[256,768]{0,1:T(8,128)(2,1)S(1)}, bf16[256,768]{0,1:T(8,128)(2,1)S(1)}, u32[]{:S(2)}, u32[]{:S(2)}) collective-permute-start(bf16[256,768]{0,1:T(8,128)(2,1)S(1)} %maximum_select_fusion), channel_id=1, source_target_pairs={{0,2},{1,3},{2,0},{3,1},{4,6},{5,7},{6,4},{7,5},{8,10},{9,11},{10,... | collective-permute-start | bytes 1179656 | tf_op jit(solution)/shard_map/ppermute | solution.py:27
  237.0 20.1 %collective-permute-start.15 = (bf16[256,768]{0,1:T(8,128)(2,1)S(1)}, bf16[256,768]{0,1:T(8,128)(2,1)S(1)}, u32[]{:S(2)}, u32[]{:S(2)}) collective-permute-start(bf16[256,768]{0,1:T(8,128)(2,1)S(1)} %maximum_select_fusion), channel_id=1, source_target_pairs={{0,3},{1,0},{2,1},{3,2},{4,7},{5,4},{6,5},{7,6},{8,11},{9,8},{10,9... | collective-permute-start | bytes 1179656 | tf_op jit(solution)/shard_map/ppermute | solution.py:27
  (23 other events, 113.2 us)

commit v12 on v11

--- a/solution.py
+++ b/solution.py
@@ -225,16 +225,21 @@
             carry_state = visit_block(
                 carry_state, below[d], seq_index - 2 * d, query_heads, query_clip, context
             )
-        selected = jnp.where(
-            is_first,
-            jnp.stack([above[1], above[2], above[3], below[1], below[2]]),
-            jnp.stack([below[1], below[2], below[3], above[1], above[2]]),
-        )
-        traded = swap_cores(selected)
-        for slot, offset in enumerate((-1, -3, -5, 3, 5)):
+        near = swap_cores(
+            jnp.where(
+                is_first,
+                jnp.stack([above[1], above[2], below[1], below[2]]),
+                jnp.stack([below[1], below[2], above[1], above[2]]),
+            )
+        )
+        for slot, offset in enumerate((-1, -3, 3, 5)):
             carry_state = visit_block(
-                carry_state, traded[slot], seq_index + sign * offset, query_heads, query_clip, context
-            )
+                carry_state, near[slot], seq_index + sign * offset, query_heads, query_clip, context
+            )
+        far = swap_cores(jnp.where(is_first, above[3], below[3]))
+        carry_state = visit_block(
+            carry_state, far, seq_index - sign * 5, query_heads, query_clip, context
+        )
         running_max, totals, accumulated = carry_state
         result = accumulated / totals[:, :, None]
         attention_local = (

time: 260 us -> 269 us (1.035)
  the two profiles are of different devices: /device:TPU:15 before, /device:TPU:83 now
where the time goes in v12:
time: 269 us; the launch traced here: 268 us
  waiting for transfers between devices  151 us (56%)
  starting transfers between devices  80 us (30%)
  matrix products  17.8 us (7%)
  other arithmetic  9.28 us (3%)
  local copies, waits for them, and re-layouts  8.37 us (3%)
    ppermute x12, waiting for transfers between devices, shifted(): return lax.ppermute(block, axes, route)  110 us
    ppermute x12, starting transfers between devices, shifted(): return lax.ppermute(block, axes, route)  40.8 us
    ppermute x4, waiting for transfers between devices, spread_weight(): received.append(lax.ppermute(row_block, ('y', 'c'), route))  35.4 us
    ppermute x5, starting transfers between devices, swap_cores(): return lax.ppermute(block, 'c', [(0, 1), (1, 0)])  18.8 us
    ppermute x4, starting transfers between devices, spread_weight(): received.append(lax.ppermute(row_block, ('y', 'c'), route))  12.3 us
    ppermute x1, starting transfers between devices, gather_attention(): partner = lax.ppermute(attention_local, 'zh', [(0, 1), (1, 0)])  8.17 us
    dot_general x13, matrix products, attend(): jnp.einsum('qhd,khd->hqk', query_heads, key_heads, preferred_element_type...  7.23 us
    dot_general x13, matrix products, attend(): jnp.einsum('hqk,khd->hqd', weights.astype(jnp.bfloat16), value_heads, pre...  6.16 us
  transfers between devices with their start and end apart: 22, of which 12 were waited for; matrix products, arithmetic and copies ran while one was open for 7% of the time, Pallas kernels for 0%

profile of v12, /device:TPU:83, one launch (start us, length us, event | category | flops | bytes accessed | tf_op | source)
XLA Modules:
  0.0 268.2 jit_solution(15605490710997653322)
XLA Ops:
  0.0 2.8 %collective-permute-start = (bf16[48,640]{1,0:T(8,128)(2,1)}, bf16[48,640]{1,0:T(8,128)(2,1)S(1)}, u32[]{:S(2)}, u32[]{:S(2)}) collective-permute-start(bf16[48,640]{1,0:T(8,128)(2,1)} %param.18), channel_id=1, source_target_pairs={{0,8},{8,0},{1,9},{9,1},{2,10},{10,2},{3,11},{11,3},{4,12},{12,4},... | collective-permute-start | bytes 184328 | tf_op jit(solution)/shard_map/ppermute | solution.py:31
  15.5 4.0 %collective-permute-start.1 = (bf16[96,640]{1,0:T(8,128)(2,1)S(1)}, bf16[96,640]{1,0:T(8,128)(2,1)S(1)}, u32[]{:S(2)}, u32[]{:S(2)}) collective-permute-start(bf16[96,640]{1,0:T(8,128)(2,1)S(1)} %maximum_select_fusion.3), channel_id=1, source_target_pairs={{0,16},{16,32},{32,48},{48,0},{1,17},{17,33},{33,49},{49,1},{2,18}... | collective-permute-start | bytes 368648 | tf_op jit(solution)/shard_map/ppermute | solution.py:27
  19.9 3.7 %collective-permute-start.2 = (bf16[96,640]{1,0:T(8,128)(2,1)S(1)}, bf16[96,640]{1,0:T(8,128)(2,1)S(1)}, u32[]{:S(2)}, u32[]{:S(2)}) collective-permute-start(bf16[96,640]{1,0:T(8,128)(2,1)S(1)} %maximum_select_fusion.3), channel_id=1, source_target_pairs={{0,32},{16,48},{32,0},{48,16},{1,33},{17,49},{33,1},{49,17},{2,34}... | collective-permute-start | bytes 368648 | tf_op jit(solution)/shard_map/ppermute | solution.py:27
  23.7 3.4 %collective-permute-start.3 = (bf16[96,640]{1,0:T(8,128)(2,1)S(1)}, bf16[96,640]{1,0:T(8,128)(2,1)S(1)}, u32[]{:S(2)}, u32[]{:S(2)}) collective-permute-start(bf16[96,640]{1,0:T(8,128)(2,1)S(1)} %maximum_select_fusion.3), channel_id=1, source_target_pairs={{0,48},{16,0},{32,16},{48,32},{1,49},{17,1},{33,17},{49,33},{2,50}... | collective-permute-start | bytes 368648 | tf_op jit(solution)/shard_map/ppermute | solution.py:27
  28.1 2.9 %collective-permute-done.2 = bf16[96,640]{1,0:T(8,128)(2,1)S(1)} collective-permute-done((bf16[96,640]{1,0:T(8,128)(2,1)S(1)}, bf16[96,640]{1,0:T(8,128)(2,1)S(1)}, u32[]{:S(2)}, u32[]{:S(2)}) %collective-permute-start.2) | collective-permute-done | bytes 122912 | tf_op jit(solution)/shard_map/ppermute | solution.py:27
  37.7 5.8 %collective-permute-start.19 = (bf16[384,640]{1,0:T(8,128)(2,1)S(1)}, bf16[384,640]{1,0:T(8,128)(2,1)S(1)}, u32[]{:S(2)}, u32[]{:S(2)}) collective-permute-start(bf16[384,640]{1,0:T(8,128)(2,1)S(1)} %bitcast.446), channel_id=1, source_target_pairs={{0,192},{64,256},{128,320},{192,384},{256,448},{320,0},{384,64},{4... | collective-permute-start | bytes 1474568 | tf_op jit(solution)/shard_map/ppermute | solution.py:124
  43.5 3.7 %collective-permute-start.18 = (bf16[384,640]{1,0:T(8,128)(2,1)S(1)}, bf16[384,640]{1,0:T(8,128)(2,1)S(1)}, u32[]{:S(2)}, u32[]{:S(2)}) collective-permute-start(bf16[384,640]{1,0:T(8,128)(2,1)S(1)} %bitcast.447), channel_id=1, source_target_pairs={{0,128},{64,192},{128,256},{192,320},{256,384},{320,448},{384,0},{... | collective-permute-start | bytes 1474568 | tf_op jit(solution)/shard_map/ppermute | solution.py:124
  49.8 25.1 %collective-permute-done.17 = bf16[384,640]{1,0:T(8,128)(2,1)S(1)} collective-permute-done((bf16[384,640]{1,0:T(8,128)(2,1)S(1)}, bf16[384,640]{1,0:T(8,128)(2,1)S(1)}, u32[]{:S(2)}, u32[]{:S(2)}) %collective-permute-start.17) | collective-permute-done | bytes 491552 | tf_op jit(solution)/shard_map/ppermute | solution.py:124
  74.9 2.8 %collective-permute-start.10 = (bf16[2,512,384]{1,2,0:T(8,128)(2,1)S(1)}, bf16[2,512,384]{1,2,0:T(8,128)(2,1)S(1)}, u32[]{:S(2)}, u32[]{:S(2)}) collective-permute-start(bf16[2,512,384]{1,2,0:T(8,128)(2,1)S(1)} %pad_maximum_fusion.1), channel_id=1, source_target_pairs={{0,48},{16,64},{32,80},{48,96},{64,112},{80,128},{96,144},{112,160... | collective-permute-start | bytes 2359304 | tf_op jit(solution)/shard_map/ppermute | solution.py:27
  80.5 2.7 %collective-permute-start.6 = (bf16[2,512,384]{1,2,0:T(8,128)(2,1)S(1)}, bf16[2,512,384]{1,2,0:T(8,128)(2,1)S(1)}, u32[]{:S(2)}, u32[]{:S(2)}) collective-permute-start(bf16[2,512,384]{1,2,0:T(8,128)(2,1)S(1)} %pad_maximum_fusion.1), channel_id=1, source_target_pairs={{0,16},{16,32},{32,48},{48,64},{64,80},{80,96},{96,112},{112,128},... | collective-permute-start | bytes 2359304 | tf_op jit(solution)/shard_map/ppermute | solution.py:27
  83.2 10.3 %collective-permute-done.18 = bf16[384,640]{1,0:T(8,128)(2,1)S(1)} collective-permute-done((bf16[384,640]{1,0:T(8,128)(2,1)S(1)}, bf16[384,640]{1,0:T(8,128)(2,1)S(1)}, u32[]{:S(2)}, u32[]{:S(2)}) %collective-permute-start.18) | collective-permute-done | bytes 491552 | tf_op jit(solution)/shard_map/ppermute | solution.py:124
  95.4 8.4 %collective-permute-start.5 = (bf16[2,512,384]{1,2,0:T(8,128)(2,1)S(1)}, bf16[2,512,384]{1,2,0:T(8,128)(2,1)S(1)}, u32[]{:S(2)}, u32[]{:S(2)}) collective-permute-start(bf16[2,512,384]{1,2,0:T(8,128)(2,1)S(1)} %pad_maximum_fusion.1), channel_id=1, source_target_pairs={{16,0},{32,16},{48,32},{64,48},{80,64},{96,80},{112,96},{128,112},... | collective-permute-start | bytes 2359304 | tf_op jit(solution)/shard_map/ppermute | solution.py:27
  104.6 9.4 %collective-permute-start.21 = (bf16[4,384,640]{2,1,0:T(8,128)(2,1)S(1)}, bf16[4,384,640]{2,1,0:T(8,128)(2,1)S(1)}, u32[]{:S(2)}, u32[]{:S(2)}) collective-permute-start(bf16[4,384,640]{2,1,0:T(8,128)(2,1)S(1)} %pad_maximum_fusion), channel_id=1, source_target_pairs={{0,8},{8,0},{1,9},{9,1},{2,10},{10,2},{3,11},{11,3},{4,12},{12,4},... | collective-permute-start | bytes 5898248 | tf_op jit(solution)/shard_map/ppermute | solution.py:31
  114.1 50.5 %collective-permute-done.8 = bf16[2,512,384]{1,2,0:T(8,128)(2,1)S(1)} collective-permute-done((bf16[2,512,384]{1,2,0:T(8,128)(2,1)S(1)}, bf16[2,512,384]{1,2,0:T(8,128)(2,1)S(1)}, u32[]{:S(2)}, u32[]{:S(2)}) %collective-permute-start.8) | collective-permute-done | bytes 786464 | tf_op jit(solution)/shard_map/ppermute | solution.py:27
  166.7 14.7 %collective-permute-done.6 = bf16[2,512,384]{1,2,0:T(8,128)(2,1)S(1)} collective-permute-done((bf16[2,512,384]{1,2,0:T(8,128)(2,1)S(1)}, bf16[2,512,384]{1,2,0:T(8,128)(2,1)S(1)}, u32[]{:S(2)}, u32[]{:S(2)}) %collective-permute-start.6) | collective-permute-done | bytes 786464 | tf_op jit(solution)/shard_map/ppermute | solution.py:27
  181.5 23.8 %collective-permute-done.5 = bf16[2,512,384]{1,2,0:T(8,128)(2,1)S(1)} collective-permute-done((bf16[2,512,384]{1,2,0:T(8,128)(2,1)S(1)}, bf16[2,512,384]{1,2,0:T(8,128)(2,1)S(1)}, u32[]{:S(2)}, u32[]{:S(2)}) %collective-permute-start.5) | collective-permute-done | bytes 786464 | tf_op jit(solution)/shard_map/ppermute | solution.py:27
  206.1 2.6 collective-permute-start.11
  226.7 8.2 %collective-permute-start.13 = (bf16[256,384]{0,1:T(8,128)(2,1)S(1)}, bf16[256,384]{0,1:T(8,128)(2,1)S(1)}, u32[]{:S(2)}, u32[]{:S(2)}) collective-permute-start(bf16[256,384]{0,1:T(8,128)(2,1)S(1)} %bitcast.493), channel_id=1, source_target_pairs={{0,4},{4,0},{1,5},{5,1},{2,6},{6,2},{3,7},{7,3},{8,12},{12,8},{9,1... | collective-permute-start | bytes 589832 | tf_op jit(solution)/shard_map/ppermute | solution.py:145
  235.0 4.8 %collective-permute-done.13 = bf16[256,384]{0,1:T(8,128)(2,1)S(1)} collective-permute-done((bf16[256,384]{0,1:T(8,128)(2,1)S(1)}, bf16[256,384]{0,1:T(8,128)(2,1)S(1)}, u32[]{:S(2)}, u32[]{:S(2)}) %collective-permute-start.13) | collective-permute-done | bytes 196640 | tf_op jit(solution)/shard_map/ppermute | solution.py:145
  240.0 3.1 %collective-permute-start.14 = (bf16[256,768]{0,1:T(8,128)(2,1)S(1)}, bf16[256,768]{0,1:T(8,128)(2,1)S(1)}, u32[]{:S(2)}, u32[]{:S(2)}) collective-permute-start(bf16[256,768]{0,1:T(8,128)(2,1)S(1)} %maximum_select_fusion.1), channel_id=1, source_target_pairs={{0,1},{1,2},{2,3},{3,0},{4,5},{5,6},{6,7},{7,4},{8,9},{9,10},{10,1... | collective-permute-start | bytes 1179656 | tf_op jit(solution)/shard_map/ppermute | solution.py:27
  243.1 2.7 %collective-permute-start.15 = (bf16[256,768]{0,1:T(8,128)(2,1)S(1)}, bf16[256,768]{0,1:T(8,128)(2,1)S(1)}, u32[]{:S(2)}, u32[]{:S(2)}) collective-permute-start(bf16[256,768]{0,1:T(8,128)(2,1)S(1)} %maximum_select_fusion.1), channel_id=1, source_target_pairs={{0,2},{1,3},{2,0},{3,1},{4,6},{5,7},{6,4},{7,5},{8,10},{9,11},{10,... | collective-permute-start | bytes 1179656 | tf_op jit(solution)/shard_map/ppermute | solution.py:27
  245.8 3.8 %collective-permute-start.16 = (bf16[256,768]{0,1:T(8,128)(2,1)S(1)}, bf16[256,768]{0,1:T(8,128)(2,1)S(1)}, u32[]{:S(2)}, u32[]{:S(2)}) collective-permute-start(bf16[256,768]{0,1:T(8,128)(2,1)S(1)} %maximum_select_fusion.1), channel_id=1, source_target_pairs={{0,3},{1,0},{2,1},{3,2},{4,7},{5,4},{6,5},{7,6},{8,11},{9,8},{10,9... | collective-permute-start | bytes 1179656 | tf_op jit(solution)/shard_map/ppermute | solution.py:27
  251.7 4.3 %collective-permute-done.15 = bf16[256,768]{0,1:T(8,128)(2,1)S(1)} collective-permute-done((bf16[256,768]{0,1:T(8,128)(2,1)S(1)}, bf16[256,768]{0,1:T(8,128)(2,1)S(1)}, u32[]{:S(2)}, u32[]{:S(2)}) %collective-permute-start.15) | collective-permute-done | bytes 393248 | tf_op jit(solution)/shard_map/ppermute | solution.py:27
  256.0 9.9 %collective-permute-done.16 = bf16[256,768]{0,1:T(8,128)(2,1)S(1)} collective-permute-done((bf16[256,768]{0,1:T(8,128)(2,1)S(1)}, bf16[256,768]{0,1:T(8,128)(2,1)S(1)}, u32[]{:S(2)}, u32[]{:S(2)}) %collective-permute-start.16) | collective-permute-done | bytes 393248 | tf_op jit(solution)/shard_map/ppermute | solution.py:27
  (197 shorter events, 52.9 us)
Async XLA Ops:
  0.0 15.1 %collective-permute-start = (bf16[48,640]{1,0:T(8,128)(2,1)}, bf16[48,640]{1,0:T(8,128)(2,1)S(1)}, u32[]{:S(2)}, u32[]{:S(2)}) collective-permute-start(bf16[48,640]{1,0:T(8,128)(2,1)} %param.18), channel_id=1, source_target_pairs={{0,8},{8,0},{1,9},{9,1},{2,10},{10,2},{3,11},{11,3},{4,12},{12,4},... | collective-permute-start | bytes 184328 | tf_op jit(solution)/shard_map/ppermute | solution.py:31
  7.3 25.6 %collective-permute-start.4 = (bf16[2,512,384]{1,2,0:T(8,128)(2,1)S(1)}, bf16[2,512,384]{1,2,0:T(8,128)(2,1)}, u32[]{:S(2)}, u32[]{:S(2)}) collective-permute-start(bf16[2,512,384]{1,2,0:T(8,128)(2,1)S(1)} %pad_maximum_fusion.1), channel_id=1, source_target_pairs={{0,8},{8,0},{1,9},{9,1},{2,10},{10,2},{3,11},{11,3},{4,12},{12,4},... | collective-permute-start | bytes 2359304 | tf_op jit(solution)/shard_map/ppermute | solution.py:31
  15.5 12.5 %collective-permute-start.1 = (bf16[96,640]{1,0:T(8,128)(2,1)S(1)}, bf16[96,640]{1,0:T(8,128)(2,1)S(1)}, u32[]{:S(2)}, u32[]{:S(2)}) collective-permute-start(bf16[96,640]{1,0:T(8,128)(2,1)S(1)} %maximum_select_fusion.3), channel_id=1, source_target_pairs={{0,16},{16,32},{32,48},{48,0},{1,17},{17,33},{33,49},{49,1},{2,18}... | collective-permute-start | bytes 368648 | tf_op jit(solution)/shard_map/ppermute | solution.py:27
  19.9 11.0 %collective-permute-start.2 = (bf16[96,640]{1,0:T(8,128)(2,1)S(1)}, bf16[96,640]{1,0:T(8,128)(2,1)S(1)}, u32[]{:S(2)}, u32[]{:S(2)}) collective-permute-start(bf16[96,640]{1,0:T(8,128)(2,1)S(1)} %maximum_select_fusion.3), channel_id=1, source_target_pairs={{0,32},{16,48},{32,0},{48,16},{1,33},{17,49},{33,1},{49,17},{2,34}... | collective-permute-start | bytes 368648 | tf_op jit(solution)/shard_map/ppermute | solution.py:27
  23.7 9.2 %collective-permute-start.3 = (bf16[96,640]{1,0:T(8,128)(2,1)S(1)}, bf16[96,640]{1,0:T(8,128)(2,1)S(1)}, u32[]{:S(2)}, u32[]{:S(2)}) collective-permute-start(bf16[96,640]{1,0:T(8,128)(2,1)S(1)} %maximum_select_fusion.3), channel_id=1, source_target_pairs={{0,48},{16,0},{32,16},{48,32},{1,49},{17,1},{33,17},{49,33},{2,50}... | collective-permute-start | bytes 368648 | tf_op jit(solution)/shard_map/ppermute | solution.py:27
  33.0 62.4 %collective-permute-start.9 = (bf16[2,512,384]{1,2,0:T(8,128)(2,1)S(1)}, bf16[2,512,384]{1,2,0:T(8,128)(2,1)S(1)}, u32[]{:S(2)}, u32[]{:S(2)}) collective-permute-start(bf16[2,512,384]{1,2,0:T(8,128)(2,1)S(1)} %pad_maximum_fusion.1), channel_id=1, source_target_pairs={{48,0},{64,16},{80,32},{96,48},{112,64},{128,80},{144,96},{160,112... | collective-permute-start | bytes 2359304 | tf_op jit(solution)/shard_map/ppermute | solution.py:27
  34.9 40.0 %collective-permute-start.17 = (bf16[384,640]{1,0:T(8,128)(2,1)S(1)}, bf16[384,640]{1,0:T(8,128)(2,1)S(1)}, u32[]{:S(2)}, u32[]{:S(2)}) collective-permute-start(bf16[384,640]{1,0:T(8,128)(2,1)S(1)} %bitcast.444), channel_id=1, source_target_pairs={{0,64},{64,128},{128,192},{192,256},{256,320},{320,384},{384,448},... | collective-permute-start | bytes 1474568 | tf_op jit(solution)/shard_map/ppermute | solution.py:124
  37.0 41.2 %collective-permute-start.20 = (bf16[384,640]{1,0:T(8,128)(2,1)S(1)}, bf16[384,640]{1,0:T(8,128)(2,1)S(1)}, u32[]{:S(2)}, u32[]{:S(2)}) collective-permute-start(bf16[384,640]{1,0:T(8,128)(2,1)S(1)} %bitcast.445), channel_id=1, source_target_pairs={{0,256},{64,320},{128,384},{192,448},{256,0},{320,64},{384,128},{4... | collective-permute-start | bytes 1474568 | tf_op jit(solution)/shard_map/ppermute | solution.py:124
  37.7 42.8 %collective-permute-start.19 = (bf16[384,640]{1,0:T(8,128)(2,1)S(1)}, bf16[384,640]{1,0:T(8,128)(2,1)S(1)}, u32[]{:S(2)}, u32[]{:S(2)}) collective-permute-start(bf16[384,640]{1,0:T(8,128)(2,1)S(1)} %bitcast.446), channel_id=1, source_target_pairs={{0,192},{64,256},{128,320},{192,384},{256,448},{320,0},{384,64},{4... | collective-permute-start | bytes 1474568 | tf_op jit(solution)/shard_map/ppermute | solution.py:124
  43.5 50.0 %collective-permute-start.18 = (bf16[384,640]{1,0:T(8,128)(2,1)S(1)}, bf16[384,640]{1,0:T(8,128)(2,1)S(1)}, u32[]{:S(2)}, u32[]{:S(2)}) collective-permute-start(bf16[384,640]{1,0:T(8,128)(2,1)S(1)} %bitcast.447), channel_id=1, source_target_pairs={{0,128},{64,192},{128,256},{192,320},{256,384},{320,448},{384,0},{... | collective-permute-start | bytes 1474568 | tf_op jit(solution)/shard_map/ppermute | solution.py:124
  74.9 29.7 %collective-permute-start.10 = (bf16[2,512,384]{1,2,0:T(8,128)(2,1)S(1)}, bf16[2,512,384]{1,2,0:T(8,128)(2,1)S(1)}, u32[]{:S(2)}, u32[]{:S(2)}) collective-permute-start(bf16[2,512,384]{1,2,0:T(8,128)(2,1)S(1)} %pad_maximum_fusion.1), channel_id=1, source_target_pairs={{0,48},{16,64},{32,80},{48,96},{64,112},{80,128},{96,144},{112,160... | collective-permute-start | bytes 2359304 | tf_op jit(solution)/shard_map/ppermute | solution.py:27
  78.2 86.4 %collective-permute-start.8 = (bf16[2,512,384]{1,2,0:T(8,128)(2,1)S(1)}, bf16[2,512,384]{1,2,0:T(8,128)(2,1)S(1)}, u32[]{:S(2)}, u32[]{:S(2)}) collective-permute-start(bf16[2,512,384]{1,2,0:T(8,128)(2,1)S(1)} %pad_maximum_fusion.1), channel_id=1, source_target_pairs={{0,32},{16,48},{32,64},{48,80},{64,96},{80,112},{96,128},{112,144}... | collective-permute-start | bytes 2359304 | tf_op jit(solution)/shard_map/ppermute | solution.py:27
  80.5 101.0 %collective-permute-start.6 = (bf16[2,512,384]{1,2,0:T(8,128)(2,1)S(1)}, bf16[2,512,384]{1,2,0:T(8,128)(2,1)S(1)}, u32[]{:S(2)}, u32[]{:S(2)}) collective-permute-start(bf16[2,512,384]{1,2,0:T(8,128)(2,1)S(1)} %pad_maximum_fusion.1), channel_id=1, source_target_pairs={{0,16},{16,32},{32,48},{48,64},{64,80},{80,96},{96,112},{112,128},... | collective-permute-start | bytes 2359304 | tf_op jit(solution)/shard_map/ppermute | solution.py:27
  93.5 88.0 %collective-permute-start.7 = (bf16[2,512,384]{1,2,0:T(8,128)(2,1)S(1)}, bf16[2,512,384]{1,2,0:T(8,128)(2,1)S(1)}, u32[]{:S(2)}, u32[]{:S(2)}) collective-permute-start(bf16[2,512,384]{1,2,0:T(8,128)(2,1)S(1)} %pad_maximum_fusion.1), channel_id=1, source_target_pairs={{32,0},{48,16},{64,32},{80,48},{96,64},{112,80},{128,96},{144,112}... | collective-permute-start | bytes 2359304 | tf_op jit(solution)/shard_map/ppermute | solution.py:27
  95.4 109.8 %collective-permute-start.5 = (bf16[2,512,384]{1,2,0:T(8,128)(2,1)S(1)}, bf16[2,512,384]{1,2,0:T(8,128)(2,1)S(1)}, u32[]{:S(2)}, u32[]{:S(2)}) collective-permute-start(bf16[2,512,384]{1,2,0:T(8,128)(2,1)S(1)} %pad_maximum_fusion.1), channel_id=1, source_target_pairs={{16,0},{32,16},{48,32},{64,48},{80,64},{96,80},{112,96},{128,112},... | collective-permute-start | bytes 2359304 | tf_op jit(solution)/shard_map/ppermute | solution.py:27
  104.6 107.9 %collective-permute-start.21 = (bf16[4,384,640]{2,1,0:T(8,128)(2,1)S(1)}, bf16[4,384,640]{2,1,0:T(8,128)(2,1)S(1)}, u32[]{:S(2)}, u32[]{:S(2)}) collective-permute-start(bf16[4,384,640]{2,1,0:T(8,128)(2,1)S(1)} %pad_maximum_fusion), channel_id=1, source_target_pairs={{0,8},{8,0},{1,9},{9,1},{2,10},{10,2},{3,11},{11,3},{4,12},{12,4},... | collective-permute-start | bytes 5898248 | tf_op jit(solution)/shard_map/ppermute | solution.py:31
  164.6 47.4 %collective-permute-start.12 = (bf16[2,512,384]{1,2,0:T(8,128)(2,1)S(1)}, bf16[2,512,384]{1,2,0:T(8,128)(2,1)S(1)}, u32[]{:S(2)}, u32[]{:S(2)}) collective-permute-start(bf16[2,512,384]{1,2,0:T(8,128)(2,1)S(1)} %broadcast_select_fusion), channel_id=1, source_target_pairs={{0,8},{8,0},{1,9},{9,1},{2,10},{10,2},{3,11},{11,3},{4,12},{12,4},... | collective-permute-start | bytes 2359304 | tf_op jit(solution)/shard_map/ppermute | solution.py:31
  206.1 7.7 %collective-permute-start.11 = (bf16[4,2,512,384]{2,3,1,0:T(8,128)(2,1)S(1)}, bf16[4,2,512,384]{2,3,1,0:T(8,128)(2,1)S(1)}, u32[]{:S(2)}, u32[]{:S(2)}) collective-permute-start(bf16[4,2,512,384]{2,3,1,0:T(8,128)(2,1)S(1)} %maximum_select_fusion), channel_id=1, source_target_pairs={{0,8},{8,0},{1,9},{9,1},{2,10},{10,2},{3,11},{11,3},{4,12},{12,4},... | collective-permute-start | bytes 9437192 | tf_op jit(solution)/shard_map/ppermute | solution.py:31
  226.7 13.1 %collective-permute-start.13 = (bf16[256,384]{0,1:T(8,128)(2,1)S(1)}, bf16[256,384]{0,1:T(8,128)(2,1)S(1)}, u32[]{:S(2)}, u32[]{:S(2)}) collective-permute-start(bf16[256,384]{0,1:T(8,128)(2,1)S(1)} %bitcast.493), channel_id=1, source_target_pairs={{0,4},{4,0},{1,5},{5,1},{2,6},{6,2},{3,7},{7,3},{8,12},{12,8},{9,1... | collective-permute-start | bytes 589832 | tf_op jit(solution)/shard_map/ppermute | solution.py:145
  240.0 11.6 %collective-permute-start.14 = (bf16[256,768]{0,1:T(8,128)(2,1)S(1)}, bf16[256,768]{0,1:T(8,128)(2,1)S(1)}, u32[]{:S(2)}, u32[]{:S(2)}) collective-permute-start(bf16[256,768]{0,1:T(8,128)(2,1)S(1)} %maximum_select_fusion.1), channel_id=1, source_target_pairs={{0,1},{1,2},{2,3},{3,0},{4,5},{5,6},{6,7},{7,4},{8,9},{9,10},{10,1... | collective-permute-start | bytes 1179656 | tf_op jit(solution)/shard_map/ppermute | solution.py:27
  243.1 12.9 %collective-permute-start.15 = (bf16[256,768]{0,1:T(8,128)(2,1)S(1)}, bf16[256,768]{0,1:T(8,128)(2,1)S(1)}, u32[]{:S(2)}, u32[]{:S(2)}) collective-permute-start(bf16[256,768]{0,1:T(8,128)(2,1)S(1)} %maximum_select_fusion.1), channel_id=1, source_target_pairs={{0,2},{1,3},{2,0},{3,1},{4,6},{5,7},{6,4},{7,5},{8,10},{9,11},{10,... | collective-permute-start | bytes 1179656 | tf_op jit(solution)/shard_map/ppermute | solution.py:27
  245.8 20.1 %collective-permute-start.16 = (bf16[256,768]{0,1:T(8,128)(2,1)S(1)}, bf16[256,768]{0,1:T(8,128)(2,1)S(1)}, u32[]{:S(2)}, u32[]{:S(2)}) collective-permute-start(bf16[256,768]{0,1:T(8,128)(2,1)S(1)} %maximum_select_fusion.1), channel_id=1, source_target_pairs={{0,3},{1,0},{2,1},{3,2},{4,7},{5,4},{6,5},{7,6},{8,11},{9,8},{10,9... | collective-permute-start | bytes 1179656 | tf_op jit(solution)/shard_map/ppermute | solution.py:27
  249.8 16.3 %copy-start.3 = (f32[256,640]{1,0:T(8,128)S(1)}, f32[256,640]{1,0:T(8,128)}, u32[]{:S(2)}) copy-start(f32[256,640]{1,0:T(8,128)} %fusion.142) | copy-start | bytes 1966084
  249.8 16.3 %copy-start.10 = (bf16[256,640]{1,0:T(8,128)(2,1)S(1)}, bf16[256,640]{1,0:T(8,128)(2,1)}, u32[]{:S(2)}) copy-start(bf16[256,640]{1,0:T(8,128)(2,1)} %param.17) | copy-start | bytes 983044
  (10 other events, 32.9 us)

commit v13 on v11

--- a/solution.py
+++ b/solution.py
@@ -205,7 +205,7 @@
         sign = 1 - 2 * core
         own_pair = swap_cores(packed)
         row_block = gather_weight(out_weight, sizes, is_first)
-        packed, row_block, own_pair = lax.optimization_barrier((packed, row_block, own_pair))
+        packed, own_pair = lax.optimization_barrier((packed, own_pair))
         weight_full = spread_weight(row_block, sizes, is_first)
 
         carry_state = visit_block(

time: 260 us -> 322 us (1.24)
  the two profiles are of different devices: /device:TPU:15 before, /device:TPU:11 now
where the time goes in v13:
time: 322 us; the launch traced here: 321 us
  waiting for transfers between devices  142 us (44%)
  starting transfers between devices  123 us (38%)
  local copies, waits for them, and re-layouts  20 us (6%)
  matrix products  18.1 us (6%)
  other arithmetic  16.4 us (5%)
    ppermute x12, waiting for transfers between devices, shifted(): return lax.ppermute(block, axes, route)  111 us
    ppermute x12, starting transfers between devices, shifted(): return lax.ppermute(block, axes, route)  69.3 us
    ppermute x4, waiting for transfers between devices, spread_weight(): received.append(lax.ppermute(row_block, ('y', 'c'), route))  27.3 us
    ppermute x1, starting transfers between devices, gather_attention(): partner = lax.ppermute(attention_local, 'zh', [(0, 1), (1, 0)])  25 us
    ppermute x4, starting transfers between devices, swap_cores(): return lax.ppermute(block, 'c', [(0, 1), (1, 0)])  15.7 us
    ppermute x4, starting transfers between devices, spread_weight(): received.append(lax.ppermute(row_block, ('y', 'c'), route))  13.1 us
  transfers between devices with their start and end apart: 21, of which 12 were waited for; matrix products, arithmetic and copies ran while one was open for 10% of the time, Pallas kernels for 0%

profile of v13, /device:TPU:11, one launch (start us, length us, event | category | flops | bytes accessed | tf_op | source)
XLA Modules:
  0.0 321.2 jit_solution(7949527307760543371)
XLA Ops:
  4.6 2.6 collective-permute-start
  17.0 4.0 %collective-permute-start.13 = (bf16[96,640]{1,0:T(8,128)(2,1)S(1)}, bf16[96,640]{1,0:T(8,128)(2,1)S(1)}, u32[]{:S(2)}, u32[]{:S(2)}) collective-permute-start(bf16[96,640]{1,0:T(8,128)(2,1)S(1)} %maximum_select_fusion.2), channel_id=1, source_target_pairs={{0,16},{16,32},{32,48},{48,0},{1,17},{17,33},{33,49},{49,1},{2,18}... | collective-permute-start | bytes 368648 | tf_op jit(solution)/shard_map/ppermute | solution.py:27
  21.7 5.8 %collective-permute-start.14 = (bf16[96,640]{1,0:T(8,128)(2,1)S(1)}, bf16[96,640]{1,0:T(8,128)(2,1)S(1)}, u32[]{:S(2)}, u32[]{:S(2)}) collective-permute-start(bf16[96,640]{1,0:T(8,128)(2,1)S(1)} %maximum_select_fusion.2), channel_id=1, source_target_pairs={{0,32},{16,48},{32,0},{48,16},{1,33},{17,49},{33,1},{49,17},{2,34}... | collective-permute-start | bytes 368648 | tf_op jit(solution)/shard_map/ppermute | solution.py:27
  40.7 6.7 %collective-permute-start.18 = (bf16[384,640]{1,0:T(8,128)(2,1)}, bf16[384,640]{1,0:T(8,128)(2,1)S(1)}, u32[]{:S(2)}, u32[]{:S(2)}) collective-permute-start(bf16[384,640]{1,0:T(8,128)(2,1)} %bitcast.110), channel_id=1, source_target_pairs={{0,192},{64,256},{128,320},{192,384},{256,448},{320,0},{384,64},{4... | collective-permute-start | bytes 1474568 | tf_op jit(solution)/shard_map/ppermute | solution.py:124
  47.4 2.9 collective-permute-start.17
  55.1 18.6 %collective-permute-done.18 = bf16[384,640]{1,0:T(8,128)(2,1)S(1)} collective-permute-done((bf16[384,640]{1,0:T(8,128)(2,1)}, bf16[384,640]{1,0:T(8,128)(2,1)S(1)}, u32[]{:S(2)}, u32[]{:S(2)}) %collective-permute-start.18) | collective-permute-done | bytes 491552 | tf_op jit(solution)/shard_map/ppermute | solution.py:124
  73.7 8.7 %collective-permute-done.17 = bf16[384,640]{1,0:T(8,128)(2,1)S(1)} collective-permute-done((bf16[384,640]{1,0:T(8,128)(2,1)}, bf16[384,640]{1,0:T(8,128)(2,1)S(1)}, u32[]{:S(2)}, u32[]{:S(2)}) %collective-permute-start.17) | collective-permute-done | bytes 491552 | tf_op jit(solution)/shard_map/ppermute | solution.py:124
  82.4 2.8 pad_maximum_fusion
  85.2 7.9 %collective-permute-start.20 = (bf16[4,384,640]{2,1,0:T(8,128)(2,1)}, bf16[4,384,640]{2,1,0:T(8,128)(2,1)}, u32[]{:S(2)}, u32[]{:S(2)}) collective-permute-start(bf16[4,384,640]{2,1,0:T(8,128)(2,1)} %pad_maximum_fusion), channel_id=1, source_target_pairs={{0,8},{8,0},{1,9},{9,1},{2,10},{10,2},{3,11},{11,3},{4,12},{12,4},... | collective-permute-start | bytes 5898248 | tf_op jit(solution)/shard_map/ppermute | solution.py:31
  96.3 4.6 %collective-permute-start.4 = (bf16[2,512,384]{1,2,0:T(8,128)(2,1)S(1)}, bf16[2,512,384]{1,2,0:T(8,128)(2,1)S(1)}, u32[]{:S(2)}, u32[]{:S(2)}) collective-permute-start(bf16[2,512,384]{1,2,0:T(8,128)(2,1)S(1)} %pad_maximum_fusion.1), channel_id=1, source_target_pairs={{0,32},{16,48},{32,64},{48,80},{64,96},{80,112},{96,128},{112,144}... | collective-permute-start | bytes 2359304 | tf_op jit(solution)/shard_map/ppermute | solution.py:27
  102.8 4.0 %collective-permute-start.1 = (bf16[2,512,384]{1,2,0:T(8,128)(2,1)S(1)}, bf16[2,512,384]{1,2,0:T(8,128)(2,1)S(1)}, u32[]{:S(2)}, u32[]{:S(2)}) collective-permute-start(bf16[2,512,384]{1,2,0:T(8,128)(2,1)S(1)} %pad_maximum_fusion.1), channel_id=1, source_target_pairs={{16,0},{32,16},{48,32},{64,48},{80,64},{96,80},{112,96},{128,112},... | collective-permute-start | bytes 2359304 | tf_op jit(solution)/shard_map/ppermute | solution.py:27
  109.7 32.1 %collective-permute-done.2 = bf16[2,512,384]{1,2,0:T(8,128)(2,1)S(1)} collective-permute-done((bf16[2,512,384]{1,2,0:T(8,128)(2,1)S(1)}, bf16[2,512,384]{1,2,0:T(8,128)(2,1)S(1)}, u32[]{:S(2)}, u32[]{:S(2)}) %collective-permute-start.2) | collective-permute-done | bytes 786464 | tf_op jit(solution)/shard_map/ppermute | solution.py:27
  143.8 36.9 %collective-permute-done.4 = bf16[2,512,384]{1,2,0:T(8,128)(2,1)S(1)} collective-permute-done((bf16[2,512,384]{1,2,0:T(8,128)(2,1)S(1)}, bf16[2,512,384]{1,2,0:T(8,128)(2,1)S(1)}, u32[]{:S(2)}, u32[]{:S(2)}) %collective-permute-start.4) | collective-permute-done | bytes 786464 | tf_op jit(solution)/shard_map/ppermute | solution.py:27
  180.6 33.0 %collective-permute-start.5 = (bf16[2,512,384]{1,2,0:T(8,128)(2,1)S(1)}, bf16[2,512,384]{1,2,0:T(8,128)(2,1)S(1)}, u32[]{:S(2)}, u32[]{:S(2)}) collective-permute-start(bf16[2,512,384]{1,2,0:T(8,128)(2,1)S(1)} %pad_maximum_fusion.1), channel_id=1, source_target_pairs={{48,0},{64,16},{80,32},{96,48},{112,64},{128,80},{144,96},{160,112... | collective-permute-start | bytes 2359304 | tf_op jit(solution)/shard_map/ppermute | solution.py:27
  214.0 4.9 %collective-permute-done.3 = bf16[2,512,384]{1,2,0:T(8,128)(2,1)S(1)} collective-permute-done((bf16[2,512,384]{1,2,0:T(8,128)(2,1)S(1)}, bf16[2,512,384]{1,2,0:T(8,128)(2,1)S(1)}, u32[]{:S(2)}, u32[]{:S(2)}) %collective-permute-start.3) | collective-permute-done | bytes 786464 | tf_op jit(solution)/shard_map/ppermute | solution.py:27
  219.0 17.6 %collective-permute-done.5 = bf16[2,512,384]{1,2,0:T(8,128)(2,1)S(1)} collective-permute-done((bf16[2,512,384]{1,2,0:T(8,128)(2,1)S(1)}, bf16[2,512,384]{1,2,0:T(8,128)(2,1)S(1)}, u32[]{:S(2)}, u32[]{:S(2)}) %collective-permute-start.5) | collective-permute-done | bytes 786464 | tf_op jit(solution)/shard_map/ppermute | solution.py:27
  237.2 3.2 %collective-permute-start.7 = (bf16[5,2,512,384]{2,3,1,0:T(8,128)(2,1)S(1)}, bf16[5,2,512,384]{2,3,1,0:T(8,128)(2,1)S(1)}, u32[]{:S(2)}, u32[]{:S(2)}) collective-permute-start(bf16[5,2,512,384]{2,3,1,0:T(8,128)(2,1)S(1)} %broadcast_select_fusion), channel_id=1, source_target_pairs={{0,8},{8,0},{1,9},{9,1},{2,10},{10,2},{3,11},{11,3},{4,12},{12,4},... | collective-permute-start | bytes 11796488 | tf_op jit(solution)/shard_map/ppermute | solution.py:31
  262.5 25.0 %collective-permute-start.8 = (bf16[256,384]{0,1:T(8,128)(2,1)S(1)}, bf16[256,384]{0,1:T(8,128)(2,1)S(1)}, u32[]{:S(2)}, u32[]{:S(2)}) collective-permute-start(bf16[256,384]{0,1:T(8,128)(2,1)S(1)} %bitcast.495), channel_id=1, source_target_pairs={{0,4},{4,0},{1,5},{5,1},{2,6},{6,2},{3,7},{7,3},{8,12},{12,8},{9,1... | collective-permute-start | bytes 589832 | tf_op jit(solution)/shard_map/ppermute | solution.py:145
  288.8 4.1 %collective-permute-done.8 = bf16[256,384]{0,1:T(8,128)(2,1)S(1)} collective-permute-done((bf16[256,384]{0,1:T(8,128)(2,1)S(1)}, bf16[256,384]{0,1:T(8,128)(2,1)S(1)}, u32[]{:S(2)}, u32[]{:S(2)}) %collective-permute-start.8) | collective-permute-done | bytes 196640 | tf_op jit(solution)/shard_map/ppermute | solution.py:145
  293.0 3.1 collective-permute-start.9
  296.1 2.8 collective-permute-start.10
  298.9 3.8 %collective-permute-start.11 = (bf16[256,768]{0,1:T(8,128)(2,1)S(1)}, bf16[256,768]{0,1:T(8,128)(2,1)S(1)}, u32[]{:S(2)}, u32[]{:S(2)}) collective-permute-start(bf16[256,768]{0,1:T(8,128)(2,1)S(1)} %maximum_select_fusion), channel_id=1, source_target_pairs={{0,3},{1,0},{2,1},{3,2},{4,7},{5,4},{6,5},{7,6},{8,11},{9,8},{10,9... | collective-permute-start | bytes 1179656 | tf_op jit(solution)/shard_map/ppermute | solution.py:27
  305.0 4.3 %collective-permute-done.10 = bf16[256,768]{0,1:T(8,128)(2,1)S(1)} collective-permute-done((bf16[256,768]{0,1:T(8,128)(2,1)S(1)}, bf16[256,768]{0,1:T(8,128)(2,1)S(1)}, u32[]{:S(2)}, u32[]{:S(2)}) %collective-permute-start.10) | collective-permute-done | bytes 393248 | tf_op jit(solution)/shard_map/ppermute | solution.py:27
  309.3 9.6 %collective-permute-done.11 = bf16[256,768]{0,1:T(8,128)(2,1)S(1)} collective-permute-done((bf16[256,768]{0,1:T(8,128)(2,1)S(1)}, bf16[256,768]{0,1:T(8,128)(2,1)S(1)}, u32[]{:S(2)}, u32[]{:S(2)}) %collective-permute-start.11) | collective-permute-done | bytes 393248 | tf_op jit(solution)/shard_map/ppermute | solution.py:27
  (219 shorter events, 70.6 us)
Async XLA Ops:
  4.6 88.6 %collective-permute-start = (bf16[2,512,384]{1,2,0:T(8,128)(2,1)S(1)}, bf16[2,512,384]{1,2,0:T(8,128)(2,1)}, u32[]{:S(2)}, u32[]{:S(2)}) collective-permute-start(bf16[2,512,384]{1,2,0:T(8,128)(2,1)S(1)} %pad_maximum_fusion.1), channel_id=1, source_target_pairs={{0,8},{8,0},{1,9},{9,1},{2,10},{10,2},{3,11},{11,3},{4,12},{12,4},... | collective-permute-start | bytes 2359304 | tf_op jit(solution)/shard_map/ppermute | solution.py:31
  7.2 8.8 %collective-permute-start.12 = (bf16[48,640]{1,0:T(8,128)(2,1)S(1)}, bf16[48,640]{1,0:T(8,128)(2,1)}, u32[]{:S(2)}, u32[]{:S(2)}) collective-permute-start(bf16[48,640]{1,0:T(8,128)(2,1)S(1)} %copy-done.15), channel_id=1, source_target_pairs={{0,8},{8,0},{1,9},{9,1},{2,10},{10,2},{3,11},{11,3},{4,12},{12,4},... | collective-permute-start | bytes 184328 | tf_op jit(solution)/shard_map/ppermute | solution.py:31
  17.0 15.1 %collective-permute-start.13 = (bf16[96,640]{1,0:T(8,128)(2,1)S(1)}, bf16[96,640]{1,0:T(8,128)(2,1)S(1)}, u32[]{:S(2)}, u32[]{:S(2)}) collective-permute-start(bf16[96,640]{1,0:T(8,128)(2,1)S(1)} %maximum_select_fusion.2), channel_id=1, source_target_pairs={{0,16},{16,32},{32,48},{48,0},{1,17},{17,33},{33,49},{49,1},{2,18}... | collective-permute-start | bytes 368648 | tf_op jit(solution)/shard_map/ppermute | solution.py:27
  21.7 12.0 %collective-permute-start.14 = (bf16[96,640]{1,0:T(8,128)(2,1)S(1)}, bf16[96,640]{1,0:T(8,128)(2,1)S(1)}, u32[]{:S(2)}, u32[]{:S(2)}) collective-permute-start(bf16[96,640]{1,0:T(8,128)(2,1)S(1)} %maximum_select_fusion.2), channel_id=1, source_target_pairs={{0,32},{16,48},{32,0},{48,16},{1,33},{17,49},{33,1},{49,17},{2,34}... | collective-permute-start | bytes 368648 | tf_op jit(solution)/shard_map/ppermute | solution.py:27
  27.5 9.0 %collective-permute-start.15 = (bf16[96,640]{1,0:T(8,128)(2,1)S(1)}, bf16[96,640]{1,0:T(8,128)(2,1)S(1)}, u32[]{:S(2)}, u32[]{:S(2)}) collective-permute-start(bf16[96,640]{1,0:T(8,128)(2,1)S(1)} %maximum_select_fusion.2), channel_id=1, source_target_pairs={{0,48},{16,0},{32,16},{48,32},{1,49},{17,1},{33,17},{49,33},{2,50}... | collective-permute-start | bytes 368648 | tf_op jit(solution)/shard_map/ppermute | solution.py:27
  37.2 18.0 %collective-permute-start.16 = (bf16[384,640]{1,0:T(8,128)(2,1)}, bf16[384,640]{1,0:T(8,128)(2,1)S(1)}, u32[]{:S(2)}, u32[]{:S(2)}) collective-permute-start(bf16[384,640]{1,0:T(8,128)(2,1)} %bitcast.110), channel_id=1, source_target_pairs={{0,64},{64,128},{128,192},{192,256},{256,320},{320,384},{384,448},... | collective-permute-start | bytes 1474568 | tf_op jit(solution)/shard_map/ppermute | solution.py:124
  39.2 15.9 %collective-permute-start.19 = (bf16[384,640]{1,0:T(8,128)(2,1)}, bf16[384,640]{1,0:T(8,128)(2,1)}, u32[]{:S(2)}, u32[]{:S(2)}) collective-permute-start(bf16[384,640]{1,0:T(8,128)(2,1)} %bitcast.110), channel_id=1, source_target_pairs={{0,256},{64,320},{128,384},{192,448},{256,0},{320,64},{384,128},{4... | collective-permute-start | bytes 1474568 | tf_op jit(solution)/shard_map/ppermute | solution.py:124
  40.7 33.0 %collective-permute-start.18 = (bf16[384,640]{1,0:T(8,128)(2,1)}, bf16[384,640]{1,0:T(8,128)(2,1)S(1)}, u32[]{:S(2)}, u32[]{:S(2)}) collective-permute-start(bf16[384,640]{1,0:T(8,128)(2,1)} %bitcast.110), channel_id=1, source_target_pairs={{0,192},{64,256},{128,320},{192,384},{256,448},{320,0},{384,64},{4... | collective-permute-start | bytes 1474568 | tf_op jit(solution)/shard_map/ppermute | solution.py:124
  47.4 35.0 %collective-permute-start.17 = (bf16[384,640]{1,0:T(8,128)(2,1)}, bf16[384,640]{1,0:T(8,128)(2,1)S(1)}, u32[]{:S(2)}, u32[]{:S(2)}) collective-permute-start(bf16[384,640]{1,0:T(8,128)(2,1)} %bitcast.110), channel_id=1, source_target_pairs={{0,128},{64,192},{128,256},{192,320},{256,384},{320,448},{384,0},{... | collective-permute-start | bytes 1474568 | tf_op jit(solution)/shard_map/ppermute | solution.py:124
  85.2 21.6 %copy-start.11 = (pred[256,512]{0,1:T(8,128)(4,1)S(1)}, pred[256,512]{0,1:T(8,128)(4,1)}, u32[]{:S(2)}) copy-start(pred[256,512]{0,1:T(8,128)(4,1)} %pad_add_fusion) | copy-start | bytes 393220
  85.2 159.4 %collective-permute-start.20 = (bf16[4,384,640]{2,1,0:T(8,128)(2,1)}, bf16[4,384,640]{2,1,0:T(8,128)(2,1)}, u32[]{:S(2)}, u32[]{:S(2)}) collective-permute-start(bf16[4,384,640]{2,1,0:T(8,128)(2,1)} %pad_maximum_fusion), channel_id=1, source_target_pairs={{0,8},{8,0},{1,9},{9,1},{2,10},{10,2},{3,11},{11,3},{4,12},{12,4},... | collective-permute-start | bytes 5898248 | tf_op jit(solution)/shard_map/ppermute | solution.py:31
  94.1 47.8 %collective-permute-start.2 = (bf16[2,512,384]{1,2,0:T(8,128)(2,1)S(1)}, bf16[2,512,384]{1,2,0:T(8,128)(2,1)S(1)}, u32[]{:S(2)}, u32[]{:S(2)}) collective-permute-start(bf16[2,512,384]{1,2,0:T(8,128)(2,1)S(1)} %pad_maximum_fusion.1), channel_id=1, source_target_pairs={{0,16},{16,32},{32,48},{48,64},{64,80},{80,96},{96,112},{112,128},... | collective-permute-start | bytes 2359304 | tf_op jit(solution)/shard_map/ppermute | solution.py:27
  96.3 84.4 %collective-permute-start.4 = (bf16[2,512,384]{1,2,0:T(8,128)(2,1)S(1)}, bf16[2,512,384]{1,2,0:T(8,128)(2,1)S(1)}, u32[]{:S(2)}, u32[]{:S(2)}) collective-permute-start(bf16[2,512,384]{1,2,0:T(8,128)(2,1)S(1)} %pad_maximum_fusion.1), channel_id=1, source_target_pairs={{0,32},{16,48},{32,64},{48,80},{64,96},{80,112},{96,128},{112,144}... | collective-permute-start | bytes 2359304 | tf_op jit(solution)/shard_map/ppermute | solution.py:27
  100.9 112.9 %collective-permute-start.6 = (bf16[2,512,384]{1,2,0:T(8,128)(2,1)S(1)}, bf16[2,512,384]{1,2,0:T(8,128)(2,1)S(1)}, u32[]{:S(2)}, u32[]{:S(2)}) collective-permute-start(bf16[2,512,384]{1,2,0:T(8,128)(2,1)S(1)} %pad_maximum_fusion.1), channel_id=1, source_target_pairs={{0,48},{16,64},{32,80},{48,96},{64,112},{80,128},{96,144},{112,160... | collective-permute-start | bytes 2359304 | tf_op jit(solution)/shard_map/ppermute | solution.py:27
  102.8 111.0 %collective-permute-start.1 = (bf16[2,512,384]{1,2,0:T(8,128)(2,1)S(1)}, bf16[2,512,384]{1,2,0:T(8,128)(2,1)S(1)}, u32[]{:S(2)}, u32[]{:S(2)}) collective-permute-start(bf16[2,512,384]{1,2,0:T(8,128)(2,1)S(1)} %pad_maximum_fusion.1), channel_id=1, source_target_pairs={{16,0},{32,16},{48,32},{64,48},{80,64},{96,80},{112,96},{128,112},... | collective-permute-start | bytes 2359304 | tf_op jit(solution)/shard_map/ppermute | solution.py:27
  141.8 77.1 %collective-permute-start.3 = (bf16[2,512,384]{1,2,0:T(8,128)(2,1)S(1)}, bf16[2,512,384]{1,2,0:T(8,128)(2,1)S(1)}, u32[]{:S(2)}, u32[]{:S(2)}) collective-permute-start(bf16[2,512,384]{1,2,0:T(8,128)(2,1)S(1)} %pad_maximum_fusion.1), channel_id=1, source_target_pairs={{32,0},{48,16},{64,32},{80,48},{96,64},{112,80},{128,96},{144,112}... | collective-permute-start | bytes 2359304 | tf_op jit(solution)/shard_map/ppermute | solution.py:27
  180.6 55.9 %collective-permute-start.5 = (bf16[2,512,384]{1,2,0:T(8,128)(2,1)S(1)}, bf16[2,512,384]{1,2,0:T(8,128)(2,1)S(1)}, u32[]{:S(2)}, u32[]{:S(2)}) collective-permute-start(bf16[2,512,384]{1,2,0:T(8,128)(2,1)S(1)} %pad_maximum_fusion.1), channel_id=1, source_target_pairs={{48,0},{64,16},{80,32},{96,48},{112,64},{128,80},{144,96},{160,112... | collective-permute-start | bytes 2359304 | tf_op jit(solution)/shard_map/ppermute | solution.py:27
  237.2 10.9 %collective-permute-start.7 = (bf16[5,2,512,384]{2,3,1,0:T(8,128)(2,1)S(1)}, bf16[5,2,512,384]{2,3,1,0:T(8,128)(2,1)S(1)}, u32[]{:S(2)}, u32[]{:S(2)}) collective-permute-start(bf16[5,2,512,384]{2,3,1,0:T(8,128)(2,1)S(1)} %broadcast_select_fusion), channel_id=1, source_target_pairs={{0,8},{8,0},{1,9},{9,1},{2,10},{10,2},{3,11},{11,3},{4,12},{12,4},... | collective-permute-start | bytes 11796488 | tf_op jit(solution)/shard_map/ppermute | solution.py:31
  262.5 30.3 %collective-permute-start.8 = (bf16[256,384]{0,1:T(8,128)(2,1)S(1)}, bf16[256,384]{0,1:T(8,128)(2,1)S(1)}, u32[]{:S(2)}, u32[]{:S(2)}) collective-permute-start(bf16[256,384]{0,1:T(8,128)(2,1)S(1)} %bitcast.495), channel_id=1, source_target_pairs={{0,4},{4,0},{1,5},{5,1},{2,6},{6,2},{3,7},{7,3},{8,12},{12,8},{9,1... | collective-permute-start | bytes 589832 | tf_op jit(solution)/shard_map/ppermute | solution.py:145
  293.0 12.0 %collective-permute-start.9 = (bf16[256,768]{0,1:T(8,128)(2,1)S(1)}, bf16[256,768]{0,1:T(8,128)(2,1)S(1)}, u32[]{:S(2)}, u32[]{:S(2)}) collective-permute-start(bf16[256,768]{0,1:T(8,128)(2,1)S(1)} %maximum_select_fusion), channel_id=1, source_target_pairs={{0,1},{1,2},{2,3},{3,0},{4,5},{5,6},{6,7},{7,4},{8,9},{9,10},{10,1... | collective-permute-start | bytes 1179656 | tf_op jit(solution)/shard_map/ppermute | solution.py:27
  296.1 13.2 %collective-permute-start.10 = (bf16[256,768]{0,1:T(8,128)(2,1)S(1)}, bf16[256,768]{0,1:T(8,128)(2,1)S(1)}, u32[]{:S(2)}, u32[]{:S(2)}) collective-permute-start(bf16[256,768]{0,1:T(8,128)(2,1)S(1)} %maximum_select_fusion), channel_id=1, source_target_pairs={{0,2},{1,3},{2,0},{3,1},{4,6},{5,7},{6,4},{7,5},{8,10},{9,11},{10,... | collective-permute-start | bytes 1179656 | tf_op jit(solution)/shard_map/ppermute | solution.py:27
  298.9 20.1 %collective-permute-start.11 = (bf16[256,768]{0,1:T(8,128)(2,1)S(1)}, bf16[256,768]{0,1:T(8,128)(2,1)S(1)}, u32[]{:S(2)}, u32[]{:S(2)}) collective-permute-start(bf16[256,768]{0,1:T(8,128)(2,1)S(1)} %maximum_select_fusion), channel_id=1, source_target_pairs={{0,3},{1,0},{2,1},{3,2},{4,7},{5,4},{6,5},{7,6},{8,11},{9,8},{10,9... | collective-permute-start | bytes 1179656 | tf_op jit(solution)/shard_map/ppermute | solution.py:27
  302.8 16.3 %copy-start.13 = (f32[256,640]{1,0:T(8,128)S(1)}, f32[256,640]{1,0:T(8,128)}, u32[]{:S(2)}) copy-start(f32[256,640]{1,0:T(8,128)} %fusion.142) | copy-start | bytes 1966084
  302.8 16.3 %copy-start.19 = (bf16[256,640]{1,0:T(8,128)(2,1)S(1)}, bf16[256,640]{1,0:T(8,128)(2,1)}, u32[]{:S(2)}) copy-start(bf16[256,640]{1,0:T(8,128)(2,1)} %param.17) | copy-start | bytes 983044
  (18 other events, 61.9 us)

commit v14 on v11

--- a/solution.py
+++ b/solution.py
@@ -206,7 +206,6 @@
         own_pair = swap_cores(packed)
         row_block = gather_weight(out_weight, sizes, is_first)
         packed, row_block, own_pair = lax.optimization_barrier((packed, row_block, own_pair))
-        weight_full = spread_weight(row_block, sizes, is_first)
 
         carry_state = visit_block(
             empty_state(head_count, row_count), packed, seq_index, query_heads, query_clip, context
@@ -225,6 +224,8 @@
             carry_state = visit_block(
                 carry_state, below[d], seq_index - 2 * d, query_heads, query_clip, context
             )
+        row_block, above[3], below[3] = lax.optimization_barrier((row_block, above[3], below[3]))
+        weight_full = spread_weight(row_block, sizes, is_first)
         selected = jnp.where(
             is_first,
             jnp.stack([above[1], above[2], above[3], below[1], below[2]]),

time: 260 us -> 296 us (1.14)
  the two profiles are of different devices: /device:TPU:15 before, /device:TPU:91 now
where the time goes in v14:
time: 296 us; the launch traced here: 295 us
  starting transfers between devices  166 us (56%)
  waiting for transfers between devices  78.2 us (26%)
  matrix products  16.8 us (6%)
  local copies, waits for them, and re-layouts  16.5 us (6%)
  other arithmetic  15.2 us (5%)
    ppermute x12, starting transfers between devices, shifted(): return lax.ppermute(block, axes, route)  119 us
    ppermute x12, waiting for transfers between devices, shifted(): return lax.ppermute(block, axes, route)  39.4 us
    ppermute x4, waiting for transfers between devices, spread_weight(): received.append(lax.ppermute(row_block, ('y', 'c'), route))  32.9 us
    ppermute x4, starting transfers between devices, spread_weight(): received.append(lax.ppermute(row_block, ('y', 'c'), route))  29.5 us
    ppermute x4, starting transfers between devices, swap_cores(): return lax.ppermute(block, 'c', [(0, 1), (1, 0)])  12.4 us
    concatenate x13, other arithmetic, allowed_keys(): return jnp.concatenate([same_clip, page_ok], axis=1)  7.26 us
    unnamed x67, local copies, waits for them, and re-layouts  7.15 us
    dot_general x13, matrix products, attend(): jnp.einsum('qhd,khd->hqk', query_heads, key_heads, preferred_element_type...  6.27 us
  transfers between devices with their start and end apart: 21, of which 11 were waited for; matrix products, arithmetic and copies ran while one was open for 10% of the time, Pallas kernels for 0%

profile of v14, /device:TPU:91, one launch (start us, length us, event | category | flops | bytes accessed | tf_op | source)
XLA Modules:
  0.0 294.8 jit_solution(12132312602106358527)
XLA Ops:
  0.0 2.8 collective-permute-start
  21.5 4.0 %collective-permute-start.1 = (bf16[96,640]{1,0:T(8,128)(2,1)S(1)}, bf16[96,640]{1,0:T(8,128)(2,1)S(1)}, u32[]{:S(2)}, u32[]{:S(2)}) collective-permute-start(bf16[96,640]{1,0:T(8,128)(2,1)S(1)} %maximum_select_fusion.2), channel_id=1, source_target_pairs={{0,16},{16,32},{32,48},{48,0},{1,17},{17,33},{33,49},{49,1},{2,18}... | collective-permute-start | bytes 368648 | tf_op jit(solution)/shard_map/ppermute | solution.py:27
  25.9 3.7 %collective-permute-start.2 = (bf16[96,640]{1,0:T(8,128)(2,1)S(1)}, bf16[96,640]{1,0:T(8,128)(2,1)S(1)}, u32[]{:S(2)}, u32[]{:S(2)}) collective-permute-start(bf16[96,640]{1,0:T(8,128)(2,1)S(1)} %maximum_select_fusion.2), channel_id=1, source_target_pairs={{0,32},{16,48},{32,0},{48,16},{1,33},{17,49},{33,1},{49,17},{2,34}... | collective-permute-start | bytes 368648 | tf_op jit(solution)/shard_map/ppermute | solution.py:27
  29.7 3.4 %collective-permute-start.3 = (bf16[96,640]{1,0:T(8,128)(2,1)S(1)}, bf16[96,640]{1,0:T(8,128)(2,1)S(1)}, u32[]{:S(2)}, u32[]{:S(2)}) collective-permute-start(bf16[96,640]{1,0:T(8,128)(2,1)S(1)} %maximum_select_fusion.2), channel_id=1, source_target_pairs={{0,48},{16,0},{32,16},{48,32},{1,49},{17,1},{33,17},{49,33},{2,50}... | collective-permute-start | bytes 368648 | tf_op jit(solution)/shard_map/ppermute | solution.py:27
  34.1 2.9 collective-permute-done.2
  40.9 7.5 %collective-permute-start.8 = (bf16[2,512,384]{1,2,0:T(8,128)(2,1)S(1)}, bf16[2,512,384]{1,2,0:T(8,128)(2,1)S(1)}, u32[]{:S(2)}, u32[]{:S(2)}) collective-permute-start(bf16[2,512,384]{1,2,0:T(8,128)(2,1)S(1)} %pad_maximum_fusion.1), channel_id=1, source_target_pairs={{0,32},{16,48},{32,64},{48,80},{64,96},{80,112},{96,128},{112,144}... | collective-permute-start | bytes 2359304 | tf_op jit(solution)/shard_map/ppermute | solution.py:27
  50.3 5.5 %collective-permute-start.10 = (bf16[2,512,384]{1,2,0:T(8,128)(2,1)S(1)}, bf16[2,512,384]{1,2,0:T(8,128)(2,1)S(1)}, u32[]{:S(2)}, u32[]{:S(2)}) collective-permute-start(bf16[2,512,384]{1,2,0:T(8,128)(2,1)S(1)} %pad_maximum_fusion.1), channel_id=1, source_target_pairs={{0,48},{16,64},{32,80},{48,96},{64,112},{80,128},{96,144},{112,160... | collective-permute-start | bytes 2359304 | tf_op jit(solution)/shard_map/ppermute | solution.py:27
  60.7 9.8 %collective-permute-done.9 = bf16[2,512,384]{1,2,0:T(8,128)(2,1)S(1)} collective-permute-done((bf16[2,512,384]{1,2,0:T(8,128)(2,1)S(1)}, bf16[2,512,384]{1,2,0:T(8,128)(2,1)S(1)}, u32[]{:S(2)}, u32[]{:S(2)}) %collective-permute-start.9) | collective-permute-done | bytes 786464 | tf_op jit(solution)/shard_map/ppermute | solution.py:27
  70.4 79.1 %collective-permute-start.7 = (bf16[2,512,384]{1,2,0:T(8,128)(2,1)S(1)}, bf16[2,512,384]{1,2,0:T(8,128)(2,1)S(1)}, u32[]{:S(2)}, u32[]{:S(2)}) collective-permute-start(bf16[2,512,384]{1,2,0:T(8,128)(2,1)S(1)} %pad_maximum_fusion.1), channel_id=1, source_target_pairs={{32,0},{48,16},{64,32},{80,48},{96,64},{112,80},{128,96},{144,112}... | collective-permute-start | bytes 2359304 | tf_op jit(solution)/shard_map/ppermute | solution.py:27
  152.4 24.8 %collective-permute-start.18 = (bf16[384,640]{1,0:T(8,128)(2,1)S(1)}, bf16[384,640]{1,0:T(8,128)(2,1)S(1)}, u32[]{:S(2)}, u32[]{:S(2)}) collective-permute-start(bf16[384,640]{1,0:T(8,128)(2,1)S(1)} %bitcast.454), channel_id=1, source_target_pairs={{0,192},{64,256},{128,320},{192,384},{256,448},{320,0},{384,64},{4... | collective-permute-start | bytes 1474568 | tf_op jit(solution)/shard_map/ppermute | solution.py:124
  179.5 8.8 %collective-permute-done.7 = bf16[2,512,384]{1,2,0:T(8,128)(2,1)S(1)} collective-permute-done((bf16[2,512,384]{1,2,0:T(8,128)(2,1)S(1)}, bf16[2,512,384]{1,2,0:T(8,128)(2,1)S(1)}, u32[]{:S(2)}, u32[]{:S(2)}) %collective-permute-start.7) | collective-permute-done | bytes 786464 | tf_op jit(solution)/shard_map/ppermute | solution.py:27
  189.0 5.4 %collective-permute-start.11 = (bf16[5,2,512,384]{2,3,1,0:T(8,128)(2,1)S(1)}, bf16[5,2,512,384]{2,3,1,0:T(8,128)(2,1)S(1)}, u32[]{:S(2)}, u32[]{:S(2)}) collective-permute-start(bf16[5,2,512,384]{2,3,1,0:T(8,128)(2,1)S(1)} %broadcast_select_fusion), channel_id=1, source_target_pairs={{0,8},{8,0},{1,9},{9,1},{2,10},{10,2},{3,11},{11,3},{4,12},{12,4},... | collective-permute-start | bytes 11796488 | tf_op jit(solution)/shard_map/ppermute | solution.py:31
  197.7 5.6 %collective-permute-done.16 = bf16[384,640]{1,0:T(8,128)(2,1)S(1)} collective-permute-done((bf16[384,640]{1,0:T(8,128)(2,1)S(1)}, bf16[384,640]{1,0:T(8,128)(2,1)S(1)}, u32[]{:S(2)}, u32[]{:S(2)}) %collective-permute-start.16) | collective-permute-done | bytes 491552 | tf_op jit(solution)/shard_map/ppermute | solution.py:124
  203.3 6.3 %collective-permute-done.18 = bf16[384,640]{1,0:T(8,128)(2,1)S(1)} collective-permute-done((bf16[384,640]{1,0:T(8,128)(2,1)S(1)}, bf16[384,640]{1,0:T(8,128)(2,1)S(1)}, u32[]{:S(2)}, u32[]{:S(2)}) %collective-permute-start.18) | collective-permute-done | bytes 491552 | tf_op jit(solution)/shard_map/ppermute | solution.py:124
  209.6 21.0 %collective-permute-done.17 = bf16[384,640]{1,0:T(8,128)(2,1)S(1)} collective-permute-done((bf16[384,640]{1,0:T(8,128)(2,1)S(1)}, bf16[384,640]{1,0:T(8,128)(2,1)S(1)}, u32[]{:S(2)}, u32[]{:S(2)}) %collective-permute-start.17) | collective-permute-done | bytes 491552 | tf_op jit(solution)/shard_map/ppermute | solution.py:124
  231.0 2.2 collective-permute-start.20
  254.6 5.8 %collective-permute-start.12 = (bf16[256,384]{0,1:T(8,128)(2,1)S(1)}, bf16[256,384]{0,1:T(8,128)(2,1)S(1)}, u32[]{:S(2)}, u32[]{:S(2)}) collective-permute-start(bf16[256,384]{0,1:T(8,128)(2,1)S(1)} %bitcast.501), channel_id=1, source_target_pairs={{0,4},{4,0},{1,5},{5,1},{2,6},{6,2},{3,7},{7,3},{8,12},{12,8},{9,1... | collective-permute-start | bytes 589832 | tf_op jit(solution)/shard_map/ppermute | solution.py:145
  260.6 5.8 %collective-permute-done.12 = bf16[256,384]{0,1:T(8,128)(2,1)S(1)} collective-permute-done((bf16[256,384]{0,1:T(8,128)(2,1)S(1)}, bf16[256,384]{0,1:T(8,128)(2,1)S(1)}, u32[]{:S(2)}, u32[]{:S(2)}) %collective-permute-start.12) | collective-permute-done | bytes 196640 | tf_op jit(solution)/shard_map/ppermute | solution.py:145
  266.5 3.1 %collective-permute-start.13 = (bf16[256,768]{0,1:T(8,128)(2,1)S(1)}, bf16[256,768]{0,1:T(8,128)(2,1)S(1)}, u32[]{:S(2)}, u32[]{:S(2)}) collective-permute-start(bf16[256,768]{0,1:T(8,128)(2,1)S(1)} %maximum_select_fusion), channel_id=1, source_target_pairs={{0,1},{1,2},{2,3},{3,0},{4,5},{5,6},{6,7},{7,4},{8,9},{9,10},{10,1... | collective-permute-start | bytes 1179656 | tf_op jit(solution)/shard_map/ppermute | solution.py:27
  269.7 2.7 collective-permute-start.14
  272.4 3.8 %collective-permute-start.15 = (bf16[256,768]{0,1:T(8,128)(2,1)S(1)}, bf16[256,768]{0,1:T(8,128)(2,1)S(1)}, u32[]{:S(2)}, u32[]{:S(2)}) collective-permute-start(bf16[256,768]{0,1:T(8,128)(2,1)S(1)} %maximum_select_fusion), channel_id=1, source_target_pairs={{0,3},{1,0},{2,1},{3,2},{4,7},{5,4},{6,5},{7,6},{8,11},{9,8},{10,9... | collective-permute-start | bytes 1179656 | tf_op jit(solution)/shard_map/ppermute | solution.py:27
  277.8 4.3 %collective-permute-done.14 = bf16[256,768]{0,1:T(8,128)(2,1)S(1)} collective-permute-done((bf16[256,768]{0,1:T(8,128)(2,1)S(1)}, bf16[256,768]{0,1:T(8,128)(2,1)S(1)}, u32[]{:S(2)}, u32[]{:S(2)}) %collective-permute-start.14) | collective-permute-done | bytes 393248 | tf_op jit(solution)/shard_map/ppermute | solution.py:27
  282.1 10.4 %collective-permute-done.15 = bf16[256,768]{0,1:T(8,128)(2,1)S(1)} collective-permute-done((bf16[256,768]{0,1:T(8,128)(2,1)S(1)}, bf16[256,768]{0,1:T(8,128)(2,1)S(1)}, u32[]{:S(2)}, u32[]{:S(2)}) %collective-permute-start.15) | collective-permute-done | bytes 393248 | tf_op jit(solution)/shard_map/ppermute | solution.py:27
  292.6 2.2 fusion.27
  (235 shorter events, 62.0 us)
Async XLA Ops:
  0.0 21.5 %collective-permute-start = (bf16[48,640]{1,0:T(8,128)(2,1)}, bf16[48,640]{1,0:T(8,128)(2,1)S(1)}, u32[]{:S(2)}, u32[]{:S(2)}) collective-permute-start(bf16[48,640]{1,0:T(8,128)(2,1)} %param.18), channel_id=1, source_target_pairs={{0,8},{8,0},{1,9},{9,1},{2,10},{10,2},{3,11},{11,3},{4,12},{12,4},... | collective-permute-start | bytes 184328 | tf_op jit(solution)/shard_map/ppermute | solution.py:31
  7.3 31.6 %collective-permute-start.4 = (bf16[2,512,384]{1,2,0:T(8,128)(2,1)S(1)}, bf16[2,512,384]{1,2,0:T(8,128)(2,1)}, u32[]{:S(2)}, u32[]{:S(2)}) collective-permute-start(bf16[2,512,384]{1,2,0:T(8,128)(2,1)S(1)} %pad_maximum_fusion.1), channel_id=1, source_target_pairs={{0,8},{8,0},{1,9},{9,1},{2,10},{10,2},{3,11},{11,3},{4,12},{12,4},... | collective-permute-start | bytes 2359304 | tf_op jit(solution)/shard_map/ppermute | solution.py:31
  13.1 44.7 %copy-start.18 = (pred[256,512]{0,1:T(8,128)(4,1)}, pred[256,512]{0,1:T(8,128)(4,1)S(1)}, u32[]{:S(2)}) copy-start(pred[256,512]{0,1:T(8,128)(4,1)S(1)} %pad_add_fusion) | copy-start | bytes 393220
  21.5 12.5 %collective-permute-start.1 = (bf16[96,640]{1,0:T(8,128)(2,1)S(1)}, bf16[96,640]{1,0:T(8,128)(2,1)S(1)}, u32[]{:S(2)}, u32[]{:S(2)}) collective-permute-start(bf16[96,640]{1,0:T(8,128)(2,1)S(1)} %maximum_select_fusion.2), channel_id=1, source_target_pairs={{0,16},{16,32},{32,48},{48,0},{1,17},{17,33},{33,49},{49,1},{2,18}... | collective-permute-start | bytes 368648 | tf_op jit(solution)/shard_map/ppermute | solution.py:27
  25.9 11.0 %collective-permute-start.2 = (bf16[96,640]{1,0:T(8,128)(2,1)S(1)}, bf16[96,640]{1,0:T(8,128)(2,1)S(1)}, u32[]{:S(2)}, u32[]{:S(2)}) collective-permute-start(bf16[96,640]{1,0:T(8,128)(2,1)S(1)} %maximum_select_fusion.2), channel_id=1, source_target_pairs={{0,32},{16,48},{32,0},{48,16},{1,33},{17,49},{33,1},{49,17},{2,34}... | collective-permute-start | bytes 368648 | tf_op jit(solution)/shard_map/ppermute | solution.py:27
  29.7 9.2 %collective-permute-start.3 = (bf16[96,640]{1,0:T(8,128)(2,1)S(1)}, bf16[96,640]{1,0:T(8,128)(2,1)S(1)}, u32[]{:S(2)}, u32[]{:S(2)}) collective-permute-start(bf16[96,640]{1,0:T(8,128)(2,1)S(1)} %maximum_select_fusion.2), channel_id=1, source_target_pairs={{0,48},{16,0},{32,16},{48,32},{1,49},{17,1},{33,17},{49,33},{2,50}... | collective-permute-start | bytes 368648 | tf_op jit(solution)/shard_map/ppermute | solution.py:27
  39.0 112.7 %collective-permute-start.6 = (bf16[2,512,384]{1,2,0:T(8,128)(2,1)S(1)}, bf16[2,512,384]{1,2,0:T(8,128)(2,1)S(1)}, u32[]{:S(2)}, u32[]{:S(2)}) collective-permute-start(bf16[2,512,384]{1,2,0:T(8,128)(2,1)S(1)} %pad_maximum_fusion.1), channel_id=1, source_target_pairs={{0,16},{16,32},{32,48},{48,64},{64,80},{80,96},{96,112},{112,128},... | collective-permute-start | bytes 2359304 | tf_op jit(solution)/shard_map/ppermute | solution.py:27
  40.9 111.5 %collective-permute-start.8 = (bf16[2,512,384]{1,2,0:T(8,128)(2,1)S(1)}, bf16[2,512,384]{1,2,0:T(8,128)(2,1)S(1)}, u32[]{:S(2)}, u32[]{:S(2)}) collective-permute-start(bf16[2,512,384]{1,2,0:T(8,128)(2,1)S(1)} %pad_maximum_fusion.1), channel_id=1, source_target_pairs={{0,32},{16,48},{32,64},{48,80},{64,96},{80,112},{96,128},{112,144}... | collective-permute-start | bytes 2359304 | tf_op jit(solution)/shard_map/ppermute | solution.py:27
  48.4 22.0 %collective-permute-start.9 = (bf16[2,512,384]{1,2,0:T(8,128)(2,1)S(1)}, bf16[2,512,384]{1,2,0:T(8,128)(2,1)S(1)}, u32[]{:S(2)}, u32[]{:S(2)}) collective-permute-start(bf16[2,512,384]{1,2,0:T(8,128)(2,1)S(1)} %pad_maximum_fusion.1), channel_id=1, source_target_pairs={{48,0},{64,16},{80,32},{96,48},{112,64},{128,80},{144,96},{160,112... | collective-permute-start | bytes 2359304 | tf_op jit(solution)/shard_map/ppermute | solution.py:27
  50.3 99.2 %collective-permute-start.10 = (bf16[2,512,384]{1,2,0:T(8,128)(2,1)S(1)}, bf16[2,512,384]{1,2,0:T(8,128)(2,1)S(1)}, u32[]{:S(2)}, u32[]{:S(2)}) collective-permute-start(bf16[2,512,384]{1,2,0:T(8,128)(2,1)S(1)} %pad_maximum_fusion.1), channel_id=1, source_target_pairs={{0,48},{16,64},{32,80},{48,96},{64,112},{80,128},{96,144},{112,160... | collective-permute-start | bytes 2359304 | tf_op jit(solution)/shard_map/ppermute | solution.py:27
  55.8 121.6 %collective-permute-start.5 = (bf16[2,512,384]{1,2,0:T(8,128)(2,1)S(1)}, bf16[2,512,384]{1,2,0:T(8,128)(2,1)S(1)}, u32[]{:S(2)}, u32[]{:S(2)}) collective-permute-start(bf16[2,512,384]{1,2,0:T(8,128)(2,1)S(1)} %pad_maximum_fusion.1), channel_id=1, source_target_pairs={{16,0},{32,16},{48,32},{64,48},{80,64},{96,80},{112,96},{128,112},... | collective-permute-start | bytes 2359304 | tf_op jit(solution)/shard_map/ppermute | solution.py:27
  70.4 117.8 %collective-permute-start.7 = (bf16[2,512,384]{1,2,0:T(8,128)(2,1)S(1)}, bf16[2,512,384]{1,2,0:T(8,128)(2,1)S(1)}, u32[]{:S(2)}, u32[]{:S(2)}) collective-permute-start(bf16[2,512,384]{1,2,0:T(8,128)(2,1)S(1)} %pad_maximum_fusion.1), channel_id=1, source_target_pairs={{32,0},{48,16},{64,32},{80,48},{96,64},{112,80},{128,96},{144,112}... | collective-permute-start | bytes 2359304 | tf_op jit(solution)/shard_map/ppermute | solution.py:27
  149.6 53.7 %collective-permute-start.16 = (bf16[384,640]{1,0:T(8,128)(2,1)S(1)}, bf16[384,640]{1,0:T(8,128)(2,1)S(1)}, u32[]{:S(2)}, u32[]{:S(2)}) collective-permute-start(bf16[384,640]{1,0:T(8,128)(2,1)S(1)} %bitcast.452), channel_id=1, source_target_pairs={{0,64},{64,128},{128,192},{192,256},{256,320},{320,384},{384,448},... | collective-permute-start | bytes 1474568 | tf_op jit(solution)/shard_map/ppermute | solution.py:124
  151.7 51.6 %collective-permute-start.19 = (bf16[384,640]{1,0:T(8,128)(2,1)S(1)}, bf16[384,640]{1,0:T(8,128)(2,1)S(1)}, u32[]{:S(2)}, u32[]{:S(2)}) collective-permute-start(bf16[384,640]{1,0:T(8,128)(2,1)S(1)} %bitcast.453), channel_id=1, source_target_pairs={{0,256},{64,320},{128,384},{192,448},{256,0},{320,64},{384,128},{4... | collective-permute-start | bytes 1474568 | tf_op jit(solution)/shard_map/ppermute | solution.py:124
  152.4 57.2 %collective-permute-start.18 = (bf16[384,640]{1,0:T(8,128)(2,1)S(1)}, bf16[384,640]{1,0:T(8,128)(2,1)S(1)}, u32[]{:S(2)}, u32[]{:S(2)}) collective-permute-start(bf16[384,640]{1,0:T(8,128)(2,1)S(1)} %bitcast.454), channel_id=1, source_target_pairs={{0,192},{64,256},{128,320},{192,384},{256,448},{320,0},{384,64},{4... | collective-permute-start | bytes 1474568 | tf_op jit(solution)/shard_map/ppermute | solution.py:124
  177.4 53.2 %collective-permute-start.17 = (bf16[384,640]{1,0:T(8,128)(2,1)S(1)}, bf16[384,640]{1,0:T(8,128)(2,1)S(1)}, u32[]{:S(2)}, u32[]{:S(2)}) collective-permute-start(bf16[384,640]{1,0:T(8,128)(2,1)S(1)} %bitcast.455), channel_id=1, source_target_pairs={{0,128},{64,192},{128,256},{192,320},{256,384},{320,448},{384,0},{... | collective-permute-start | bytes 1474568 | tf_op jit(solution)/shard_map/ppermute | solution.py:124
  189.0 49.2 %collective-permute-start.11 = (bf16[5,2,512,384]{2,3,1,0:T(8,128)(2,1)S(1)}, bf16[5,2,512,384]{2,3,1,0:T(8,128)(2,1)S(1)}, u32[]{:S(2)}, u32[]{:S(2)}) collective-permute-start(bf16[5,2,512,384]{2,3,1,0:T(8,128)(2,1)S(1)} %broadcast_select_fusion), channel_id=1, source_target_pairs={{0,8},{8,0},{1,9},{9,1},{2,10},{10,2},{3,11},{11,3},{4,12},{12,4},... | collective-permute-start | bytes 11796488 | tf_op jit(solution)/shard_map/ppermute | solution.py:31
  231.0 6.8 %collective-permute-start.20 = (bf16[4,384,640]{2,1,0:T(8,128)(2,1)S(1)}, bf16[4,384,640]{2,1,0:T(8,128)(2,1)S(1)}, u32[]{:S(2)}, u32[]{:S(2)}) collective-permute-start(bf16[4,384,640]{2,1,0:T(8,128)(2,1)S(1)} %pad_maximum_fusion), channel_id=1, source_target_pairs={{0,8},{8,0},{1,9},{9,1},{2,10},{10,2},{3,11},{11,3},{4,12},{12,4},... | collective-permute-start | bytes 5898248 | tf_op jit(solution)/shard_map/ppermute | solution.py:31
  254.6 11.8 %collective-permute-start.12 = (bf16[256,384]{0,1:T(8,128)(2,1)S(1)}, bf16[256,384]{0,1:T(8,128)(2,1)S(1)}, u32[]{:S(2)}, u32[]{:S(2)}) collective-permute-start(bf16[256,384]{0,1:T(8,128)(2,1)S(1)} %bitcast.501), channel_id=1, source_target_pairs={{0,4},{4,0},{1,5},{5,1},{2,6},{6,2},{3,7},{7,3},{8,12},{12,8},{9,1... | collective-permute-start | bytes 589832 | tf_op jit(solution)/shard_map/ppermute | solution.py:145
  266.5 11.2 %collective-permute-start.13 = (bf16[256,768]{0,1:T(8,128)(2,1)S(1)}, bf16[256,768]{0,1:T(8,128)(2,1)S(1)}, u32[]{:S(2)}, u32[]{:S(2)}) collective-permute-start(bf16[256,768]{0,1:T(8,128)(2,1)S(1)} %maximum_select_fusion), channel_id=1, source_target_pairs={{0,1},{1,2},{2,3},{3,0},{4,5},{5,6},{6,7},{7,4},{8,9},{9,10},{10,1... | collective-permute-start | bytes 1179656 | tf_op jit(solution)/shard_map/ppermute | solution.py:27
  269.7 12.4 %collective-permute-start.14 = (bf16[256,768]{0,1:T(8,128)(2,1)S(1)}, bf16[256,768]{0,1:T(8,128)(2,1)S(1)}, u32[]{:S(2)}, u32[]{:S(2)}) collective-permute-start(bf16[256,768]{0,1:T(8,128)(2,1)S(1)} %maximum_select_fusion), channel_id=1, source_target_pairs={{0,2},{1,3},{2,0},{3,1},{4,6},{5,7},{6,4},{7,5},{8,10},{9,11},{10,... | collective-permute-start | bytes 1179656 | tf_op jit(solution)/shard_map/ppermute | solution.py:27
  272.4 20.1 %collective-permute-start.15 = (bf16[256,768]{0,1:T(8,128)(2,1)S(1)}, bf16[256,768]{0,1:T(8,128)(2,1)S(1)}, u32[]{:S(2)}, u32[]{:S(2)}) collective-permute-start(bf16[256,768]{0,1:T(8,128)(2,1)S(1)} %maximum_select_fusion), channel_id=1, source_target_pairs={{0,3},{1,0},{2,1},{3,2},{4,7},{5,4},{6,5},{7,6},{8,11},{9,8},{10,9... | collective-permute-start | bytes 1179656 | tf_op jit(solution)/shard_map/ppermute | solution.py:27
  276.3 16.3 %copy-start.20 = (f32[256,640]{1,0:T(8,128)S(1)}, f32[256,640]{1,0:T(8,128)}, u32[]{:S(2)}) copy-start(f32[256,640]{1,0:T(8,128)} %fusion.142) | copy-start | bytes 1966084
  276.3 16.3 %copy-start.27 = (bf16[256,640]{1,0:T(8,128)(2,1)S(1)}, bf16[256,640]{1,0:T(8,128)(2,1)}, u32[]{:S(2)}) copy-start(bf16[256,640]{1,0:T(8,128)(2,1)} %param.17) | copy-start | bytes 983044
  (26 other events, 62.0 us)

commit v15 on v13

--- a/solution.py
+++ b/solution.py
@@ -205,15 +205,14 @@
         sign = 1 - 2 * core
         own_pair = swap_cores(packed)
         row_block = gather_weight(out_weight, sizes, is_first)
-        packed, own_pair = lax.optimization_barrier((packed, own_pair))
-        weight_full = spread_weight(row_block, sizes, is_first)
-
         carry_state = visit_block(
             empty_state(head_count, row_count), packed, seq_index, query_heads, query_clip, context
         )
         carry_state = visit_block(
             carry_state, own_pair, seq_index + sign, query_heads, query_clip, context
         )
+        packed, row_block, carry_state = lax.optimization_barrier((packed, row_block, carry_state))
+        weight_full = spread_weight(row_block, sizes, is_first)
         above = {}
         below = {}
         for d in range(1, 4):

time: 322 us -> 283 us (0.88)
  waiting for transfers between devices: 142 us -> 73.9 us
  starting transfers between devices: 123 us -> 152 us
    ppermute x4, starting transfers between devices: 15.7 us -> 87.8 us  [swap_cores(): return lax.ppermute(block, 'c', [(0, 1), (1, 0)])]
    ppermute x12, waiting for transfers between devices: 111 us -> 52.5 us  [shifted(): return lax.ppermute(block, axes, route)]
    ppermute x12, starting transfers between devices: 69.3 us -> 44.8 us  [shifted(): return lax.ppermute(block, axes, route)]
    ppermute x1, starting transfers between devices: 25 us -> 6.81 us  [gather_attention(): partner = lax.ppermute(attention_local, 'zh', [(0, 1), (1, 0)])]
    ppermute x4, waiting for transfers between devices: 27.3 us -> 13.9 us  [spread_weight(): received.append(lax.ppermute(row_block, ('y', 'c'), route))]
    dot_general x13, matrix products: 6.04 us -> 9.41 us  [attend(): jnp.einsum('hqk,khd->hqd', weights.astype(jnp.bfloat16), value_heads, pre...]
  transfers between devices with their start and end apart: 21 -> 21, of which waited for: 12 -> 11; matrix products, arithmetic and copies ran while one was open for 10% -> 11% of each run, Pallas kernels for 0% -> 0%
where the time goes in v15:
time: 283 us; the launch traced here: 282 us
  starting transfers between devices  152 us (54%)
  waiting for transfers between devices  73.9 us (26%)
  matrix products  21.2 us (7%)
  local copies, waits for them, and re-layouts  17.5 us (6%)
  other arithmetic  15.5 us (5%)
    ppermute x4, starting transfers between devices, swap_cores(): return lax.ppermute(block, 'c', [(0, 1), (1, 0)])  87.8 us
    ppermute x12, waiting for transfers between devices, shifted(): return lax.ppermute(block, axes, route)  52.5 us
    ppermute x12, starting transfers between devices, shifted(): return lax.ppermute(block, axes, route)  44.8 us
    ppermute x4, waiting for transfers between devices, spread_weight(): received.append(lax.ppermute(row_block, ('y', 'c'), route))  13.9 us
    ppermute x4, starting transfers between devices, spread_weight(): received.append(lax.ppermute(row_block, ('y', 'c'), route))  13 us
    dot_general x13, matrix products, attend(): jnp.einsum('hqk,khd->hqd', weights.astype(jnp.bfloat16), value_heads, pre...  9.41 us
    dot_general x13, matrix products, attend(): jnp.einsum('qhd,khd->hqk', query_heads, key_heads, preferred_element_type...  7.36 us
    ppermute x1, starting transfers between devices, gather_attention(): partner = lax.ppermute(attention_local, 'zh', [(0, 1), (1, 0)])  6.81 us
  transfers between devices with their start and end apart: 21, of which 11 were waited for; matrix products, arithmetic and copies ran while one was open for 11% of the time, Pallas kernels for 0%

profile of v15, /device:TPU:11, one launch (start us, length us, event | category | flops | bytes accessed | tf_op | source)
XLA Modules:
  0.0 282.1 jit_solution(14318224565043275140)
XLA Ops:
  0.0 2.8 %collective-permute-start = (bf16[48,640]{1,0:T(8,128)(2,1)}, bf16[48,640]{1,0:T(8,128)(2,1)S(1)}, u32[]{:S(2)}, u32[]{:S(2)}) collective-permute-start(bf16[48,640]{1,0:T(8,128)(2,1)} %param.18), channel_id=1, source_target_pairs={{0,8},{8,0},{1,9},{9,1},{2,10},{10,2},{3,11},{11,3},{4,12},{12,4},... | collective-permute-start | bytes 184328 | tf_op jit(solution)/shard_map/ppermute | solution.py:31
  18.7 4.0 %collective-permute-start.1 = (bf16[96,640]{1,0:T(8,128)(2,1)S(1)}, bf16[96,640]{1,0:T(8,128)(2,1)S(1)}, u32[]{:S(2)}, u32[]{:S(2)}) collective-permute-start(bf16[96,640]{1,0:T(8,128)(2,1)S(1)} %maximum_select_fusion.2), channel_id=1, source_target_pairs={{0,16},{16,32},{32,48},{48,0},{1,17},{17,33},{33,49},{49,1},{2,18}... | collective-permute-start | bytes 368648 | tf_op jit(solution)/shard_map/ppermute | solution.py:27
  23.1 5.8 %collective-permute-start.2 = (bf16[96,640]{1,0:T(8,128)(2,1)S(1)}, bf16[96,640]{1,0:T(8,128)(2,1)S(1)}, u32[]{:S(2)}, u32[]{:S(2)}) collective-permute-start(bf16[96,640]{1,0:T(8,128)(2,1)S(1)} %maximum_select_fusion.2), channel_id=1, source_target_pairs={{0,32},{16,48},{32,0},{48,16},{1,33},{17,49},{33,1},{49,17},{2,34}... | collective-permute-start | bytes 368648 | tf_op jit(solution)/shard_map/ppermute | solution.py:27
  28.9 2.2 collective-permute-start.3
  47.8 6.7 %collective-permute-start.18 = (bf16[384,640]{1,0:T(8,128)(2,1)}, bf16[384,640]{1,0:T(8,128)(2,1)S(1)}, u32[]{:S(2)}, u32[]{:S(2)}) collective-permute-start(bf16[384,640]{1,0:T(8,128)(2,1)} %bitcast.10), channel_id=1, source_target_pairs={{0,192},{64,256},{128,320},{192,384},{256,448},{320,0},{384,64},{4... | collective-permute-start | bytes 1474568 | tf_op jit(solution)/shard_map/ppermute | solution.py:124
  54.5 2.9 %collective-permute-start.17 = (bf16[384,640]{1,0:T(8,128)(2,1)}, bf16[384,640]{1,0:T(8,128)(2,1)S(1)}, u32[]{:S(2)}, u32[]{:S(2)}) collective-permute-start(bf16[384,640]{1,0:T(8,128)(2,1)} %bitcast.10), channel_id=1, source_target_pairs={{0,128},{64,192},{128,256},{192,320},{256,384},{320,448},{384,0},{... | collective-permute-start | bytes 1474568 | tf_op jit(solution)/shard_map/ppermute | solution.py:124
  60.2 3.9 %collective-permute-start.8 = (bf16[2,512,384]{1,2,0:T(8,128)(2,1)}, bf16[2,512,384]{1,2,0:T(8,128)(2,1)S(1)}, u32[]{:S(2)}, u32[]{:S(2)}) collective-permute-start(bf16[2,512,384]{1,2,0:T(8,128)(2,1)} %pad_maximum_fusion.1), channel_id=1, source_target_pairs={{0,32},{16,48},{32,64},{48,80},{64,96},{80,112},{96,128},{112,144}... | collective-permute-start | bytes 2359304 | tf_op jit(solution)/shard_map/ppermute | solution.py:27
  65.5 4.1 %collective-permute-start.10 = (bf16[2,512,384]{1,2,0:T(8,128)(2,1)}, bf16[2,512,384]{1,2,0:T(8,128)(2,1)S(1)}, u32[]{:S(2)}, u32[]{:S(2)}) collective-permute-start(bf16[2,512,384]{1,2,0:T(8,128)(2,1)} %pad_maximum_fusion.1), channel_id=1, source_target_pairs={{0,48},{16,64},{32,80},{48,96},{64,112},{80,128},{96,144},{112,160... | collective-permute-start | bytes 2359304 | tf_op jit(solution)/shard_map/ppermute | solution.py:27
  69.6 11.9 %collective-permute-done.18 = bf16[384,640]{1,0:T(8,128)(2,1)S(1)} collective-permute-done((bf16[384,640]{1,0:T(8,128)(2,1)}, bf16[384,640]{1,0:T(8,128)(2,1)S(1)}, u32[]{:S(2)}, u32[]{:S(2)}) %collective-permute-start.18) | collective-permute-done | bytes 491552 | tf_op jit(solution)/shard_map/ppermute | solution.py:124
  81.5 6.9 %collective-permute-start.5 = (bf16[2,512,384]{1,2,0:T(8,128)(2,1)}, bf16[2,512,384]{1,2,0:T(8,128)(2,1)S(1)}, u32[]{:S(2)}, u32[]{:S(2)}) collective-permute-start(bf16[2,512,384]{1,2,0:T(8,128)(2,1)} %pad_maximum_fusion.1), channel_id=1, source_target_pairs={{16,0},{32,16},{48,32},{64,48},{80,64},{96,80},{112,96},{128,112},... | collective-permute-start | bytes 2359304 | tf_op jit(solution)/shard_map/ppermute | solution.py:27
  90.5 4.1 %collective-permute-start.7 = (bf16[2,512,384]{1,2,0:T(8,128)(2,1)}, bf16[2,512,384]{1,2,0:T(8,128)(2,1)S(1)}, u32[]{:S(2)}, u32[]{:S(2)}) collective-permute-start(bf16[2,512,384]{1,2,0:T(8,128)(2,1)} %pad_maximum_fusion.1), channel_id=1, source_target_pairs={{32,0},{48,16},{64,32},{80,48},{96,64},{112,80},{128,96},{144,112}... | collective-permute-start | bytes 2359304 | tf_op jit(solution)/shard_map/ppermute | solution.py:27
  94.6 2.8 pad_maximum_fusion
  98.4 4.9 %collective-permute-done.6 = bf16[2,512,384]{1,2,0:T(8,128)(2,1)S(1)} collective-permute-done((bf16[2,512,384]{1,2,0:T(8,128)(2,1)}, bf16[2,512,384]{1,2,0:T(8,128)(2,1)S(1)}, u32[]{:S(2)}, u32[]{:S(2)}) %collective-permute-start.6) | collective-permute-done | bytes 786464 | tf_op jit(solution)/shard_map/ppermute | solution.py:27
  105.3 77.0 %collective-permute-start.20 = (bf16[4,384,640]{2,1,0:T(8,128)(2,1)}, bf16[4,384,640]{2,1,0:T(8,128)(2,1)S(1)}, u32[]{:S(2)}, u32[]{:S(2)}) collective-permute-start(bf16[4,384,640]{2,1,0:T(8,128)(2,1)} %pad_maximum_fusion), channel_id=1, source_target_pairs={{0,8},{8,0},{1,9},{9,1},{2,10},{10,2},{3,11},{11,3},{4,12},{12,4},... | collective-permute-start | bytes 5898248 | tf_op jit(solution)/shard_map/ppermute | solution.py:31
  182.6 27.6 %collective-permute-done.7 = bf16[2,512,384]{1,2,0:T(8,128)(2,1)S(1)} collective-permute-done((bf16[2,512,384]{1,2,0:T(8,128)(2,1)}, bf16[2,512,384]{1,2,0:T(8,128)(2,1)S(1)}, u32[]{:S(2)}, u32[]{:S(2)}) %collective-permute-start.7) | collective-permute-done | bytes 786464 | tf_op jit(solution)/shard_map/ppermute | solution.py:27
  210.9 6.0 %collective-permute-start.11 = (bf16[5,2,512,384]{2,3,1,0:T(8,128)(2,1)S(1)}, bf16[5,2,512,384]{2,3,1,0:T(8,128)(2,1)S(1)}, u32[]{:S(2)}, u32[]{:S(2)}) collective-permute-start(bf16[5,2,512,384]{2,3,1,0:T(8,128)(2,1)S(1)} %broadcast_select_fusion), channel_id=1, source_target_pairs={{0,8},{8,0},{1,9},{9,1},{2,10},{10,2},{3,11},{11,3},{4,12},{12,4},... | collective-permute-start | bytes 11796488 | tf_op jit(solution)/shard_map/ppermute | solution.py:31
  238.2 6.8 %collective-permute-start.12 = (bf16[256,384]{0,1:T(8,128)(2,1)S(1)}, bf16[256,384]{0,1:T(8,128)(2,1)S(1)}, u32[]{:S(2)}, u32[]{:S(2)}) collective-permute-start(bf16[256,384]{0,1:T(8,128)(2,1)S(1)} %bitcast.208), channel_id=1, source_target_pairs={{0,4},{4,0},{1,5},{5,1},{2,6},{6,2},{3,7},{7,3},{8,12},{12,8},{9,1... | collective-permute-start | bytes 589832 | tf_op jit(solution)/shard_map/ppermute | solution.py:145
  247.0 6.7 %collective-permute-done.12 = bf16[256,384]{0,1:T(8,128)(2,1)S(1)} collective-permute-done((bf16[256,384]{0,1:T(8,128)(2,1)S(1)}, bf16[256,384]{0,1:T(8,128)(2,1)S(1)}, u32[]{:S(2)}, u32[]{:S(2)}) %collective-permute-start.12) | collective-permute-done | bytes 196640 | tf_op jit(solution)/shard_map/ppermute | solution.py:145
  253.8 3.2 %collective-permute-start.13 = (bf16[256,768]{0,1:T(8,128)(2,1)S(1)}, bf16[256,768]{0,1:T(8,128)(2,1)S(1)}, u32[]{:S(2)}, u32[]{:S(2)}) collective-permute-start(bf16[256,768]{0,1:T(8,128)(2,1)S(1)} %maximum_select_fusion), channel_id=1, source_target_pairs={{0,1},{1,2},{2,3},{3,0},{4,5},{5,6},{6,7},{7,4},{8,9},{9,10},{10,1... | collective-permute-start | bytes 1179656 | tf_op jit(solution)/shard_map/ppermute | solution.py:27
  257.0 2.7 collective-permute-start.14
  259.7 4.0 %collective-permute-start.15 = (bf16[256,768]{0,1:T(8,128)(2,1)S(1)}, bf16[256,768]{0,1:T(8,128)(2,1)S(1)}, u32[]{:S(2)}, u32[]{:S(2)}) collective-permute-start(bf16[256,768]{0,1:T(8,128)(2,1)S(1)} %maximum_select_fusion), channel_id=1, source_target_pairs={{0,3},{1,0},{2,1},{3,2},{4,7},{5,4},{6,5},{7,6},{8,11},{9,8},{10,9... | collective-permute-start | bytes 1179656 | tf_op jit(solution)/shard_map/ppermute | solution.py:27
  264.4 4.4 %collective-permute-done.14 = bf16[256,768]{0,1:T(8,128)(2,1)S(1)} collective-permute-done((bf16[256,768]{0,1:T(8,128)(2,1)S(1)}, bf16[256,768]{0,1:T(8,128)(2,1)S(1)}, u32[]{:S(2)}, u32[]{:S(2)}) %collective-permute-start.14) | collective-permute-done | bytes 393248 | tf_op jit(solution)/shard_map/ppermute | solution.py:27
  268.9 11.0 %collective-permute-done.15 = bf16[256,768]{0,1:T(8,128)(2,1)S(1)} collective-permute-done((bf16[256,768]{0,1:T(8,128)(2,1)S(1)}, bf16[256,768]{0,1:T(8,128)(2,1)S(1)}, u32[]{:S(2)}, u32[]{:S(2)}) %collective-permute-start.15) | collective-permute-done | bytes 393248 | tf_op jit(solution)/shard_map/ppermute | solution.py:27
  279.9 2.1 fusion.27
  (222 shorter events, 66.1 us)
Async XLA Ops:
  0.0 18.6 %collective-permute-start = (bf16[48,640]{1,0:T(8,128)(2,1)}, bf16[48,640]{1,0:T(8,128)(2,1)S(1)}, u32[]{:S(2)}, u32[]{:S(2)}) collective-permute-start(bf16[48,640]{1,0:T(8,128)(2,1)} %param.18), channel_id=1, source_target_pairs={{0,8},{8,0},{1,9},{9,1},{2,10},{10,2},{3,11},{11,3},{4,12},{12,4},... | collective-permute-start | bytes 184328 | tf_op jit(solution)/shard_map/ppermute | solution.py:31
  9.8 28.8 %collective-permute-start.4 = (bf16[2,512,384]{1,2,0:T(8,128)(2,1)}, bf16[2,512,384]{1,2,0:T(8,128)(2,1)}, u32[]{:S(2)}, u32[]{:S(2)}) collective-permute-start(bf16[2,512,384]{1,2,0:T(8,128)(2,1)} %pad_maximum_fusion.1), channel_id=1, source_target_pairs={{0,8},{8,0},{1,9},{9,1},{2,10},{10,2},{3,11},{11,3},{4,12},{12,4},... | collective-permute-start | bytes 2359304 | tf_op jit(solution)/shard_map/ppermute | solution.py:31
  18.7 13.9 %collective-permute-start.1 = (bf16[96,640]{1,0:T(8,128)(2,1)S(1)}, bf16[96,640]{1,0:T(8,128)(2,1)S(1)}, u32[]{:S(2)}, u32[]{:S(2)}) collective-permute-start(bf16[96,640]{1,0:T(8,128)(2,1)S(1)} %maximum_select_fusion.2), channel_id=1, source_target_pairs={{0,16},{16,32},{32,48},{48,0},{1,17},{17,33},{33,49},{49,1},{2,18}... | collective-permute-start | bytes 368648 | tf_op jit(solution)/shard_map/ppermute | solution.py:27
  23.1 12.1 %collective-permute-start.2 = (bf16[96,640]{1,0:T(8,128)(2,1)S(1)}, bf16[96,640]{1,0:T(8,128)(2,1)S(1)}, u32[]{:S(2)}, u32[]{:S(2)}) collective-permute-start(bf16[96,640]{1,0:T(8,128)(2,1)S(1)} %maximum_select_fusion.2), channel_id=1, source_target_pairs={{0,32},{16,48},{32,0},{48,16},{1,33},{17,49},{33,1},{49,17},{2,34}... | collective-permute-start | bytes 368648 | tf_op jit(solution)/shard_map/ppermute | solution.py:27
  28.9 9.1 %collective-permute-start.3 = (bf16[96,640]{1,0:T(8,128)(2,1)S(1)}, bf16[96,640]{1,0:T(8,128)(2,1)S(1)}, u32[]{:S(2)}, u32[]{:S(2)}) collective-permute-start(bf16[96,640]{1,0:T(8,128)(2,1)S(1)} %maximum_select_fusion.2), channel_id=1, source_target_pairs={{0,48},{16,0},{32,16},{48,32},{1,49},{17,1},{33,17},{49,33},{2,50}... | collective-permute-start | bytes 368648 | tf_op jit(solution)/shard_map/ppermute | solution.py:27
  43.5 16.7 %collective-permute-start.16 = (bf16[384,640]{1,0:T(8,128)(2,1)}, bf16[384,640]{1,0:T(8,128)(2,1)}, u32[]{:S(2)}, u32[]{:S(2)}) collective-permute-start(bf16[384,640]{1,0:T(8,128)(2,1)} %bitcast.10), channel_id=1, source_target_pairs={{0,64},{64,128},{128,192},{192,256},{256,320},{320,384},{384,448},... | collective-permute-start | bytes 1474568 | tf_op jit(solution)/shard_map/ppermute | solution.py:124
  46.3 19.2 %collective-permute-start.19 = (bf16[384,640]{1,0:T(8,128)(2,1)}, bf16[384,640]{1,0:T(8,128)(2,1)}, u32[]{:S(2)}, u32[]{:S(2)}) collective-permute-start(bf16[384,640]{1,0:T(8,128)(2,1)} %bitcast.10), channel_id=1, source_target_pairs={{0,256},{64,320},{128,384},{192,448},{256,0},{320,64},{384,128},{4... | collective-permute-start | bytes 1474568 | tf_op jit(solution)/shard_map/ppermute | solution.py:124
  47.8 33.7 %collective-permute-start.18 = (bf16[384,640]{1,0:T(8,128)(2,1)}, bf16[384,640]{1,0:T(8,128)(2,1)S(1)}, u32[]{:S(2)}, u32[]{:S(2)}) collective-permute-start(bf16[384,640]{1,0:T(8,128)(2,1)} %bitcast.10), channel_id=1, source_target_pairs={{0,192},{64,256},{128,320},{192,384},{256,448},{320,0},{384,64},{4... | collective-permute-start | bytes 1474568 | tf_op jit(solution)/shard_map/ppermute | solution.py:124
  54.5 36.0 %collective-permute-start.17 = (bf16[384,640]{1,0:T(8,128)(2,1)}, bf16[384,640]{1,0:T(8,128)(2,1)S(1)}, u32[]{:S(2)}, u32[]{:S(2)}) collective-permute-start(bf16[384,640]{1,0:T(8,128)(2,1)} %bitcast.10), channel_id=1, source_target_pairs={{0,128},{64,192},{128,256},{192,320},{256,384},{320,448},{384,0},{... | collective-permute-start | bytes 1474568 | tf_op jit(solution)/shard_map/ppermute | solution.py:124
  58.1 45.3 %collective-permute-start.6 = (bf16[2,512,384]{1,2,0:T(8,128)(2,1)}, bf16[2,512,384]{1,2,0:T(8,128)(2,1)S(1)}, u32[]{:S(2)}, u32[]{:S(2)}) collective-permute-start(bf16[2,512,384]{1,2,0:T(8,128)(2,1)} %pad_maximum_fusion.1), channel_id=1, source_target_pairs={{0,16},{16,32},{32,48},{48,64},{64,80},{80,96},{96,112},{112,128},... | collective-permute-start | bytes 2359304 | tf_op jit(solution)/shard_map/ppermute | solution.py:27
  60.2 45.1 %collective-permute-start.8 = (bf16[2,512,384]{1,2,0:T(8,128)(2,1)}, bf16[2,512,384]{1,2,0:T(8,128)(2,1)S(1)}, u32[]{:S(2)}, u32[]{:S(2)}) collective-permute-start(bf16[2,512,384]{1,2,0:T(8,128)(2,1)} %pad_maximum_fusion.1), channel_id=1, source_target_pairs={{0,32},{16,48},{32,64},{48,80},{64,96},{80,112},{96,128},{112,144}... | collective-permute-start | bytes 2359304 | tf_op jit(solution)/shard_map/ppermute | solution.py:27
  65.5 116.8 %collective-permute-start.10 = (bf16[2,512,384]{1,2,0:T(8,128)(2,1)}, bf16[2,512,384]{1,2,0:T(8,128)(2,1)S(1)}, u32[]{:S(2)}, u32[]{:S(2)}) collective-permute-start(bf16[2,512,384]{1,2,0:T(8,128)(2,1)} %pad_maximum_fusion.1), channel_id=1, source_target_pairs={{0,48},{16,64},{32,80},{48,96},{64,112},{80,128},{96,144},{112,160... | collective-permute-start | bytes 2359304 | tf_op jit(solution)/shard_map/ppermute | solution.py:27
  81.5 100.9 %collective-permute-start.5 = (bf16[2,512,384]{1,2,0:T(8,128)(2,1)}, bf16[2,512,384]{1,2,0:T(8,128)(2,1)S(1)}, u32[]{:S(2)}, u32[]{:S(2)}) collective-permute-start(bf16[2,512,384]{1,2,0:T(8,128)(2,1)} %pad_maximum_fusion.1), channel_id=1, source_target_pairs={{16,0},{32,16},{48,32},{64,48},{80,64},{96,80},{112,96},{128,112},... | collective-permute-start | bytes 2359304 | tf_op jit(solution)/shard_map/ppermute | solution.py:27
  90.5 119.7 %collective-permute-start.7 = (bf16[2,512,384]{1,2,0:T(8,128)(2,1)}, bf16[2,512,384]{1,2,0:T(8,128)(2,1)S(1)}, u32[]{:S(2)}, u32[]{:S(2)}) collective-permute-start(bf16[2,512,384]{1,2,0:T(8,128)(2,1)} %pad_maximum_fusion.1), channel_id=1, source_target_pairs={{32,0},{48,16},{64,32},{80,48},{96,64},{112,80},{128,96},{144,112}... | collective-permute-start | bytes 2359304 | tf_op jit(solution)/shard_map/ppermute | solution.py:27
  103.3 107.0 %collective-permute-start.9 = (bf16[2,512,384]{1,2,0:T(8,128)(2,1)}, bf16[2,512,384]{1,2,0:T(8,128)(2,1)S(1)}, u32[]{:S(2)}, u32[]{:S(2)}) collective-permute-start(bf16[2,512,384]{1,2,0:T(8,128)(2,1)} %pad_maximum_fusion.1), channel_id=1, source_target_pairs={{48,0},{64,16},{80,32},{96,48},{112,64},{128,80},{144,96},{160,112... | collective-permute-start | bytes 2359304 | tf_op jit(solution)/shard_map/ppermute | solution.py:27
  105.3 115.7 %collective-permute-start.20 = (bf16[4,384,640]{2,1,0:T(8,128)(2,1)}, bf16[4,384,640]{2,1,0:T(8,128)(2,1)S(1)}, u32[]{:S(2)}, u32[]{:S(2)}) collective-permute-start(bf16[4,384,640]{2,1,0:T(8,128)(2,1)} %pad_maximum_fusion), channel_id=1, source_target_pairs={{0,8},{8,0},{1,9},{9,1},{2,10},{10,2},{3,11},{11,3},{4,12},{12,4},... | collective-permute-start | bytes 5898248 | tf_op jit(solution)/shard_map/ppermute | solution.py:31
  210.9 12.3 %collective-permute-start.11 = (bf16[5,2,512,384]{2,3,1,0:T(8,128)(2,1)S(1)}, bf16[5,2,512,384]{2,3,1,0:T(8,128)(2,1)S(1)}, u32[]{:S(2)}, u32[]{:S(2)}) collective-permute-start(bf16[5,2,512,384]{2,3,1,0:T(8,128)(2,1)S(1)} %broadcast_select_fusion), channel_id=1, source_target_pairs={{0,8},{8,0},{1,9},{9,1},{2,10},{10,2},{3,11},{11,3},{4,12},{12,4},... | collective-permute-start | bytes 11796488 | tf_op jit(solution)/shard_map/ppermute | solution.py:31
  238.2 15.4 %collective-permute-start.12 = (bf16[256,384]{0,1:T(8,128)(2,1)S(1)}, bf16[256,384]{0,1:T(8,128)(2,1)S(1)}, u32[]{:S(2)}, u32[]{:S(2)}) collective-permute-start(bf16[256,384]{0,1:T(8,128)(2,1)S(1)} %bitcast.208), channel_id=1, source_target_pairs={{0,4},{4,0},{1,5},{5,1},{2,6},{6,2},{3,7},{7,3},{8,12},{12,8},{9,1... | collective-permute-start | bytes 589832 | tf_op jit(solution)/shard_map/ppermute | solution.py:145
  253.6 26.2 %copy-start.17 = (bf16[256,640]{1,0:T(8,128)(2,1)S(1)}, bf16[256,640]{1,0:T(8,128)(2,1)}, u32[]{:S(2)}) copy-start(bf16[256,640]{1,0:T(8,128)(2,1)} %param.17) | copy-start | bytes 983044
  253.8 10.6 %collective-permute-start.13 = (bf16[256,768]{0,1:T(8,128)(2,1)S(1)}, bf16[256,768]{0,1:T(8,128)(2,1)S(1)}, u32[]{:S(2)}, u32[]{:S(2)}) collective-permute-start(bf16[256,768]{0,1:T(8,128)(2,1)S(1)} %maximum_select_fusion), channel_id=1, source_target_pairs={{0,1},{1,2},{2,3},{3,0},{4,5},{5,6},{6,7},{7,4},{8,9},{9,10},{10,1... | collective-permute-start | bytes 1179656 | tf_op jit(solution)/shard_map/ppermute | solution.py:27
  257.0 11.9 %collective-permute-start.14 = (bf16[256,768]{0,1:T(8,128)(2,1)S(1)}, bf16[256,768]{0,1:T(8,128)(2,1)S(1)}, u32[]{:S(2)}, u32[]{:S(2)}) collective-permute-start(bf16[256,768]{0,1:T(8,128)(2,1)S(1)} %maximum_select_fusion), channel_id=1, source_target_pairs={{0,2},{1,3},{2,0},{3,1},{4,6},{5,7},{6,4},{7,5},{8,10},{9,11},{10,... | collective-permute-start | bytes 1179656 | tf_op jit(solution)/shard_map/ppermute | solution.py:27
  259.7 20.1 %collective-permute-start.15 = (bf16[256,768]{0,1:T(8,128)(2,1)S(1)}, bf16[256,768]{0,1:T(8,128)(2,1)S(1)}, u32[]{:S(2)}, u32[]{:S(2)}) collective-permute-start(bf16[256,768]{0,1:T(8,128)(2,1)S(1)} %maximum_select_fusion), channel_id=1, source_target_pairs={{0,3},{1,0},{2,1},{3,2},{4,7},{5,4},{6,5},{7,6},{8,11},{9,8},{10,9... | collective-permute-start | bytes 1179656 | tf_op jit(solution)/shard_map/ppermute | solution.py:27
  263.7 16.2 %copy-start.3 = (bf16[8,384,640]{2,1,0:T(8,128)(2,1)S(1)}, bf16[8,384,640]{2,1,0:T(8,128)(2,1)}, u32[]{:S(2)}) copy-start(bf16[8,384,640]{2,1,0:T(8,128)(2,1)} %fusion.116) | copy-start | bytes 11796484
  263.8 16.1 %copy-start.11 = (f32[256,640]{1,0:T(8,128)S(1)}, f32[256,640]{1,0:T(8,128)}, u32[]{:S(2)}) copy-start(f32[256,640]{1,0:T(8,128)} %fusion.142) | copy-start | bytes 1966084
  (16 other events, 48.0 us)
